TPU v7x, 32 devices: a whole 2x2x4 slice. The times are simulated.
32 devices in a mesh: scene: 8 (over y, x, core), seq: 4 (over z).
Axes of the slice: x: 2, y: 2, z: 4, core: 2. Of those that a mesh axis runs over, the one named last changes fastest.
Arguments:
- tokens: bfloat16 [24576, 1024], P(('scene', 'seq')), may hold values from -6 to 6
- image_count: int32 [8], P('scene'), may hold values from 576 to 2304, as said below
- norm_params: float32 [1024, 4], P('scene'), may hold values from -1.5 to 1.5, as said below
- w_qkv: float32 [1024, 3072], P('scene'), may hold values from -0.1875 to 0.1875
- w_proj: float32 [1024, 1024], P('scene'), may hold values from -6 to 6
- w_fc1: float32 [1024, 4096], P('scene'), may hold values from -0.1875 to 0.1875
- w_fc2: float32 [4096, 1024], P('scene'), may hold values from -0.09375 to 0.09375
- w_unpatch: float32 [1024, 128], P('scene'), may hold values from -0.1875 to 0.1875
- w_dec1: float32 [32, 64], replicated, may hold values from -0.375 to 0.375
- b_dec1: float32 [64], replicated, may hold values from -3 to 3
- w_dec2: float32 [64, 4], replicated, may hold values from -0.75 to 0.75
- cot_out: bfloat16 [24576, 1024], P(('scene', 'seq')), may hold values from -6 to 6
- cot_dec: bfloat16 [2048, 16], P(('scene', 'seq')), may hold values from -6 to 6
Outputs:
- block_out: bfloat16 [24576, 1024], P(('scene', 'seq'))
- decoded: float32 [2048, 16], P(('scene', 'seq'))
- grad_tokens: bfloat16 [24576, 1024], P(('scene', 'seq'))
- grad_norm_one: float32 [1024, 2], P('scene')
- grad_norm_two: float32 [1024, 2], P('scene')
- grad_qkv: float32 [1024, 3072], P('scene')
- grad_proj: float32 [1024, 1024], P('scene')
- grad_fc1: float32 [1024, 4096], P('scene')
- grad_fc2: float32 [4096, 1024], P('scene')
- grad_unpatch: float32 [1024, 128], P('scene')
- grad_dec1: float32 [32, 64], replicated
- grad_bdec1: float32 [64], replicated
- grad_dec2: float32 [64, 4], replicated
Inputs may be any that keep to these rules, and one draw needn't show every extreme that they name: `image_count`: each scene has either 576 or 2304 image tokens, and some scene has each. `norm_params`: columns 0 and 2 are gains, columns 1 and 3 biases.
All inputs are finite; a program needn't handle non-finite values.
Results may differ from a plain program's by a relative error of at most 0.028.
The roundings to bfloat16 on the way count: a program that leaves them out, or rounds other values in their place, can miss the bound.
Values may be sent and summed in bfloat16 or wider, within the bound.
No kernel may reach another device: no remote copies, remote signals or barrier semaphores. Data moves between devices by JAX's collectives and lax.ppermute only.
A program may use at most 256 MiB of HBM per device.

v0:
```python
import jax
import jax.numpy as jnp
from jax import lax
from jax.sharding import PartitionSpec as P

H = 16
TF = 32
PP = 4
OUT = 4
TG = 16
IMG_DEV = 576


EPS = 1e-05
NEG_FILL = -1e30


def layer_norm(rows_in, gain, shift):
    center = rows_in - jnp.mean(rows_in, axis=-1, keepdims=True)
    spread = jnp.mean(center * center, axis=-1, keepdims=True)
    return center * lax.rsqrt(spread + EPS) * gain + shift


def gelu_exact(values_in):
    return jax.nn.gelu(values_in, approximate=False)


def contract_last(left, right):
    return lax.dot_general(
        left, right, (((1,), (1,)), ((), ())), preferred_element_type=jnp.float32
    )


def contract_first(left, right):
    return lax.dot_general(
        left, right, (((0,), (0,)), ((), ())), preferred_element_type=jnp.float32
    )


def split_heads(rows_in, head_dim):
    return rows_in.reshape(rows_in.shape[0], H, head_dim).transpose(1, 0, 2)


def join_heads(head_rows):
    return head_rows.transpose(1, 0, 2).reshape(
        head_rows.shape[1], head_rows.shape[0] * head_rows.shape[2]
    )


def per_device(
    tokens,
    image_count,
    norm_params,
    w_qkv,
    w_proj,
    w_fc1,
    w_fc2,
    w_unpatch,
    w_dec1,
    b_dec1,
    w_dec2,
    cot_out,
    cot_dec,
):
    seq_count = lax.axis_size("seq")
    seq_rank = lax.axis_index("seq")
    tok_rows = tokens.shape[0]
    model_width = tokens.shape[1]
    head_dim = model_width // H
    score_scale = head_dim ** (-0.5)
    full_rows = tok_rows * seq_count
    plane_cells = TG * TG
    cells_dev = plane_cells // seq_count
    first_cell = seq_rank * cells_dev
    live_image = image_count[0] // seq_count
    local_pos = jnp.arange(tok_rows, dtype=jnp.int32)
    row_live = (local_pos >= IMG_DEV) | (local_pos < live_image)
    key_pos = jnp.arange(full_rows, dtype=jnp.int32) % tok_rows
    key_live = (key_pos >= IMG_DEV) | (key_pos < live_image)
    norm_low, qkv_w, proj_w, fc1_w, fc2_w, unpatch_w = (
        lax.all_gather(norm_params.astype(jnp.bfloat16), "scene", axis=0, tiled=True),
        lax.all_gather(w_qkv.astype(jnp.bfloat16), "scene", axis=0, tiled=True),
        lax.all_gather(w_proj.astype(jnp.bfloat16), "scene", axis=0, tiled=True),
        lax.all_gather(w_fc1.astype(jnp.bfloat16), "scene", axis=0, tiled=True),
        lax.all_gather(w_fc2.astype(jnp.bfloat16), "scene", axis=0, tiled=True),
        lax.all_gather(w_unpatch.astype(jnp.bfloat16), "scene", axis=0, tiled=True),
    )
    norm_full = norm_low.astype(jnp.float32)
    inputs_f = tokens.astype(jnp.float32)
    normed_one, norm_one_pull = jax.vjp(layer_norm, inputs_f, norm_full[:, 0], norm_full[:, 1])
    normed_one_b = normed_one.astype(jnp.bfloat16)
    qkv_rows = jnp.dot(normed_one_b, qkv_w, preferred_element_type=jnp.float32).astype(jnp.bfloat16)
    query_rows = qkv_rows[:, :model_width]
    key_rows = qkv_rows[:, model_width : 2 * model_width]
    value_rows = qkv_rows[:, 2 * model_width :]
    keys_all, values_all = (
        lax.all_gather(key_rows, "seq", axis=0, tiled=True),
        lax.all_gather(value_rows, "seq", axis=0, tiled=True),
    )
    query_heads = split_heads(query_rows, head_dim)
    key_heads = split_heads(keys_all, head_dim)
    value_heads = split_heads(values_all, head_dim)

    def head_scores(queries, key_block):
        raw_scores = (
            jnp.einsum("qd,kd->qk", queries, key_block, preferred_element_type=jnp.float32)
            * score_scale
        )
        return jnp.where(key_live[None, :], raw_scores, NEG_FILL)

    def head_forward(parts):
        queries, key_block, value_block = parts
        scores = head_scores(queries, key_block)
        row_peak = jnp.max(scores, axis=1, keepdims=True)
        exponent = jnp.exp(scores - row_peak)
        row_total = jnp.sum(exponent, axis=1, keepdims=True)
        attn_probs = (exponent / row_total).astype(jnp.bfloat16)
        return (
            jnp.dot(attn_probs, value_block, preferred_element_type=jnp.float32),
            row_peak,
            row_total,
        )

    head_out, row_peaks, row_totals = lax.map(head_forward, (query_heads, key_heads, value_heads))
    mixed_rows = join_heads(head_out).astype(jnp.bfloat16)
    middle = inputs_f + jnp.dot(mixed_rows, proj_w, preferred_element_type=jnp.float32)
    normed_two, norm_two_pull = jax.vjp(layer_norm, middle, norm_full[:, 2], norm_full[:, 3])
    normed_two_b = normed_two.astype(jnp.bfloat16)
    pre_act = jnp.dot(normed_two_b, fc1_w, preferred_element_type=jnp.float32)
    activated, gelu_pull = jax.vjp(gelu_exact, pre_act)
    activated_b = activated.astype(jnp.bfloat16)
    result = jnp.where(
        row_live[:, None],
        middle + jnp.dot(activated_b, fc2_w, preferred_element_type=jnp.float32),
        0.0,
    )
    block_out = result.astype(jnp.bfloat16)
    triplane = result[IMG_DEV:].astype(jnp.bfloat16)
    planes = jnp.dot(triplane, unpatch_w, preferred_element_type=jnp.float32).astype(jnp.bfloat16)
    all_planes = lax.all_gather(planes, "seq", axis=0, tiled=True)

    def take_plane(offset):
        return lax.dynamic_slice_in_dim(all_planes, offset + first_cell, cells_dev, 0).astype(
            jnp.float32
        )

    point_feat = (take_plane(0) + take_plane(plane_cells) + take_plane(2 * plane_cells)).reshape(
        cells_dev * PP, TF
    )
    hidden_pre = (
        jnp.dot(
            point_feat, w_dec1, precision=lax.Precision.HIGHEST, preferred_element_type=jnp.float32
        )
        + b_dec1
    )
    hidden_act, dec_gelu_pull = jax.vjp(gelu_exact, hidden_pre)
    decoded_flat = jnp.dot(
        hidden_act, w_dec2, precision=lax.Precision.HIGHEST, preferred_element_type=jnp.float32
    )
    decoded = (
        decoded_flat.reshape(cells_dev, PP, OUT).transpose(0, 2, 1).reshape(cells_dev, OUT * PP)
    )
    grad_dec = (
        cot_dec.astype(jnp.float32)
        .reshape(cells_dev, OUT, PP)
        .transpose(0, 2, 1)
        .reshape(cells_dev * PP, OUT)
    )
    grad_w2 = lax.dot_general(
        hidden_act,
        grad_dec,
        (((0,), (0,)), ((), ())),
        precision=lax.Precision.HIGHEST,
        preferred_element_type=jnp.float32,
    )
    grad_act = lax.dot_general(
        grad_dec,
        w_dec2,
        (((1,), (1,)), ((), ())),
        precision=lax.Precision.HIGHEST,
        preferred_element_type=jnp.float32,
    )
    (grad_hidden,) = dec_gelu_pull(grad_act)
    grad_b1 = jnp.sum(grad_hidden, axis=0)
    grad_w1 = lax.dot_general(
        point_feat,
        grad_hidden,
        (((0,), (0,)), ((), ())),
        precision=lax.Precision.HIGHEST,
        preferred_element_type=jnp.float32,
    )
    grad_feat = lax.dot_general(
        grad_hidden,
        w_dec1,
        (((1,), (1,)), ((), ())),
        precision=lax.Precision.HIGHEST,
        preferred_element_type=jnp.float32,
    )
    grad_feat = grad_feat.reshape(cells_dev, PP * TF)
    spread_back = jnp.zeros((3 * plane_cells, PP * TF), jnp.float32)
    for offset in (0, plane_cells, 2 * plane_cells):
        spread_back = lax.dynamic_update_slice_in_dim(
            spread_back, grad_feat, offset + first_cell, 0
        )
    plane_grad = lax.psum_scatter(
        spread_back.astype(jnp.bfloat16), "seq", scatter_dimension=0, tiled=True
    )
    grad_unpatch = contract_first(triplane, plane_grad)
    grad_tri = contract_last(plane_grad, unpatch_w)
    dec_grads = lax.psum((grad_w1, grad_b1, grad_w2), ("scene", "seq"))
    grad_result = jnp.where(row_live[:, None], cot_out.astype(jnp.float32), 0.0)
    grad_result = jnp.concatenate([grad_result[:IMG_DEV], grad_result[IMG_DEV:] + grad_tri], axis=0)
    branch_grad = grad_result.astype(jnp.bfloat16)
    grad_fc2 = contract_first(activated_b, branch_grad)
    (grad_pre,) = gelu_pull(contract_last(branch_grad, fc2_w))
    pre_grad = grad_pre.astype(jnp.bfloat16)
    grad_fc1 = contract_first(normed_two_b, pre_grad)
    grad_mid_norm, grad_gain_two, grad_shift_two = norm_two_pull(contract_last(pre_grad, fc1_w))
    grad_mid = grad_result + grad_mid_norm
    mid_grad = grad_mid.astype(jnp.bfloat16)
    grad_proj = contract_first(mixed_rows, mid_grad)
    grad_mixed = contract_last(mid_grad, proj_w).astype(jnp.bfloat16)
    grad_mixed_heads = split_heads(grad_mixed, head_dim)

    def head_backward(parts):
        queries, key_block, value_block, grad_out, row_peak, row_total = parts
        scores = head_scores(queries, key_block)
        attn_probs = jnp.exp(scores - row_peak) / row_total
        grad_probs = jnp.einsum(
            "qd,kd->qk", grad_out, value_block, preferred_element_type=jnp.float32
        )
        row_inner = jnp.sum(attn_probs * grad_probs, axis=1, keepdims=True)
        grad_scores = (attn_probs * (grad_probs - row_inner)).astype(jnp.bfloat16)
        grad_query = (
            jnp.dot(grad_scores, key_block, preferred_element_type=jnp.float32) * score_scale
        )
        grad_keys = (
            jnp.einsum("qk,qd->kd", grad_scores, queries, preferred_element_type=jnp.float32)
            * score_scale
        )
        grad_values = jnp.einsum(
            "qk,qd->kd",
            attn_probs.astype(jnp.bfloat16),
            grad_out,
            preferred_element_type=jnp.float32,
        )
        return (grad_query, grad_keys, grad_values)

    grad_query_h, grad_keys_h, grad_values_h = lax.map(
        head_backward,
        (query_heads, key_heads, value_heads, grad_mixed_heads, row_peaks, row_totals),
    )
    own_keys, own_values = (
        lax.psum_scatter(
            join_heads(grad_keys_h).astype(jnp.bfloat16), "seq", scatter_dimension=0, tiled=True
        ).astype(jnp.float32),
        lax.psum_scatter(
            join_heads(grad_values_h).astype(jnp.bfloat16), "seq", scatter_dimension=0, tiled=True
        ).astype(jnp.float32),
    )
    grad_qkv_rows = jnp.concatenate(
        [join_heads(grad_query_h), own_keys, own_values], axis=1
    ).astype(jnp.bfloat16)
    grad_qkv = contract_first(normed_one_b, grad_qkv_rows)
    grad_in_norm, grad_gain_one, grad_shift_one = norm_one_pull(contract_last(grad_qkv_rows, qkv_w))
    grad_tokens = (grad_mid + grad_in_norm).astype(jnp.bfloat16)
    grad_norm = jnp.stack([grad_gain_one, grad_shift_one, grad_gain_two, grad_shift_two], axis=1)
    owned_grads = (
        lax.psum_scatter(grad_norm, "scene", scatter_dimension=0, tiled=True),
        lax.psum_scatter(grad_qkv, "scene", scatter_dimension=0, tiled=True),
        lax.psum_scatter(grad_proj, "scene", scatter_dimension=0, tiled=True),
        lax.psum_scatter(grad_fc1, "scene", scatter_dimension=0, tiled=True),
        lax.psum_scatter(grad_fc2, "scene", scatter_dimension=0, tiled=True),
        lax.psum_scatter(grad_unpatch, "scene", scatter_dimension=0, tiled=True),
    )
    norm_part, qkv_part, proj_part, fc1_part, fc2_part, unpatch_part = owned_grads
    owned_grads = (
        lax.psum(norm_part.astype(jnp.bfloat16), "seq").astype(jnp.float32),
        lax.psum(qkv_part.astype(jnp.bfloat16), "seq").astype(jnp.float32),
        lax.psum(proj_part.astype(jnp.bfloat16), "seq").astype(jnp.float32),
        lax.psum(fc1_part.astype(jnp.bfloat16), "seq").astype(jnp.float32),
        lax.psum(fc2_part.astype(jnp.bfloat16), "seq").astype(jnp.float32),
        lax.psum(unpatch_part.astype(jnp.bfloat16), "seq").astype(jnp.float32),
    )
    owned_norm = owned_grads[0]
    return (
        block_out,
        decoded,
        grad_tokens,
        owned_norm[:, :2],
        owned_norm[:, 2:],
        owned_grads[1],
        owned_grads[2],
        owned_grads[3],
        owned_grads[4],
        owned_grads[5],
        dec_grads[0],
        dec_grads[1],
        dec_grads[2],
    )


def solution(mesh):
    in_specs = (
        P(("scene", "seq"), None),
        P("scene"),
        P("scene", None),
        P("scene", None),
        P("scene", None),
        P("scene", None),
        P("scene", None),
        P("scene", None),
        P(),
        P(),
        P(),
        P(("scene", "seq"), None),
        P(("scene", "seq"), None),
    )
    out_specs = (
        P(("scene", "seq"), None),
        P(("scene", "seq"), None),
        P(("scene", "seq"), None),
        P("scene", None),
        P("scene", None),
        P("scene", None),
        P("scene", None),
        P("scene", None),
        P("scene", None),
        P("scene", None),
        P(),
        P(),
        P(),
    )
    return jax.shard_map(
        per_device, mesh=mesh, in_specs=in_specs, out_specs=out_specs, check_vma=False
    )
```

profile of v0, /device:TPU:0, one launch (start us, length us, event | category | flops | bytes accessed | tf_op | source)
XLA Modules:
  0.0 1995.5 jit_solution(2982431660007807180)
XLA Ops:
  10.5 10.4 all_gather.27
  23.9 34.7 %all-gather.7.cloned.1.call-done = bf16[1024,3072]{1,0:T(8,128)(2,1)} async-done(((bf16[128,3072]{1,0:T(8,128)(2,1)}), bf16[1024,3072]{1,0:T(8,128)(2,1)}) %all-gather.7.cloned.1.call-update) | async-done | bytes 6291472 | tf_op jit(solution)/shard_map/all_gather | solution.py:82
  58.6 8.4 convolution_convert_fusion
  77.7 10.4 all_gather.34
  93.6 91.1 %all-gather.9.cloned.1.call-done = bf16[3072,1024]{1,0:T(8,128)(2,1)} async-done(((bf16[768,1024]{1,0:T(8,128)(2,1)}), bf16[3072,1024]{1,0:T(8,128)(2,1)}) %all-gather.9.cloned.1.call-update) | async-done | bytes 6291472 | tf_op jit(solution)/shard_map/all_gather | solution.py:97
  184.7 8.8 copy.59
  193.5 12.1 copy.62
  205.6 94.8 %all-gather.11.cloned.1.call-done = bf16[3072,1024]{1,0:T(8,128)(2,1)} async-done(((bf16[768,1024]{1,0:T(8,128)(2,1)}), bf16[3072,1024]{1,0:T(8,128)(2,1)}) %all-gather.11.cloned.1.call-update) | async-done | bytes 6291472 | tf_op jit(solution)/shard_map/all_gather | solution.py:98
  300.4 8.7 copy.60
  309.1 12.2 copy.63
  322.6 156.4 %while.30 = (s32[]{:T(128)}, bf16[16,768,64]{1,2,0:T(8,128)(2,1)}, f32[16,768,1]{1,2,0:T(1,128)}, f32[16,768,1]{1,2,0:T(1,128)}, bf16[16,768,64]{2,1,0:T(8,128)(...) while((s32[]{:T(128)}, bf16[16,768,64]{1,2,0:T(8,128)(2,1)}, ...), condition=%wide.region_5.6_spmd.clone, body=%wide.region_2.5_spmd.clone.sunk | while | flops 632317440 | bytes 30319724 | solution.py:124
  486.6 38.6 %multiply_convert_fusion.1 = (bf16[768,4096]{1,0:T(8,128)(2,1)}, f32[768,4096]{1,0:T(8,128)}, f32[768,4096]{1,0:T(8,128)}) fusion(bf16[1024,4096]{1,0:T(8,128)(2,1)} %all-gather.15.cloned.1.call-done, f32[768,1024]{1,0:T(8,128)S(1)} %get-tuple-element.298, f32[1024]{0:T(1024)S(1)} %bitcast.176, f32[1024]{0:T(1024)S(1)} %bitcast.172, f32[768]{0:T(1024)S(1)} %fusion.106, ...), kind=kOutput, calls=%fused_computation.77 | convolution fusion | flops 6650855424 | bytes 43005952 | tf_op jit(solution)/shard_map/dot_general | solution.py:129
  525.2 11.0 select_convert_fusion
  536.5 14.0 all_gather.35
  565.3 12.4 reduce-scatter.12.cloned.1.call-done
  580.0 18.6 add_convert_fusion
  598.6 12.3 multiply_reduce_fusion.1
  617.6 547.7 %while.31 = (s32[]{:T(128)}, bf16[16,768,64]{1,2,0:T(8,128)(2,1)S(1)}, bf16[16,3072,64]{1,2,0:T(8,128)(2,1)}, bf16[16,3072,64]{1,2,0:T(8,128)(2,1)}, bf16[16,768...) while((s32[]{:T(128)}, ...), condition=%wide.region_13.14_spmd.clone, body=%wide.region_11.13_spmd.clone.sunk | while | flops 1533815040 | bytes 132156608 | solution.py:249
  628.7 11.1 multiply_convert_fusion.3
  662.9 11.1 multiply_convert_fusion.3
  697.1 11.1 multiply_convert_fusion.3
  731.3 11.1 multiply_convert_fusion.3
  765.5 11.1 multiply_convert_fusion.3
  799.7 11.1 multiply_convert_fusion.3
  833.9 11.1 multiply_convert_fusion.3
  868.1 11.1 multiply_convert_fusion.3
  902.4 11.1 multiply_convert_fusion.3
  936.5 11.1 multiply_convert_fusion.3
  970.8 11.1 multiply_convert_fusion.3
  1005.0 11.1 multiply_convert_fusion.3
  1039.3 11.1 multiply_convert_fusion.3
  1073.5 11.1 multiply_convert_fusion.3
  1107.7 11.1 multiply_convert_fusion.3
  1142.0 11.1 multiply_convert_fusion.3
  1175.5 13.3 fusion.116
  1190.7 13.2 fusion.90
  1204.2 71.5 %reduce-scatter.16.cloned.1.call-done = bf16[768,1024]{0,1:T(8,128)(2,1)} async-done(((bf16[3072,1024]{0,1:T(8,128)(2,1)}), bf16[768,1024]{0,1:T(8,128)(2,1)}) %reduce-scatter.16.cloned.1.call-update) | async-done | bytes 1572880 | tf_op jit(solution)/shard_map/reduce_scatter | solution.py:257
  1275.7 113.6 %reduce-scatter.14.cloned.1.call-done = bf16[768,1024]{0,1:T(8,128)(2,1)} async-done(((bf16[3072,1024]{0,1:T(8,128)(2,1)}), bf16[768,1024]{0,1:T(8,128)(2,1)}) %reduce-scatter.14.cloned.1.call-update) | async-done | bytes 1572880 | tf_op jit(solution)/shard_map/reduce_scatter | solution.py:254
  1389.3 12.8 fusion.82
  1405.2 9.4 fusion.80
  1419.3 24.9 %reduce-scatter.20.cloned.1.call-done = f32[128,1024]{1,0:T(8,128)} async-done(((f32[1024,1024]{1,0:T(8,128)}), f32[128,1024]{1,0:T(8,128)}) %reduce-scatter.20.cloned.1.call-update) | async-done | bytes 524304 | tf_op jit(solution)/shard_map/reduce_scatter | solution.py:271
  1446.0 118.0 %reduce-scatter.22.cloned.1.call-done = f32[128,4096]{1,0:T(8,128)} async-done(((f32[1024,4096]{1,0:T(8,128)}), f32[128,4096]{1,0:T(8,128)}) %reduce-scatter.22.cloned.1.call-update) | async-done | bytes 2097168 | tf_op jit(solution)/shard_map/reduce_scatter | solution.py:272
  1566.7 116.9 %reduce-scatter.24.cloned.1.call-done = f32[512,1024]{1,0:T(8,128)} async-done(((f32[4096,1024]{1,0:T(8,128)}), f32[512,1024]{1,0:T(8,128)}) %reduce-scatter.24.cloned.1.call-update) | async-done | bytes 2097168 | tf_op jit(solution)/shard_map/reduce_scatter | solution.py:273
  1686.4 93.1 %reduce-scatter.18.cloned.1.call-done = f32[128,3072]{1,0:T(8,128)} async-done(((f32[1024,3072]{1,0:T(8,128)}), f32[128,3072]{1,0:T(8,128)}) %reduce-scatter.18.cloned.1.call-update) | async-done | bytes 1572880 | tf_op jit(solution)/shard_map/reduce_scatter | solution.py:270
  1783.4 39.7 %all-reduce = (f32[32,64]{1,0:T(8,128)}, f32[64]{0:T(128)}, f32[64,4]{0,1:T(4,128)}) all-reduce(f32[32,64]{1,0:T(8,128)S(1)} %fusion.126, f32[64]{0:T(128)S(1)} %copy-done.62, f32[64,4]{0,1:T(4,128)S(1)} %fusion.102), channel_id=1, replica_groups=mesh['scene'=8,'seq'=4] {'scene','seq'}, use_global_device_ids=true, to_apply=%region_34.35 | all-reduce | flops 2368 | bytes 18944 | tf_op jit(solution)/shard_map/psum | solution.py:210
  1828.4 26.4 %reduce-scatter.28.cloned.1.call-done = f32[128,4]{1,0:T(8,128)} async-done(((f32[1024,4]{1,0:T(8,128)}), f32[128,4]{1,0:T(8,128)}) %reduce-scatter.28.cloned.1.call-update) | async-done | bytes 2064
  1855.7 20.6 %all-reduce.1 = (bf16[128,4]{0,1:T(4,128)(2,1)S(1)}, bf16[128,128]{1,0:T(8,128)(2,1)S(1)}) all-reduce(bf16[128,4]{0,1:T(4,128)(2,1)S(1)} %copy.74, bf16[128,128]{1,0:T(8,128)(2,1)S(1)} %convert_element_type.192), channel_id=1, replica_groups=mesh['scene'=8,'seq'=4] {'seq'}, use_global_device_ids=true, to_apply=%region_23.24 | all-reduce | flops 16896 | bytes 67584 | tf_op jit(solution)/shard_map/psum | solution.py:278
  1877.5 102.6 %all-reduce.5.cloned.1.call-done = (bf16[128,3072]{1,0:T(8,128)(2,1)}, bf16[128,1024]{1,0:T(8,128)(2,1)}, bf16[128,4096]{1,0:T(8,128)(2,1)}, bf16[512,1024]{1,0:T(8,128)(2,1)}) async-done(((bf16[128,3072]{1,0:T(8,128)(2,1)}, bf16[128,1024]{1,0:T(8,128)(2,1)}, bf16[128,4096]{1,0:T(8,128)(2,1)}, bf16[512,1024]{1,0:T(8,128)(2,1)}), (bf16[128,3072]{1,0:T(8,128)(2,1)}, bf16[128,1024]{1,0:T(8,128)(2,1)}, ...) | async-done | bytes 3145744 | tf_op jit(solution)/shard_map/psum | solution.py:279
  (488 shorter events, 627.4 us)
Async XLA Ops:
  7.2 544.8 %copy-start = (f32[32,64]{1,0:T(8,128)S(1)}, f32[32,64]{1,0:T(8,128)}, u32[]{:S(2)}) copy-start(f32[32,64]{1,0:T(8,128)} %param.25) | copy-start | bytes 24580
  7.2 15.5 copy-start.6
  7.2 51.4 %all-gather.7.cloned.1.call-start = ((), (), s32[]{:S(2)}) async-start(), calls=%async_computation.9 | async-start | bytes 7077888 | tf_op jit(solution)/shard_map/all_gather | solution.py:82
  9.8 175.0 %all-gather.9.cloned.1.call-start = ((), (), s32[]{:S(2)}) async-start(), calls=%async_computation.10 | async-start | bytes 7864320 | tf_op jit(solution)/shard_map/all_gather | solution.py:97
  22.7 35.9 %copy-start.44 = (f32[768]{0:T(1024)}, f32[768]{0:T(1024)S(1)}, u32[]{:S(2)}) copy-start(f32[768]{0:T(1024)S(1)} %broadcast_multiply_fusion.1) | copy-start | bytes 9220
  23.8 34.8 %copy-start.50 = (f32[768]{0:T(1024)}, f32[768]{0:T(1024)S(1)}, u32[]{:S(2)}) copy-start(f32[768]{0:T(1024)S(1)} %fusion.105) | copy-start | bytes 9220
  23.9 34.8 %copy-start.52 = (f32[1024,1]{0,1:T(1,128)}, f32[1024,1]{0,1:T(1,128)S(1)}, u32[]{:S(2)}) copy-start(f32[1024,1]{0,1:T(1,128)S(1)} %get-tuple-element.293) | copy-start | bytes 12292
  23.9 34.8 %copy-start.56 = (f32[1024,1]{0,1:T(1,128)}, f32[1024,1]{0,1:T(1,128)S(1)}, u32[]{:S(2)}) copy-start(f32[1024,1]{0,1:T(1,128)S(1)} %get-tuple-element.294) | copy-start | bytes 12292
  23.9 462.7 %copy-start.30 = (f32[1024,1]{0,1:T(1,128)}, f32[1024,1]{0,1:T(1,128)S(1)}, u32[]{:S(2)}) copy-start(f32[1024,1]{0,1:T(1,128)S(1)} %get-tuple-element.291) | copy-start | bytes 12292
  23.9 462.7 %copy-start.33 = (f32[1024,1]{0,1:T(1,128)}, f32[1024,1]{0,1:T(1,128)S(1)}, u32[]{:S(2)}) copy-start(f32[1024,1]{0,1:T(1,128)S(1)} %get-tuple-element.292) | copy-start | bytes 12292
  69.3 231.2 %all-gather.11.cloned.1.call-start = ((), (), s32[]{:S(2)}) async-start(), calls=%async_computation.11 | async-start | bytes 7864320 | tf_op jit(solution)/shard_map/all_gather | solution.py:98
  70.0 409.0 %all-gather.13.cloned.1.call-start = ((), (), s32[]{:S(2)}) async-start(), calls=%async_computation.12 | async-start | bytes 2359296 | tf_op jit(solution)/shard_map/all_gather | solution.py:83
  70.8 17.3 copy-start.55
  70.8 415.7 %all-gather.15.cloned.1.call-start = ((), (), s32[]{:S(2)}) async-start(), calls=%async_computation.13 | async-start | bytes 9437184 | tf_op jit(solution)/shard_map/all_gather | solution.py:84
  73.6 451.6 %all-gather.17.cloned.1.call-start = ((), (), s32[]{:S(2)}) async-start(), calls=%async_computation.14 | async-start | bytes 9437184 | tf_op jit(solution)/shard_map/all_gather | solution.py:85
  76.4 501.2 %reduce-scatter.12.cloned.1.call-start = ((), (), s32[]{:S(2)}) async-start(), calls=%async_computation.15 | async-start | bytes 245760 | tf_op jit(solution)/shard_map/reduce_scatter | solution.py:205
  485.1 125.8 %copy-start.4 = (f32[768,1024]{1,0:T(8,128)}, f32[768,1024]{1,0:T(8,128)S(1)}, u32[]{:S(2)}) copy-start(f32[768,1024]{1,0:T(8,128)S(1)} %get-tuple-element.298) | copy-start | bytes 9437188
  485.2 40.0 %copy-start.24 = (f32[768]{0:T(1024)}, f32[768]{0:T(1024)S(1)}, u32[]{:S(2)}) copy-start(f32[768]{0:T(1024)S(1)} %broadcast_multiply_fusion) | copy-start | bytes 9220
  486.6 38.6 %copy-start.27 = (f32[768]{0:T(1024)}, f32[768]{0:T(1024)S(1)}, u32[]{:S(2)}) copy-start(f32[768]{0:T(1024)S(1)} %fusion.106) | copy-start | bytes 9220
  486.6 38.6 %copy-start.61 = (pred[768]{0:T(1024)(128)(4,1)S(1)}, pred[768]{0:T(1024)(128)(4,1)}, u32[]{:S(2)}) copy-start(pred[768]{0:T(1024)(128)(4,1)} %fusion.104) | copy-start | bytes 2308
  536.2 14.3 copy-start.42
  552.0 13.3 copy-start.22
  559.9 715.8 %reduce-scatter.16.cloned.1.call-start = ((), (), s32[]{:S(2)}) async-start(), calls=%async_computation.17 | async-start | bytes 7864320 | tf_op jit(solution)/shard_map/reduce_scatter | solution.py:257
  580.0 18.6 copy-start.25
  580.0 18.6 copy-start.28
  580.0 18.6 copy-start.31
  598.6 12.3 copy-start.49
  1166.5 222.8 %reduce-scatter.14.cloned.1.call-start = ((), (), s32[]{:S(2)}) async-start(), calls=%async_computation.16 | async-start | bytes 7864320 | tf_op jit(solution)/shard_map/reduce_scatter | solution.py:254
  1167.3 276.9 %reduce-scatter.20.cloned.1.call-start = ((), (), s32[]{:S(2)}) async-start(), calls=%async_computation.19 | async-start | bytes 4718592 | tf_op jit(solution)/shard_map/reduce_scatter | solution.py:271
  1173.6 390.4 %reduce-scatter.22.cloned.1.call-start = ((), (), s32[]{:S(2)}) async-start(), calls=%async_computation.20 | async-start | bytes 18874368 | tf_op jit(solution)/shard_map/reduce_scatter | solution.py:272
  1188.9 494.8 %reduce-scatter.24.cloned.1.call-start = ((), (), s32[]{:S(2)}) async-start(), calls=%async_computation.21 | async-start | bytes 18874368 | tf_op jit(solution)/shard_map/reduce_scatter | solution.py:273
  1203.8 185.5 %copy-start.7 = (bf16[768,1024]{1,0:T(8,128)(2,1)S(1)}, bf16[768,1024]{1,0:T(8,128)(2,1)}, u32[]{:S(2)}) copy-start(bf16[768,1024]{1,0:T(8,128)(2,1)} %param.17) | copy-start | bytes 4718596
  1203.8 185.5 %copy-start.18 = (bf16[16,768,64]{1,2,0:T(8,128)(2,1)S(1)}, bf16[16,768,64]{1,2,0:T(8,128)(2,1)}, u32[]{:S(2)}) copy-start(bf16[16,768,64]{1,2,0:T(8,128)(2,1)} %copy-done.17) | copy-start | bytes 4718596
  1203.8 185.5 %copy-start.45 = (f32[768]{0:T(1024)S(1)}, f32[768]{0:T(1024)}, u32[]{:S(2)}) copy-start(f32[768]{0:T(1024)} %copy-done.44) | copy-start | bytes 9220
  1203.8 185.5 %copy-start.51 = (f32[768]{0:T(1024)S(1)}, f32[768]{0:T(1024)}, u32[]{:S(2)}) copy-start(f32[768]{0:T(1024)} %copy-done.50) | copy-start | bytes 9220
  1203.9 185.5 %copy-start.53 = (f32[1024,1]{0,1:T(1,128)S(1)}, f32[1024,1]{0,1:T(1,128)}, u32[]{:S(2)}) copy-start(f32[1024,1]{0,1:T(1,128)} %copy-done.52) | copy-start | bytes 12292
  1203.9 185.5 %copy-start.57 = (f32[1024,1]{0,1:T(1,128)S(1)}, f32[1024,1]{0,1:T(1,128)}, u32[]{:S(2)}) copy-start(f32[1024,1]{0,1:T(1,128)} %copy-done.56) | copy-start | bytes 12292
  1203.9 575.6 %reduce-scatter.18.cloned.1.call-start = ((), (), s32[]{:S(2)}) async-start(), calls=%async_computation.18 | async-start | bytes 14155776 | tf_op jit(solution)/shard_map/reduce_scatter | solution.py:270
  1402.2 421.0 %reduce-scatter.26.cloned.1.call-start = ((), (), s32[]{:S(2)}) async-start(), calls=%async_computation.22 | async-start | bytes 589824 | tf_op jit(solution)/shard_map/reduce_scatter | solution.py:274
  1405.1 449.7 %reduce-scatter.28.cloned.1.call-start = ((), (), s32[]{:S(2)}) async-start(), calls=%async_computation.23 | async-start | bytes 589824
  1419.2 560.9 %all-reduce.5.cloned.1.call-start = ((), (), s32[]{:S(2)}) async-start(), calls=%async_computation.24 | async-start | bytes 6291456 | tf_op jit(solution)/shard_map/psum | solution.py:279
  1566.7 215.2 %copy-start.38 = (f32[256,64]{0,1:T(8,128)S(1)}, f32[256,64]{0,1:T(8,128)}, u32[]{:S(2)}) copy-start(f32[256,64]{0,1:T(8,128)} %copy-done.37) | copy-start | bytes 196612
  1566.7 215.2 %copy-start.40 = (f32[256,64]{0,1:T(8,128)S(1)}, f32[256,64]{0,1:T(8,128)}, u32[]{:S(2)}) copy-start(f32[256,64]{0,1:T(8,128)} %copy-done.39) | copy-start | bytes 196612
  1566.7 215.2 %copy-start.60 = (f32[64,4]{0,1:T(4,128)S(1)}, f32[64,4]{0,1:T(4,128)}, u32[]{:S(2)}) copy-start(f32[64,4]{0,1:T(4,128)} %param.27) | copy-start | bytes 3076
  1566.7 216.2 %copy-start.54 = (bf16[256,4]{0,1:T(4,128)(2,1)S(1)}, bf16[256,4]{0,1:T(4,128)(2,1)}, u32[]{:S(2)}) copy-start(bf16[256,4]{0,1:T(4,128)(2,1)} %reshape.158) | copy-start | bytes 6148
  1566.7 216.4 %copy-start.23 = (f32[256,32]{1,0:T(8,128)S(1)}, f32[256,32]{1,0:T(8,128)}, u32[]{:S(2)}) copy-start(f32[256,32]{1,0:T(8,128)} %copy-done.22) | copy-start | bytes 98308
  1566.7 216.3 %copy-start.36 = (f32[256,64]{0,1:T(8,128)S(1)}, f32[256,64]{0,1:T(8,128)}, u32[]{:S(2)}) copy-start(f32[256,64]{0,1:T(8,128)} %copy-done.35) | copy-start | bytes 196612
  1566.7 216.7 %copy-start.62 = (f32[64]{0:T(128)S(1)}, f32[64]{0:T(128)}, u32[]{:S(2)}) copy-start(f32[64]{0:T(128)} %get-tuple-element.305) | copy-start | bytes 772
  (62 other events, 307.0 us)
Sparse Core Ops, SparseCore 0:
  10.5 48.1 all-gather.6
  69.4 115.3 all-gather.8
  186.9 113.5 all-gather.10
  302.8 25.9 all-gather.12
  331.1 54.2 all-gather.14
  387.7 54.2 all-gather.16
  560.0 17.6 reduce-scatter.11
  1166.6 109.0 reduce-scatter.15
  1278.0 111.2 reduce-scatter.13
  1392.5 51.6 reduce-scatter.19
  1447.8 116.1 reduce-scatter.21
  1567.4 116.1 reduce-scatter.23
  1687.2 92.2 reduce-scatter.17
  1783.0 34.1 reduce-scatter.25
  1820.7 34.1 reduce-scatter.27
  1858.4 121.6 all-reduce.4
where the time goes:
time: 2010 us; the launch traced here: 2000 us
  waiting for transfers between devices  902 us (45%)
  matrix products  630 us (31%)
  other arithmetic  253 us (13%)
  local copies, waits for them, and re-layouts  98.4 us (5%)
  blocking collectives  95.1 us (5%)
    convert_element_type x16, other arithmetic, head_backward(): grad_scores = (attn_probs * (grad_probs - row_inner)).astype(jnp.bfloat16)  177 us
    dot_general x32, matrix products, head_scores(): jnp.einsum('qd,kd->qk', queries, key_block, preferred_element_type=jnp.fl...  164 us
    reduce_scatter x1, waiting for transfers between devices, per_device(): lax.psum_scatter(grad_fc1, 'scene', scatter_dimension=0, tiled=True)  118 us
    reduce_scatter x1, waiting for transfers between devices, per_device(): lax.psum_scatter(grad_fc2, 'scene', scatter_dimension=0, tiled=True)  117 us
    reduce_scatter x1, waiting for transfers between devices, per_device(): lax.psum_scatter(join_heads(grad_keys_h).astype(jnp.bfloat16), 'seq', sca...  114 us
    psum x1, waiting for transfers between devices, per_device(): lax.psum(qkv_part.astype(jnp.bfloat16), 'seq').astype(jnp.float32)  103 us
    all_gather x1, waiting for transfers between devices, per_device(): lax.all_gather(value_rows, 'seq', axis=0, tiled=True)  94.8 us
    reduce_scatter x1, waiting for transfers between devices, per_device(): lax.psum_scatter(grad_qkv, 'scene', scatter_dimension=0, tiled=True)  93.1 us
  transfers between devices with their start and end apart: 16, of which 12 were waited for; matrix products, arithmetic and copies ran while one was open for 17% of the time, Pallas kernels for 0%

commit v1 on v0

v1 whole, which is shorter than its diff:
```python
import functools

import jax
import jax.numpy as jnp
from jax import lax
from jax.experimental import pallas as pl
from jax.experimental.pallas import tpu as pltpu
from jax.sharding import PartitionSpec as P

H = 16
TF = 32
PP = 4
OUT = 4
TG = 16
IMG_DEV = 576

EPS = 1e-05
NEG_FILL = -1e30
LOG2E = 1.4426950408889634
VMEM_BYTES = 60 * 2**20

NT = (((1,), (1,)), ((), ()))
NN = (((1,), (0,)), ((), ()))
TN = (((0,), (0,)), ((), ()))


def mxu(left, right, dims):
    return lax.dot_general(left, right, dims, preferred_element_type=jnp.float32)


def exact(left, right, dims):
    return lax.dot_general(
        left, right, dims, precision=lax.Precision.HIGHEST, preferred_element_type=jnp.float32
    )


def gelu_parts(v):
    a = jnp.abs(v) * 0.7071067811865476
    t = 1.0 / (1.0 + 0.3275911 * a)
    poly = t * (
        0.254829592
        + t * (-0.284496736 + t * (1.421413741 + t * (-1.453152027 + t * 1.061405429)))
    )
    e = jnp.exp(-a * a)
    tail = 0.5 * poly * e
    cdf = jnp.where(v >= 0.0, 1.0 - tail, tail)
    return v * cdf, cdf + v * (e * 0.3989422804014327)


def pair_keys(block, bias, head, half):
    lane = lax.broadcasted_iota(jnp.int32, block.shape, 1)
    mine = (lane < half) if head == 0 else (lane >= half)
    flag = half if head == 0 else 0
    zero = jnp.zeros_like(block)
    return jnp.where(mine, block, jnp.where(lane == flag, bias, zero))


def pair_queries(block, head, half):
    lane = lax.broadcasted_iota(jnp.int32, block.shape, 1)
    mine = (lane < half) if head == 0 else (lane >= half)
    flag = half if head == 0 else 0
    zero = jnp.zeros_like(block)
    return jnp.where(mine, block, jnp.where(lane == flag, jnp.ones_like(block), zero))


def pair_mask(block, head, half):
    lane = lax.broadcasted_iota(jnp.int32, block.shape, 1)
    mine = (lane < half) if head == 0 else (lane >= half)
    return jnp.where(mine, block, jnp.zeros_like(block))


def attn_fwd_kernel(*refs, n, scale):
    q_ref, bias_ref = refs[0], refs[1]
    k_refs, v_refs = refs[2 : 2 + n], refs[2 + n : 2 + 2 * n]
    o_ref, lse_ref, s_buf, k_buf, vt_buf, acc_buf = refs[2 + 2 * n :]
    tq = q_ref.shape[0]
    tk = k_refs[0].shape[0]
    half = q_ref.shape[1] // 2
    ext = half + 16
    q = q_ref[...]
    qs = [pair_queries(q, h, half) for h in range(2)]
    bias = bias_ref[...]
    ones = jnp.ones((16, tk), jnp.bfloat16)
    for i in range(n):
        kb = k_refs[i][...]
        vt = v_refs[i][...].T
        for h in range(2):
            k_buf[i, h] = pair_keys(kb, bias, h, half)
            vt_buf[i, h, :half] = vt[h * half : h * half + half]
            vt_buf[i, h, half:] = ones

    def score(j, slot, peak):
        out = []
        for h in range(2):
            s = mxu(k_buf[j, h], qs[h], NT)
            s_buf[slot, h] = s
            out.append(jnp.maximum(peak[h], jnp.max(s, axis=0, keepdims=True)))
        return out

    def mix(j, slot, before, peak):
        for h in range(2):
            fade = jnp.exp2((before[h] - peak[h]) * scale)
            p = jnp.exp2((s_buf[slot, h] - peak[h]) * scale).astype(jnp.bfloat16)
            acc_buf[h] = acc_buf[h] * fade + mxu(vt_buf[j, h], p, NN)

    start = [jnp.full((1, tq), -3e38, jnp.float32)] * 2
    acc_buf[...] = jnp.zeros(acc_buf.shape, jnp.float32)
    first = score(0, 0, start)

    def body(j, carry):
        before, peak = carry
        fresh = score(j, lax.rem(j, 2), peak)
        mix(j - 1, lax.rem(j - 1, 2), before, peak)
        return (peak, fresh)

    before, peak = lax.fori_loop(1, n, body, (start, first))
    mix(n - 1, (n - 1) % 2, before, peak)
    outs = []
    for h in range(2):
        acc = acc_buf[h]
        total = acc[half : half + 1]
        outs.append(acc[:half] / total)
        lse_ref[h : h + 1, :] = peak[h] * scale + jnp.log2(total)
    o_ref[...] = jnp.concatenate(outs, axis=0).T.astype(jnp.bfloat16)


def attn_fwd(q_rows, kv_rows, bias, head_dim):
    n = len(kv_rows)
    tq, width = q_rows.shape[0], kv_rows[0].shape[1] // 2
    tk = kv_rows[0].shape[0]
    lanes = 2 * head_dim
    pairs = width // lanes
    scale = head_dim**-0.5 * LOG2E
    block = lambda rows, off: pl.BlockSpec((rows, lanes), lambda h: (0, h + off))
    flops = 4 * tq * tk * n * width
    return pl.pallas_call(
        functools.partial(attn_fwd_kernel, n=n, scale=scale),
        grid=(pairs,),
        in_specs=[block(tq, 0), pl.BlockSpec((tk, lanes), lambda h: (0, 0))]
        + [block(tk, 0)] * n
        + [block(tk, pairs)] * n,
        out_specs=(block(tq, 0), pl.BlockSpec((None, 2, tq), lambda h: (h, 0, 0))),
        out_shape=(
            jax.ShapeDtypeStruct((tq, width), jnp.bfloat16),
            jax.ShapeDtypeStruct((pairs, 2, tq), jnp.float32),
        ),
        scratch_shapes=[
            pltpu.VMEM((2, 2, tk, tq), jnp.float32),
            pltpu.VMEM((n, 2, tk, lanes), jnp.bfloat16),
            pltpu.VMEM((n, 2, head_dim + 16, tk), jnp.bfloat16),
            pltpu.VMEM((2, head_dim + 16, tq), jnp.float32),
        ],
        compiler_params=pltpu.CompilerParams(vmem_limit_bytes=VMEM_BYTES),
        cost_estimate=pl.CostEstimate(
            flops=flops * 4, bytes_accessed=2 * width * (2 * tq + 2 * n * tk), transcendentals=0
        ),
        name="attn_fwd",
    )(q_rows, bias, *kv_rows, *kv_rows)


def attn_bwd_kernel(
    q_ref, k_ref, v_ref, do_ref, lse_ref, del_ref, bias_ref,
    dq_ref, dk_ref, dv_ref,
    s_buf, dp_buf, qm, km, dom, kt, qt, dot, dqa, dka, dva, *, tk, tq, scale, post
):
    nq = q_ref.shape[0] // tq
    nk = k_ref.shape[0] // tk
    half = q_ref.shape[1] // 2
    for i in range(nk):
        rows = slice(i * tk, i * tk + tk)
        for h in range(2):
            km[h, rows] = pair_keys(k_ref[rows, :], bias_ref[...], h, half)
    for h in range(2):
        qm[h] = pair_queries(q_ref[...], h, half)
        dom[h] = pair_mask(do_ref[...], h, half)
    kt[...] = k_ref[...].T
    qt[...] = q_ref[...].T
    dot[...] = do_ref[...].T
    for acc in (dqa, dka, dva):
        acc[...] = jnp.zeros(acc.shape, jnp.float32)

    def place(t):
        if isinstance(t, int):
            return t // nq * tk, t % nq * tq, t % 2
        return (
            pl.multiple_of(lax.div(t, nq) * tk, tk),
            pl.multiple_of(lax.rem(t, nq) * tq, tq),
            lax.rem(t, 2),
        )

    def score(t):
        k0, q0, slot = place(t)
        ks, qs = pl.ds(k0, tk), pl.ds(q0, tq)
        vv = v_ref[ks, :]
        for h in range(2):
            s_buf[slot, h] = mxu(km[h, ks, :], qm[h, qs, :], NT)
            dp_buf[slot, h] = mxu(vv, dom[h, qs, :], NT)

    def grads(t):
        k0, q0, slot = place(t)
        ks, qs = pl.ds(k0, tk), pl.ds(q0, tq)
        for h in range(2):
            p = jnp.exp2(s_buf[slot, h] * scale - lse_ref[h : h + 1, qs])
            ds = (p * (dp_buf[slot, h] - del_ref[h : h + 1, qs])).astype(jnp.bfloat16)
            pb = p.astype(jnp.bfloat16)
            r = slice(half * h, half * h + half)
            dqa[r, qs] += mxu(kt[r, ks], ds, NN)
            dva[r, ks] += mxu(dot[r, qs], pb, NT)
            dka[r, ks] += mxu(qt[r, qs], ds, NT)

    score(0)

    def body(t, carry):
        score(t)
        grads(t - 1)
        return carry

    lax.fori_loop(1, nq * nk, body, 0)
    grads(nq * nk - 1)
    dq_ref[...] = (dqa[...] * post).T.astype(jnp.bfloat16)
    dk_ref[...] = (dka[...] * post).T.astype(jnp.bfloat16)
    dv_ref[...] = dva[...].T.astype(jnp.bfloat16)


def attn_bwd(q, k, v, do, lse, delta, bias, head_dim):
    rows, width = q.shape
    tk = bias.shape[0]
    tq = tk
    lanes = 2 * head_dim
    pairs = width // lanes
    block = pl.BlockSpec((rows, lanes), lambda h: (0, h))
    stat = pl.BlockSpec((None, 2, rows), lambda h: (h, 0, 0))
    return pl.pallas_call(
        functools.partial(
            attn_bwd_kernel, tk=tk, tq=tq, scale=head_dim**-0.5 * LOG2E, post=head_dim**-0.5
        ),
        grid=(pairs,),
        in_specs=[block] * 4 + [stat] * 2 + [pl.BlockSpec((tk, lanes), lambda h: (0, 0))],
        out_specs=(block,) * 3,
        out_shape=(jax.ShapeDtypeStruct((rows, width), jnp.bfloat16),) * 3,
        scratch_shapes=[
            pltpu.VMEM((2, 2, tk, tq), jnp.float32),
            pltpu.VMEM((2, 2, tk, tq), jnp.float32),
            pltpu.VMEM((2, rows, lanes), jnp.bfloat16),
            pltpu.VMEM((2, rows, lanes), jnp.bfloat16),
            pltpu.VMEM((2, rows, lanes), jnp.bfloat16),
            pltpu.VMEM((lanes, rows), jnp.bfloat16),
            pltpu.VMEM((lanes, rows), jnp.bfloat16),
            pltpu.VMEM((lanes, rows), jnp.bfloat16),
            pltpu.VMEM((lanes, rows), jnp.float32),
            pltpu.VMEM((lanes, rows), jnp.float32),
            pltpu.VMEM((lanes, rows), jnp.float32),
        ],
        compiler_params=pltpu.CompilerParams(vmem_limit_bytes=VMEM_BYTES),
        cost_estimate=pl.CostEstimate(
            flops=10 * rows * rows * width * 4, bytes_accessed=14 * rows * width, transcendentals=0
        ),
        name="attn_bwd",
    )(q, k, v, do, lse, delta, bias)


def fc1_kernel(x_ref, w_ref, act_ref, slope_ref):
    act, slope = gelu_parts(mxu(x_ref[...], w_ref[...], NN))
    act_ref[...] = act.astype(jnp.bfloat16)
    slope_ref[...] = slope.astype(jnp.bfloat16)


def fc1_gelu(x, w):
    rows, depth = x.shape
    cols = w.shape[1]
    tile = 512
    spec = pl.BlockSpec((rows, tile), lambda i: (0, i))
    return pl.pallas_call(
        fc1_kernel,
        grid=(cols // tile,),
        in_specs=[
            pl.BlockSpec((rows, depth), lambda i: (0, 0)),
            pl.BlockSpec((depth, tile), lambda i: (0, i)),
        ],
        out_specs=(spec, spec),
        out_shape=(jax.ShapeDtypeStruct((rows, cols), jnp.bfloat16),) * 2,
        compiler_params=pltpu.CompilerParams(vmem_limit_bytes=VMEM_BYTES),
        cost_estimate=pl.CostEstimate(
            flops=2 * rows * cols * depth,
            bytes_accessed=2 * (rows * depth + depth * cols + 2 * rows * cols),
            transcendentals=0,
        ),
        name="fc1_gelu",
    )(x, w)


def normalize(v):
    center = v - jnp.mean(v, axis=-1, keepdims=True)
    spread = jnp.mean(center * center, axis=-1, keepdims=True)
    inv = lax.rsqrt(spread + EPS)
    return center * inv, inv


def norm_back(g, u, inv, gain):
    q = g * gain
    back = inv * (
        q - jnp.mean(q, axis=-1, keepdims=True) - u * jnp.mean(q * u, axis=-1, keepdims=True)
    )
    return back, jnp.sum(g * u, axis=0), jnp.sum(g, axis=0)


def per_device(
    tokens,
    image_count,
    norm_params,
    w_qkv,
    w_proj,
    w_fc1,
    w_fc2,
    w_unpatch,
    w_dec1,
    b_dec1,
    w_dec2,
    cot_out,
    cot_dec,
):
    seq_count = lax.axis_size("seq")
    rank = lax.axis_index("seq")
    scene_rank = lax.axis_index("scene")
    tok_rows, width = tokens.shape
    head_dim = width // H
    cols = width // seq_count
    cells = TG * TG
    bf16, f32 = jnp.bfloat16, jnp.float32
    live_image = image_count[0] // seq_count
    pos = jnp.arange(tok_rows, dtype=jnp.int32)
    row_live = (pos >= IMG_DEV) | (pos < live_image)
    bias = jnp.broadcast_to(
        jnp.where(row_live, 0.0, NEG_FILL).astype(bf16)[:, None], (tok_rows, 2 * head_dim)
    )

    def hop(x, step):
        return lax.ppermute(
            x, "seq", [(i, i + step) for i in range(seq_count) if 0 <= i + step < seq_count]
        )

    def turn(x, step):
        return lax.ppermute(x, "seq", [(i, (i + step) % seq_count) for i in range(seq_count)])

    def slot_of(chunk):
        return jnp.where(chunk <= rank, rank - chunk, chunk)

    ups, downs = [tokens], [tokens]
    for _ in range(seq_count - 1):
        ups.append(hop(ups[-1], 1))
        downs.append(hop(downs[-1], -1))
    slots = [tokens]
    for d in range(1, seq_count):
        pick = ups[d]
        for r in range(d):
            pick = jnp.where(rank == r, downs[d - r], pick)
        slots.append(pick)

    def gather(w):
        return lax.all_gather(w.astype(bf16), "scene", axis=0, tiled=True)

    small = gather(
        jnp.concatenate(
            [w_unpatch, norm_params, jnp.zeros((w_unpatch.shape[0], 124), f32)], axis=1
        )
    )
    unpatch_w = small[:, : PP * TF]
    norm_full = small[:, PP * TF : PP * TF + 4].astype(f32)
    gain_one, shift_one, gain_two, shift_two = (norm_full[:, i] for i in range(4))
    qkv_w = gather(w_qkv)
    proj_w = gather(w_proj)
    fc1_w = gather(w_fc1)
    fc2_w = gather(w_fc2)
    cot_cells = lax.all_gather(cot_dec, "seq", axis=0, tiled=True)

    def own_cols(base):
        return lax.dynamic_slice_in_dim(qkv_w, base * width + rank * cols, cols, 1)

    own_w = [own_cols(i) for i in range(3)]
    a1 = []
    kv_rows, head_q, head_k, head_v = [], [], [], []
    for d in range(seq_count):
        u, _ = normalize(slots[d].astype(f32))
        a = (u * gain_one + shift_one).astype(bf16)
        a1.append(a)
        if d == 0:
            q_rows = mxu(a, qkv_w[:, :width], NN).astype(bf16)
        kv = mxu(a, qkv_w[:, width:], NN).astype(bf16)
        kv_rows.append(kv)
        if d == 0:
            head_q.append(lax.dynamic_slice_in_dim(q_rows, rank * cols, cols, 1))
        else:
            head_q.append(mxu(a, own_w[0], NN).astype(bf16))
        head_k.append(lax.dynamic_slice_in_dim(kv, rank * cols, cols, 1))
        head_v.append(lax.dynamic_slice_in_dim(kv, width + rank * cols, cols, 1))
    mixed, lse = attn_fwd(q_rows, kv_rows, bias, head_dim)
    lse = lse.reshape(H, tok_rows)

    inputs_f = tokens.astype(f32)
    middle = inputs_f + mxu(mixed, proj_w, NN)
    u_two, inv_two = normalize(middle)
    a2 = (u_two * gain_two + shift_two).astype(bf16)
    act, slope = fc1_gelu(a2, fc1_w)
    result = jnp.where(row_live[:, None], middle + mxu(act, fc2_w, NN), 0.0)
    block_out = result.astype(bf16)

    triplane = block_out[IMG_DEV:]
    planes = mxu(triplane, unpatch_w, NN).astype(bf16)
    all_planes = lax.all_gather(planes, "seq", axis=0, tiled=True).astype(f32)
    feat = all_planes[:cells] + all_planes[cells : 2 * cells] + all_planes[2 * cells :]
    dh = w_dec1.shape[1]
    eye = jnp.eye(PP, dtype=f32)
    dec1 = jnp.einsum("fh,pq->pfqh", w_dec1, eye).reshape(PP * TF, PP * dh)
    dec2 = jnp.einsum("ho,pq->phoq", w_dec2, eye).reshape(PP * dh, OUT * PP)
    hidden_pre = exact(feat, dec1, NN) + jnp.tile(b_dec1, PP)
    zdec, zslope = gelu_parts(hidden_pre)
    decoded_all = exact(zdec, dec2, NN)
    cells_dev = cells // seq_count
    decoded = lax.dynamic_slice_in_dim(decoded_all, rank * cells_dev, cells_dev, 0)
    cot_f = cot_cells.astype(f32)
    grad_hidden = exact(cot_f, dec2, NT) * zslope
    gfeat = exact(grad_hidden, dec1, NT).astype(bf16)
    grad_w2 = jnp.einsum(
        "phop->ho", exact(zdec, cot_f, TN).reshape(PP, dh, OUT, PP)
    )
    grad_b1 = jnp.sum(jnp.sum(grad_hidden, axis=0).reshape(PP, dh), axis=0)
    grad_w1 = jnp.einsum(
        "pfph->fh", exact(feat, grad_hidden, TN).reshape(PP, TF, PP, dh)
    )
    tri_rows = tok_rows - IMG_DEV
    plane_grad = lax.dynamic_slice_in_dim(
        jnp.concatenate([gfeat] * 4, axis=0), lax.rem(rank * tri_rows, cells), tri_rows, 0
    )
    grad_unpatch = mxu(triplane, plane_grad, TN)
    grad_tri = mxu(plane_grad, unpatch_w, NT)

    grad_result = jnp.where(row_live[:, None], cot_out.astype(f32), 0.0)
    grad_result = jnp.concatenate([grad_result[:IMG_DEV], grad_result[IMG_DEV:] + grad_tri], axis=0)
    branch = grad_result.astype(bf16)
    grad_pre = (mxu(branch, fc2_w, NT) * slope.astype(f32)).astype(bf16)
    back_two, gain_grad_two, shift_grad_two = norm_back(
        mxu(grad_pre, fc1_w, NT), u_two, inv_two, gain_two
    )
    grad_mid = grad_result + back_two
    mid_grad = grad_mid.astype(bf16)
    grad_mixed = mxu(mid_grad, proj_w, NT).astype(bf16)

    head_of = (jnp.arange(width) // head_dim)[None, :] == jnp.arange(H)[:, None]
    delta = exact(
        head_of.astype(f32), grad_mixed.astype(f32) * mixed.astype(f32), NT
    )
    heads_dev = H // seq_count
    stats = jnp.concatenate(
        [lse.reshape(seq_count, heads_dev, tok_rows), delta.reshape(seq_count, heads_dev, tok_rows)],
        axis=1,
    )

    def piece(x, chunk, size, axis):
        return lax.dynamic_slice_in_dim(x, chunk * size, size, axis)

    do_all = jnp.zeros((seq_count * tok_rows, cols), bf16)
    stat_all = jnp.zeros((2 * heads_dev, seq_count * tok_rows), f32)
    for d in range(seq_count):
        to = lax.rem(rank + d, seq_count)
        got = piece(grad_mixed, to, cols, 1)
        got_stat = lax.dynamic_index_in_dim(stats, to, 0, keepdims=False)
        if d:
            got, got_stat = turn(got, d), turn(got_stat, d)
        at = slot_of(lax.rem(rank - d + seq_count, seq_count)) * tok_rows
        do_all = lax.dynamic_update_slice_in_dim(do_all, got, at, 0)
        stat_all = lax.dynamic_update_slice_in_dim(stat_all, got_stat, at, 1)
    pairs_dev = heads_dev // 2
    dq, dk, dv = attn_bwd(
        jnp.concatenate(head_q, axis=0),
        jnp.concatenate(head_k, axis=0),
        jnp.concatenate(head_v, axis=0),
        do_all,
        stat_all[:heads_dev].reshape(pairs_dev, 2, seq_count * tok_rows),
        stat_all[heads_dev:].reshape(pairs_dev, 2, seq_count * tok_rows),
        bias,
        head_dim,
    )
    head_grads = jnp.concatenate([dq, dk, dv], axis=1)

    row_grads = jnp.zeros((3, tok_rows, width), bf16)
    for d in range(seq_count):
        to = lax.rem(rank + d, seq_count)
        got = piece(head_grads, slot_of(to), tok_rows, 0)
        if d:
            got = turn(got, d)
        source = lax.rem(rank - d + seq_count, seq_count)
        row_grads = lax.dynamic_update_slice(
            row_grads,
            got.reshape(tok_rows, 3, cols).transpose(1, 0, 2),
            (0, 0, source * cols),
        )
    grad_in = sum(
        mxu(row_grads[i], qkv_w[:, i * width : (i + 1) * width], NT) for i in range(3)
    )
    u_one, inv_one = normalize(inputs_f)
    back_one, gain_grad_one, shift_grad_one = norm_back(grad_in, u_one, inv_one, gain_one)
    grad_tokens = (grad_mid + back_one).astype(bf16)

    def over_scene(g):
        return lax.psum_scatter(g.astype(bf16), "scene", scatter_dimension=0, tiled=True)

    def over_seq(part):
        size = part.shape[1] // seq_count
        total = piece(part, rank, size, 1).astype(f32)
        for d in range(1, seq_count):
            to = lax.rem(rank + d, seq_count)
            total = total + turn(piece(part, to, size, 1), d).astype(f32)
        return over_cols(total.astype(bf16))

    def over_cols(mine):
        size = mine.shape[1]
        out = jnp.zeros((mine.shape[0], size * seq_count), f32)
        for d in range(seq_count):
            got = turn(mine, d) if d else mine
            source = lax.rem(rank - d + seq_count, seq_count)
            out = lax.dynamic_update_slice_in_dim(out, got.astype(f32), source * size, 1)
        return out

    fc2_part = over_scene(mxu(act, branch, TN))
    fc1_part = over_scene(mxu(a2, grad_pre, TN))
    proj_part = over_scene(
        jnp.concatenate([mxu(mixed, mid_grad, TN).astype(bf16), grad_unpatch.astype(bf16)], axis=1)
    )
    grad_fc2 = over_seq(fc2_part)
    grad_fc1 = over_seq(fc1_part)
    grad_proj_all = over_seq(
        jnp.pad(proj_part, ((0, 0), (0, 128 * seq_count - PP * TF)))
    )
    grad_proj = grad_proj_all[:, :width]
    grad_unp = grad_proj_all[:, width : width + PP * TF]
    own_qkv = mxu(jnp.concatenate(a1, axis=0), head_grads, TN)
    qkv_all = over_cols(over_scene(own_qkv))
    shard = qkv_all.shape[0]
    grad_qkv = (
        qkv_all.reshape(shard, seq_count, 3, cols).transpose(0, 2, 1, 3).reshape(shard, 3 * width)
    )

    def own_rows(total):
        return lax.dynamic_slice_in_dim(total, scene_rank * shard, shard, 1).T

    norm_one = lax.psum(jnp.stack([gain_grad_one, shift_grad_one]), ("scene", "seq"))
    norm_two = lax.psum(jnp.stack([gain_grad_two, shift_grad_two]), ("scene", "seq"))
    dec_grads = lax.psum((grad_w1, grad_b1, grad_w2), "scene")
    return (
        block_out,
        decoded,
        grad_tokens,
        own_rows(norm_one),
        own_rows(norm_two),
        grad_qkv,
        grad_proj,
        grad_fc1,
        grad_fc2,
        grad_unp,
        dec_grads[0],
        dec_grads[1],
        dec_grads[2],
    )


def solution(mesh):
    rows = P(("scene", "seq"), None)
    shard = P("scene", None)
    in_specs = (
        rows, P("scene"), shard, shard, shard, shard, shard, shard, P(), P(), P(), rows, rows
    )
    out_specs = (rows,) * 3 + (shard,) * 7 + (P(),) * 3
    return jax.shard_map(
        per_device, mesh=mesh, in_specs=in_specs, out_specs=out_specs, check_vma=False
    )
```

time: 2010 us -> 917 us (0.46)
  waiting for transfers between devices: 902 us -> 185 us
  matrix products: 630 us -> 127 us
  Pallas kernels: 0 us -> 246 us
  other arithmetic: 253 us -> 36.9 us
  starting transfers between devices: 1.34 us -> 78.9 us
  blocking collectives: 95.1 us -> 149 us
  local copies, waits for them, and re-layouts: 98.4 us -> 72.8 us
    reduce_scatter x8 -> x3, waiting for transfers between devices: 551 us -> 0.02 us  [over_scene(): lax.psum_scatter(g.astype(bf16), 'scene', scatter_dimension=0, tiled=True)]
    dot_general x133 -> x30, matrix products: 630 us -> 127 us  [the longest x23 121 us: mxu(): lax.dot_general(left, right, dims, preferred_element_type=jnp.float32)]
    pallas_call x0 -> x3, Pallas kernels: none -> 246 us  [the longest x1 141 us: attn_bwd(): pl.pallas_call(functools.partial(attn_bwd_kernel, tk=tk, tq=tq, scale=hea...]
    all_gather x6 -> x4, waiting for transfers between devices: 221 us -> 0.01 us  [gather(): return lax.all_gather(w.astype(bf16), 'scene', axis=0, tiled=True)]
    convert_element_type x33 -> x11, other arithmetic: 211 us -> 20.2 us  [the longest x4 8.69 us: gather(): return lax.all_gather(w.astype(bf16), 'scene', axis=0, tiled=True)]
    ppermute x0 -> x36, waiting for transfers between devices: none -> 185 us  [the longest x30 138 us: turn(): lax.ppermute(x, 'seq', [(i, (i + step) % seq_count) for i in range(seq_co...]
    psum x1 -> x0, waiting for transfers between devices: 103 us -> none  [per_device(): lax.psum(qkv_part.astype(jnp.bfloat16), 'seq').astype(jnp.float32)]
    ppermute x0 -> x36, starting transfers between devices: none -> 78.4 us  [the longest x30 56.9 us: turn(): lax.ppermute(x, 'seq', [(i, (i + step) % seq_count) for i in range(seq_co...]
  transfers between devices with their start and end apart: 16 -> 44, of which waited for: 12 -> 16; matrix products, arithmetic and copies ran while one was open for 17% -> 18% of each run, Pallas kernels for 0% -> 12%
where the time goes in v1:
time: 917 us; the launch traced here: 913 us
  Pallas kernels  246 us (27%)
  waiting for transfers between devices  185 us (20%)
  blocking collectives  149 us (16%)
  matrix products  127 us (14%)
  starting transfers between devices  78.9 us (9%)
  local copies, waits for them, and re-layouts  72.8 us (8%)
  other arithmetic  36.9 us (4%)
  between operations  16.6 us (2%)
    pallas_call x1, Pallas kernels, attn_bwd(): pl.pallas_call(functools.partial(attn_bwd_kernel, tk=tk, tq=tq, scale=hea...  141 us
    ppermute x30, waiting for transfers between devices, turn(): lax.ppermute(x, 'seq', [(i, (i + step) % seq_count) for i in range(seq_co...  138 us
    dot_general x23, matrix products, mxu(): lax.dot_general(left, right, dims, preferred_element_type=jnp.float32)  121 us
    pallas_call x1, Pallas kernels, attn_fwd(): pl.pallas_call(functools.partial(attn_fwd_kernel, n=n, scale=scale), grid...  84 us
    psum x1, blocking collectives, per_device(): lax.psum(jnp.stack([gain_grad_one, shift_grad_one]), ('scene', 'seq'))  62.7 us
    ppermute x30, starting transfers between devices, turn(): lax.ppermute(x, 'seq', [(i, (i + step) % seq_count) for i in range(seq_co...  56.9 us
    ppermute x6, waiting for transfers between devices, hop(): lax.ppermute(x, 'seq', [(i, i + step) for i in range(seq_count) if 0 <= i...  47.6 us
    all_gather x1, blocking collectives, per_device(): cot_cells = lax.all_gather(cot_dec, 'seq', axis=0, tiled=True)  34.2 us
  transfers between devices with their start and end apart: 44, of which 16 were waited for; matrix products, arithmetic and copies ran while one was open for 18% of the time, Pallas kernels for 12%

profile of v1, /device:TPU:0, one launch (start us, length us, event | category | flops | bytes accessed | tf_op | source)
XLA Modules:
  0.0 912.6 jit_solution(15577661284743597280)
XLA Ops:
  14.9 6.7 collective-permute-start.1
  21.6 31.4 %collective-permute-done = bf16[768,1024]{1,0:T(8,128)(2,1)} collective-permute-done((bf16[768,1024]{1,0:T(8,128)(2,1)S(1)}, bf16[768,1024]{1,0:T(8,128)(2,1)}, u32[]{:S(2)}, u32[]{:S(2)}) %collective-permute-start) | collective-permute-done | bytes 1572896 | tf_op jit(solution)/shard_map/ppermute | solution.py:338
  54.3 5.8 collective-permute-start.3
  66.4 34.2 %all-gather = bf16[4,64,16]{1,2,0:T(8,128)(2,1)S(1)} all-gather(bf16[1,64,16]{1,2,0:T(8,128)(2,1)S(1)} %bitcast.105), channel_id=1, replica_groups=mesh['scene'=8,'seq'=4] {'seq'}, dimensions={0}, use_global_device_ids=true | all-gather | bytes 10240 | tf_op jit(solution)/shard_map/all_gather | solution.py:374
  106.8 5.0 collective-permute-start.5
  111.8 11.1 %all_gather.21 = bf16[1024,256]{1,0:T(8,128)(2,1)S(1)} all-gather(bf16[128,256]{1,0:T(8,128)(2,1)S(1)} %maximum_maximum_fusion), channel_id=1, replica_groups=mesh['scene'=8,'seq'=4] {'scene'}, dimensions={0}, use_global_device_ids=true | all-gather | bytes 589824 | tf_op jit(solution)/shard_map/all_gather | solution.py:360
  125.7 14.9 %collective-permute-done.4 = bf16[768,1024]{1,0:T(8,128)(2,1)S(1)} collective-permute-done((bf16[768,1024]{1,0:T(8,128)(2,1)}, bf16[768,1024]{1,0:T(8,128)(2,1)S(1)}, u32[]{:S(2)}, u32[]{:S(2)}) %collective-permute-start.4) | collective-permute-done | bytes 1572896 | tf_op jit(solution)/shard_map/ppermute | solution.py:338
  141.8 4.4 convert_reduce_fusion.1
  147.9 4.0 fusion.32
  151.9 6.0 fusion.58.refs_0_
  157.9 4.8 convolution_convert_fusion.5.refs_2_.refs_6_
  162.8 4.8 convolution_convert_fusion.4.refs_3_.refs_7_
  167.6 4.8 convolution_convert_fusion.3.refs_4_.refs_8_
  172.4 4.8 convolution_convert_fusion.2.refs_5_.refs_9_
  178.1 84.0 %attn_fwd.1 = (bf16[768,1024]{1,0:T(8,128)(2,1)}, f32[8,2,768]{2,1,0:T(2,128)}) custom-call(bf16[768,1024]{1,0:T(8,128)(2,1)} %fusion.58.refs_0_, bf16[768,128]{1,0:T(8,128)(2,1)} %broadcast_in_dim.90.refs_1_.bias_ref, bf16[768,2048]{1,0:T(8,128)(2,1)} %convolution_convert_fusion.5.refs_2_.refs_6_, ...), custom_call_target="tpu_custom_call" | custom-call | flops 38654705664 | bytes 15728640 | tf_op jit(solution)/shard_map/attn_fwd/pallas_call | solution.py:136
  273.5 4.4 fusion.110
  289.9 21.0 %fc1_gelu.1 = (bf16[768,4096]{1,0:T(8,128)(2,1)}, bf16[768,4096]{1,0:T(8,128)(2,1)}) custom-call(bf16[768,1024]{1,0:T(8,128)(2,1)} %add_convert_fusion.x_ref, bf16[1024,4096]{1,0:T(8,128)(2,1)} %all-gather.10.cloned.1.call-done.w_ref), custom_call_target="tpu_custom_call" | custom-call | flops 6442450944 | bytes 22544384 | tf_op jit(solution)/shard_map/fc1_gelu/pallas_call | solution.py:273
  310.9 11.0 %select_convert_fusion = bf16[768,1024]{1,0:T(8,128)(2,1)S(1)} fusion(f32[768,1024]{1,0:T(8,128)S(1)} %get-tuple-element.132, bf16[768,4096]{1,0:T(8,128)(2,1)} %get-tuple-element.21, bf16[4096,1024]{1,0:T(8,128)(2,1)} %all-gather.12.cloned.1.call-done, pred[768]{0:T(1024)(128)(4,1)S(1)} %copy-done.68), kind=kOutput, calls=%fused_computation.67 | convolution fusion | flops 6444810240 | bytes 19399424 | tf_op jit(solution)/shard_map/dot_general | solution.py:28
  322.2 15.2 %all_gather.26 = bf16[768,128]{1,0:T(8,128)(2,1)S(1)} all-gather(bf16[192,128]{1,0:T(8,128)(2,1)S(1)} %convolution_convert_fusion.13), channel_id=1, replica_groups=mesh['scene'=8,'seq'=4] {'seq'}, dimensions={0}, use_global_device_ids=true | all-gather | bytes 245760 | tf_op jit(solution)/shard_map/all_gather | solution.py:409
  341.9 13.4 %multiply_convert_fusion = bf16[768,4096]{1,0:T(8,128)(2,1)} fusion(bf16[768,4096]{1,0:T(8,128)(2,1)} %get-tuple-element.22, bf16[4096,1024]{1,0:T(8,128)(2,1)} %all-gather.12.cloned.1.call-done, f32[192,1024]{1,0:T(8,128)S(1)} %convolution_add_fusion, f32[576,1024]{1,0:T(8,128)S(1)} %copy-done.5), kind=kOutput, calls=%fused_computation | convolution fusion | flops 6455033856 | bytes 24117248 | tf_op jit(solution)/shard_map/dot_general | solution.py:28
  355.2 12.4 %multiply_reduce_fusion = (f32[1024]{0:T(1024)}, f32[768]{0:T(1024)S(1)}, f32[768]{0:T(1024)S(1)}, f32[1024]{0:T(1024)}, f32[768,1024]{1,0:T(8,128)S(1)}) fusion(f32[768,1024]{1,0:T(8,128)S(1)} %get-tuple-element.132, f32[768]{0:T(1024)S(1)} %add_rsqrt_fusion, f32[768]{0:T(1024)S(1)} %broadcast_multiply_fusion.4, f32[1024]{0:T(1024)S(1)} %get-tuple-element.74, ...), kind=kOutput, calls=%fused_computation.58 | convolution fusion | flops 6449524736 | bytes 20996096 | tf_op jit(solution)/shard_map/dot_general | solution.py:28
  379.4 14.5 %collective-permute-done.9 = f32[8,768]{1,0:T(8,128)S(1)} collective-permute-done((f32[8,768]{1,0:T(8,128)S(1)}, f32[8,768]{1,0:T(8,128)S(1)}, u32[]{:S(2)}, u32[]{:S(2)}) %collective-permute-start.9) | collective-permute-done | bytes 24608 | tf_op jit(solution)/shard_map/ppermute | solution.py:343
  393.9 9.3 %collective-permute-done.10 = f32[8,768]{1,0:T(8,128)S(1)} collective-permute-done((f32[8,768]{1,0:T(8,128)S(1)}, f32[8,768]{1,0:T(8,128)S(1)}, u32[]{:S(2)}, u32[]{:S(2)}) %collective-permute-start.10) | collective-permute-done | bytes 24608 | tf_op jit(solution)/shard_map/ppermute | solution.py:343
  407.8 141.4 %attn_bwd.1 = (bf16[3072,256]{1,0:T(8,128)(2,1)}, bf16[3072,256]{1,0:T(8,128)(2,1)}, bf16[3072,256]{1,0:T(8,128)(2,1)}) custom-call(bf16[3072,256]{1,0:T(8,128)(2,1)} %pad_maximum_fusion.2.q_ref, bf16[3072,256]{1,0:T(8,128)(2,1)} %pad_maximum_fusion.3.k_ref, bf16[3072,256]{1,0:T(8,128)(2,1)} %pad_maximum_fusion.4.v_ref, bf16[3072,256]{1,0:T(8,128)(2,1)} %copy-done.20, ...), custom_call_target="tpu_custom_call" | custom-call | flops 96636764160 | bytes 11010048 | tf_op jit(solution)/shard_map/attn_bwd/pallas_call | solution.py:233
  555.8 6.4 fusion.61
  564.1 3.2 convolution_convert_fusion.6
  570.2 11.6 %convolution_convert_fusion.1 = bf16[1024,4096]{1,0:T(8,128)(2,1)} fusion(bf16[768,1024]{1,0:T(8,128)(2,1)} %add_convert_fusion.x_ref, bf16[768,4096]{1,0:T(8,128)(2,1)} %multiply_convert_fusion), kind=kOutput, calls=%fused_computation.2 | convolution fusion | flops 6446645248 | bytes 16252928 | tf_op jit(solution)/shard_map/dot_general | solution.py:28
  584.0 11.7 %convolution_convert_fusion = bf16[4096,1024]{1,0:T(8,128)(2,1)} fusion(bf16[768,4096]{1,0:T(8,128)(2,1)} %get-tuple-element.21, f32[192,1024]{1,0:T(8,128)S(1)} %copy-done.11, f32[576,1024]{1,0:T(8,128)S(1)} %copy-done.6), kind=kOutput, calls=%fused_computation.1 | convolution fusion | flops 6449790976 | bytes 17825792 | tf_op jit(solution)/shard_map/dot_general | solution.py:28
  596.0 4.1 constant_dynamic-slice_fusion.8
  603.0 2.9 collective-permute-start.14
  608.2 25.4 %all-reduce.2 = (f32[32,64]{1,0:T(8,128)}, f32[64]{0:T(128)}, f32[64,4]{0,1:T(4,128)}) all-reduce(f32[32,64]{1,0:T(8,128)S(1)} %select_reduce_fusion, f32[64]{0:T(128)S(1)} %reduce_sum.226, f32[64,4]{0,1:T(4,128)S(1)} %select_reduce_fusion.1), channel_id=1, replica_groups=mesh['scene'=8,'seq'=4] {'scene'}, use_global_device_ids=true, to_apply=%region_25.26 | all-reduce | flops 2368 | bytes 18944 | tf_op jit(solution)/shard_map/psum | solution.py:548
  641.1 38.7 %collective-permute-done.13 = bf16[768,768]{1,0:T(8,128)(2,1)} collective-permute-done((bf16[768,768]{1,0:T(8,128)(2,1)S(1)}, bf16[768,768]{1,0:T(8,128)(2,1)}, u32[]{:S(2)}, u32[]{:S(2)}) %collective-permute-start.13) | collective-permute-done | bytes 1179680 | tf_op jit(solution)/shard_map/ppermute | solution.py:343
  689.7 4.7 fusion.54
  696.7 4.3 fusion.27
  701.0 62.7 %all-reduce.1 = (f32[2,1024]{1,0:T(2,128)S(1)}, f32[2,1024]{1,0:T(2,128)S(1)}) all-reduce(f32[2,1024]{1,0:T(2,128)S(1)} %pad_maximum_fusion.5, f32[2,1024]{1,0:T(2,128)S(1)} %pad_maximum_fusion.6), channel_id=1, replica_groups=mesh['scene'=8,'seq'=4] {'scene','seq'}, use_global_device_ids=true, to_apply=%region_16.17 | all-reduce | flops 4096 | bytes 32768 | tf_op jit(solution)/shard_map/psum | solution.py:546
  764.3 4.6 fusion.26
  771.4 3.0 collective-permute-start.17
  778.9 7.3 collective-permute-done.16
  789.1 5.6 collective-permute-start.20
  798.2 6.3 collective-permute-done.19
  809.7 3.5 collective-permute-done.21
  823.0 3.2 collective-permute-start.32
  827.4 15.8 %collective-permute-done.25 = bf16[128,1024]{1,0:T(8,128)(2,1)S(1)} collective-permute-done((bf16[128,1024]{1,0:T(8,128)(2,1)S(1)}, bf16[128,1024]{1,0:T(8,128)(2,1)S(1)}, u32[]{:S(2)}, u32[]{:S(2)}) %collective-permute-start.25) | collective-permute-done | bytes 262176 | tf_op jit(solution)/shard_map/ppermute | solution.py:343
  844.5 11.4 %collective-permute-start.27 = (bf16[128,1024]{1,0:T(8,128)(2,1)S(1)}, bf16[128,1024]{1,0:T(8,128)(2,1)S(1)}, u32[]{:S(2)}, u32[]{:S(2)}) collective-permute-start(bf16[128,1024]{1,0:T(8,128)(2,1)S(1)} %get-tuple-element.86), channel_id=1, source_target_pairs={{0,1},{1,2},{2,3},{3,0},{4,5},{5,6},{6,7},{7,4},{8,9},{9,10},{10,1... | collective-permute-start | bytes 786440 | tf_op jit(solution)/shard_map/ppermute | solution.py:343
  857.9 2.8 collective-permute-start.29
  860.8 15.3 %collective-permute-done.31 = bf16[512,256]{1,0:T(8,128)(2,1)S(1)} collective-permute-done((bf16[512,256]{1,0:T(8,128)(2,1)S(1)}, bf16[512,256]{1,0:T(8,128)(2,1)S(1)}, u32[]{:S(2)}, u32[]{:S(2)}) %collective-permute-start.31) | collective-permute-done | bytes 262176 | tf_op jit(solution)/shard_map/ppermute | solution.py:343
  883.4 8.3 collective-permute-done.28
  891.9 12.2 %collective-permute-done.34 = bf16[512,256]{1,0:T(8,128)(2,1)S(1)} collective-permute-done((bf16[512,256]{1,0:T(8,128)(2,1)S(1)}, bf16[512,256]{1,0:T(8,128)(2,1)S(1)}, u32[]{:S(2)}, u32[]{:S(2)}) %collective-permute-start.34) | collective-permute-done | bytes 262176 | tf_op jit(solution)/shard_map/ppermute | solution.py:343
  (387 shorter events, 151.4 us)
Async XLA Ops:
  7.2 144.7 %all-gather.6.cloned.1.call-start = ((), (), s32[]{:S(2)}) async-start(), calls=%async_computation.4 | async-start | bytes 7077888 | tf_op jit(solution)/shard_map/all_gather | solution.py:360
  9.7 263.8 %all-gather.8.cloned.1.call-start = ((), (), s32[]{:S(2)}) async-start(), calls=%async_computation.5 | async-start | bytes 2359296 | tf_op jit(solution)/shard_map/all_gather | solution.py:360
  10.5 279.4 %all-gather.10.cloned.1.call-start = ((), (), s32[]{:S(2)}) async-start(), calls=%async_computation.6 | async-start | bytes 9437184 | tf_op jit(solution)/shard_map/all_gather | solution.py:360
  13.3 51.4 %copy-start.61 = (f32[32,64]{1,0:T(8,128)S(1)}, f32[32,64]{1,0:T(8,128)}, u32[]{:S(2)}) copy-start(f32[32,64]{1,0:T(8,128)} %param.21) | copy-start | bytes 24580
  13.3 52.3 %copy-start.65 = (f32[64,4]{0,1:T(4,128)S(1)}, f32[64,4]{0,1:T(4,128)}, u32[]{:S(2)}) copy-start(f32[64,4]{0,1:T(4,128)} %param.23) | copy-start | bytes 3076
  13.3 53.1 %copy-start.62 = (bf16[64,16]{0,1:T(8,128)(2,1)S(1)}, bf16[64,16]{0,1:T(8,128)(2,1)}, u32[]{:S(2)}) copy-start(bf16[64,16]{0,1:T(8,128)(2,1)} %param.25) | copy-start | bytes 6148
  13.3 88.0 %copy-start.16 = (bf16[768,1024]{1,0:T(8,128)(2,1)S(1)}, bf16[768,1024]{1,0:T(8,128)(2,1)}, u32[]{:S(2)}) copy-start(bf16[768,1024]{1,0:T(8,128)(2,1)} %param.24) | copy-start | bytes 4718596
  13.4 297.5 %all-gather.12.cloned.1.call-start = ((), (), s32[]{:S(2)}) async-start(), calls=%async_computation.7 | async-start | bytes 9437184 | tf_op jit(solution)/shard_map/all_gather | solution.py:360
  13.4 39.6 %collective-permute-start = (bf16[768,1024]{1,0:T(8,128)(2,1)S(1)}, bf16[768,1024]{1,0:T(8,128)(2,1)}, u32[]{:S(2)}, u32[]{:S(2)}) collective-permute-start(bf16[768,1024]{1,0:T(8,128)(2,1)S(1)} %copy-done), channel_id=1, source_target_pairs={{1,0},{2,1},{3,2},{5,4},{6,5},{7,6},{9,8},{10,9},{11,10},{13,12},{... | collective-permute-start | bytes 4718600 | tf_op jit(solution)/shard_map/ppermute | solution.py:338
  14.9 39.4 %collective-permute-start.1 = (bf16[768,1024]{1,0:T(8,128)(2,1)S(1)}, bf16[768,1024]{1,0:T(8,128)(2,1)}, u32[]{:S(2)}, u32[]{:S(2)}) collective-permute-start(bf16[768,1024]{1,0:T(8,128)(2,1)S(1)} %copy-done), channel_id=1, source_target_pairs={{0,1},{1,2},{2,3},{4,5},{5,6},{6,7},{8,9},{9,10},{10,11},{12,13},{... | collective-permute-start | bytes 4718600 | tf_op jit(solution)/shard_map/ppermute | solution.py:338
  53.0 52.5 %collective-permute-start.2 = (bf16[768,1024]{1,0:T(8,128)(2,1)}, bf16[768,1024]{1,0:T(8,128)(2,1)}, u32[]{:S(2)}, u32[]{:S(2)}) collective-permute-start(bf16[768,1024]{1,0:T(8,128)(2,1)} %collective-permute-done), channel_id=1, source_target_pairs={{1,0},{2,1},{3,2},{5,4},{6,5},{7,6},{9,8},{10,9},{11,10},{13,12},{... | collective-permute-start | bytes 4718600 | tf_op jit(solution)/shard_map/ppermute | solution.py:338
  54.3 52.5 %collective-permute-start.3 = (bf16[768,1024]{1,0:T(8,128)(2,1)}, bf16[768,1024]{1,0:T(8,128)(2,1)}, u32[]{:S(2)}, u32[]{:S(2)}) collective-permute-start(bf16[768,1024]{1,0:T(8,128)(2,1)} %collective-permute-done.1), channel_id=1, source_target_pairs={{0,1},{1,2},{2,3},{4,5},{5,6},{6,7},{8,9},{9,10},{10,11},{12,13},{... | collective-permute-start | bytes 4718600 | tf_op jit(solution)/shard_map/ppermute | solution.py:338
  62.9 706.0 %reduce-scatter.7.cloned.1.call-start = ((), (), s32[]{:S(2)}) async-start(), calls=%async_computation.8 | async-start | bytes 1769472 | tf_op jit(solution)/shard_map/reduce_scatter | solution.py:505
  105.5 35.0 %collective-permute-start.4 = (bf16[768,1024]{1,0:T(8,128)(2,1)}, bf16[768,1024]{1,0:T(8,128)(2,1)S(1)}, u32[]{:S(2)}, u32[]{:S(2)}) collective-permute-start(bf16[768,1024]{1,0:T(8,128)(2,1)} %collective-permute-done.2), channel_id=1, source_target_pairs={{1,0},{2,1},{3,2},{5,4},{6,5},{7,6},{9,8},{10,9},{11,10},{13,12},{... | collective-permute-start | bytes 4718600 | tf_op jit(solution)/shard_map/ppermute | solution.py:338
  106.8 35.0 %collective-permute-start.5 = (bf16[768,1024]{1,0:T(8,128)(2,1)}, bf16[768,1024]{1,0:T(8,128)(2,1)S(1)}, u32[]{:S(2)}, u32[]{:S(2)}) collective-permute-start(bf16[768,1024]{1,0:T(8,128)(2,1)} %collective-permute-done.3), channel_id=1, source_target_pairs={{0,1},{1,2},{2,3},{4,5},{5,6},{6,7},{8,9},{9,10},{10,11},{12,13},{... | collective-permute-start | bytes 4718600 | tf_op jit(solution)/shard_map/ppermute | solution.py:338
  371.4 33.1 %collective-permute-start.6 = (bf16[768,256]{1,0:T(8,128)(2,1)S(1)}, bf16[768,256]{1,0:T(8,128)(2,1)}, u32[]{:S(2)}, u32[]{:S(2)}) collective-permute-start(bf16[768,256]{1,0:T(8,128)(2,1)S(1)} %get-tuple-element.109), channel_id=1, source_target_pairs={{0,1},{1,2},{2,3},{3,0},{4,5},{5,6},{6,7},{7,4},{8,9},{9,10},{10,1... | collective-permute-start | bytes 1179656 | tf_op jit(solution)/shard_map/ppermute | solution.py:343
  372.3 33.3 %collective-permute-start.7 = (bf16[768,256]{1,0:T(8,128)(2,1)S(1)}, bf16[768,256]{1,0:T(8,128)(2,1)}, u32[]{:S(2)}, u32[]{:S(2)}) collective-permute-start(bf16[768,256]{1,0:T(8,128)(2,1)S(1)} %get-tuple-element.108), channel_id=1, source_target_pairs={{0,2},{1,3},{2,0},{3,1},{4,6},{5,7},{6,4},{7,5},{8,10},{9,11},{10,... | collective-permute-start | bytes 1179656 | tf_op jit(solution)/shard_map/ppermute | solution.py:343
  374.7 31.9 %collective-permute-start.8 = (bf16[768,256]{1,0:T(8,128)(2,1)S(1)}, bf16[768,256]{1,0:T(8,128)(2,1)S(1)}, u32[]{:S(2)}, u32[]{:S(2)}) collective-permute-start(bf16[768,256]{1,0:T(8,128)(2,1)S(1)} %get-tuple-element.107), channel_id=1, source_target_pairs={{0,3},{1,0},{2,1},{3,2},{4,7},{5,4},{6,5},{7,6},{8,11},{9,8},{10,9... | collective-permute-start | bytes 1179656 | tf_op jit(solution)/shard_map/ppermute | solution.py:343
  377.2 16.7 %collective-permute-start.9 = (f32[8,768]{1,0:T(8,128)S(1)}, f32[8,768]{1,0:T(8,128)S(1)}, u32[]{:S(2)}, u32[]{:S(2)}) collective-permute-start(f32[8,768]{1,0:T(8,128)S(1)} %get-tuple-element.125), channel_id=1, source_target_pairs={{0,1},{1,2},{2,3},{3,0},{4,5},{5,6},{6,7},{7,4},{8,9},{9,10},{10,1... | collective-permute-start | bytes 73736 | tf_op jit(solution)/shard_map/ppermute | solution.py:343
  378.6 24.5 %collective-permute-start.10 = (f32[8,768]{1,0:T(8,128)S(1)}, f32[8,768]{1,0:T(8,128)S(1)}, u32[]{:S(2)}, u32[]{:S(2)}) collective-permute-start(f32[8,768]{1,0:T(8,128)S(1)} %get-tuple-element.126), channel_id=1, source_target_pairs={{0,2},{1,3},{2,0},{3,1},{4,6},{5,7},{6,4},{7,5},{8,10},{9,11},{10,... | collective-permute-start | bytes 73736 | tf_op jit(solution)/shard_map/ppermute | solution.py:343
  393.9 9.3 %collective-permute-start.11 = (f32[8,768]{1,0:T(8,128)S(1)}, f32[8,768]{1,0:T(8,128)S(1)}, u32[]{:S(2)}, u32[]{:S(2)}) collective-permute-start(f32[8,768]{1,0:T(8,128)S(1)} %get-tuple-element.124), channel_id=1, source_target_pairs={{0,3},{1,0},{2,1},{3,2},{4,7},{5,4},{6,5},{7,6},{8,11},{9,8},{10,9... | collective-permute-start | bytes 73736 | tf_op jit(solution)/shard_map/ppermute | solution.py:343
  562.2 224.5 %reduce-scatter.13.cloned.1.call-start = ((), (), s32[]{:S(2)}) async-start(), calls=%async_computation.11 | async-start | bytes 2654208
  570.2 245.8 %reduce-scatter.9.cloned.1.call-start = ((), (), s32[]{:S(2)}) async-start(), calls=%async_computation.9 | async-start | bytes 9437184 | tf_op jit(solution)/shard_map/reduce_scatter | solution.py:505
  581.9 239.9 %reduce-scatter.11.cloned.1.call-start = ((), (), s32[]{:S(2)}) async-start(), calls=%async_computation.10 | async-start | bytes 9437184 | tf_op jit(solution)/shard_map/reduce_scatter | solution.py:505
  600.1 38.7 %collective-permute-start.12 = (bf16[768,768]{1,0:T(8,128)(2,1)}, bf16[768,768]{1,0:T(8,128)(2,1)}, u32[]{:S(2)}, u32[]{:S(2)}) collective-permute-start(bf16[768,768]{1,0:T(8,128)(2,1)} %get-tuple-element.95), channel_id=1, source_target_pairs={{0,1},{1,2},{2,3},{3,0},{4,5},{5,6},{6,7},{7,4},{8,9},{9,10},{10,1... | collective-permute-start | bytes 3538952 | tf_op jit(solution)/shard_map/ppermute | solution.py:343
  601.4 78.4 %collective-permute-start.13 = (bf16[768,768]{1,0:T(8,128)(2,1)S(1)}, bf16[768,768]{1,0:T(8,128)(2,1)}, u32[]{:S(2)}, u32[]{:S(2)}) collective-permute-start(bf16[768,768]{1,0:T(8,128)(2,1)S(1)} %get-tuple-element.94), channel_id=1, source_target_pairs={{0,2},{1,3},{2,0},{3,1},{4,6},{5,7},{6,4},{7,5},{8,10},{9,11},{10,... | collective-permute-start | bytes 3538952 | tf_op jit(solution)/shard_map/ppermute | solution.py:343
  603.0 79.0 %collective-permute-start.14 = (bf16[768,768]{1,0:T(8,128)(2,1)}, bf16[768,768]{1,0:T(8,128)(2,1)}, u32[]{:S(2)}, u32[]{:S(2)}) collective-permute-start(bf16[768,768]{1,0:T(8,128)(2,1)} %get-tuple-element.93), channel_id=1, source_target_pairs={{0,3},{1,0},{2,1},{3,2},{4,7},{5,4},{6,5},{7,6},{8,11},{9,8},{10,9... | collective-permute-start | bytes 3538952 | tf_op jit(solution)/shard_map/ppermute | solution.py:343
  768.9 9.9 %collective-permute-start.15 = (bf16[128,768]{1,0:T(8,128)(2,1)}, bf16[128,768]{1,0:T(8,128)(2,1)S(1)}, u32[]{:S(2)}, u32[]{:S(2)}) collective-permute-start(bf16[128,768]{1,0:T(8,128)(2,1)} %reduce-scatter.7.cloned.1.call-done), channel_id=1, source_target_pairs={{0,1},{1,2},{2,3},{3,0},{4,5},{5,6},{6,7},{7,4},{8,9},{9,10},{10,1... | collective-permute-start | bytes 589832 | tf_op jit(solution)/shard_map/ppermute | solution.py:343
  770.5 15.8 %collective-permute-start.16 = (bf16[128,768]{1,0:T(8,128)(2,1)}, bf16[128,768]{1,0:T(8,128)(2,1)S(1)}, u32[]{:S(2)}, u32[]{:S(2)}) collective-permute-start(bf16[128,768]{1,0:T(8,128)(2,1)} %reduce-scatter.7.cloned.1.call-done), channel_id=1, source_target_pairs={{0,2},{1,3},{2,0},{3,1},{4,6},{5,7},{6,4},{7,5},{8,10},{9,11},{10,... | collective-permute-start | bytes 589832 | tf_op jit(solution)/shard_map/ppermute | solution.py:343
  771.4 15.0 %collective-permute-start.17 = (bf16[128,768]{1,0:T(8,128)(2,1)}, bf16[128,768]{1,0:T(8,128)(2,1)S(1)}, u32[]{:S(2)}, u32[]{:S(2)}) collective-permute-start(bf16[128,768]{1,0:T(8,128)(2,1)} %reduce-scatter.7.cloned.1.call-done), channel_id=1, source_target_pairs={{0,3},{1,0},{2,1},{3,2},{4,7},{5,4},{6,5},{7,6},{8,11},{9,8},{10,9... | collective-permute-start | bytes 589832 | tf_op jit(solution)/shard_map/ppermute | solution.py:343
  789.1 9.1 %collective-permute-start.20 = (bf16[128,384]{0,1:T(8,128)(2,1)}, bf16[128,384]{0,1:T(8,128)(2,1)S(1)}, u32[]{:S(2)}, u32[]{:S(2)}) collective-permute-start(bf16[128,384]{0,1:T(8,128)(2,1)} %get-tuple-element.121), channel_id=1, source_target_pairs={{0,3},{1,0},{2,1},{3,2},{4,7},{5,4},{6,5},{7,6},{8,11},{9,8},{10,9... | collective-permute-start | bytes 294920 | tf_op jit(solution)/shard_map/ppermute | solution.py:343
  794.7 9.8 %collective-permute-start.19 = (bf16[128,384]{0,1:T(8,128)(2,1)}, bf16[128,384]{0,1:T(8,128)(2,1)}, u32[]{:S(2)}, u32[]{:S(2)}) collective-permute-start(bf16[128,384]{0,1:T(8,128)(2,1)} %get-tuple-element.120), channel_id=1, source_target_pairs={{0,2},{1,3},{2,0},{3,1},{4,6},{5,7},{6,4},{7,5},{8,10},{9,11},{10,... | collective-permute-start | bytes 294920 | tf_op jit(solution)/shard_map/ppermute | solution.py:343
  795.1 9.4 %collective-permute-start.18 = (bf16[128,384]{0,1:T(8,128)(2,1)}, bf16[128,384]{0,1:T(8,128)(2,1)}, u32[]{:S(2)}, u32[]{:S(2)}) collective-permute-start(bf16[128,384]{0,1:T(8,128)(2,1)} %get-tuple-element.119), channel_id=1, source_target_pairs={{0,1},{1,2},{2,3},{3,0},{4,5},{5,6},{6,7},{7,4},{8,9},{9,10},{10,1... | collective-permute-start | bytes 294920 | tf_op jit(solution)/shard_map/ppermute | solution.py:343
  805.7 7.5 collective-permute-start.21
  805.8 10.1 %collective-permute-start.22 = (bf16[128,384]{0,1:T(8,128)(2,1)S(1)}, bf16[128,384]{0,1:T(8,128)(2,1)S(1)}, u32[]{:S(2)}, u32[]{:S(2)}) collective-permute-start(bf16[128,384]{0,1:T(8,128)(2,1)S(1)} %add_convert_fusion.3), channel_id=1, source_target_pairs={{0,2},{1,3},{2,0},{3,1},{4,6},{5,7},{6,4},{7,5},{8,10},{9,11},{10,... | collective-permute-start | bytes 294920 | tf_op jit(solution)/shard_map/ppermute | solution.py:343
  806.9 13.4 %collective-permute-start.23 = (bf16[128,384]{0,1:T(8,128)(2,1)S(1)}, bf16[128,384]{0,1:T(8,128)(2,1)S(1)}, u32[]{:S(2)}, u32[]{:S(2)}) collective-permute-start(bf16[128,384]{0,1:T(8,128)(2,1)S(1)} %add_convert_fusion.3), channel_id=1, source_target_pairs={{0,3},{1,0},{2,1},{3,2},{4,7},{5,4},{6,5},{7,6},{8,11},{9,8},{10,9... | collective-permute-start | bytes 294920 | tf_op jit(solution)/shard_map/ppermute | solution.py:343
  817.2 10.2 %collective-permute-start.26 = (bf16[128,1024]{1,0:T(8,128)(2,1)S(1)}, bf16[128,1024]{1,0:T(8,128)(2,1)S(1)}, u32[]{:S(2)}, u32[]{:S(2)}) collective-permute-start(bf16[128,1024]{1,0:T(8,128)(2,1)S(1)} %get-tuple-element.117), channel_id=1, source_target_pairs={{0,3},{1,0},{2,1},{3,2},{4,7},{5,4},{6,5},{7,6},{8,11},{9,8},{10,9... | collective-permute-start | bytes 786440 | tf_op jit(solution)/shard_map/ppermute | solution.py:343
  819.6 23.6 %collective-permute-start.25 = (bf16[128,1024]{1,0:T(8,128)(2,1)S(1)}, bf16[128,1024]{1,0:T(8,128)(2,1)S(1)}, u32[]{:S(2)}, u32[]{:S(2)}) collective-permute-start(bf16[128,1024]{1,0:T(8,128)(2,1)S(1)} %get-tuple-element.118), channel_id=1, source_target_pairs={{0,2},{1,3},{2,0},{3,1},{4,6},{5,7},{6,4},{7,5},{8,10},{9,11},{10,... | collective-permute-start | bytes 786440 | tf_op jit(solution)/shard_map/ppermute | solution.py:343
  819.6 23.6 %collective-permute-start.24 = (bf16[128,1024]{1,0:T(8,128)(2,1)S(1)}, bf16[128,1024]{1,0:T(8,128)(2,1)S(1)}, u32[]{:S(2)}, u32[]{:S(2)}) collective-permute-start(bf16[128,1024]{1,0:T(8,128)(2,1)S(1)} %get-tuple-element.116), channel_id=1, source_target_pairs={{0,1},{1,2},{2,3},{3,0},{4,5},{5,6},{6,7},{7,4},{8,9},{9,10},{10,1... | collective-permute-start | bytes 786440 | tf_op jit(solution)/shard_map/ppermute | solution.py:343
  823.0 34.9 %collective-permute-start.32 = (bf16[512,256]{1,0:T(8,128)(2,1)S(1)}, bf16[512,256]{1,0:T(8,128)(2,1)S(1)}, u32[]{:S(2)}, u32[]{:S(2)}) collective-permute-start(bf16[512,256]{1,0:T(8,128)(2,1)S(1)} %get-tuple-element.114), channel_id=1, source_target_pairs={{0,3},{1,0},{2,1},{3,2},{4,7},{5,4},{6,5},{7,6},{8,11},{9,8},{10,9... | collective-permute-start | bytes 786440 | tf_op jit(solution)/shard_map/ppermute | solution.py:343
  826.3 49.8 %collective-permute-start.31 = (bf16[512,256]{1,0:T(8,128)(2,1)S(1)}, bf16[512,256]{1,0:T(8,128)(2,1)S(1)}, u32[]{:S(2)}, u32[]{:S(2)}) collective-permute-start(bf16[512,256]{1,0:T(8,128)(2,1)S(1)} %get-tuple-element.115), channel_id=1, source_target_pairs={{0,2},{1,3},{2,0},{3,1},{4,6},{5,7},{6,4},{7,5},{8,10},{9,11},{10,... | collective-permute-start | bytes 786440 | tf_op jit(solution)/shard_map/ppermute | solution.py:343
  827.4 48.7 %collective-permute-start.30 = (bf16[512,256]{1,0:T(8,128)(2,1)S(1)}, bf16[512,256]{1,0:T(8,128)(2,1)S(1)}, u32[]{:S(2)}, u32[]{:S(2)}) collective-permute-start(bf16[512,256]{1,0:T(8,128)(2,1)S(1)} %get-tuple-element.113), channel_id=1, source_target_pairs={{0,1},{1,2},{2,3},{3,0},{4,5},{5,6},{6,7},{7,4},{8,9},{9,10},{10,1... | collective-permute-start | bytes 786440 | tf_op jit(solution)/shard_map/ppermute | solution.py:343
  844.5 36.0 %collective-permute-start.27 = (bf16[128,1024]{1,0:T(8,128)(2,1)S(1)}, bf16[128,1024]{1,0:T(8,128)(2,1)S(1)}, u32[]{:S(2)}, u32[]{:S(2)}) collective-permute-start(bf16[128,1024]{1,0:T(8,128)(2,1)S(1)} %get-tuple-element.86), channel_id=1, source_target_pairs={{0,1},{1,2},{2,3},{3,0},{4,5},{5,6},{6,7},{7,4},{8,9},{9,10},{10,1... | collective-permute-start | bytes 786440 | tf_op jit(solution)/shard_map/ppermute | solution.py:343
  855.9 35.7 %collective-permute-start.28 = (bf16[128,1024]{1,0:T(8,128)(2,1)S(1)}, bf16[128,1024]{1,0:T(8,128)(2,1)S(1)}, u32[]{:S(2)}, u32[]{:S(2)}) collective-permute-start(bf16[128,1024]{1,0:T(8,128)(2,1)S(1)} %get-tuple-element.86), channel_id=1, source_target_pairs={{0,2},{1,3},{2,0},{3,1},{4,6},{5,7},{6,4},{7,5},{8,10},{9,11},{10,... | collective-permute-start | bytes 786440 | tf_op jit(solution)/shard_map/ppermute | solution.py:343
  857.9 33.8 %collective-permute-start.29 = (bf16[128,1024]{1,0:T(8,128)(2,1)S(1)}, bf16[128,1024]{1,0:T(8,128)(2,1)S(1)}, u32[]{:S(2)}, u32[]{:S(2)}) collective-permute-start(bf16[128,1024]{1,0:T(8,128)(2,1)S(1)} %get-tuple-element.86), channel_id=1, source_target_pairs={{0,3},{1,0},{2,1},{3,2},{4,7},{5,4},{6,5},{7,6},{8,11},{9,8},{10,9... | collective-permute-start | bytes 786440 | tf_op jit(solution)/shard_map/ppermute | solution.py:343
  877.4 14.4 %collective-permute-start.33 = (bf16[512,256]{1,0:T(8,128)(2,1)S(1)}, bf16[512,256]{1,0:T(8,128)(2,1)S(1)}, u32[]{:S(2)}, u32[]{:S(2)}) collective-permute-start(bf16[512,256]{1,0:T(8,128)(2,1)S(1)} %get-tuple-element.84), channel_id=1, source_target_pairs={{0,1},{1,2},{2,3},{3,0},{4,5},{5,6},{6,7},{7,4},{8,9},{9,10},{10,1... | collective-permute-start | bytes 786440 | tf_op jit(solution)/shard_map/ppermute | solution.py:343
  878.5 25.6 %collective-permute-start.34 = (bf16[512,256]{1,0:T(8,128)(2,1)S(1)}, bf16[512,256]{1,0:T(8,128)(2,1)S(1)}, u32[]{:S(2)}, u32[]{:S(2)}) collective-permute-start(bf16[512,256]{1,0:T(8,128)(2,1)S(1)} %get-tuple-element.84), channel_id=1, source_target_pairs={{0,2},{1,3},{2,0},{3,1},{4,6},{5,7},{6,4},{7,5},{8,10},{9,11},{10,... | collective-permute-start | bytes 786440 | tf_op jit(solution)/shard_map/ppermute | solution.py:343
  880.5 23.7 %collective-permute-start.35 = (bf16[512,256]{1,0:T(8,128)(2,1)S(1)}, bf16[512,256]{1,0:T(8,128)(2,1)S(1)}, u32[]{:S(2)}, u32[]{:S(2)}) collective-permute-start(bf16[512,256]{1,0:T(8,128)(2,1)S(1)} %get-tuple-element.84), channel_id=1, source_target_pairs={{0,3},{1,0},{2,1},{3,2},{4,7},{5,4},{6,5},{7,6},{8,11},{9,8},{10,9... | collective-permute-start | bytes 786440 | tf_op jit(solution)/shard_map/ppermute | solution.py:343
  (73 other events, 762.6 us)
Sparse Core Ops, SparseCore 0:
  10.5 48.1 all-gather.5
  60.5 27.7 all-gather.7
  90.2 54.9 all-gather.9
  146.9 53.5 all-gather.11
  562.3 38.7 reduce-scatter.6
  604.4 42.3 reduce-scatter.12
  650.2 71.4 reduce-scatter.8
  725.2 72.0 reduce-scatter.10

commit v2 on v1

v2 whole, which is shorter than its diff:
```python
import functools

import jax
import jax.numpy as jnp
from jax import lax
from jax.experimental import pallas as pl
from jax.experimental.pallas import tpu as pltpu
from jax.sharding import PartitionSpec as P

H = 16
TF = 32
PP = 4
OUT = 4
TG = 16
IMG_DEV = 576

EPS = 1e-05
NEG_FILL = -1e30
LOG2E = 1.4426950408889634
VMEM_BYTES = 60 * 2**20

NT = (((1,), (1,)), ((), ()))
NN = (((1,), (0,)), ((), ()))
TN = (((0,), (0,)), ((), ()))


def mxu(left, right, dims):
    return lax.dot_general(left, right, dims, preferred_element_type=jnp.float32)


def exact(left, right, dims):
    return lax.dot_general(
        left, right, dims, precision=lax.Precision.HIGHEST, preferred_element_type=jnp.float32
    )


def gelu_parts(v):
    a = jnp.abs(v) * 0.7071067811865476
    t = 1.0 / (1.0 + 0.3275911 * a)
    poly = t * (
        0.254829592
        + t * (-0.284496736 + t * (1.421413741 + t * (-1.453152027 + t * 1.061405429)))
    )
    e = jnp.exp(-a * a)
    tail = 0.5 * poly * e
    cdf = jnp.where(v >= 0.0, 1.0 - tail, tail)
    return v * cdf, cdf + v * (e * 0.3989422804014327)


def pair_keys(block, bias, head, half):
    lane = lax.broadcasted_iota(jnp.int32, block.shape, 1)
    mine = (lane < half) if head == 0 else (lane >= half)
    flag = half if head == 0 else 0
    zero = jnp.zeros_like(block)
    return jnp.where(mine, block, jnp.where(lane == flag, bias, zero))


def pair_queries(block, head, half):
    lane = lax.broadcasted_iota(jnp.int32, block.shape, 1)
    mine = (lane < half) if head == 0 else (lane >= half)
    flag = half if head == 0 else 0
    zero = jnp.zeros_like(block)
    return jnp.where(mine, block, jnp.where(lane == flag, jnp.ones_like(block), zero))


def pair_mask(block, head, half):
    lane = lax.broadcasted_iota(jnp.int32, block.shape, 1)
    mine = (lane < half) if head == 0 else (lane >= half)
    return jnp.where(mine, block, jnp.zeros_like(block))


def attn_fwd_kernel(*refs, first, last, sub, scale):
    q_ref, k_ref, v_ref, bias_ref = refs[:4]
    refs = refs[4:]
    if not first:
        acc_in, peak_in = refs[:2]
        refs = refs[2:]
    out_a, out_b, s_buf, k_buf, vt_buf, acc_buf = refs
    tq, lanes = q_ref.shape
    n = k_ref.shape[0] // sub
    half = lanes // 2
    q = q_ref[...]
    qs = [pair_queries(q, h, half) for h in range(2)]
    ones = jnp.ones((16, sub), jnp.bfloat16)
    for i in range(n):
        rows = slice(i * sub, i * sub + sub)
        kb, bias = k_ref[rows, :], bias_ref[rows, :]
        vt = v_ref[rows, :].T
        for h in range(2):
            k_buf[i, h] = pair_keys(kb, bias, h, half)
            vt_buf[i, h, :half] = vt[h * half : h * half + half]
            vt_buf[i, h, half:] = ones

    def score(j, peak):
        out = []
        for h in range(2):
            s = mxu(k_buf[j, h], qs[h], NT)
            s_buf[j % 2, h] = s
            out.append(jnp.maximum(peak[h], jnp.max(s, axis=0, keepdims=True)))
        return out

    def mix(j, before, peak):
        for h in range(2):
            p = jnp.exp2((s_buf[j % 2, h] - peak[h]) * scale).astype(jnp.bfloat16)
            part = mxu(vt_buf[j, h], p, NN)
            if first and j == 0:
                acc_buf[h] = part
            else:
                fade = jnp.exp2((before[h] - peak[h]) * scale)
                old = acc_in[h] if j == 0 else acc_buf[h]
                acc_buf[h] = old * fade + part

    if first:
        before = [jnp.full((1, tq), -3e38, jnp.float32)] * 2
    else:
        before = [peak_in[h : h + 1, :] for h in range(2)]
    peak = score(0, before)
    for j in range(1, n):
        fresh = score(j, peak)
        mix(j - 1, before, peak)
        before, peak = peak, fresh
    mix(n - 1, before, peak)
    if last:
        outs = []
        for h in range(2):
            acc = acc_buf[h]
            total = acc[half : half + 1]
            outs.append(acc[:half] / total)
            out_b[h : h + 1, :] = peak[h] * scale + jnp.log2(total)
        out_a[...] = jnp.concatenate(outs, axis=0).T.astype(jnp.bfloat16)
    else:
        for h in range(2):
            out_a[h] = acc_buf[h]
            out_b[h : h + 1, :] = peak[h]


def attn_fwd(q_rows, kv_rows, bias, state, last, head_dim):
    lanes = 2 * head_dim
    tq, tk = q_rows.shape[0], kv_rows.shape[0]
    pairs = kv_rows.shape[1] // (3 * lanes)
    width = pairs * lanes
    ext = head_dim + 16
    sub = 256
    first = state is None
    block = lambda rows, off: pl.BlockSpec((rows, lanes), lambda h: (0, 3 * h + off))
    stat = pl.BlockSpec((None, 2, tq), lambda h: (h, 0, 0))
    carry = pl.BlockSpec((None, 2, ext, tq), lambda h: (h, 0, 0, 0))
    stat_shape = jax.ShapeDtypeStruct((pairs, 2, tq), jnp.float32)
    if last:
        out_specs = (pl.BlockSpec((tq, lanes), lambda h: (0, h)), stat)
        out_shape = (jax.ShapeDtypeStruct((tq, width), jnp.bfloat16), stat_shape)
    else:
        out_specs = (carry, stat)
        out_shape = (jax.ShapeDtypeStruct((pairs, 2, ext, tq), jnp.float32), stat_shape)
    return pl.pallas_call(
        functools.partial(
            attn_fwd_kernel, first=first, last=last, sub=sub, scale=head_dim**-0.5 * LOG2E
        ),
        grid=(pairs,),
        in_specs=[block(tq, 0), block(tk, 1), block(tk, 2), pl.BlockSpec((tk, lanes), lambda h: (0, 0))]
        + ([] if first else [carry, stat]),
        out_specs=out_specs,
        out_shape=out_shape,
        scratch_shapes=[
            pltpu.VMEM((2, 2, sub, tq), jnp.float32),
            pltpu.VMEM((tk // sub, 2, sub, lanes), jnp.bfloat16),
            pltpu.VMEM((tk // sub, 2, ext, sub), jnp.bfloat16),
            pltpu.VMEM((2, ext, tq), jnp.float32),
        ],
        compiler_params=pltpu.CompilerParams(vmem_limit_bytes=VMEM_BYTES),
        cost_estimate=pl.CostEstimate(
            flops=16 * tq * tk * width, bytes_accessed=2 * width * (2 * tq + 2 * tk), transcendentals=0
        ),
        name="attn_fwd",
    )(q_rows, kv_rows, kv_rows, bias, *(() if first else state))


def attn_bwd_kernel(
    q_ref, k_ref, v_ref, do_ref, lse_ref, del_ref, bias_ref,
    out_ref,
    s_buf, dp_buf, qm, km, dom, kt, qt, dot, dqa, dka, dva, *, tk, tq, scale, post
):
    nq = q_ref.shape[0] // tq
    nk = k_ref.shape[0] // tk
    half = q_ref.shape[1] // 2
    for i in range(nk):
        rows = slice(i * tk, i * tk + tk)
        for h in range(2):
            km[h, rows] = pair_keys(k_ref[rows, :], bias_ref[...], h, half)
    for h in range(2):
        qm[h] = pair_queries(q_ref[...], h, half)
        dom[h] = pair_mask(do_ref[...], h, half)
    kt[...] = k_ref[...].T
    qt[...] = q_ref[...].T
    dot[...] = do_ref[...].T
    for acc in (dqa, dka, dva):
        acc[...] = jnp.zeros(acc.shape, jnp.float32)

    def place(t):
        if isinstance(t, int):
            return t // nq * tk, t % nq * tq, t % 2
        return (
            pl.multiple_of(lax.div(t, nq) * tk, tk),
            pl.multiple_of(lax.rem(t, nq) * tq, tq),
            lax.rem(t, 2),
        )

    def score(t):
        k0, q0, slot = place(t)
        ks, qs = pl.ds(k0, tk), pl.ds(q0, tq)
        vv = v_ref[ks, :]
        for h in range(2):
            s_buf[slot, h] = mxu(km[h, ks, :], qm[h, qs, :], NT)
            dp_buf[slot, h] = mxu(vv, dom[h, qs, :], NT)

    def grads(t):
        k0, q0, slot = place(t)
        ks, qs = pl.ds(k0, tk), pl.ds(q0, tq)
        for h in range(2):
            p = jnp.exp2(s_buf[slot, h] * scale - lse_ref[h : h + 1, qs])
            ds = (p * (dp_buf[slot, h] - del_ref[h : h + 1, qs])).astype(jnp.bfloat16)
            pb = p.astype(jnp.bfloat16)
            r = slice(half * h, half * h + half)
            dqa[r, qs] += mxu(kt[r, ks], ds, NN)
            dva[r, ks] += mxu(dot[r, qs], pb, NT)
            dka[r, ks] += mxu(qt[r, qs], ds, NT)

    score(0)

    def body(t, carry):
        score(t)
        grads(t - 1)
        return carry

    lax.fori_loop(1, nq * nk, body, 0)
    grads(nq * nk - 1)
    lanes = 2 * half
    out_ref[:, :lanes] = (dqa[...] * post).T.astype(jnp.bfloat16)
    out_ref[:, lanes : 2 * lanes] = (dka[...] * post).T.astype(jnp.bfloat16)
    out_ref[:, 2 * lanes :] = dva[...].T.astype(jnp.bfloat16)


def attn_bwd(qkv, do, lse, delta, bias, pair, head_dim):
    rows = qkv.shape[0]
    tk = bias.shape[0]
    tq = tk
    lanes = 2 * head_dim
    block = lambda at: pl.BlockSpec((rows, lanes), lambda h: (0, at))
    stat = pl.BlockSpec((None, 2, rows), lambda h: (pair, 0, 0))
    return pl.pallas_call(
        functools.partial(
            attn_bwd_kernel, tk=tk, tq=tq, scale=head_dim**-0.5 * LOG2E, post=head_dim**-0.5
        ),
        grid=(1,),
        in_specs=[block(3 * pair), block(3 * pair + 1), block(3 * pair + 2), block(pair)]
        + [stat] * 2
        + [pl.BlockSpec((tk, lanes), lambda h: (0, 0))],
        out_specs=pl.BlockSpec((rows, 3 * lanes), lambda h: (0, 0)),
        out_shape=jax.ShapeDtypeStruct((rows, 3 * lanes), jnp.bfloat16),
        scratch_shapes=[
            pltpu.VMEM((2, 2, tk, tq), jnp.float32),
            pltpu.VMEM((2, 2, tk, tq), jnp.float32),
            pltpu.VMEM((2, rows, lanes), jnp.bfloat16),
            pltpu.VMEM((2, rows, lanes), jnp.bfloat16),
            pltpu.VMEM((2, rows, lanes), jnp.bfloat16),
            pltpu.VMEM((lanes, rows), jnp.bfloat16),
            pltpu.VMEM((lanes, rows), jnp.bfloat16),
            pltpu.VMEM((lanes, rows), jnp.bfloat16),
            pltpu.VMEM((lanes, rows), jnp.float32),
            pltpu.VMEM((lanes, rows), jnp.float32),
            pltpu.VMEM((lanes, rows), jnp.float32),
        ],
        compiler_params=pltpu.CompilerParams(vmem_limit_bytes=VMEM_BYTES),
        cost_estimate=pl.CostEstimate(
            flops=40 * rows * rows * lanes, bytes_accessed=14 * rows * lanes, transcendentals=0
        ),
        name="attn_bwd",
    )(qkv, qkv, qkv, do, lse, delta, bias)


def fc1_kernel(x_ref, w_ref, act_ref, slope_ref):
    act, slope = gelu_parts(mxu(x_ref[...], w_ref[...], NN))
    act_ref[...] = act.astype(jnp.bfloat16)
    slope_ref[...] = slope.astype(jnp.bfloat16)


def fc1_gelu(x, w):
    rows, depth = x.shape
    cols = w.shape[1]
    tile = 512
    spec = pl.BlockSpec((rows, tile), lambda i: (0, i))
    return pl.pallas_call(
        fc1_kernel,
        grid=(cols // tile,),
        in_specs=[
            pl.BlockSpec((rows, depth), lambda i: (0, 0)),
            pl.BlockSpec((depth, tile), lambda i: (0, i)),
        ],
        out_specs=(spec, spec),
        out_shape=(jax.ShapeDtypeStruct((rows, cols), jnp.bfloat16),) * 2,
        compiler_params=pltpu.CompilerParams(vmem_limit_bytes=VMEM_BYTES),
        cost_estimate=pl.CostEstimate(
            flops=2 * rows * cols * depth,
            bytes_accessed=2 * (rows * depth + depth * cols + 2 * rows * cols),
            transcendentals=0,
        ),
        name="fc1_gelu",
    )(x, w)


def normalize(v):
    center = v - jnp.mean(v, axis=-1, keepdims=True)
    spread = jnp.mean(center * center, axis=-1, keepdims=True)
    inv = lax.rsqrt(spread + EPS)
    return center * inv, inv


def norm_back(g, u, inv, gain):
    q = g * gain
    back = inv * (
        q - jnp.mean(q, axis=-1, keepdims=True) - u * jnp.mean(q * u, axis=-1, keepdims=True)
    )
    return back, jnp.sum(g * u, axis=0), jnp.sum(g, axis=0)


def per_device(
    tokens,
    image_count,
    norm_params,
    w_qkv,
    w_proj,
    w_fc1,
    w_fc2,
    w_unpatch,
    w_dec1,
    b_dec1,
    w_dec2,
    cot_out,
    cot_dec,
):
    seq_count = lax.axis_size("seq")
    rank = lax.axis_index("seq")
    scene_rank = lax.axis_index("scene")
    tok_rows, width = tokens.shape
    head_dim = width // H
    cols = width // seq_count
    cells = TG * TG
    bf16, f32 = jnp.bfloat16, jnp.float32
    live_image = image_count[0] // seq_count
    pos = jnp.arange(tok_rows, dtype=jnp.int32)
    row_live = (pos >= IMG_DEV) | (pos < live_image)
    bias = jnp.broadcast_to(
        jnp.where(row_live, 0.0, NEG_FILL).astype(bf16)[:, None], (tok_rows, 2 * head_dim)
    )

    def hop(x, step):
        return lax.ppermute(
            x, "seq", [(i, i + step) for i in range(seq_count) if 0 <= i + step < seq_count]
        )

    def turn(x, step):
        return lax.ppermute(x, "seq", [(i, (i + step) % seq_count) for i in range(seq_count)])

    def ahead(d):
        return lax.rem(rank + d, seq_count)

    def behind(d):
        return lax.rem(rank - d + seq_count, seq_count)

    def slot_of(chunk):
        return jnp.where(chunk <= rank, rank - chunk, chunk)

    def piece(x, chunk, size, axis):
        return lax.dynamic_slice_in_dim(x, chunk * size, size, axis)

    cot_row = jnp.pad(cot_dec.reshape(1, -1), ((0, 15), (0, width - cot_dec.size)))
    parcel = jnp.concatenate([tokens, cot_row], axis=0)
    ups, downs = [parcel], [parcel]

    def move_on():
        ups.append(hop(ups[-1], 1))
        downs.append(hop(downs[-1], -1))

    move_on()
    move_on()

    def slot(d):
        pick = ups[d]
        for r in range(d):
            pick = jnp.where(rank == r, downs[d - r], pick)
        return pick

    lanes = 2 * head_dim
    pairs = width // lanes
    shard = w_qkv.shape[0]
    scene_count = width // shard

    def gather(w):
        return lax.all_gather(w.astype(bf16), "scene", axis=0, tiled=True)

    pair_order = w_qkv.astype(bf16).reshape(shard, 3, pairs, lanes).transpose(0, 2, 1, 3)
    first_w = lax.all_gather(
        jnp.concatenate(
            [
                pair_order.reshape(shard, 3 * width),
                w_unpatch.astype(bf16),
                jnp.pad(norm_params.astype(bf16), ((0, 0), (0, 124))),
            ],
            axis=1,
        ),
        "scene",
        axis=0,
        tiled=True,
    )
    qkv_w = first_w[:, : 3 * width]
    unpatch_w = first_w[:, 3 * width : 3 * width + PP * TF]
    norm_full = first_w[:, 3 * width + PP * TF : 3 * width + PP * TF + 4].astype(f32)
    gain_one, shift_one, gain_two, shift_two = (norm_full[:, i] for i in range(4))
    proj_w = gather(w_proj)
    fc1_w = gather(w_fc1)
    fc2_w = gather(w_fc2)

    a1, own, slots = [], [], []
    state = None
    for d in range(seq_count):
        slots.append(slot(d))
        u, _ = normalize(slots[d][:tok_rows].astype(f32))
        a = (u * gain_one + shift_one).astype(bf16)
        a1.append(a)
        qkv = mxu(a, qkv_w, NN).astype(bf16)
        own.append(piece(qkv, rank, 3 * cols, 1))
        if d == 0:
            q_rows = qkv
        state = attn_fwd(q_rows, qkv, bias, state, d == seq_count - 1, head_dim)
        if d + 2 < seq_count:
            ups[d + 2], downs[d + 2], state = lax.optimization_barrier(
                (ups[d + 2], downs[d + 2], state)
            )
            if d + 3 < seq_count:
                move_on()
    mixed, lse = state
    lse = lse.reshape(H, tok_rows)

    inputs_f = tokens.astype(f32)
    middle = inputs_f + mxu(mixed, proj_w, NN)
    u_two, inv_two = normalize(middle)
    a2 = (u_two * gain_two + shift_two).astype(bf16)
    act, slope = fc1_gelu(a2, fc1_w)
    triplane = (middle[IMG_DEV:] + mxu(act[IMG_DEV:], fc2_w, NN)).astype(bf16)
    tri_rows = tok_rows - IMG_DEV
    planes = mxu(triplane, unpatch_w, NN).astype(bf16)
    all_planes = jnp.zeros((seq_count * tri_rows, PP * TF), bf16)
    for d in range(seq_count):
        got = turn(planes, d) if d else planes
        all_planes = lax.dynamic_update_slice_in_dim(all_planes, got, behind(d) * tri_rows, 0)
    image_live = pos[:IMG_DEV] < live_image
    image_out = jnp.where(
        image_live[:, None], middle[:IMG_DEV] + mxu(act[:IMG_DEV], fc2_w, NN), 0.0
    ).astype(bf16)
    image_out, all_planes = lax.optimization_barrier((image_out, all_planes))
    block_out = jnp.concatenate([image_out, triplane], axis=0)

    cot_rows = jnp.zeros((seq_count, width), bf16)
    for d in range(seq_count):
        chunk = jnp.where(rank >= d, rank - d, d)
        cot_rows = lax.dynamic_update_slice_in_dim(
            cot_rows, slots[d][tok_rows : tok_rows + 1], chunk, 0
        )
    cot_cells = cot_rows[:, : cot_dec.size].reshape(cells, OUT * PP)
    planes_f = all_planes.astype(f32)
    feat = planes_f[:cells] + planes_f[cells : 2 * cells] + planes_f[2 * cells :]
    dh = w_dec1.shape[1]
    eye = jnp.eye(PP, dtype=f32)
    dec1 = jnp.einsum("fh,pq->pfqh", w_dec1, eye).reshape(PP * TF, PP * dh)
    dec2 = jnp.einsum("ho,pq->phoq", w_dec2, eye).reshape(PP * dh, OUT * PP)
    hidden_pre = exact(feat, dec1, NN) + jnp.tile(b_dec1, PP)
    zdec, zslope = gelu_parts(hidden_pre)
    decoded_all = exact(zdec, dec2, NN)
    cells_dev = cells // seq_count
    decoded = lax.dynamic_slice_in_dim(decoded_all, rank * cells_dev, cells_dev, 0)
    cot_f = cot_cells.astype(f32)
    grad_hidden = exact(cot_f, dec2, NT) * zslope
    gfeat = exact(grad_hidden, dec1, NT).astype(bf16)
    grad_w2 = jnp.einsum(
        "phop->ho", exact(zdec, cot_f, TN).reshape(PP, dh, OUT, PP)
    )
    grad_b1 = jnp.sum(jnp.sum(grad_hidden, axis=0).reshape(PP, dh), axis=0)
    grad_w1 = jnp.einsum(
        "pfph->fh", exact(feat, grad_hidden, TN).reshape(PP, TF, PP, dh)
    )
    plane_grad = lax.dynamic_slice_in_dim(
        jnp.concatenate([gfeat] * 4, axis=0), lax.rem(rank * tri_rows, cells), tri_rows, 0
    )
    grad_unpatch = mxu(triplane, plane_grad, TN)
    grad_tri = mxu(plane_grad, unpatch_w, NT)

    grad_result = jnp.where(row_live[:, None], cot_out.astype(f32), 0.0)
    grad_result = jnp.concatenate([grad_result[:IMG_DEV], grad_result[IMG_DEV:] + grad_tri], axis=0)
    branch = grad_result.astype(bf16)
    fc2_grad = mxu(act, branch, TN).astype(bf16)
    grad_pre = (mxu(branch, fc2_w, NT) * slope.astype(f32)).astype(bf16)
    back_two, gain_grad_two, shift_grad_two = norm_back(
        mxu(grad_pre, fc1_w, NT), u_two, inv_two, gain_two
    )
    grad_mid = grad_result + back_two
    mid_grad = grad_mid.astype(bf16)
    grad_mixed = mxu(mid_grad, proj_w, NT).astype(bf16)
    head_of = (jnp.arange(width) // head_dim)[None, :] == jnp.arange(H)[:, None]
    delta = exact(
        head_of.astype(f32), grad_mixed.astype(f32) * mixed.astype(f32), NT
    )
    heads_dev = H // seq_count
    stats = jnp.concatenate(
        [lse.reshape(seq_count, heads_dev, tok_rows), delta.reshape(seq_count, heads_dev, tok_rows)],
        axis=1,
    )
    parts, rest = [], stats
    for _ in range(3):
        top = lax.reduce_precision(rest, 8, 7)
        parts.append(top.astype(bf16))
        rest = rest - top
    stat_cols = jnp.concatenate(parts, axis=1).reshape(seq_count, -1, cols)
    stat_rows = stat_cols.shape[1]
    pad_rows = -stat_rows % 16
    letter = jnp.concatenate(
        [grad_mixed]
        + [
            jnp.pad(
                stat_cols.transpose(1, 0, 2).reshape(stat_rows, width), ((0, pad_rows), (0, 0))
            )
        ],
        axis=0,
    )
    letter, late_a2, late_pre, late_mid = lax.optimization_barrier((letter, a2, grad_pre, mid_grad))
    norm_cols = jnp.stack([gain_grad_two, shift_grad_two], axis=1).astype(bf16)
    wide_grad = jnp.concatenate(
        [
            mxu(late_a2, late_pre, TN).astype(bf16),
            mxu(mixed, late_mid, TN).astype(bf16),
            grad_unpatch.astype(bf16),
            jnp.pad(norm_cols, ((0, 0), (0, 128 * seq_count - PP * TF - 2))),
        ],
        axis=1,
    )
    do_all = jnp.zeros((seq_count * tok_rows, cols), bf16)
    stat_all = jnp.zeros((3, 2 * heads_dev, seq_count * tok_rows), f32)
    for d in range(seq_count):
        got = piece(letter, ahead(d), cols, 1)
        if d:
            got = turn(got, d)
        at = slot_of(behind(d)) * tok_rows
        do_all = lax.dynamic_update_slice_in_dim(do_all, got[:tok_rows], at, 0)
        got_stat = got[tok_rows : tok_rows + stat_rows].reshape(3, 2 * heads_dev, tok_rows)
        stat_all = lax.dynamic_update_slice_in_dim(stat_all, got_stat.astype(f32), at, 2)
    stat_all = stat_all[0] + stat_all[1] + stat_all[2]
    pairs_dev = heads_dev // 2
    lse_all = stat_all[:heads_dev].reshape(pairs_dev, 2, seq_count * tok_rows)
    delta_all = stat_all[heads_dev:].reshape(pairs_dev, 2, seq_count * tok_rows)
    own_all = jnp.concatenate(own, axis=0)
    dec_grads = lax.psum((grad_w1, grad_b1, grad_w2), "scene")

    def over_scene(g):
        return lax.psum_scatter(g, "scene", scatter_dimension=0, tiled=True)

    fc2_part = over_scene(fc2_grad)
    wide_part = over_scene(wide_grad)
    (own_all, do_all, lse_all, delta_all, wide_grad, dec_grads) = lax.optimization_barrier(
        (own_all, do_all, lse_all, delta_all, wide_grad, dec_grads)
    )

    def sum_pieces(part):
        size = part.shape[1] // seq_count
        return [
            turn(piece(part, ahead(d), size, 1), d) if d else piece(part, rank, size, 1)
            for d in range(seq_count)
        ]

    def over_seq(pieces):
        return over_cols(sum(x.astype(f32) for x in pieces).astype(bf16))

    def over_cols(mine):
        size = mine.shape[1]
        out = jnp.zeros((mine.shape[0], size * seq_count), f32)
        for d in range(seq_count):
            got = turn(mine, d) if d else mine
            out = lax.dynamic_update_slice_in_dim(out, got.astype(f32), behind(d) * size, 1)
        return out

    def exchange(mine):
        pieces = [piece(mine, slot_of(ahead(d)), tok_rows, 0) for d in range(seq_count)]
        return [turn(x, d) if d else x for d, x in enumerate(pieces)]

    moved, head_grads = [], []
    for p in range(pairs_dev):
        mine = attn_bwd(own_all, do_all, lse_all, delta_all, bias, p, head_dim)
        if p:
            mine, moved[-1], head_grads[-1], fc2_pieces = lax.optimization_barrier(
                (mine, moved[-1], head_grads[-1], fc2_pieces)
            )
        else:
            own_all, mine, fc2_part = lax.optimization_barrier((own_all, mine, fc2_part))
            fc2_pieces = sum_pieces(fc2_part)
        head_grads.append(mine)
        moved.append(exchange(mine))
    row_grads = jnp.zeros((tok_rows, 3 * width), bf16)
    for p in range(pairs_dev):
        for d in range(seq_count):
            row_grads = lax.dynamic_update_slice_in_dim(
                row_grads, moved[p][d], behind(d) * 3 * cols + p * 3 * lanes, 1
            )
    a1_all = jnp.concatenate(a1, axis=0)
    own_qkv = jnp.concatenate(
        [mxu(a1_all, part, TN).astype(bf16) for part in head_grads], axis=1
    )
    got_qkv = lax.all_to_all(
        own_qkv.reshape(scene_count, shard, 3 * cols), "scene", 0, 0, tiled=True
    )
    qkv_part = jnp.sum(got_qkv.astype(f32), axis=0).astype(bf16)

    grad_in = mxu(row_grads, qkv_w, NT)
    u_one, inv_one = normalize(inputs_f)
    back_one, gain_grad_one, shift_grad_one = norm_back(grad_in, u_one, inv_one, gain_one)
    grad_tokens = (grad_mid + back_one).astype(bf16)

    grad_fc2 = over_seq(fc2_pieces)
    grad_wide = over_seq(sum_pieces(wide_part))
    hidden = w_fc1.shape[1]
    grad_fc1, grad_misc = grad_wide[:, :hidden], grad_wide[:, hidden:]
    grad_proj = grad_misc[:, :width]
    grad_unp = grad_misc[:, width : width + PP * TF]
    norm_two = grad_misc[:, width + PP * TF : width + PP * TF + 2]
    qkv_all = over_cols(qkv_part)
    grad_qkv = qkv_all.reshape(shard, pairs, 3, lanes).transpose(0, 2, 1, 3).reshape(shard, 3 * width)

    norm_one = lax.psum(jnp.stack([gain_grad_one, shift_grad_one]), "scene")
    norm_one = lax.psum(lax.dynamic_slice_in_dim(norm_one, scene_rank * shard, shard, 1), "seq").T
    return (
        block_out,
        decoded,
        grad_tokens,
        norm_one,
        norm_two,
        grad_qkv,
        grad_proj,
        grad_fc1,
        grad_fc2,
        grad_unp,
        dec_grads[0],
        dec_grads[1],
        dec_grads[2],
    )


def solution(mesh):
    rows = P(("scene", "seq"), None)
    shard = P("scene", None)
    in_specs = (
        rows, P("scene"), shard, shard, shard, shard, shard, shard, P(), P(), P(), rows, rows
    )
    out_specs = (rows,) * 3 + (shard,) * 7 + (P(),) * 3
    return jax.shard_map(
        per_device, mesh=mesh, in_specs=in_specs, out_specs=out_specs, check_vma=False
    )
```

time: 917 us -> 776 us (0.85); the launches traced: 913 us -> 761 us
  blocking collectives: 149 us -> 48.3 us
  waiting for transfers between devices: 185 us -> 135 us
  other arithmetic: 36.9 us -> 62.8 us
  local copies, waits for them, and re-layouts: 72.8 us -> 58.3 us
  Pallas kernels: 246 us -> 235 us
  starting transfers between devices: 78.9 us -> 68.1 us
  matrix products: 127 us -> 137 us
    all_gather x3 -> x0, blocking collectives: 60.5 us -> none  [the longest x1 34.2 us: per_device(): cot_cells = lax.all_gather(cot_dec, 'seq', axis=0, tiled=True)]
    psum x1 -> x2, blocking collectives: 62.7 us -> 23.5 us  [the longest x1 13.8 us: per_device(): norm_one = lax.psum(jnp.stack([gain_grad_one, shift_grad_one]), 'scene')]
    ppermute x30 -> x27, waiting for transfers between devices: 138 us -> 98.5 us  [turn(): lax.ppermute(x, 'seq', [(i, (i + step) % seq_count) for i in range(seq_co...]
    pallas_call x1 -> x4, Pallas kernels: 84 us -> 69.4 us  [attn_fwd(): pl.pallas_call(functools.partial(attn_fwd_kernel, first=first, last=last,...]
    concatenate x5 -> x7, other arithmetic: 4.01 us -> 17.3 us  [the longest x1 10.5 us: per_device(): jnp.concatenate([mxu(late_a2, late_pre, TN).astype(bf16), mxu(mixed, late...]
    ppermute x30 -> x27, starting transfers between devices: 56.9 us -> 44.7 us  [turn(): lax.ppermute(x, 'seq', [(i, (i + step) % seq_count) for i in range(seq_co...]
    ppermute x6, waiting for transfers between devices: 47.6 us -> 35.9 us  [hop(): lax.ppermute(x, 'seq', [(i, i + step) for i in range(seq_count) if 0 <= i...]
    dynamic_slice x5 -> x0, local copies, waits for them, and re-layouts: 9.94 us -> none  [the longest x4 8.17 us: per_device(): head_v.append(lax.dynamic_slice_in_dim(kv, width + rank * cols, cols, 1))]
  transfers between devices with their start and end apart: 44 -> 40, of which waited for: 16 -> 15; matrix products, arithmetic and copies ran while one was open for 18% -> 28% of each run, Pallas kernels for 12% -> 31%
where the time goes in v2:
time: 776 us; the launch traced here: 761 us
  Pallas kernels  235 us (30%)
  matrix products  137 us (18%)
  waiting for transfers between devices  135 us (17%)
  starting transfers between devices  68.1 us (9%)
  other arithmetic  62.8 us (8%)
  local copies, waits for them, and re-layouts  58.3 us (8%)
  blocking collectives  48.3 us (6%)
  between operations  16.9 us (2%)
    pallas_call x2, Pallas kernels, attn_bwd(): pl.pallas_call(functools.partial(attn_bwd_kernel, tk=tk, tq=tq, scale=hea...  144 us
    dot_general x19, matrix products, mxu(): lax.dot_general(left, right, dims, preferred_element_type=jnp.float32)  129 us
    ppermute x27, waiting for transfers between devices, turn(): lax.ppermute(x, 'seq', [(i, (i + step) % seq_count) for i in range(seq_co...  98.5 us
    pallas_call x4, Pallas kernels, attn_fwd(): pl.pallas_call(functools.partial(attn_fwd_kernel, first=first, last=last,...  69.4 us
    ppermute x27, starting transfers between devices, turn(): lax.ppermute(x, 'seq', [(i, (i + step) % seq_count) for i in range(seq_co...  44.7 us
    ppermute x6, waiting for transfers between devices, hop(): lax.ppermute(x, 'seq', [(i, i + step) for i in range(seq_count) if 0 <= i...  35.9 us
    psum x1, blocking collectives, per_device(): dec_grads = lax.psum((grad_w1, grad_b1, grad_w2), 'scene')  24.8 us
    pallas_call x1, Pallas kernels, fc1_gelu(): pl.pallas_call(fc1_kernel, grid=(cols // tile,), in_specs=[pl.BlockSpec((...  21.3 us
  transfers between devices with their start and end apart: 40, of which 15 were waited for; matrix products, arithmetic and copies ran while one was open for 28% of the time, Pallas kernels for 31%

profile of v2, /device:TPU:0, one launch (start us, length us, event | category | flops | bytes accessed | tf_op | source)
XLA Modules:
  0.0 761.1 jit_solution(12146481648985674180)
XLA Ops:
  17.0 5.0 collective-permute-start.1
  32.5 24.1 %collective-permute-done.1 = bf16[784,1024]{1,0:T(8,128)(2,1)S(1)} collective-permute-done((bf16[784,1024]{1,0:T(8,128)(2,1)}, bf16[784,1024]{1,0:T(8,128)(2,1)S(1)}, u32[]{:S(2)}, u32[]{:S(2)}) %collective-permute-start.1) | collective-permute-done | bytes 1605664 | tf_op jit(solution)/shard_map/ppermute | solution.py:357
  57.7 3.1 collective-permute-done
  62.8 4.5 collective-permute-start.2
  72.5 10.2 %convolution_convert_fusion.5.refs_0_.refs_1_.refs_2_ = bf16[768,3072]{1,0:T(8,128)(2,1)} fusion(bf16[768,1024]{1,0:T(8,128)(2,1)S(1)} %get-tuple-element.215, bf16[1024,3328]{0,1:T(8,128)(2,1)} %all-gather.5.cloned.1.call-done), kind=kOutput, calls=%fused_computation.10 | convolution fusion | flops 4834197504 | bytes 12582912 | tf_op jit(solution)/shard_map/dot_general | solution.py:28
  83.5 16.2 %attn_fwd.4 = (f32[8,2,80,768]{3,2,1,0:T(8,128)}, f32[8,2,768]{2,1,0:T(2,128)}) custom-call(bf16[768,3072]{1,0:T(8,128)(2,1)} %convolution_convert_fusion.5.refs_0_.refs_1_.refs_2_, bf16[768,3072]{1,0:T(8,128)(2,1)} %convolution_convert_fusion.5.refs_0_.refs_1_.refs_2_, bf16[768,3072]{1,0:T(8,128)(2,1)} %convolution_convert_fusion.5.refs_0_.refs_1_.refs_2_, ...), custom_call_target="tpu_custom_call" | custom-call | flops 9663676416 | bytes 6291456 | tf_op jit(solution)/shard_map/attn_fwd/pallas_call | solution.py:155
  99.7 5.0 collective-permute-done.3
  105.9 5.9 collective-permute-start.4
  111.9 9.1 %convolution_convert_fusion.4.refs_1_.refs_2_ = bf16[768,3072]{1,0:T(8,128)(2,1)} fusion(bf16[768,1024]{1,0:T(8,128)(2,1)} %get-tuple-element.214, bf16[1024,3328]{0,1:T(8,128)(2,1)} %all-gather.5.cloned.1.call-done), kind=kOutput, calls=%fused_computation.9 | convolution fusion | flops 4834197504 | bytes 12582912 | tf_op jit(solution)/shard_map/dot_general | solution.py:28
  120.9 17.6 %attn_fwd.5 = (f32[8,2,80,768]{3,2,1,0:T(8,128)}, f32[8,2,768]{2,1,0:T(2,128)}) custom-call(bf16[768,3072]{1,0:T(8,128)(2,1)} %convolution_convert_fusion.5.refs_0_.refs_1_.refs_2_, bf16[768,3072]{1,0:T(8,128)(2,1)} %convolution_convert_fusion.4.refs_1_.refs_2_, bf16[768,3072]{1,0:T(8,128)(2,1)} %convolution_convert_fusion.4.refs_1_.refs_2_, ...), custom_call_target="tpu_custom_call" | custom-call | flops 9663676416 | bytes 6291456 | tf_op jit(solution)/shard_map/attn_fwd/pallas_call | solution.py:155
  142.2 2.9 select_select_fusion
  153.5 9.5 %convolution_convert_fusion.2.refs_1_.refs_2_ = bf16[768,3072]{1,0:T(8,128)(2,1)} fusion(bf16[768,1024]{1,0:T(8,128)(2,1)S(1)} %get-tuple-element.212, bf16[1024,3328]{0,1:T(8,128)(2,1)} %all-gather.5.cloned.1.call-done), kind=kOutput, calls=%fused_computation.7 | convolution fusion | flops 4834197504 | bytes 12582912 | tf_op jit(solution)/shard_map/dot_general | solution.py:28
  163.0 17.6 %attn_fwd.6 = (f32[8,2,80,768]{3,2,1,0:T(8,128)}, f32[8,2,768]{2,1,0:T(2,128)}) custom-call(bf16[768,3072]{1,0:T(8,128)(2,1)} %convolution_convert_fusion.5.refs_0_.refs_1_.refs_2_, bf16[768,3072]{1,0:T(8,128)(2,1)} %convolution_convert_fusion.2.refs_1_.refs_2_, bf16[768,3072]{1,0:T(8,128)(2,1)} %convolution_convert_fusion.2.refs_1_.refs_2_, ...), custom_call_target="tpu_custom_call" | custom-call | flops 9663676416 | bytes 6291456 | tf_op jit(solution)/shard_map/attn_fwd/pallas_call | solution.py:155
  180.6 9.5 %convolution_convert_fusion.3.refs_1_.refs_2_ = bf16[768,3072]{1,0:T(8,128)(2,1)} fusion(bf16[768,1024]{1,0:T(8,128)(2,1)S(1)} %copy-done.34, bf16[1024,3328]{0,1:T(8,128)(2,1)} %all-gather.5.cloned.1.call-done), kind=kOutput, calls=%fused_computation.8 | convolution fusion | flops 4834197504 | bytes 12582912 | tf_op jit(solution)/shard_map/dot_general | solution.py:28
  190.1 18.1 %attn_fwd.7 = (bf16[768,1024]{1,0:T(8,128)(2,1)}, f32[8,2,768]{2,1,0:T(2,128)}) custom-call(bf16[768,3072]{1,0:T(8,128)(2,1)} %convolution_convert_fusion.5.refs_0_.refs_1_.refs_2_, bf16[768,3072]{1,0:T(8,128)(2,1)} %convolution_convert_fusion.3.refs_1_.refs_2_, bf16[768,3072]{1,0:T(8,128)(2,1)} %convolution_convert_fusion.3.refs_1_.refs_2_, ...), custom_call_target="tpu_custom_call" | custom-call | flops 9663676416 | bytes 6291456 | tf_op jit(solution)/shard_map/attn_fwd/pallas_call | solution.py:155
  208.2 3.9 fusion.122
  215.6 21.3 %fc1_gelu.1 = (bf16[768,4096]{1,0:T(8,128)(2,1)}, bf16[768,4096]{1,0:T(8,128)(2,1)}) custom-call(bf16[768,1024]{1,0:T(8,128)(2,1)} %add_convert_fusion.x_ref, bf16[1024,4096]{1,0:T(8,128)(2,1)} %all-gather.9.cloned.1.call-done.w_ref), custom_call_target="tpu_custom_call" | custom-call | flops 6442450944 | bytes 22544384 | tf_op jit(solution)/shard_map/fc1_gelu/pallas_call | solution.py:292
  237.0 5.8 fusion.62
  245.4 3.0 collective-permute-start.7
  252.2 6.1 fusion.51
  267.7 11.8 %convolution_convert_fusion = bf16[4096,1024]{1,0:T(8,128)(2,1)} fusion(bf16[768,4096]{1,0:T(8,128)(2,1)} %get-tuple-element.72, f32[192,1024]{1,0:T(8,128)S(1)} %convolution_add_fusion, f32[576,1024]{1,0:T(8,128)S(1)} %copy-done.7), kind=kOutput, calls=%fused_computation.4 | convolution fusion | flops 6449790976 | bytes 17825792 | tf_op jit(solution)/shard_map/dot_general | solution.py:28
  279.8 3.2 constant_dynamic-slice_fusion.20
  286.4 3.2 pad_maximum_fusion.1.q_ref.k_ref.v_ref
  290.3 14.6 %multiply_convert_fusion = bf16[768,4096]{1,0:T(8,128)(2,1)} fusion(bf16[768,4096]{1,0:T(8,128)(2,1)} %get-tuple-element.75, bf16[4096,1024]{1,0:T(8,128)(2,1)} %all-gather.11.cloned.1.call-done, f32[192,1024]{1,0:T(8,128)S(1)} %copy-done.12, f32[576,1024]{1,0:T(8,128)S(1)} %copy-done.8), kind=kOutput, calls=%fused_computation.2 | convolution fusion | flops 6455033856 | bytes 24117248 | tf_op jit(solution)/shard_map/dot_general | solution.py:28
  304.9 11.8 %multiply_reduce_fusion = (bf16[1024]{0:T(1024)(128)(2,1)S(1)}, f32[768]{0:T(1024)S(1)}, f32[768]{0:T(1024)S(1)}, bf16[1024]{0:T(1024)(128)(2,1)S(1)}, f32[768,1024]{1,0:T(8,128)S(1)}) fusion(f32[768,1024]{1,0:T(8,128)S(1)} %copy-done.3, f32[768]{0:T(1024)S(1)} %add_rsqrt_fusion, f32[768]{0:T(1024)S(1)} %broadcast_multiply_fusion.4, f32[1024]{0:T(1024)S(1)} %bitcast.94, ...), kind=kOutput, calls=%fused_computation.67 | convolution fusion | flops 6449524736 | bytes 20992000 | tf_op jit(solution)/shard_map/dot_general | solution.py:28
  335.7 9.9 %convolution_convert_fusion.1 = bf16[1024,4096]{1,0:T(8,128)(2,1)S(1)} fusion(bf16[768,1024]{1,0:T(8,128)(2,1)S(1)} %copy-done.36, bf16[768,4096]{1,0:T(8,128)(2,1)} %multiply_convert_fusion), kind=kOutput, calls=%fused_computation.5 | convolution fusion | flops 6446645248 | bytes 16252928 | tf_op jit(solution)/shard_map/dot_general | solution.py:28
  345.7 10.5 %fusion.1 = bf16[1024,5632]{1,0:T(8,128)(2,1)} fusion(bf16[1024,2]{1,0:T(8,128)(2,1)S(1)} %copy-done.38, bf16[1024,128]{1,0:T(8,128)(2,1)S(1)} %convolution_convert_fusion.10, bf16[1024,1024]{1,0:T(8,128)(2,1)S(1)} %convolution_convert_fusion.6, bf16[1024,4096]{1,0:T(8,128)(2,1)S(1)} %convolution_convert_fusion.1), kind=kLoop, calls=%fused_computation.3 | loop fusion | flops 57671680 | bytes 22286336 | tf_op jit(solution)/shard_map/concatenate | solution.py:536
  357.7 24.8 %all-reduce.4 = (f32[32,64]{1,0:T(8,128)}, f32[64]{0:T(128)}, f32[64,4]{0,1:T(4,128)}) all-reduce(f32[32,64]{1,0:T(8,128)S(1)} %select_reduce_fusion, f32[64]{0:T(128)S(1)} %reduce_sum.234, f32[64,4]{0,1:T(4,128)S(1)} %fusion.65), channel_id=1, replica_groups=mesh['scene'=8,'seq'=4] {'scene'}, use_global_device_ids=true, to_apply=%region_15.16 | all-reduce | flops 2368 | bytes 18944 | tf_op jit(solution)/shard_map/psum | solution.py:560
  395.2 72.1 %attn_bwd.2 = bf16[3072,384]{1,0:T(8,128)(2,1)} custom-call(bf16[3072,768]{1,0:T(8,128)(2,1)} %pad_maximum_fusion.1.q_ref.k_ref.v_ref, bf16[3072,768]{1,0:T(8,128)(2,1)} %pad_maximum_fusion.1.q_ref.k_ref.v_ref, bf16[3072,768]{1,0:T(8,128)(2,1)} %pad_maximum_fusion.1.q_ref.k_ref.v_ref, bf16[3072,256]{1,0:T(8,128)(2,1)} %copy-done.26, ...), custom_call_target="tpu_custom_call" | custom-call | flops 48318382080 | bytes 5505024 | tf_op jit(solution)/shard_map/attn_bwd/pallas_call | solution.py:250
  481.0 10.1 %collective-permute-start.12 = (bf16[768,384]{1,0:T(8,128)(2,1)}, bf16[768,384]{1,0:T(8,128)(2,1)}, u32[]{:S(2)}, u32[]{:S(2)}) collective-permute-start(bf16[768,384]{1,0:T(8,128)(2,1)} %get-tuple-element.191), channel_id=1, source_target_pairs={{0,1},{1,2},{2,3},{3,0},{4,5},{5,6},{6,7},{7,4},{8,9},{9,10},{10,1... | collective-permute-start | bytes 1769480 | tf_op jit(solution)/shard_map/ppermute | solution.py:362
  491.1 72.0 %attn_bwd.3 = bf16[3072,384]{1,0:T(8,128)(2,1)} custom-call(bf16[3072,768]{1,0:T(8,128)(2,1)} %pad_maximum_fusion.1.q_ref.k_ref.v_ref, bf16[3072,768]{1,0:T(8,128)(2,1)} %pad_maximum_fusion.1.q_ref.k_ref.v_ref, bf16[3072,768]{1,0:T(8,128)(2,1)} %pad_maximum_fusion.1.q_ref.k_ref.v_ref, bf16[3072,256]{1,0:T(8,128)(2,1)} %copy-done.26, ...), custom_call_target="tpu_custom_call" | custom-call | flops 48318382080 | bytes 5505024 | tf_op jit(solution)/shard_map/attn_bwd/pallas_call | solution.py:250
  567.0 3.8 collective-permute-start.32
  570.8 4.3 convolution_convert_fusion.9
  575.1 4.4 convolution_convert_fusion.8
  581.0 3.8 all-to-all-start
  593.9 35.4 %collective-permute-done.18 = bf16[768,384]{1,0:T(8,128)(2,1)S(1)} collective-permute-done((bf16[768,384]{1,0:T(8,128)(2,1)S(1)}, bf16[768,384]{1,0:T(8,128)(2,1)S(1)}, u32[]{:S(2)}, u32[]{:S(2)}) %collective-permute-start.18) | collective-permute-done | bytes 589856 | tf_op jit(solution)/shard_map/ppermute | solution.py:362
  629.4 11.2 %collective-permute-done.19 = bf16[768,384]{1,0:T(8,128)(2,1)S(1)} collective-permute-done((bf16[768,384]{1,0:T(8,128)(2,1)S(1)}, bf16[768,384]{1,0:T(8,128)(2,1)S(1)}, u32[]{:S(2)}, u32[]{:S(2)}) %collective-permute-start.19) | collective-permute-done | bytes 589856 | tf_op jit(solution)/shard_map/ppermute | solution.py:362
  641.0 9.1 %fusion.31 = (f32[1024]{0:T(1024)S(1)}, f32[768]{0:T(1024)S(1)}, f32[768]{0:T(1024)S(1)}, f32[1024]{0:T(1024)S(1)}, f32[768,1024]{1,0:T(8,128)}) fusion(bf16[768,1024]{1,0:T(8,128)(2,1)S(1)} %copy-done.1, f32[768]{0:T(1024)S(1)} %copy-done.52, f32[768]{0:T(1024)S(1)} %copy-done.47, f32[1024]{0:T(1024)S(1)} %bitcast.91, ...), kind=kOutput, calls=%fused_computation.52 | convolution fusion | flops 4839698432 | bytes 15753216 | tf_op jit(solution)/shard_map/dot_general | solution.py:28
  650.1 13.8 %psum.38 = f32[2,1024]{1,0:T(2,128)S(1)} all-reduce(f32[2,1024]{1,0:T(2,128)S(1)} %pad_maximum_fusion.8), channel_id=1, replica_groups=mesh['scene'=8,'seq'=4] {'scene'}, use_global_device_ids=true, to_apply=%region_26.27 | all-reduce | flops 2048 | bytes 16384 | tf_op jit(solution)/shard_map/psum | solution.py:635
  663.9 9.8 %psum.39 = f32[128,2]{0,1:T(2,128)} all-reduce(f32[128,2]{0,1:T(2,128)S(1)} %fusion.101), channel_id=1, replica_groups=mesh['scene'=8,'seq'=4] {'seq'}, use_global_device_ids=true, to_apply=%region_27.28 | all-reduce | flops 256 | bytes 2048 | tf_op jit(solution)/shard_map/psum | solution.py:636
  673.7 4.3 fusion.30
  685.8 4.1 collective-permute-done.27
  691.8 5.8 collective-permute-done.21
  697.6 7.3 collective-permute-done.23
  704.9 18.4 %collective-permute-done.22 = bf16[128,1408]{1,0:T(8,128)(2,1)S(1)} collective-permute-done((bf16[128,1408]{1,0:T(8,128)(2,1)S(1)}, bf16[128,1408]{1,0:T(8,128)(2,1)S(1)}, u32[]{:S(2)}, u32[]{:S(2)}) %collective-permute-start.22) | collective-permute-done | bytes 360480 | tf_op jit(solution)/shard_map/ppermute | solution.py:362
  725.7 3.6 collective-permute-done.28
  731.5 3.0 copy.103
  738.7 11.4 %collective-permute-done.25 = bf16[128,1408]{1,0:T(8,128)(2,1)S(1)} collective-permute-done((bf16[128,1408]{1,0:T(8,128)(2,1)S(1)}, bf16[128,1408]{1,0:T(8,128)(2,1)S(1)}, u32[]{:S(2)}, u32[]{:S(2)}) %collective-permute-start.25) | collective-permute-done | bytes 360480 | tf_op jit(solution)/shard_map/ppermute | solution.py:362
  (353 shorter events, 148.3 us)
Async XLA Ops:
  7.2 62.3 %all-gather.5.cloned.1.call-start = ((), (), s32[]{:S(2)}) async-start(), calls=%async_computation.3 | async-start | bytes 7667712 | tf_op jit(solution)/shard_map/all_gather | solution.py:402
  11.8 196.5 %all-gather.7.cloned.1.call-start = ((), (), s32[]{:S(2)}) async-start(), calls=%async_computation.4 | async-start | bytes 2359296 | tf_op jit(solution)/shard_map/all_gather | solution.py:399
  12.6 203.0 %all-gather.9.cloned.1.call-start = ((), (), s32[]{:S(2)}) async-start(), calls=%async_computation.5 | async-start | bytes 9437184 | tf_op jit(solution)/shard_map/all_gather | solution.py:399
  15.4 221.6 %all-gather.11.cloned.1.call-start = ((), (), s32[]{:S(2)}) async-start(), calls=%async_computation.6 | async-start | bytes 9437184 | tf_op jit(solution)/shard_map/all_gather | solution.py:399
  17.0 39.6 %collective-permute-start.1 = (bf16[784,1024]{1,0:T(8,128)(2,1)}, bf16[784,1024]{1,0:T(8,128)(2,1)S(1)}, u32[]{:S(2)}, u32[]{:S(2)}) collective-permute-start(bf16[784,1024]{1,0:T(8,128)(2,1)} %fusion.54), channel_id=1, source_target_pairs={{0,1},{1,2},{2,3},{4,5},{5,6},{6,7},{8,9},{9,10},{10,11},{12,13},{... | collective-permute-start | bytes 4816904 | tf_op jit(solution)/shard_map/ppermute | solution.py:357
  22.0 38.8 %collective-permute-start = (bf16[784,1024]{1,0:T(8,128)(2,1)}, bf16[784,1024]{1,0:T(8,128)(2,1)}, u32[]{:S(2)}, u32[]{:S(2)}) collective-permute-start(bf16[784,1024]{1,0:T(8,128)(2,1)} %fusion.54), channel_id=1, source_target_pairs={{1,0},{2,1},{3,2},{5,4},{6,5},{7,6},{9,8},{10,9},{11,10},{13,12},{... | collective-permute-start | bytes 4816904 | tf_op jit(solution)/shard_map/ppermute | solution.py:357
  24.5 442.7 %reduce-scatter.3.cloned.1.call-start = ((), (), s32[]{:S(2)}) async-start(), calls=%async_computation.7 | async-start | bytes 9437184 | tf_op jit(solution)/shard_map/reduce_scatter | solution.py:563
  32.5 50.2 %copy-start.51 = (f32[768]{0:T(1024)}, f32[768]{0:T(1024)S(1)}, u32[]{:S(2)}) copy-start(f32[768]{0:T(1024)S(1)} %add_rsqrt_fusion.4) | copy-start | bytes 9220
  62.8 36.8 %collective-permute-start.2 = (bf16[784,1024]{1,0:T(8,128)(2,1)}, bf16[784,1024]{1,0:T(8,128)(2,1)}, u32[]{:S(2)}, u32[]{:S(2)}) collective-permute-start(bf16[784,1024]{1,0:T(8,128)(2,1)} %copy-done.20), channel_id=1, source_target_pairs={{0,1},{1,2},{2,3},{4,5},{5,6},{6,7},{8,9},{9,10},{10,11},{12,13},{... | collective-permute-start | bytes 4816904 | tf_op jit(solution)/shard_map/ppermute | solution.py:357
  67.4 37.3 %collective-permute-start.3 = (bf16[784,1024]{1,0:T(8,128)(2,1)}, bf16[784,1024]{1,0:T(8,128)(2,1)}, u32[]{:S(2)}, u32[]{:S(2)}) collective-permute-start(bf16[784,1024]{1,0:T(8,128)(2,1)} %collective-permute-done), channel_id=1, source_target_pairs={{1,0},{2,1},{3,2},{5,4},{6,5},{7,6},{9,8},{10,9},{11,10},{13,12},{... | collective-permute-start | bytes 4816904 | tf_op jit(solution)/shard_map/ppermute | solution.py:357
  70.3 79.4 %copy-start.48 = (f32[1024,1]{0,1:T(1,128)}, f32[1024,1]{0,1:T(1,128)S(1)}, u32[]{:S(2)}) copy-start(f32[1024,1]{0,1:T(1,128)S(1)} %get-tuple-element.211) | copy-start | bytes 12292
  104.6 36.3 %collective-permute-start.5 = (bf16[784,1024]{1,0:T(8,128)(2,1)}, bf16[784,1024]{1,0:T(8,128)(2,1)S(1)}, u32[]{:S(2)}, u32[]{:S(2)}) collective-permute-start(bf16[784,1024]{1,0:T(8,128)(2,1)} %collective-permute-done.3), channel_id=1, source_target_pairs={{1,0},{2,1},{3,2},{5,4},{6,5},{7,6},{9,8},{10,9},{11,10},{13,12},{... | collective-permute-start | bytes 4816904 | tf_op jit(solution)/shard_map/ppermute | solution.py:357
  105.9 36.3 %collective-permute-start.4 = (bf16[784,1024]{1,0:T(8,128)(2,1)}, bf16[784,1024]{1,0:T(8,128)(2,1)}, u32[]{:S(2)}, u32[]{:S(2)}) collective-permute-start(bf16[784,1024]{1,0:T(8,128)(2,1)} %collective-permute-done.2), channel_id=1, source_target_pairs={{0,1},{1,2},{2,3},{4,5},{5,6},{6,7},{8,9},{9,10},{10,11},{12,13},{... | collective-permute-start | bytes 4816904 | tf_op jit(solution)/shard_map/ppermute | solution.py:357
  245.4 13.0 %collective-permute-start.7 = (bf16[192,128]{1,0:T(8,128)(2,1)S(1)}, bf16[192,128]{1,0:T(8,128)(2,1)S(1)}, u32[]{:S(2)}, u32[]{:S(2)}) collective-permute-start(bf16[192,128]{1,0:T(8,128)(2,1)S(1)} %get-tuple-element.219), channel_id=1, source_target_pairs={{0,2},{1,3},{2,0},{3,1},{4,6},{5,7},{6,4},{7,5},{8,10},{9,11},{10,... | collective-permute-start | bytes 147464 | tf_op jit(solution)/shard_map/ppermute | solution.py:362
  248.4 9.9 %collective-permute-start.6 = (bf16[192,128]{1,0:T(8,128)(2,1)S(1)}, bf16[192,128]{1,0:T(8,128)(2,1)S(1)}, u32[]{:S(2)}, u32[]{:S(2)}) collective-permute-start(bf16[192,128]{1,0:T(8,128)(2,1)S(1)} %get-tuple-element.219), channel_id=1, source_target_pairs={{0,1},{1,2},{2,3},{3,0},{4,5},{5,6},{6,7},{7,4},{8,9},{9,10},{10,1... | collective-permute-start | bytes 147464 | tf_op jit(solution)/shard_map/ppermute | solution.py:362
  249.4 9.0 %collective-permute-start.8 = (bf16[192,128]{1,0:T(8,128)(2,1)S(1)}, bf16[192,128]{1,0:T(8,128)(2,1)S(1)}, u32[]{:S(2)}, u32[]{:S(2)}) collective-permute-start(bf16[192,128]{1,0:T(8,128)(2,1)S(1)} %get-tuple-element.219), channel_id=1, source_target_pairs={{0,3},{1,0},{2,1},{3,2},{4,7},{5,4},{6,5},{7,6},{8,11},{9,8},{10,9... | collective-permute-start | bytes 147464 | tf_op jit(solution)/shard_map/ppermute | solution.py:362
  279.6 400.8 %reduce-scatter.5.cloned.1.call-start = ((), (), s32[]{:S(2)}) async-start(), calls=%async_computation.8 | async-start | bytes 12976128 | tf_op jit(solution)/shard_map/reduce_scatter | solution.py:563
  328.1 56.1 %collective-permute-start.11 = (bf16[848,256]{1,0:T(8,128)(2,1)}, bf16[848,256]{1,0:T(8,128)(2,1)}, u32[]{:S(2)}, u32[]{:S(2)}) collective-permute-start(bf16[848,256]{1,0:T(8,128)(2,1)} %get-tuple-element.193), channel_id=1, source_target_pairs={{0,3},{1,0},{2,1},{3,2},{4,7},{5,4},{6,5},{7,6},{8,11},{9,8},{10,9... | collective-permute-start | bytes 1302536 | tf_op jit(solution)/shard_map/ppermute | solution.py:362
  328.9 56.1 %collective-permute-start.10 = (bf16[848,256]{1,0:T(8,128)(2,1)}, bf16[848,256]{1,0:T(8,128)(2,1)}, u32[]{:S(2)}, u32[]{:S(2)}) collective-permute-start(bf16[848,256]{1,0:T(8,128)(2,1)} %get-tuple-element.194), channel_id=1, source_target_pairs={{0,2},{1,3},{2,0},{3,1},{4,6},{5,7},{6,4},{7,5},{8,10},{9,11},{10,... | collective-permute-start | bytes 1302536 | tf_op jit(solution)/shard_map/ppermute | solution.py:362
  329.7 56.2 %collective-permute-start.9 = (bf16[848,256]{1,0:T(8,128)(2,1)}, bf16[848,256]{1,0:T(8,128)(2,1)}, u32[]{:S(2)}, u32[]{:S(2)}) collective-permute-start(bf16[848,256]{1,0:T(8,128)(2,1)} %get-tuple-element.195), channel_id=1, source_target_pairs={{0,1},{1,2},{2,3},{3,0},{4,5},{5,6},{6,7},{7,4},{8,9},{9,10},{10,1... | collective-permute-start | bytes 1302536 | tf_op jit(solution)/shard_map/ppermute | solution.py:362
  469.2 11.1 %collective-permute-start.17 = (bf16[512,256]{1,0:T(8,128)(2,1)S(1)}, bf16[512,256]{1,0:T(8,128)(2,1)S(1)}, u32[]{:S(2)}, u32[]{:S(2)}) collective-permute-start(bf16[512,256]{1,0:T(8,128)(2,1)S(1)} %get-tuple-element.199), channel_id=1, source_target_pairs={{0,3},{1,0},{2,1},{3,2},{4,7},{5,4},{6,5},{7,6},{8,11},{9,8},{10,9... | collective-permute-start | bytes 786440 | tf_op jit(solution)/shard_map/ppermute | solution.py:362
  472.4 90.7 %collective-permute-start.16 = (bf16[512,256]{1,0:T(8,128)(2,1)}, bf16[512,256]{1,0:T(8,128)(2,1)}, u32[]{:S(2)}, u32[]{:S(2)}) collective-permute-start(bf16[512,256]{1,0:T(8,128)(2,1)} %get-tuple-element.200), channel_id=1, source_target_pairs={{0,2},{1,3},{2,0},{3,1},{4,6},{5,7},{6,4},{7,5},{8,10},{9,11},{10,... | collective-permute-start | bytes 786440 | tf_op jit(solution)/shard_map/ppermute | solution.py:362
  473.0 90.2 %collective-permute-start.15 = (bf16[512,256]{1,0:T(8,128)(2,1)S(1)}, bf16[512,256]{1,0:T(8,128)(2,1)}, u32[]{:S(2)}, u32[]{:S(2)}) collective-permute-start(bf16[512,256]{1,0:T(8,128)(2,1)S(1)} %get-tuple-element.201), channel_id=1, source_target_pairs={{0,1},{1,2},{2,3},{3,0},{4,5},{5,6},{6,7},{7,4},{8,9},{9,10},{10,1... | collective-permute-start | bytes 786440 | tf_op jit(solution)/shard_map/ppermute | solution.py:362
  477.0 86.1 %collective-permute-start.14 = (bf16[768,384]{1,0:T(8,128)(2,1)}, bf16[768,384]{1,0:T(8,128)(2,1)S(1)}, u32[]{:S(2)}, u32[]{:S(2)}) collective-permute-start(bf16[768,384]{1,0:T(8,128)(2,1)} %get-tuple-element.189), channel_id=1, source_target_pairs={{0,3},{1,0},{2,1},{3,2},{4,7},{5,4},{6,5},{7,6},{8,11},{9,8},{10,9... | collective-permute-start | bytes 1769480 | tf_op jit(solution)/shard_map/ppermute | solution.py:362
  479.7 83.5 %collective-permute-start.13 = (bf16[768,384]{1,0:T(8,128)(2,1)}, bf16[768,384]{1,0:T(8,128)(2,1)S(1)}, u32[]{:S(2)}, u32[]{:S(2)}) collective-permute-start(bf16[768,384]{1,0:T(8,128)(2,1)} %get-tuple-element.190), channel_id=1, source_target_pairs={{0,2},{1,3},{2,0},{3,1},{4,6},{5,7},{6,4},{7,5},{8,10},{9,11},{10,... | collective-permute-start | bytes 1769480 | tf_op jit(solution)/shard_map/ppermute | solution.py:362
  481.0 82.2 %collective-permute-start.12 = (bf16[768,384]{1,0:T(8,128)(2,1)}, bf16[768,384]{1,0:T(8,128)(2,1)}, u32[]{:S(2)}, u32[]{:S(2)}) collective-permute-start(bf16[768,384]{1,0:T(8,128)(2,1)} %get-tuple-element.191), channel_id=1, source_target_pairs={{0,1},{1,2},{2,3},{3,0},{4,5},{5,6},{6,7},{7,4},{8,9},{9,10},{10,1... | collective-permute-start | bytes 1769480 | tf_op jit(solution)/shard_map/ppermute | solution.py:362
  491.1 79.7 %copy-start.31 = (bf16[768,1024]{1,0:T(8,128)(2,1)S(1)}, bf16[768,1024]{1,0:T(8,128)(2,1)}, u32[]{:S(2)}) copy-start(bf16[768,1024]{1,0:T(8,128)(2,1)} %copy-done.30) | copy-start | bytes 4718596
  566.9 24.9 %collective-permute-start.31 = (bf16[512,256]{1,0:T(8,128)(2,1)}, bf16[512,256]{1,0:T(8,128)(2,1)}, u32[]{:S(2)}, u32[]{:S(2)}) collective-permute-start(bf16[512,256]{1,0:T(8,128)(2,1)} %get-tuple-element.178), channel_id=1, source_target_pairs={{0,2},{1,3},{2,0},{3,1},{4,6},{5,7},{6,4},{7,5},{8,10},{9,11},{10,... | collective-permute-start | bytes 786440 | tf_op jit(solution)/shard_map/ppermute | solution.py:362
  566.9 22.0 %collective-permute-start.30 = (bf16[512,256]{1,0:T(8,128)(2,1)}, bf16[512,256]{1,0:T(8,128)(2,1)}, u32[]{:S(2)}, u32[]{:S(2)}) collective-permute-start(bf16[512,256]{1,0:T(8,128)(2,1)} %get-tuple-element.178), channel_id=1, source_target_pairs={{0,1},{1,2},{2,3},{3,0},{4,5},{5,6},{6,7},{7,4},{8,9},{9,10},{10,1... | collective-permute-start | bytes 786440 | tf_op jit(solution)/shard_map/ppermute | solution.py:362
  567.0 25.9 %collective-permute-start.32 = (bf16[512,256]{1,0:T(8,128)(2,1)}, bf16[512,256]{1,0:T(8,128)(2,1)}, u32[]{:S(2)}, u32[]{:S(2)}) collective-permute-start(bf16[512,256]{1,0:T(8,128)(2,1)} %get-tuple-element.178), channel_id=1, source_target_pairs={{0,3},{1,0},{2,1},{3,2},{4,7},{5,4},{6,5},{7,6},{8,11},{9,8},{10,9... | collective-permute-start | bytes 786440 | tf_op jit(solution)/shard_map/ppermute | solution.py:362
  581.0 97.0 %all-to-all-start = ((bf16[8,128,768]{1,2,0:T(8,128)(2,1)}), bf16[8,128,768]{1,2,0:T(8,128)(2,1)S(1)}, u32[]{:S(2)}, u32[]{:S(2)}) async-start(bf16[8,128,768]{1,2,0:T(8,128)(2,1)} %copy_bitcast_fusion), calls=%async_computation.2 | async-start | bytes 3145728 | tf_op jit(solution)/shard_map/all_to_all | solution.py:615
  587.6 53.3 %copy-start.1 = (bf16[768,1024]{1,0:T(8,128)(2,1)S(1)}, bf16[768,1024]{1,0:T(8,128)(2,1)}, u32[]{:S(2)}) copy-start(bf16[768,1024]{1,0:T(8,128)(2,1)} %param.13) | copy-start | bytes 4718596
  587.6 53.3 %copy-start.47 = (f32[768]{0:T(1024)S(1)}, f32[768]{0:T(1024)}, u32[]{:S(2)}) copy-start(f32[768]{0:T(1024)} %copy-done.46) | copy-start | bytes 9220
  587.6 53.3 %copy-start.49 = (f32[1024,1]{0,1:T(1,128)S(1)}, f32[1024,1]{0,1:T(1,128)}, u32[]{:S(2)}) copy-start(f32[1024,1]{0,1:T(1,128)} %copy-done.48) | copy-start | bytes 12292
  587.6 53.3 %copy-start.52 = (f32[768]{0:T(1024)S(1)}, f32[768]{0:T(1024)}, u32[]{:S(2)}) copy-start(f32[768]{0:T(1024)} %copy-done.51) | copy-start | bytes 9220
  587.7 53.1 %collective-permute-start.20 = (bf16[768,384]{1,0:T(8,128)(2,1)S(1)}, bf16[768,384]{1,0:T(8,128)(2,1)S(1)}, u32[]{:S(2)}, u32[]{:S(2)}) collective-permute-start(bf16[768,384]{1,0:T(8,128)(2,1)S(1)} %get-tuple-element.185), channel_id=1, source_target_pairs={{0,3},{1,0},{2,1},{3,2},{4,7},{5,4},{6,5},{7,6},{8,11},{9,8},{10,9... | collective-permute-start | bytes 1769480 | tf_op jit(solution)/shard_map/ppermute | solution.py:362
  588.2 52.4 %collective-permute-start.19 = (bf16[768,384]{1,0:T(8,128)(2,1)S(1)}, bf16[768,384]{1,0:T(8,128)(2,1)S(1)}, u32[]{:S(2)}, u32[]{:S(2)}) collective-permute-start(bf16[768,384]{1,0:T(8,128)(2,1)S(1)} %get-tuple-element.186), channel_id=1, source_target_pairs={{0,2},{1,3},{2,0},{3,1},{4,6},{5,7},{6,4},{7,5},{8,10},{9,11},{10,... | collective-permute-start | bytes 1769480 | tf_op jit(solution)/shard_map/ppermute | solution.py:362
  588.9 40.4 %collective-permute-start.18 = (bf16[768,384]{1,0:T(8,128)(2,1)S(1)}, bf16[768,384]{1,0:T(8,128)(2,1)S(1)}, u32[]{:S(2)}, u32[]{:S(2)}) collective-permute-start(bf16[768,384]{1,0:T(8,128)(2,1)S(1)} %get-tuple-element.187), channel_id=1, source_target_pairs={{0,1},{1,2},{2,3},{3,0},{4,5},{5,6},{6,7},{7,4},{8,9},{9,10},{10,1... | collective-permute-start | bytes 1769480 | tf_op jit(solution)/shard_map/ppermute | solution.py:362
  593.9 46.9 %copy-start.19 = (f32[512,1024]{1,0:T(8,128)}, f32[512,1024]{1,0:T(8,128)S(1)}, u32[]{:S(2)}) copy-start(f32[512,1024]{1,0:T(8,128)S(1)} %convert_dynamic-update-slice_fusion.4) | copy-start | bytes 6291460
  678.3 51.0 %collective-permute-start.29 = (bf16[128,768]{0,1:T(8,128)(2,1)S(1)}, bf16[128,768]{0,1:T(8,128)(2,1)}, u32[]{:S(2)}, u32[]{:S(2)}) collective-permute-start(bf16[128,768]{0,1:T(8,128)(2,1)S(1)} %reduce_sum.240), channel_id=1, source_target_pairs={{0,3},{1,0},{2,1},{3,2},{4,7},{5,4},{6,5},{7,6},{8,11},{9,8},{10,9... | collective-permute-start | bytes 589832 | tf_op jit(solution)/shard_map/ppermute | solution.py:362
  679.9 10.0 %collective-permute-start.27 = (bf16[128,768]{0,1:T(8,128)(2,1)S(1)}, bf16[128,768]{0,1:T(8,128)(2,1)S(1)}, u32[]{:S(2)}, u32[]{:S(2)}) collective-permute-start(bf16[128,768]{0,1:T(8,128)(2,1)S(1)} %reduce_sum.240), channel_id=1, source_target_pairs={{0,1},{1,2},{2,3},{3,0},{4,5},{5,6},{6,7},{7,4},{8,9},{9,10},{10,1... | collective-permute-start | bytes 589832 | tf_op jit(solution)/shard_map/ppermute | solution.py:362
  681.6 16.0 %collective-permute-start.21 = (bf16[128,1408]{1,0:T(8,128)(2,1)S(1)}, bf16[128,1408]{1,0:T(8,128)(2,1)S(1)}, u32[]{:S(2)}, u32[]{:S(2)}) collective-permute-start(bf16[128,1408]{1,0:T(8,128)(2,1)S(1)} %get-tuple-element.196), channel_id=1, source_target_pairs={{0,1},{1,2},{2,3},{3,0},{4,5},{5,6},{6,7},{7,4},{8,9},{9,10},{10,1... | collective-permute-start | bytes 1081352 | tf_op jit(solution)/shard_map/ppermute | solution.py:362
  683.2 21.7 %collective-permute-start.23 = (bf16[128,1408]{1,0:T(8,128)(2,1)S(1)}, bf16[128,1408]{1,0:T(8,128)(2,1)S(1)}, u32[]{:S(2)}, u32[]{:S(2)}) collective-permute-start(bf16[128,1408]{1,0:T(8,128)(2,1)S(1)} %get-tuple-element.197), channel_id=1, source_target_pairs={{0,3},{1,0},{2,1},{3,2},{4,7},{5,4},{6,5},{7,6},{8,11},{9,8},{10,9... | collective-permute-start | bytes 1081352 | tf_op jit(solution)/shard_map/ppermute | solution.py:362
  685.5 37.8 %collective-permute-start.22 = (bf16[128,1408]{1,0:T(8,128)(2,1)S(1)}, bf16[128,1408]{1,0:T(8,128)(2,1)S(1)}, u32[]{:S(2)}, u32[]{:S(2)}) collective-permute-start(bf16[128,1408]{1,0:T(8,128)(2,1)S(1)} %get-tuple-element.198), channel_id=1, source_target_pairs={{0,2},{1,3},{2,0},{3,1},{4,6},{5,7},{6,4},{7,5},{8,10},{9,11},{10,... | collective-permute-start | bytes 1081352 | tf_op jit(solution)/shard_map/ppermute | solution.py:362
  689.9 39.4 %collective-permute-start.28 = (bf16[128,768]{0,1:T(8,128)(2,1)S(1)}, bf16[128,768]{0,1:T(8,128)(2,1)S(1)}, u32[]{:S(2)}, u32[]{:S(2)}) collective-permute-start(bf16[128,768]{0,1:T(8,128)(2,1)S(1)} %reduce_sum.240), channel_id=1, source_target_pairs={{0,2},{1,3},{2,0},{3,1},{4,6},{5,7},{6,4},{7,5},{8,10},{9,11},{10,... | collective-permute-start | bytes 589832 | tf_op jit(solution)/shard_map/ppermute | solution.py:362
  724.8 12.9 %collective-permute-start.24 = (bf16[128,1408]{1,0:T(8,128)(2,1)S(1)}, bf16[128,1408]{1,0:T(8,128)(2,1)}, u32[]{:S(2)}, u32[]{:S(2)}) collective-permute-start(bf16[128,1408]{1,0:T(8,128)(2,1)S(1)} %get-tuple-element.180), channel_id=1, source_target_pairs={{0,1},{1,2},{2,3},{3,0},{4,5},{5,6},{6,7},{7,4},{8,9},{9,10},{10,1... | collective-permute-start | bytes 1081352 | tf_op jit(solution)/shard_map/ppermute | solution.py:362
  734.5 15.6 %collective-permute-start.25 = (bf16[128,1408]{1,0:T(8,128)(2,1)S(1)}, bf16[128,1408]{1,0:T(8,128)(2,1)S(1)}, u32[]{:S(2)}, u32[]{:S(2)}) collective-permute-start(bf16[128,1408]{1,0:T(8,128)(2,1)S(1)} %get-tuple-element.180), channel_id=1, source_target_pairs={{0,2},{1,3},{2,0},{3,1},{4,6},{5,7},{6,4},{7,5},{8,10},{9,11},{10,... | collective-permute-start | bytes 1081352 | tf_op jit(solution)/shard_map/ppermute | solution.py:362
  734.5 15.7 %collective-permute-start.26 = (bf16[128,1408]{1,0:T(8,128)(2,1)S(1)}, bf16[128,1408]{1,0:T(8,128)(2,1)S(1)}, u32[]{:S(2)}, u32[]{:S(2)}) collective-permute-start(bf16[128,1408]{1,0:T(8,128)(2,1)S(1)} %get-tuple-element.180), channel_id=1, source_target_pairs={{0,3},{1,0},{2,1},{3,2},{4,7},{5,4},{6,5},{7,6},{8,11},{9,8},{10,9... | collective-permute-start | bytes 1081352 | tf_op jit(solution)/shard_map/ppermute | solution.py:362
  (52 other events, 352.0 us)
Sparse Core Ops, SparseCore 0:
  11.9 51.6 all-gather.4
  66.0 27.7 all-gather.6
  95.7 54.2 all-gather.8
  151.7 54.2 all-gather.10
  279.7 70.8 reduce-scatter.2
  357.8 88.4 reduce-scatter.4

commit v3 on v2

--- a/solution.py
+++ b/solution.py
@@ -175,11 +175,11 @@
     )(q_rows, kv_rows, kv_rows, bias, *(() if first else state))
 
 
-def attn_bwd_kernel(
-    q_ref, k_ref, v_ref, do_ref, lse_ref, del_ref, bias_ref,
-    out_ref,
-    s_buf, dp_buf, qm, km, dom, kt, qt, dot, dqa, dka, dva, *, tk, tq, scale, post
-):
+def attn_bwd_kernel(*refs, tk, tq, scale, post):
+    q_ref, k_ref, v_ref, bias_ref = refs[:4]
+    letters = refs[4:-14]
+    out_ref = refs[-14]
+    s_buf, dp_buf, lse_ref, del_ref, qm, km, dom, kt, qt, dot, dqa, dka, dva = refs[-13:]
     nq = q_ref.shape[0] // tq
     nk = k_ref.shape[0] // tk
     half = q_ref.shape[1] // 2
@@ -189,10 +189,24 @@
             km[h, rows] = pair_keys(k_ref[rows, :], bias_ref[...], h, half)
     for h in range(2):
         qm[h] = pair_queries(q_ref[...], h, half)
-        dom[h] = pair_mask(do_ref[...], h, half)
     kt[...] = k_ref[...].T
     qt[...] = q_ref[...].T
-    dot[...] = do_ref[...].T
+    per_row = tk // (2 * half)
+    for i, letter in enumerate(letters):
+        rows = slice(i * tk, i * tk + tk)
+        do = letter[:tk, :]
+        dot[:, rows] = do.T
+        for h in range(2):
+            dom[h, rows] = pair_mask(do, h, half)
+        count = 4 * per_row
+        stat = letter[tk : tk + 3 * count, :].astype(jnp.float32)
+        stat = stat[:count] + stat[count : 2 * count] + stat[2 * count :]
+        for kind, buf in enumerate((lse_ref, del_ref)):
+            for h in range(2):
+                at = (kind * 2 + h) * per_row
+                buf[h : h + 1, rows] = jnp.concatenate(
+                    [stat[at + j : at + j + 1] for j in range(per_row)], axis=1
+                )
     for acc in (dqa, dka, dva):
         acc[...] = jnp.zeros(acc.shape, jnp.float32)
 
@@ -240,26 +254,26 @@
     out_ref[:, 2 * lanes :] = dva[...].T.astype(jnp.bfloat16)
 
 
-def attn_bwd(qkv, do, lse, delta, bias, pair, head_dim):
+def attn_bwd(qkv, letters, bias, pair, head_dim):
     rows = qkv.shape[0]
     tk = bias.shape[0]
-    tq = tk
     lanes = 2 * head_dim
     block = lambda at: pl.BlockSpec((rows, lanes), lambda h: (0, at))
-    stat = pl.BlockSpec((None, 2, rows), lambda h: (pair, 0, 0))
     return pl.pallas_call(
         functools.partial(
-            attn_bwd_kernel, tk=tk, tq=tq, scale=head_dim**-0.5 * LOG2E, post=head_dim**-0.5
+            attn_bwd_kernel, tk=tk, tq=tk, scale=head_dim**-0.5 * LOG2E, post=head_dim**-0.5
         ),
         grid=(1,),
-        in_specs=[block(3 * pair), block(3 * pair + 1), block(3 * pair + 2), block(pair)]
-        + [stat] * 2
-        + [pl.BlockSpec((tk, lanes), lambda h: (0, 0))],
+        in_specs=[block(3 * pair), block(3 * pair + 1), block(3 * pair + 2)]
+        + [pl.BlockSpec((tk, lanes), lambda h: (0, 0))]
+        + [pl.BlockSpec((letters[0].shape[0], lanes), lambda h: (0, pair))] * len(letters),
         out_specs=pl.BlockSpec((rows, 3 * lanes), lambda h: (0, 0)),
         out_shape=jax.ShapeDtypeStruct((rows, 3 * lanes), jnp.bfloat16),
         scratch_shapes=[
-            pltpu.VMEM((2, 2, tk, tq), jnp.float32),
-            pltpu.VMEM((2, 2, tk, tq), jnp.float32),
+            pltpu.VMEM((2, 2, tk, tk), jnp.float32),
+            pltpu.VMEM((2, 2, tk, tk), jnp.float32),
+            pltpu.VMEM((2, rows), jnp.float32),
+            pltpu.VMEM((2, rows), jnp.float32),
             pltpu.VMEM((2, rows, lanes), jnp.bfloat16),
             pltpu.VMEM((2, rows, lanes), jnp.bfloat16),
             pltpu.VMEM((2, rows, lanes), jnp.bfloat16),
@@ -275,7 +289,7 @@
             flops=40 * rows * rows * lanes, bytes_accessed=14 * rows * lanes, transcendentals=0
         ),
         name="attn_bwd",
-    )(qkv, qkv, qkv, do, lse, delta, bias)
+    )(qkv, qkv, qkv, bias, *letters)
 
 
 def fc1_kernel(x_ref, w_ref, act_ref, slope_ref):
@@ -367,9 +381,6 @@
     def behind(d):
         return lax.rem(rank - d + seq_count, seq_count)
 
-    def slot_of(chunk):
-        return jnp.where(chunk <= rank, rank - chunk, chunk)
-
     def piece(x, chunk, size, axis):
         return lax.dynamic_slice_in_dim(x, chunk * size, size, axis)
 
@@ -420,15 +431,18 @@
     fc1_w = gather(w_fc1)
     fc2_w = gather(w_fc2)
 
-    a1, own, slots = [], [], []
+    slots = []
     state = None
+    a1_all = jnp.zeros((seq_count * tok_rows, width), bf16)
+    own_all = jnp.zeros((seq_count * tok_rows, 3 * cols), bf16)
     for d in range(seq_count):
         slots.append(slot(d))
         u, _ = normalize(slots[d][:tok_rows].astype(f32))
         a = (u * gain_one + shift_one).astype(bf16)
-        a1.append(a)
         qkv = mxu(a, qkv_w, NN).astype(bf16)
-        own.append(piece(qkv, rank, 3 * cols, 1))
+        at = jnp.where(rank >= d, d, rank - d + seq_count) * tok_rows
+        a1_all = lax.dynamic_update_slice_in_dim(a1_all, a, at, 0)
+        own_all = lax.dynamic_update_slice_in_dim(own_all, piece(qkv, rank, 3 * cols, 1), at, 0)
         if d == 0:
             q_rows = qkv
         state = attn_fwd(q_rows, qkv, bias, state, d == seq_count - 1, head_dim)
@@ -509,64 +523,44 @@
     delta = exact(
         head_of.astype(f32), grad_mixed.astype(f32) * mixed.astype(f32), NT
     )
-    heads_dev = H // seq_count
-    stats = jnp.concatenate(
-        [lse.reshape(seq_count, heads_dev, tok_rows), delta.reshape(seq_count, heads_dev, tok_rows)],
-        axis=1,
-    )
-    parts, rest = [], stats
+    pairs_dev = pairs // seq_count
+    parts, rest = [], jnp.stack([lse, delta])
     for _ in range(3):
         top = lax.reduce_precision(rest, 8, 7)
         parts.append(top.astype(bf16))
         rest = rest - top
-    stat_cols = jnp.concatenate(parts, axis=1).reshape(seq_count, -1, cols)
-    stat_rows = stat_cols.shape[1]
-    pad_rows = -stat_rows % 16
+    stats = jnp.stack(parts).reshape(3, 2, pairs, 2, tok_rows // lanes, lanes)
+    stats = stats.transpose(0, 1, 3, 4, 2, 5).reshape(-1, width)
     letter = jnp.concatenate(
-        [grad_mixed]
-        + [
-            jnp.pad(
-                stat_cols.transpose(1, 0, 2).reshape(stat_rows, width), ((0, pad_rows), (0, 0))
-            )
-        ],
-        axis=0,
+        [grad_mixed, jnp.pad(stats, ((0, -stats.shape[0] % 16), (0, 0)))], axis=0
     )
     letter, late_a2, late_pre, late_mid = lax.optimization_barrier((letter, a2, grad_pre, mid_grad))
+    letters = [piece(letter, ahead(d), cols, 1) for d in range(seq_count)]
+    letters = [turn(x, d) if d else x for d, x in enumerate(letters)]
+    fc1_grad = mxu(late_a2, late_pre, TN).astype(bf16)
     norm_cols = jnp.stack([gain_grad_two, shift_grad_two], axis=1).astype(bf16)
-    wide_grad = jnp.concatenate(
+    misc_grad = jnp.concatenate(
         [
-            mxu(late_a2, late_pre, TN).astype(bf16),
             mxu(mixed, late_mid, TN).astype(bf16),
             grad_unpatch.astype(bf16),
             jnp.pad(norm_cols, ((0, 0), (0, 128 * seq_count - PP * TF - 2))),
         ],
         axis=1,
     )
-    do_all = jnp.zeros((seq_count * tok_rows, cols), bf16)
-    stat_all = jnp.zeros((3, 2 * heads_dev, seq_count * tok_rows), f32)
-    for d in range(seq_count):
-        got = piece(letter, ahead(d), cols, 1)
-        if d:
-            got = turn(got, d)
-        at = slot_of(behind(d)) * tok_rows
-        do_all = lax.dynamic_update_slice_in_dim(do_all, got[:tok_rows], at, 0)
-        got_stat = got[tok_rows : tok_rows + stat_rows].reshape(3, 2 * heads_dev, tok_rows)
-        stat_all = lax.dynamic_update_slice_in_dim(stat_all, got_stat.astype(f32), at, 2)
-    stat_all = stat_all[0] + stat_all[1] + stat_all[2]
-    pairs_dev = heads_dev // 2
-    lse_all = stat_all[:heads_dev].reshape(pairs_dev, 2, seq_count * tok_rows)
-    delta_all = stat_all[heads_dev:].reshape(pairs_dev, 2, seq_count * tok_rows)
-    own_all = jnp.concatenate(own, axis=0)
-    dec_grads = lax.psum((grad_w1, grad_b1, grad_w2), "scene")
 
     def over_scene(g):
         return lax.psum_scatter(g, "scene", scatter_dimension=0, tiled=True)
 
+    def swap_scene(g):
+        got = lax.all_to_all(g.reshape(scene_count, shard, -1), "scene", 0, 0, tiled=True)
+        return jnp.sum(got.astype(f32), axis=0).astype(bf16)
+
     fc2_part = over_scene(fc2_grad)
-    wide_part = over_scene(wide_grad)
-    (own_all, do_all, lse_all, delta_all, wide_grad, dec_grads) = lax.optimization_barrier(
-        (own_all, do_all, lse_all, delta_all, wide_grad, dec_grads)
-    )
+    own_all, letters, fc2_part, fc1_grad, misc_grad = lax.optimization_barrier(
+        (own_all, letters, fc2_part, fc1_grad, misc_grad)
+    )
+    fc1_part = over_scene(fc1_grad)
+    misc_part = swap_scene(misc_grad)
 
     def sum_pieces(part):
         size = part.shape[1] // seq_count
@@ -575,61 +569,66 @@
             for d in range(seq_count)
         ]
 
-    def over_seq(pieces):
-        return over_cols(sum(x.astype(f32) for x in pieces).astype(bf16))
-
-    def over_cols(mine):
-        size = mine.shape[1]
-        out = jnp.zeros((mine.shape[0], size * seq_count), f32)
-        for d in range(seq_count):
-            got = turn(mine, d) if d else mine
+    def blocks_of(pieces):
+        mine = sum(x.astype(f32) for x in pieces).astype(bf16)
+        return [turn(mine, d) if d else mine for d in range(seq_count)]
+
+    def side_by_side(blocks):
+        size = blocks[0].shape[1]
+        out = jnp.zeros((blocks[0].shape[0], size * seq_count), f32)
+        for d, got in enumerate(blocks):
             out = lax.dynamic_update_slice_in_dim(out, got.astype(f32), behind(d) * size, 1)
         return out
 
     def exchange(mine):
-        pieces = [piece(mine, slot_of(ahead(d)), tok_rows, 0) for d in range(seq_count)]
+        pieces = [piece(mine, (seq_count - d) % seq_count, tok_rows, 0) for d in range(seq_count)]
         return [turn(x, d) if d else x for d, x in enumerate(pieces)]
 
+    fc2_pieces = sum_pieces(fc2_part)
     moved, head_grads = [], []
+    dec_grads = (grad_w1, grad_b1, grad_w2)
     for p in range(pairs_dev):
-        mine = attn_bwd(own_all, do_all, lse_all, delta_all, bias, p, head_dim)
-        if p:
-            mine, moved[-1], head_grads[-1], fc2_pieces = lax.optimization_barrier(
-                (mine, moved[-1], head_grads[-1], fc2_pieces)
+        mine = attn_bwd(own_all, letters, bias, p, head_dim)
+        if p == 0:
+            own_all, mine, fc2_pieces = lax.optimization_barrier((own_all, mine, fc2_pieces))
+            fc2_blocks = blocks_of(fc2_pieces)
+        else:
+            (mine, moved[-1], head_grads[-1], fc2_blocks, fc1_part, misc_part, dec_grads) = (
+                lax.optimization_barrier(
+                    (mine, moved[-1], head_grads[-1], fc2_blocks, fc1_part, misc_part, dec_grads)
+                )
             )
-        else:
-            own_all, mine, fc2_part = lax.optimization_barrier((own_all, mine, fc2_part))
-            fc2_pieces = sum_pieces(fc2_part)
         head_grads.append(mine)
         moved.append(exchange(mine))
+    own_qkv = jnp.concatenate(
+        [mxu(a1_all, part, TN).astype(bf16) for part in head_grads], axis=1
+    )
+    qkv_part = swap_scene(own_qkv)
+    dec_grads = lax.psum(dec_grads, "scene")
+    wide_part = jnp.concatenate([fc1_part, misc_part], axis=1)
+    moved[-1], dec_grads, wide_part, qkv_part = lax.optimization_barrier(
+        (moved[-1], dec_grads, wide_part, qkv_part)
+    )
     row_grads = jnp.zeros((tok_rows, 3 * width), bf16)
     for p in range(pairs_dev):
         for d in range(seq_count):
             row_grads = lax.dynamic_update_slice_in_dim(
                 row_grads, moved[p][d], behind(d) * 3 * cols + p * 3 * lanes, 1
             )
-    a1_all = jnp.concatenate(a1, axis=0)
-    own_qkv = jnp.concatenate(
-        [mxu(a1_all, part, TN).astype(bf16) for part in head_grads], axis=1
-    )
-    got_qkv = lax.all_to_all(
-        own_qkv.reshape(scene_count, shard, 3 * cols), "scene", 0, 0, tiled=True
-    )
-    qkv_part = jnp.sum(got_qkv.astype(f32), axis=0).astype(bf16)
 
     grad_in = mxu(row_grads, qkv_w, NT)
     u_one, inv_one = normalize(inputs_f)
     back_one, gain_grad_one, shift_grad_one = norm_back(grad_in, u_one, inv_one, gain_one)
     grad_tokens = (grad_mid + back_one).astype(bf16)
 
-    grad_fc2 = over_seq(fc2_pieces)
-    grad_wide = over_seq(sum_pieces(wide_part))
+    grad_fc2 = side_by_side(fc2_blocks)
+    grad_wide = side_by_side(blocks_of(sum_pieces(wide_part)))
     hidden = w_fc1.shape[1]
     grad_fc1, grad_misc = grad_wide[:, :hidden], grad_wide[:, hidden:]
     grad_proj = grad_misc[:, :width]
     grad_unp = grad_misc[:, width : width + PP * TF]
     norm_two = grad_misc[:, width + PP * TF : width + PP * TF + 2]
-    qkv_all = over_cols(qkv_part)
+    qkv_all = side_by_side([turn(qkv_part, d) if d else qkv_part for d in range(seq_count)])
     grad_qkv = qkv_all.reshape(shard, pairs, 3, lanes).transpose(0, 2, 1, 3).reshape(shard, 3 * width)
 
     norm_one = lax.psum(jnp.stack([gain_grad_one, shift_grad_one]), "scene")

time: 776 us -> 780 us (level)
  waiting for transfers between devices: 135 us -> 97.7 us
  local copies, waits for them, and re-layouts: 58.3 us -> 83.3 us
  matrix products: 137 us -> 145 us
    ppermute x27, waiting for transfers between devices: 98.5 us -> 61.5 us  [turn(): lax.ppermute(x, 'seq', [(i, (i + step) % seq_count) for i in range(seq_co...]
    all_to_all x1 -> x2, starting transfers between devices: 3.83 us -> 18.5 us  [swap_scene(): lax.all_to_all(g.reshape(scene_count, shard, -1), 'scene', 0, 0, tiled=True)]
    dynamic_update_slice x7 -> x8, local copies, waits for them, and re-layouts: 2.19 us -> 15.1 us  [per_device(): lax.dynamic_update_slice_in_dim(row_grads, moved[p][d], behind(d) * 3 * c...]
    dynamic_update_slice x12 -> x16, other arithmetic: 8.54 us -> 19.6 us  [the longest x12 13.2 us: side_by_side(): lax.dynamic_update_slice_in_dim(out, got.astype(f32), behind(d) * size, 1)]
    ppermute x27, starting transfers between devices: 44.7 us -> 35.3 us  [turn(): lax.ppermute(x, 'seq', [(i, (i + step) % seq_count) for i in range(seq_co...]
    unnamed x125 -> x171, local copies, waits for them, and re-layouts: 20.2 us -> 18.2 us
  transfers between devices with their start and end apart: 40 -> 41, of which waited for: 15 -> 13; matrix products, arithmetic and copies ran while one was open for 28% -> 30% of each run, Pallas kernels for 31% -> 31%
where the time goes in v3:
time: 780 us; the launch traced here: 767 us
  Pallas kernels  235 us (30%)
  matrix products  145 us (19%)
  waiting for transfers between devices  97.7 us (13%)
  local copies, waits for them, and re-layouts  83.3 us (11%)
  starting transfers between devices  73.7 us (9%)
  other arithmetic  65.4 us (8%)
  blocking collectives  50.5 us (6%)
  between operations  16.5 us (2%)
    pallas_call x2, Pallas kernels, attn_bwd(): pl.pallas_call(functools.partial(attn_bwd_kernel, tk=tk, tq=tk, scale=hea...  144 us
    dot_general x19, matrix products, mxu(): lax.dot_general(left, right, dims, preferred_element_type=jnp.float32)  133 us
    pallas_call x4, Pallas kernels, attn_fwd(): pl.pallas_call(functools.partial(attn_fwd_kernel, first=first, last=last,...  69.5 us
    ppermute x27, waiting for transfers between devices, turn(): lax.ppermute(x, 'seq', [(i, (i + step) % seq_count) for i in range(seq_co...  61.5 us
    ppermute x6, waiting for transfers between devices, hop(): lax.ppermute(x, 'seq', [(i, i + step) for i in range(seq_count) if 0 <= i...  36.1 us
    ppermute x27, starting transfers between devices, turn(): lax.ppermute(x, 'seq', [(i, (i + step) % seq_count) for i in range(seq_co...  35.3 us
    psum x1, blocking collectives, per_device(): dec_grads = lax.psum(dec_grads, 'scene')  26.3 us
    pallas_call x1, Pallas kernels, fc1_gelu(): pl.pallas_call(fc1_kernel, grid=(cols // tile,), in_specs=[pl.BlockSpec((...  21.2 us
  transfers between devices with their start and end apart: 41, of which 13 were waited for; matrix products, arithmetic and copies ran while one was open for 30% of the time, Pallas kernels for 31%

profile of v3, /device:TPU:0, one launch (start us, length us, event | category | flops | bytes accessed | tf_op | source)
XLA Modules:
  0.0 767.2 jit_solution(4324451524174307876)
XLA Ops:
  17.0 5.2 collective-permute-start.1
  26.6 3.3 convert_select_fusion
  31.0 3.3 slice.128
  34.4 22.4 %collective-permute-done.1 = bf16[784,1024]{1,0:T(8,128)(2,1)S(1)} collective-permute-done((bf16[784,1024]{1,0:T(8,128)(2,1)}, bf16[784,1024]{1,0:T(8,128)(2,1)S(1)}, u32[]{:S(2)}, u32[]{:S(2)}) %collective-permute-start.1) | collective-permute-done | bytes 1605664 | tf_op jit(solution)/shard_map/ppermute | solution.py:371
  57.9 3.1 collective-permute-done
  62.9 4.6 collective-permute-start.2
  70.5 9.9 %convolution_convert_fusion.5.refs_0_.refs_1_.refs_2_ = bf16[768,3072]{1,0:T(8,128)(2,1)} fusion(bf16[1024,3328]{0,1:T(8,128)(2,1)} %all-gather.5.cloned.1.call-done, bf16[768,1024]{1,0:T(8,128)(2,1)S(1)} %copy-done, f32[1024]{0:T(1024)S(1)} %bitcast.110, f32[1024]{0:T(1024)S(1)} %bitcast.100, f32[768]{0:T(1024)S(1)} %add_rsqrt_fusion.4, ...), kind=kOutput, calls=%fused_computation.6 | convolution fusion | flops 4838916096 | bytes 12597248 | tf_op jit(solution)/shard_map/dot_general | solution.py:28
  81.2 16.0 %attn_fwd.4 = (f32[8,2,80,768]{3,2,1,0:T(8,128)}, f32[8,2,768]{2,1,0:T(2,128)}) custom-call(bf16[768,3072]{1,0:T(8,128)(2,1)} %convolution_convert_fusion.5.refs_0_.refs_1_.refs_2_, bf16[768,3072]{1,0:T(8,128)(2,1)} %convolution_convert_fusion.5.refs_0_.refs_1_.refs_2_, bf16[768,3072]{1,0:T(8,128)(2,1)} %convolution_convert_fusion.5.refs_0_.refs_1_.refs_2_, ...), custom_call_target="tpu_custom_call" | custom-call | flops 9663676416 | bytes 6291456 | tf_op jit(solution)/shard_map/attn_fwd/pallas_call | solution.py:155
  99.6 5.3 collective-permute-done.3
  106.2 6.0 collective-permute-start.4
  112.2 9.8 %convolution_convert_fusion.4.refs_1_.refs_2_ = bf16[768,3072]{1,0:T(8,128)(2,1)} fusion(bf16[1024,3328]{0,1:T(8,128)(2,1)} %all-gather.5.cloned.1.call-done, f32[768]{0:T(1024)S(1)} %add_rsqrt_fusion.3, f32[768]{0:T(1024)S(1)} %broadcast_multiply_fusion.7, f32[1024]{0:T(1024)S(1)} %bitcast.111, f32[1024]{0:T(1024)S(1)} %bitcast.101, ...), kind=kOutput, calls=%fused_computation.5 | convolution fusion | flops 4838916096 | bytes 12599296 | tf_op jit(solution)/shard_map/dot_general | solution.py:28
  122.0 17.6 %attn_fwd.5 = (f32[8,2,80,768]{3,2,1,0:T(8,128)}, f32[8,2,768]{2,1,0:T(2,128)}) custom-call(bf16[768,3072]{1,0:T(8,128)(2,1)} %convolution_convert_fusion.5.refs_0_.refs_1_.refs_2_, bf16[768,3072]{1,0:T(8,128)(2,1)} %convolution_convert_fusion.4.refs_1_.refs_2_, bf16[768,3072]{1,0:T(8,128)(2,1)} %convolution_convert_fusion.4.refs_1_.refs_2_, ...), custom_call_target="tpu_custom_call" | custom-call | flops 9663676416 | bytes 6291456 | tf_op jit(solution)/shard_map/attn_fwd/pallas_call | solution.py:155
  150.2 10.4 %convolution_convert_fusion.2.refs_1_.refs_2_ = bf16[768,3072]{1,0:T(8,128)(2,1)} fusion(bf16[1024,3328]{0,1:T(8,128)(2,1)} %all-gather.5.cloned.1.call-done, f32[768]{0:T(1024)S(1)} %add_rsqrt_fusion.1, f32[768]{0:T(1024)S(1)} %broadcast_multiply_fusion.5, f32[1024]{0:T(1024)S(1)} %bitcast.112, f32[1024]{0:T(1024)S(1)} %bitcast.102, ...), kind=kOutput, calls=%fused_computation.3 | convolution fusion | flops 4838916096 | bytes 12599296 | tf_op jit(solution)/shard_map/dot_general | solution.py:28
  160.6 17.8 %attn_fwd.6 = (f32[8,2,80,768]{3,2,1,0:T(8,128)}, f32[8,2,768]{2,1,0:T(2,128)}) custom-call(bf16[768,3072]{1,0:T(8,128)(2,1)} %convolution_convert_fusion.5.refs_0_.refs_1_.refs_2_, bf16[768,3072]{1,0:T(8,128)(2,1)} %convolution_convert_fusion.2.refs_1_.refs_2_, bf16[768,3072]{1,0:T(8,128)(2,1)} %convolution_convert_fusion.2.refs_1_.refs_2_, ...), custom_call_target="tpu_custom_call" | custom-call | flops 9663676416 | bytes 6291456 | tf_op jit(solution)/shard_map/attn_fwd/pallas_call | solution.py:155
  178.5 10.8 %convolution_convert_fusion.3.refs_1_.refs_2_ = bf16[768,3072]{1,0:T(8,128)(2,1)} fusion(bf16[1024,3328]{0,1:T(8,128)(2,1)} %all-gather.5.cloned.1.call-done, f32[768]{0:T(1024)S(1)} %add_rsqrt_fusion.2, f32[768]{0:T(1024)S(1)} %broadcast_multiply_fusion.6, f32[1024]{0:T(1024)S(1)} %bitcast.113, f32[1024]{0:T(1024)S(1)} %bitcast.103, ...), kind=kOutput, calls=%fused_computation.4 | convolution fusion | flops 4838916096 | bytes 12599296 | tf_op jit(solution)/shard_map/dot_general | solution.py:28
  189.2 18.1 %attn_fwd.7 = (bf16[768,1024]{1,0:T(8,128)(2,1)}, f32[8,2,768]{2,1,0:T(2,128)}) custom-call(bf16[768,3072]{1,0:T(8,128)(2,1)} %convolution_convert_fusion.5.refs_0_.refs_1_.refs_2_, bf16[768,3072]{1,0:T(8,128)(2,1)} %convolution_convert_fusion.3.refs_1_.refs_2_, bf16[768,3072]{1,0:T(8,128)(2,1)} %convolution_convert_fusion.3.refs_1_.refs_2_, ...), custom_call_target="tpu_custom_call" | custom-call | flops 9663676416 | bytes 6291456 | tf_op jit(solution)/shard_map/attn_fwd/pallas_call | solution.py:155
  207.3 3.9 fusion.126
  214.7 21.2 %fc1_gelu.1 = (bf16[768,4096]{1,0:T(8,128)(2,1)}, bf16[768,4096]{1,0:T(8,128)(2,1)}) custom-call(bf16[768,1024]{1,0:T(8,128)(2,1)} %add_convert_fusion.x_ref, bf16[1024,4096]{1,0:T(8,128)(2,1)} %all-gather.9.cloned.1.call-done.w_ref), custom_call_target="tpu_custom_call" | custom-call | flops 6442450944 | bytes 22544384 | tf_op jit(solution)/shard_map/fc1_gelu/pallas_call | solution.py:306
  235.9 5.9 fusion.62
  244.6 3.0 collective-permute-start.7
  251.4 6.1 fusion.49
  266.6 11.9 %convolution_convert_fusion.1 = bf16[4096,1024]{1,0:T(8,128)(2,1)} fusion(bf16[768,4096]{1,0:T(8,128)(2,1)} %get-tuple-element.90, f32[192,1024]{1,0:T(8,128)S(1)} %convolution_add_fusion, f32[576,1024]{1,0:T(8,128)S(1)} %copy-done.9), kind=kOutput, calls=%fused_computation.2 | convolution fusion | flops 6449790976 | bytes 17825792 | tf_op jit(solution)/shard_map/dot_general | solution.py:28
  295.0 13.5 %multiply_convert_fusion = bf16[768,4096]{1,0:T(8,128)(2,1)} fusion(bf16[768,4096]{1,0:T(8,128)(2,1)} %get-tuple-element.93, bf16[4096,1024]{1,0:T(8,128)(2,1)} %all-gather.11.cloned.1.call-done, f32[192,1024]{1,0:T(8,128)S(1)} %copy-done.15, f32[576,1024]{1,0:T(8,128)S(1)} %copy-done.10), kind=kOutput, calls=%fused_computation | convolution fusion | flops 6455033856 | bytes 24117248 | tf_op jit(solution)/shard_map/dot_general | solution.py:28
  308.5 12.2 %multiply_reduce_fusion = (bf16[1024]{0:T(1024)(128)(2,1)S(1)}, f32[768]{0:T(1024)S(1)}, f32[768]{0:T(1024)S(1)}, bf16[1024]{0:T(1024)(128)(2,1)S(1)}, f32[768,1024]{1,0:T(8,128)S(1)}) fusion(f32[768,1024]{1,0:T(8,128)S(1)} %copy-done.3, f32[768]{0:T(1024)S(1)} %copy-done.56, f32[768]{0:T(1024)S(1)} %copy-done.45, f32[1024]{0:T(1024)S(1)} %bitcast.119, ...), kind=kOutput, calls=%fused_computation.64 | convolution fusion | flops 6449524736 | bytes 20992000 | tf_op jit(solution)/shard_map/dot_general | solution.py:28
  339.3 3.2 convolution_convert_fusion.6
  342.5 9.1 %convolution_convert_fusion = bf16[1024,4096]{1,0:T(8,128)(2,1)} fusion(bf16[768,1024]{1,0:T(8,128)(2,1)S(1)} %copy-done.27, bf16[768,4096]{1,0:T(8,128)(2,1)S(1)} %bitcast.125), kind=kOutput, calls=%fused_computation.1 | convolution fusion | flops 6446645248 | bytes 16252928 | tf_op jit(solution)/shard_map/dot_general | solution.py:28
  351.7 3.1 pad_maximum_fusion.1
  354.8 16.5 %collective-permute-done.10.refs_6_ = bf16[848,256]{1,0:T(8,128)(2,1)} collective-permute-done((bf16[848,256]{1,0:T(8,128)(2,1)}, bf16[848,256]{1,0:T(8,128)(2,1)}, u32[]{:S(2)}, u32[]{:S(2)}) %collective-permute-start.10) | collective-permute-done | bytes 434208 | tf_op jit(solution)/shard_map/ppermute | solution.py:376
  377.0 3.3 constant_dynamic-update-slice_fusion.5
  399.1 4.7 all-to-all-start
  403.8 72.0 %attn_bwd.2 = bf16[3072,384]{1,0:T(8,128)(2,1)} custom-call(bf16[3072,768]{1,0:T(8,128)(2,1)} %dynamic-slice_dynamic-update-slice_fusion.refs_0_.refs_1_.refs_2_, bf16[3072,768]{1,0:T(8,128)(2,1)} %dynamic-slice_dynamic-update-slice_fusion.refs_0_.refs_1_.refs_2_, bf16[3072,768]{1,0:T(8,128)(2,1)} %dynamic-slice_dynamic-update-slice_fusion.refs_0_.refs_1_.refs_2_, ...), custom_call_target="tpu_custom_call" | custom-call | flops 48318382080 | bytes 5505024 | tf_op jit(solution)/shard_map/attn_bwd/pallas_call | solution.py:262
  481.6 3.2 collective-permute-start.17
  486.7 72.4 %attn_bwd.3 = bf16[3072,384]{1,0:T(8,128)(2,1)} custom-call(bf16[3072,768]{1,0:T(8,128)(2,1)} %dynamic-slice_dynamic-update-slice_fusion.refs_0_.refs_1_.refs_2_, bf16[3072,768]{1,0:T(8,128)(2,1)} %dynamic-slice_dynamic-update-slice_fusion.refs_0_.refs_1_.refs_2_, bf16[3072,768]{1,0:T(8,128)(2,1)} %dynamic-slice_dynamic-update-slice_fusion.refs_0_.refs_1_.refs_2_, ...), custom_call_target="tpu_custom_call" | custom-call | flops 48318382080 | bytes 5505024 | tf_op jit(solution)/shard_map/attn_bwd/pallas_call | solution.py:262
  561.9 3.2 fusion.123
  565.1 6.3 convolution_convert_fusion.8
  575.5 13.9 %all-to-all-start.1 = ((bf16[8,128,768]{1,2,0:T(8,128)(2,1)}), bf16[8,128,768]{1,2,0:T(8,128)(2,1)S(1)}, u32[]{:S(2)}, u32[]{:S(2)}) async-start(bf16[8,128,768]{1,2,0:T(8,128)(2,1)} %copy_bitcast_fusion.1), calls=%async_computation.3 | async-start | bytes 3145728 | tf_op jit(solution)/shard_map/all_to_all | solution.py:555
  604.3 26.3 %all-reduce.4 = (f32[32,64]{1,0:T(8,128)}, f32[64]{0:T(128)}, f32[64,4]{0,1:T(4,128)}) all-reduce(f32[32,64]{1,0:T(8,128)} %select_reduce_fusion, f32[64]{0:T(128)} %reduce_sum.247, f32[64,4]{0,1:T(4,128)S(1)} %fusion.65), channel_id=1, replica_groups=mesh['scene'=8,'seq'=4] {'scene'}, use_global_device_ids=true, to_apply=%region_21.22 | all-reduce | flops 2368 | bytes 18944 | tf_op jit(solution)/shard_map/psum | solution.py:607
  637.8 5.0 collective-permute-done.22
  652.8 10.5 %fusion.29 = (f32[1024]{0:T(1024)S(1)}, f32[768]{0:T(1024)S(1)}, f32[768]{0:T(1024)S(1)}, f32[1024]{0:T(1024)S(1)}, f32[768,1024]{1,0:T(8,128)}) fusion(bf16[768,1024]{1,0:T(8,128)(2,1)S(1)} %copy-done, f32[768]{0:T(1024)S(1)} %copy-done.48, f32[768]{0:T(1024)S(1)} %copy-done.43, f32[1024]{0:T(1024)S(1)} %bitcast.108, ...), kind=kOutput, calls=%fused_computation.47 | convolution fusion | flops 4839698432 | bytes 15753216 | tf_op jit(solution)/shard_map/dot_general | solution.py:28
  663.3 12.9 %psum.38 = f32[2,1024]{1,0:T(2,128)S(1)} all-reduce(f32[2,1024]{1,0:T(2,128)S(1)} %pad_maximum_fusion.4), channel_id=1, replica_groups=mesh['scene'=8,'seq'=4] {'scene'}, use_global_device_ids=true, to_apply=%region_29.30 | all-reduce | flops 2048 | bytes 16384 | tf_op jit(solution)/shard_map/psum | solution.py:634
  676.2 11.3 %psum.39 = f32[128,2]{0,1:T(2,128)} all-reduce(f32[128,2]{0,1:T(2,128)S(1)} %fusion.102), channel_id=1, replica_groups=mesh['scene'=8,'seq'=4] {'seq'}, use_global_device_ids=true, to_apply=%region_30.31 | all-reduce | flops 256 | bytes 2048 | tf_op jit(solution)/shard_map/psum | solution.py:635
  687.7 3.8 collective-permute-start.26
  691.5 4.3 fusion.28
  700.9 3.4 collective-permute-done.26
  704.2 19.4 %collective-permute-done.25 = bf16[128,1408]{1,0:T(8,128)(2,1)S(1)} collective-permute-done((bf16[128,1408]{1,0:T(8,128)(2,1)S(1)}, bf16[128,1408]{1,0:T(8,128)(2,1)S(1)}, u32[]{:S(2)}, u32[]{:S(2)}) %collective-permute-start.25) | collective-permute-done | bytes 360480 | tf_op jit(solution)/shard_map/ppermute | solution.py:376
  732.2 7.8 %collective-permute-done.27 = bf16[128,1408]{1,0:T(8,128)(2,1)} collective-permute-done((bf16[128,1408]{1,0:T(8,128)(2,1)}, bf16[128,1408]{1,0:T(8,128)(2,1)}, u32[]{:S(2)}, u32[]{:S(2)}) %collective-permute-start.27) | collective-permute-done | bytes 360480 | tf_op jit(solution)/shard_map/ppermute | solution.py:376
  742.0 8.4 %collective-permute-done.28 = bf16[128,1408]{1,0:T(8,128)(2,1)S(1)} collective-permute-done((bf16[128,1408]{1,0:T(8,128)(2,1)}, bf16[128,1408]{1,0:T(8,128)(2,1)S(1)}, u32[]{:S(2)}, u32[]{:S(2)}) %collective-permute-start.28) | collective-permute-done | bytes 360480 | tf_op jit(solution)/shard_map/ppermute | solution.py:376
  756.5 3.1 slice.135
  (391 shorter events, 182.5 us)
Async XLA Ops:
  7.2 62.5 %all-gather.5.cloned.1.call-start = ((), (), s32[]{:S(2)}) async-start(), calls=%async_computation.4 | async-start | bytes 7667712 | tf_op jit(solution)/shard_map/all_gather | solution.py:413
  11.8 195.5 %all-gather.7.cloned.1.call-start = ((), (), s32[]{:S(2)}) async-start(), calls=%async_computation.5 | async-start | bytes 2359296 | tf_op jit(solution)/shard_map/all_gather | solution.py:410
  12.6 202.1 %all-gather.9.cloned.1.call-start = ((), (), s32[]{:S(2)}) async-start(), calls=%async_computation.6 | async-start | bytes 9437184 | tf_op jit(solution)/shard_map/all_gather | solution.py:410
  15.5 220.4 %all-gather.11.cloned.1.call-start = ((), (), s32[]{:S(2)}) async-start(), calls=%async_computation.7 | async-start | bytes 9437184 | tf_op jit(solution)/shard_map/all_gather | solution.py:410
  17.0 39.7 %collective-permute-start.1 = (bf16[784,1024]{1,0:T(8,128)(2,1)}, bf16[784,1024]{1,0:T(8,128)(2,1)S(1)}, u32[]{:S(2)}, u32[]{:S(2)}) collective-permute-start(bf16[784,1024]{1,0:T(8,128)(2,1)} %fusion.52), channel_id=1, source_target_pairs={{0,1},{1,2},{2,3},{4,5},{5,6},{6,7},{8,9},{9,10},{10,11},{12,13},{... | collective-permute-start | bytes 4816904 | tf_op jit(solution)/shard_map/ppermute | solution.py:371
  22.2 38.8 %collective-permute-start = (bf16[784,1024]{1,0:T(8,128)(2,1)}, bf16[784,1024]{1,0:T(8,128)(2,1)}, u32[]{:S(2)}, u32[]{:S(2)}) collective-permute-start(bf16[784,1024]{1,0:T(8,128)(2,1)} %fusion.52), channel_id=1, source_target_pairs={{1,0},{2,1},{3,2},{5,4},{6,5},{7,6},{9,8},{10,9},{11,10},{13,12},{... | collective-permute-start | bytes 4816904 | tf_op jit(solution)/shard_map/ppermute | solution.py:371
  24.7 346.5 %reduce-scatter.3.cloned.1.call-start = ((), (), s32[]{:S(2)}) async-start(), calls=%async_computation.8 | async-start | bytes 9437184 | tf_op jit(solution)/shard_map/reduce_scatter | solution.py:552
  30.1 230.5 %copy-start.68 = (f32[256,16]{0,1:T(8,128)}, f32[256,16]{0,1:T(8,128)S(1)}, u32[]{:S(2)}) copy-start(f32[256,16]{0,1:T(8,128)S(1)} %reshape.315) | copy-start | bytes 49156
  62.8 49.4 %copy-start.4 = (bf16[784,1024]{1,0:T(8,128)(2,1)}, bf16[784,1024]{1,0:T(8,128)(2,1)S(1)}, u32[]{:S(2)}) copy-start(bf16[784,1024]{1,0:T(8,128)(2,1)S(1)} %broadcast_select_fusion) | copy-start | bytes 4816900
  62.9 36.7 %collective-permute-start.2 = (bf16[784,1024]{1,0:T(8,128)(2,1)}, bf16[784,1024]{1,0:T(8,128)(2,1)}, u32[]{:S(2)}, u32[]{:S(2)}) collective-permute-start(bf16[784,1024]{1,0:T(8,128)(2,1)} %copy-done.19), channel_id=1, source_target_pairs={{0,1},{1,2},{2,3},{4,5},{5,6},{6,7},{8,9},{9,10},{10,11},{12,13},{... | collective-permute-start | bytes 4816904 | tf_op jit(solution)/shard_map/ppermute | solution.py:371
  67.5 37.4 %collective-permute-start.3 = (bf16[784,1024]{1,0:T(8,128)(2,1)}, bf16[784,1024]{1,0:T(8,128)(2,1)}, u32[]{:S(2)}, u32[]{:S(2)}) collective-permute-start(bf16[784,1024]{1,0:T(8,128)(2,1)} %collective-permute-done), channel_id=1, source_target_pairs={{1,0},{2,1},{3,2},{5,4},{6,5},{7,6},{9,8},{10,9},{11,10},{13,12},{... | collective-permute-start | bytes 4816904 | tf_op jit(solution)/shard_map/ppermute | solution.py:371
  70.4 108.0 %copy-start.38 = (f32[1024,1]{0,1:T(1,128)}, f32[1024,1]{0,1:T(1,128)S(1)}, u32[]{:S(2)}) copy-start(f32[1024,1]{0,1:T(1,128)S(1)} %get-tuple-element.244) | copy-start | bytes 12292
  70.4 108.0 %copy-start.40 = (f32[1024,1]{0,1:T(1,128)}, f32[1024,1]{0,1:T(1,128)S(1)}, u32[]{:S(2)}) copy-start(f32[1024,1]{0,1:T(1,128)S(1)} %get-tuple-element.243) | copy-start | bytes 12292
  70.5 141.3 %copy-start.57 = (f32[1024,1]{0,1:T(1,128)}, f32[1024,1]{0,1:T(1,128)S(1)}, u32[]{:S(2)}) copy-start(f32[1024,1]{0,1:T(1,128)S(1)} %get-tuple-element.241) | copy-start | bytes 12292
  104.9 36.5 %collective-permute-start.5 = (bf16[784,1024]{1,0:T(8,128)(2,1)}, bf16[784,1024]{1,0:T(8,128)(2,1)}, u32[]{:S(2)}, u32[]{:S(2)}) collective-permute-start(bf16[784,1024]{1,0:T(8,128)(2,1)} %collective-permute-done.3), channel_id=1, source_target_pairs={{1,0},{2,1},{3,2},{5,4},{6,5},{7,6},{9,8},{10,9},{11,10},{13,12},{... | collective-permute-start | bytes 4816904 | tf_op jit(solution)/shard_map/ppermute | solution.py:371
  106.2 36.4 %collective-permute-start.4 = (bf16[784,1024]{1,0:T(8,128)(2,1)}, bf16[784,1024]{1,0:T(8,128)(2,1)}, u32[]{:S(2)}, u32[]{:S(2)}) collective-permute-start(bf16[784,1024]{1,0:T(8,128)(2,1)} %collective-permute-done.2), channel_id=1, source_target_pairs={{0,1},{1,2},{2,3},{4,5},{5,6},{6,7},{8,9},{9,10},{10,11},{12,13},{... | collective-permute-start | bytes 4816904 | tf_op jit(solution)/shard_map/ppermute | solution.py:371
  146.9 113.7 %copy-start.35 = (bf16[256,16]{1,0:T(8,128)(2,1)}, bf16[256,16]{1,0:T(8,128)(2,1)S(1)}, u32[]{:S(2)}) copy-start(bf16[256,16]{1,0:T(8,128)(2,1)S(1)} %reshape.316) | copy-start | bytes 24580
  244.6 13.0 %collective-permute-start.7 = (bf16[192,128]{1,0:T(8,128)(2,1)S(1)}, bf16[192,128]{1,0:T(8,128)(2,1)S(1)}, u32[]{:S(2)}, u32[]{:S(2)}) collective-permute-start(bf16[192,128]{1,0:T(8,128)(2,1)S(1)} %get-tuple-element.248), channel_id=1, source_target_pairs={{0,2},{1,3},{2,0},{3,1},{4,6},{5,7},{6,4},{7,5},{8,10},{9,11},{10,... | collective-permute-start | bytes 147464 | tf_op jit(solution)/shard_map/ppermute | solution.py:376
  247.6 10.0 %collective-permute-start.6 = (bf16[192,128]{1,0:T(8,128)(2,1)S(1)}, bf16[192,128]{1,0:T(8,128)(2,1)S(1)}, u32[]{:S(2)}, u32[]{:S(2)}) collective-permute-start(bf16[192,128]{1,0:T(8,128)(2,1)S(1)} %get-tuple-element.248), channel_id=1, source_target_pairs={{0,1},{1,2},{2,3},{3,0},{4,5},{5,6},{6,7},{7,4},{8,9},{9,10},{10,1... | collective-permute-start | bytes 147464 | tf_op jit(solution)/shard_map/ppermute | solution.py:376
  249.6 8.1 %collective-permute-start.8 = (bf16[192,128]{1,0:T(8,128)(2,1)S(1)}, bf16[192,128]{1,0:T(8,128)(2,1)S(1)}, u32[]{:S(2)}, u32[]{:S(2)}) collective-permute-start(bf16[192,128]{1,0:T(8,128)(2,1)S(1)} %get-tuple-element.248), channel_id=1, source_target_pairs={{0,3},{1,0},{2,1},{3,2},{4,7},{5,4},{6,5},{7,6},{8,11},{9,8},{10,9... | collective-permute-start | bytes 147464 | tf_op jit(solution)/shard_map/ppermute | solution.py:376
  278.5 283.2 %reduce-scatter.5.cloned.1.call-start = ((), (), s32[]{:S(2)}) async-start(), calls=%async_computation.9 | async-start | bytes 9437184 | tf_op jit(solution)/shard_map/reduce_scatter | solution.py:552
  335.8 19.0 %collective-permute-start.11 = (bf16[848,256]{1,0:T(8,128)(2,1)}, bf16[848,256]{1,0:T(8,128)(2,1)}, u32[]{:S(2)}, u32[]{:S(2)}) collective-permute-start(bf16[848,256]{1,0:T(8,128)(2,1)} %get-tuple-element.227), channel_id=1, source_target_pairs={{0,3},{1,0},{2,1},{3,2},{4,7},{5,4},{6,5},{7,6},{8,11},{9,8},{10,9... | collective-permute-start | bytes 1302536 | tf_op jit(solution)/shard_map/ppermute | solution.py:376
  336.7 34.5 %collective-permute-start.10 = (bf16[848,256]{1,0:T(8,128)(2,1)}, bf16[848,256]{1,0:T(8,128)(2,1)}, u32[]{:S(2)}, u32[]{:S(2)}) collective-permute-start(bf16[848,256]{1,0:T(8,128)(2,1)} %get-tuple-element.228), channel_id=1, source_target_pairs={{0,2},{1,3},{2,0},{3,1},{4,6},{5,7},{6,4},{7,5},{8,10},{9,11},{10,... | collective-permute-start | bytes 1302536 | tf_op jit(solution)/shard_map/ppermute | solution.py:376
  337.1 34.1 %collective-permute-start.9 = (bf16[848,256]{1,0:T(8,128)(2,1)}, bf16[848,256]{1,0:T(8,128)(2,1)}, u32[]{:S(2)}, u32[]{:S(2)}) collective-permute-start(bf16[848,256]{1,0:T(8,128)(2,1)} %get-tuple-element.229), channel_id=1, source_target_pairs={{0,1},{1,2},{2,3},{3,0},{4,5},{5,6},{6,7},{7,4},{8,9},{9,10},{10,1... | collective-permute-start | bytes 1302536 | tf_op jit(solution)/shard_map/ppermute | solution.py:376
  392.3 83.4 %collective-permute-start.14 = (bf16[512,256]{1,0:T(8,128)(2,1)S(1)}, bf16[512,256]{1,0:T(8,128)(2,1)S(1)}, u32[]{:S(2)}, u32[]{:S(2)}) collective-permute-start(bf16[512,256]{1,0:T(8,128)(2,1)S(1)} %get-tuple-element.234), channel_id=1, source_target_pairs={{0,3},{1,0},{2,1},{3,2},{4,7},{5,4},{6,5},{7,6},{8,11},{9,8},{10,9... | collective-permute-start | bytes 786440 | tf_op jit(solution)/shard_map/ppermute | solution.py:376
  392.4 83.4 %collective-permute-start.13 = (bf16[512,256]{1,0:T(8,128)(2,1)S(1)}, bf16[512,256]{1,0:T(8,128)(2,1)S(1)}, u32[]{:S(2)}, u32[]{:S(2)}) collective-permute-start(bf16[512,256]{1,0:T(8,128)(2,1)S(1)} %get-tuple-element.235), channel_id=1, source_target_pairs={{0,2},{1,3},{2,0},{3,1},{4,6},{5,7},{6,4},{7,5},{8,10},{9,11},{10,... | collective-permute-start | bytes 786440 | tf_op jit(solution)/shard_map/ppermute | solution.py:376
  394.9 80.9 %collective-permute-start.12 = (bf16[512,256]{1,0:T(8,128)(2,1)S(1)}, bf16[512,256]{1,0:T(8,128)(2,1)S(1)}, u32[]{:S(2)}, u32[]{:S(2)}) collective-permute-start(bf16[512,256]{1,0:T(8,128)(2,1)S(1)} %get-tuple-element.236), channel_id=1, source_target_pairs={{0,1},{1,2},{2,3},{3,0},{4,5},{5,6},{6,7},{7,4},{8,9},{9,10},{10,1... | collective-permute-start | bytes 786440 | tf_op jit(solution)/shard_map/ppermute | solution.py:376
  399.1 160.0 %all-to-all-start = ((bf16[8,128,1536]{1,2,0:T(8,128)(2,1)}), bf16[8,128,1536]{1,2,0:T(8,128)(2,1)}, u32[]{:S(2)}, u32[]{:S(2)}) async-start(bf16[8,128,1536]{1,2,0:T(8,128)(2,1)} %copy_bitcast_fusion), calls=%async_computation.2 | async-start | bytes 6291456 | tf_op jit(solution)/shard_map/all_to_all | solution.py:555
  475.9 83.2 %copy-start.30 = (bf16[512,256]{1,0:T(8,128)(2,1)}, bf16[512,256]{1,0:T(8,128)(2,1)S(1)}, u32[]{:S(2)}) copy-start(bf16[512,256]{1,0:T(8,128)(2,1)S(1)} %add_convert_fusion.2) | copy-start | bytes 786436
  476.0 10.0 %collective-permute-start.20 = (bf16[512,256]{1,0:T(8,128)(2,1)S(1)}, bf16[512,256]{1,0:T(8,128)(2,1)S(1)}, u32[]{:S(2)}, u32[]{:S(2)}) collective-permute-start(bf16[512,256]{1,0:T(8,128)(2,1)S(1)} %add_convert_fusion.2), channel_id=1, source_target_pairs={{0,3},{1,0},{2,1},{3,2},{4,7},{5,4},{6,5},{7,6},{8,11},{9,8},{10,9... | collective-permute-start | bytes 786440 | tf_op jit(solution)/shard_map/ppermute | solution.py:376
  478.1 83.5 %collective-permute-start.19 = (bf16[512,256]{1,0:T(8,128)(2,1)S(1)}, bf16[512,256]{1,0:T(8,128)(2,1)}, u32[]{:S(2)}, u32[]{:S(2)}) collective-permute-start(bf16[512,256]{1,0:T(8,128)(2,1)S(1)} %add_convert_fusion.2), channel_id=1, source_target_pairs={{0,2},{1,3},{2,0},{3,1},{4,6},{5,7},{6,4},{7,5},{8,10},{9,11},{10,... | collective-permute-start | bytes 786440 | tf_op jit(solution)/shard_map/ppermute | solution.py:376
  478.1 83.5 %collective-permute-start.18 = (bf16[512,256]{1,0:T(8,128)(2,1)S(1)}, bf16[512,256]{1,0:T(8,128)(2,1)}, u32[]{:S(2)}, u32[]{:S(2)}) collective-permute-start(bf16[512,256]{1,0:T(8,128)(2,1)S(1)} %add_convert_fusion.2), channel_id=1, source_target_pairs={{0,1},{1,2},{2,3},{3,0},{4,5},{5,6},{6,7},{7,4},{8,9},{9,10},{10,1... | collective-permute-start | bytes 786440 | tf_op jit(solution)/shard_map/ppermute | solution.py:376
  481.6 80.0 %collective-permute-start.17 = (bf16[768,384]{1,0:T(8,128)(2,1)}, bf16[768,384]{1,0:T(8,128)(2,1)}, u32[]{:S(2)}, u32[]{:S(2)}) collective-permute-start(bf16[768,384]{1,0:T(8,128)(2,1)} %get-tuple-element.223), channel_id=1, source_target_pairs={{0,3},{1,0},{2,1},{3,2},{4,7},{5,4},{6,5},{7,6},{8,11},{9,8},{10,9... | collective-permute-start | bytes 1769480 | tf_op jit(solution)/shard_map/ppermute | solution.py:376
  484.8 76.9 %collective-permute-start.16 = (bf16[768,384]{1,0:T(8,128)(2,1)S(1)}, bf16[768,384]{1,0:T(8,128)(2,1)}, u32[]{:S(2)}, u32[]{:S(2)}) collective-permute-start(bf16[768,384]{1,0:T(8,128)(2,1)S(1)} %get-tuple-element.224), channel_id=1, source_target_pairs={{0,2},{1,3},{2,0},{3,1},{4,6},{5,7},{6,4},{7,5},{8,10},{9,11},{10,... | collective-permute-start | bytes 1769480 | tf_op jit(solution)/shard_map/ppermute | solution.py:376
  486.7 75.0 %collective-permute-start.15 = (bf16[768,384]{1,0:T(8,128)(2,1)S(1)}, bf16[768,384]{1,0:T(8,128)(2,1)}, u32[]{:S(2)}, u32[]{:S(2)}) collective-permute-start(bf16[768,384]{1,0:T(8,128)(2,1)S(1)} %get-tuple-element.225), channel_id=1, source_target_pairs={{0,1},{1,2},{2,3},{3,0},{4,5},{5,6},{6,7},{7,4},{8,9},{9,10},{10,1... | collective-permute-start | bytes 1769480 | tf_op jit(solution)/shard_map/ppermute | solution.py:376
  575.5 62.0 %all-to-all-start.1 = ((bf16[8,128,768]{1,2,0:T(8,128)(2,1)}), bf16[8,128,768]{1,2,0:T(8,128)(2,1)S(1)}, u32[]{:S(2)}, u32[]{:S(2)}) async-start(bf16[8,128,768]{1,2,0:T(8,128)(2,1)} %copy_bitcast_fusion.1), calls=%async_computation.3 | async-start | bytes 3145728 | tf_op jit(solution)/shard_map/all_to_all | solution.py:555
  589.4 48.4 %collective-permute-start.23 = (bf16[768,384]{1,0:T(8,128)(2,1)}, bf16[768,384]{1,0:T(8,128)(2,1)}, u32[]{:S(2)}, u32[]{:S(2)}) collective-permute-start(bf16[768,384]{1,0:T(8,128)(2,1)} %get-tuple-element.219), channel_id=1, source_target_pairs={{0,3},{1,0},{2,1},{3,2},{4,7},{5,4},{6,5},{7,6},{8,11},{9,8},{10,9... | collective-permute-start | bytes 1769480 | tf_op jit(solution)/shard_map/ppermute | solution.py:376
  589.4 53.4 %collective-permute-start.22 = (bf16[768,384]{1,0:T(8,128)(2,1)}, bf16[768,384]{1,0:T(8,128)(2,1)}, u32[]{:S(2)}, u32[]{:S(2)}) collective-permute-start(bf16[768,384]{1,0:T(8,128)(2,1)} %get-tuple-element.220), channel_id=1, source_target_pairs={{0,2},{1,3},{2,0},{3,1},{4,6},{5,7},{6,4},{7,5},{8,10},{9,11},{10,... | collective-permute-start | bytes 1769480 | tf_op jit(solution)/shard_map/ppermute | solution.py:376
  590.8 52.0 %collective-permute-start.21 = (bf16[768,384]{1,0:T(8,128)(2,1)}, bf16[768,384]{1,0:T(8,128)(2,1)}, u32[]{:S(2)}, u32[]{:S(2)}) collective-permute-start(bf16[768,384]{1,0:T(8,128)(2,1)} %get-tuple-element.221), channel_id=1, source_target_pairs={{0,1},{1,2},{2,3},{3,0},{4,5},{5,6},{6,7},{7,4},{8,9},{9,10},{10,1... | collective-permute-start | bytes 1769480 | tf_op jit(solution)/shard_map/ppermute | solution.py:376
  642.8 83.9 %collective-permute-start.32 = (bf16[128,768]{0,1:T(8,128)(2,1)S(1)}, bf16[128,768]{0,1:T(8,128)(2,1)S(1)}, u32[]{:S(2)}, u32[]{:S(2)}) collective-permute-start(bf16[128,768]{0,1:T(8,128)(2,1)S(1)} %reduce_sum.249), channel_id=1, source_target_pairs={{0,3},{1,0},{2,1},{3,2},{4,7},{5,4},{6,5},{7,6},{8,11},{9,8},{10,9... | collective-permute-start | bytes 589832 | tf_op jit(solution)/shard_map/ppermute | solution.py:376
  642.8 53.2 %collective-permute-start.30 = (bf16[128,768]{0,1:T(8,128)(2,1)S(1)}, bf16[128,768]{0,1:T(8,128)(2,1)}, u32[]{:S(2)}, u32[]{:S(2)}) collective-permute-start(bf16[128,768]{0,1:T(8,128)(2,1)S(1)} %reduce_sum.249), channel_id=1, source_target_pairs={{0,1},{1,2},{2,3},{3,0},{4,5},{5,6},{6,7},{7,4},{8,9},{9,10},{10,1... | collective-permute-start | bytes 589832 | tf_op jit(solution)/shard_map/ppermute | solution.py:376
  687.6 13.2 %collective-permute-start.24 = (bf16[128,1408]{1,0:T(8,128)(2,1)S(1)}, bf16[128,1408]{1,0:T(8,128)(2,1)S(1)}, u32[]{:S(2)}, u32[]{:S(2)}) collective-permute-start(bf16[128,1408]{1,0:T(8,128)(2,1)S(1)} %get-tuple-element.231), channel_id=1, source_target_pairs={{0,1},{1,2},{2,3},{3,0},{4,5},{5,6},{6,7},{7,4},{8,9},{9,10},{10,1... | collective-permute-start | bytes 1081352 | tf_op jit(solution)/shard_map/ppermute | solution.py:376
  687.7 16.5 %collective-permute-start.26 = (bf16[128,1408]{1,0:T(8,128)(2,1)S(1)}, bf16[128,1408]{1,0:T(8,128)(2,1)S(1)}, u32[]{:S(2)}, u32[]{:S(2)}) collective-permute-start(bf16[128,1408]{1,0:T(8,128)(2,1)S(1)} %get-tuple-element.232), channel_id=1, source_target_pairs={{0,3},{1,0},{2,1},{3,2},{4,7},{5,4},{6,5},{7,6},{8,11},{9,8},{10,9... | collective-permute-start | bytes 1081352 | tf_op jit(solution)/shard_map/ppermute | solution.py:376
  691.5 32.1 %collective-permute-start.25 = (bf16[128,1408]{1,0:T(8,128)(2,1)S(1)}, bf16[128,1408]{1,0:T(8,128)(2,1)S(1)}, u32[]{:S(2)}, u32[]{:S(2)}) collective-permute-start(bf16[128,1408]{1,0:T(8,128)(2,1)S(1)} %get-tuple-element.233), channel_id=1, source_target_pairs={{0,2},{1,3},{2,0},{3,1},{4,6},{5,7},{6,4},{7,5},{8,10},{9,11},{10,... | collective-permute-start | bytes 1081352 | tf_op jit(solution)/shard_map/ppermute | solution.py:376
  696.0 30.6 %collective-permute-start.31 = (bf16[128,768]{0,1:T(8,128)(2,1)S(1)}, bf16[128,768]{0,1:T(8,128)(2,1)S(1)}, u32[]{:S(2)}, u32[]{:S(2)}) collective-permute-start(bf16[128,768]{0,1:T(8,128)(2,1)S(1)} %reduce_sum.249), channel_id=1, source_target_pairs={{0,2},{1,3},{2,0},{3,1},{4,6},{5,7},{6,4},{7,5},{8,10},{9,11},{10,... | collective-permute-start | bytes 589832 | tf_op jit(solution)/shard_map/ppermute | solution.py:376
  726.6 13.5 %collective-permute-start.27 = (bf16[128,1408]{1,0:T(8,128)(2,1)}, bf16[128,1408]{1,0:T(8,128)(2,1)}, u32[]{:S(2)}, u32[]{:S(2)}) collective-permute-start(bf16[128,1408]{1,0:T(8,128)(2,1)} %get-tuple-element.214), channel_id=1, source_target_pairs={{0,1},{1,2},{2,3},{3,0},{4,5},{5,6},{6,7},{7,4},{8,9},{9,10},{10,1... | collective-permute-start | bytes 1081352 | tf_op jit(solution)/shard_map/ppermute | solution.py:376
  728.4 21.9 %collective-permute-start.28 = (bf16[128,1408]{1,0:T(8,128)(2,1)}, bf16[128,1408]{1,0:T(8,128)(2,1)S(1)}, u32[]{:S(2)}, u32[]{:S(2)}) collective-permute-start(bf16[128,1408]{1,0:T(8,128)(2,1)} %get-tuple-element.214), channel_id=1, source_target_pairs={{0,2},{1,3},{2,0},{3,1},{4,6},{5,7},{6,4},{7,5},{8,10},{9,11},{10,... | collective-permute-start | bytes 1081352 | tf_op jit(solution)/shard_map/ppermute | solution.py:376
  730.1 21.2 %collective-permute-start.29 = (bf16[128,1408]{1,0:T(8,128)(2,1)}, bf16[128,1408]{1,0:T(8,128)(2,1)S(1)}, u32[]{:S(2)}, u32[]{:S(2)}) collective-permute-start(bf16[128,1408]{1,0:T(8,128)(2,1)} %get-tuple-element.214), channel_id=1, source_target_pairs={{0,3},{1,0},{2,1},{3,2},{4,7},{5,4},{6,5},{7,6},{8,11},{9,8},{10,9... | collective-permute-start | bytes 1081352 | tf_op jit(solution)/shard_map/ppermute | solution.py:376
  (75 other events, 693.3 us)
Sparse Core Ops, SparseCore 0:
  11.9 51.6 all-gather.4
  66.0 27.7 all-gather.6
  95.7 54.2 all-gather.8
  152.3 54.2 all-gather.10
  278.6 70.3 reduce-scatter.2
  371.4 104.9 reduce-scatter.4

commit v4 on v3

--- a/solution.py
+++ b/solution.py
@@ -431,18 +431,15 @@
     fc1_w = gather(w_fc1)
     fc2_w = gather(w_fc2)
 
-    slots = []
+    slots, a1, qkv_rows = [], [], []
     state = None
-    a1_all = jnp.zeros((seq_count * tok_rows, width), bf16)
-    own_all = jnp.zeros((seq_count * tok_rows, 3 * cols), bf16)
     for d in range(seq_count):
         slots.append(slot(d))
         u, _ = normalize(slots[d][:tok_rows].astype(f32))
         a = (u * gain_one + shift_one).astype(bf16)
         qkv = mxu(a, qkv_w, NN).astype(bf16)
-        at = jnp.where(rank >= d, d, rank - d + seq_count) * tok_rows
-        a1_all = lax.dynamic_update_slice_in_dim(a1_all, a, at, 0)
-        own_all = lax.dynamic_update_slice_in_dim(own_all, piece(qkv, rank, 3 * cols, 1), at, 0)
+        a1.append(a)
+        qkv_rows.append(qkv)
         if d == 0:
             q_rows = qkv
         state = attn_fwd(q_rows, qkv, bias, state, d == seq_count - 1, head_dim)
@@ -454,6 +451,13 @@
                 move_on()
     mixed, lse = state
     lse = lse.reshape(H, tok_rows)
+
+    def in_turn(blocks):
+        out = jnp.zeros((seq_count * tok_rows, blocks[0].shape[1]), blocks[0].dtype)
+        for d, block in enumerate(blocks):
+            at = jnp.where(rank >= d, d, rank - d + seq_count) * tok_rows
+            out = lax.dynamic_update_slice_in_dim(out, block, at, 0)
+        return out
 
     inputs_f = tokens.astype(f32)
     middle = inputs_f + mxu(mixed, proj_w, NN)
@@ -534,9 +538,12 @@
     letter = jnp.concatenate(
         [grad_mixed, jnp.pad(stats, ((0, -stats.shape[0] % 16), (0, 0)))], axis=0
     )
-    letter, late_a2, late_pre, late_mid = lax.optimization_barrier((letter, a2, grad_pre, mid_grad))
+    letter, late_a2, late_pre, late_mid, qkv_rows = lax.optimization_barrier(
+        (letter, a2, grad_pre, mid_grad, qkv_rows)
+    )
     letters = [piece(letter, ahead(d), cols, 1) for d in range(seq_count)]
     letters = [turn(x, d) if d else x for d, x in enumerate(letters)]
+    own_all = in_turn([piece(x, rank, 3 * cols, 1) for x in qkv_rows])
     fc1_grad = mxu(late_a2, late_pre, TN).astype(bf16)
     norm_cols = jnp.stack([gain_grad_two, shift_grad_two], axis=1).astype(bf16)
     misc_grad = jnp.concatenate(
@@ -551,23 +558,21 @@
     def over_scene(g):
         return lax.psum_scatter(g, "scene", scatter_dimension=0, tiled=True)
 
-    def swap_scene(g):
-        got = lax.all_to_all(g.reshape(scene_count, shard, -1), "scene", 0, 0, tiled=True)
-        return jnp.sum(got.astype(f32), axis=0).astype(bf16)
-
     fc2_part = over_scene(fc2_grad)
-    own_all, letters, fc2_part, fc1_grad, misc_grad = lax.optimization_barrier(
-        (own_all, letters, fc2_part, fc1_grad, misc_grad)
+    dec_flat = jnp.concatenate([grad_w1.reshape(-1), grad_b1, grad_w2.reshape(-1)])
+    dec_flat = jnp.pad(dec_flat, (0, -dec_flat.size % width)).reshape(-1, width)
+    own_all, letters, fc2_part, fc1_grad, misc_grad, dec_flat = lax.optimization_barrier(
+        (own_all, letters, fc2_part, fc1_grad, misc_grad, dec_flat)
     )
     fc1_part = over_scene(fc1_grad)
-    misc_part = swap_scene(misc_grad)
-
-    def sum_pieces(part):
-        size = part.shape[1] // seq_count
-        return [
-            turn(piece(part, ahead(d), size, 1), d) if d else piece(part, rank, size, 1)
-            for d in range(seq_count)
-        ]
+    misc_part = over_scene(misc_grad)
+
+    def sum_pieces(*parts):
+        def block(at):
+            cut = [piece(part, at, part.shape[1] // seq_count, 1) for part in parts]
+            return jnp.concatenate(cut, axis=1) if len(cut) > 1 else cut[0]
+
+        return [turn(block(ahead(d)), d) if d else block(rank) for d in range(seq_count)]
 
     def blocks_of(pieces):
         mine = sum(x.astype(f32) for x in pieces).astype(bf16)
@@ -586,53 +591,71 @@
 
     fc2_pieces = sum_pieces(fc2_part)
     moved, head_grads = [], []
-    dec_grads = (grad_w1, grad_b1, grad_w2)
     for p in range(pairs_dev):
         mine = attn_bwd(own_all, letters, bias, p, head_dim)
         if p == 0:
             own_all, mine, fc2_pieces = lax.optimization_barrier((own_all, mine, fc2_pieces))
             fc2_blocks = blocks_of(fc2_pieces)
         else:
-            (mine, moved[-1], head_grads[-1], fc2_blocks, fc1_part, misc_part, dec_grads) = (
+            mine, moved[-1], head_grads[-1], a1, fc2_blocks, fc1_part, misc_part = (
                 lax.optimization_barrier(
-                    (mine, moved[-1], head_grads[-1], fc2_blocks, fc1_part, misc_part, dec_grads)
+                    (mine, moved[-1], head_grads[-1], a1, fc2_blocks, fc1_part, misc_part)
                 )
             )
         head_grads.append(mine)
         moved.append(exchange(mine))
-    own_qkv = jnp.concatenate(
-        [mxu(a1_all, part, TN).astype(bf16) for part in head_grads], axis=1
-    )
-    qkv_part = swap_scene(own_qkv)
-    dec_grads = lax.psum(dec_grads, "scene")
-    wide_part = jnp.concatenate([fc1_part, misc_part], axis=1)
-    moved[-1], dec_grads, wide_part, qkv_part = lax.optimization_barrier(
-        (moved[-1], dec_grads, wide_part, qkv_part)
-    )
-    row_grads = jnp.zeros((tok_rows, 3 * width), bf16)
-    for p in range(pairs_dev):
-        for d in range(seq_count):
-            row_grads = lax.dynamic_update_slice_in_dim(
-                row_grads, moved[p][d], behind(d) * 3 * cols + p * 3 * lanes, 1
-            )
-
-    grad_in = mxu(row_grads, qkv_w, NT)
+    moved[-1][1], head_grads = lax.optimization_barrier((moved[-1][1], head_grads))
+    a1_all = in_turn(a1)
+    own_qkv = [mxu(a1_all, part, TN).astype(bf16) for part in head_grads]
+    qkv_part = over_scene(jnp.concatenate(own_qkv, axis=1))
+    grad_fc2 = side_by_side(fc2_blocks)
+
+    def pair_weights(p):
+        return jnp.concatenate(
+            [
+                lax.dynamic_slice_in_dim(
+                    qkv_w, behind(d) * 3 * cols + p * 3 * lanes, 3 * lanes, 1
+                )
+                for d in range(seq_count)
+            ],
+            axis=1,
+        )
+
+    def pair_part(pieces, weights):
+        return mxu(jnp.concatenate(pieces, axis=1), weights, NT)
+
+    grad_in = sum(pair_part(moved[p], pair_weights(p)) for p in range(pairs_dev - 1))
+    last_weights = pair_weights(pairs_dev - 1)
+    moved[-1], grad_in, last_weights, grad_fc2, fc1_part, misc_part = lax.optimization_barrier(
+        (moved[-1], grad_in, last_weights, grad_fc2, fc1_part, misc_part)
+    )
+    wide_pieces = sum_pieces(fc1_part, misc_part)
+    grad_in = grad_in + pair_part(moved[-1], last_weights)
     u_one, inv_one = normalize(inputs_f)
     back_one, gain_grad_one, shift_grad_one = norm_back(grad_in, u_one, inv_one, gain_one)
     grad_tokens = (grad_mid + back_one).astype(bf16)
 
-    grad_fc2 = side_by_side(fc2_blocks)
-    grad_wide = side_by_side(blocks_of(sum_pieces(wide_part)))
-    hidden = w_fc1.shape[1]
-    grad_fc1, grad_misc = grad_wide[:, :hidden], grad_wide[:, hidden:]
+    sums = jnp.concatenate([jnp.stack([gain_grad_one, shift_grad_one]), dec_flat], axis=0)
+    sums, wide_pieces = lax.optimization_barrier((sums, wide_pieces))
+    wide_blocks = blocks_of(wide_pieces)
+    cut = w_fc1.shape[1] // seq_count
+    grad_fc1 = side_by_side([x[:, :cut] for x in wide_blocks])
+    grad_misc = side_by_side([x[:, cut:] for x in wide_blocks])
     grad_proj = grad_misc[:, :width]
     grad_unp = grad_misc[:, width : width + PP * TF]
     norm_two = grad_misc[:, width + PP * TF : width + PP * TF + 2]
     qkv_all = side_by_side([turn(qkv_part, d) if d else qkv_part for d in range(seq_count)])
     grad_qkv = qkv_all.reshape(shard, pairs, 3, lanes).transpose(0, 2, 1, 3).reshape(shard, 3 * width)
 
-    norm_one = lax.psum(jnp.stack([gain_grad_one, shift_grad_one]), "scene")
-    norm_one = lax.psum(lax.dynamic_slice_in_dim(norm_one, scene_rank * shard, shard, 1), "seq").T
+    sums = lax.psum(sums, "scene")
+    norm_one = lax.psum(lax.dynamic_slice_in_dim(sums[:2], scene_rank * shard, shard, 1), "seq").T
+    dec_flat = sums[2:].reshape(-1)
+    ends = (w_dec1.size, w_dec1.size + dh, w_dec1.size + dh + w_dec2.size)
+    dec_grads = (
+        dec_flat[: ends[0]].reshape(w_dec1.shape),
+        dec_flat[ends[0] : ends[1]],
+        dec_flat[ends[1] : ends[2]].reshape(w_dec2.shape),
+    )
     return (
         block_out,
         decoded,

time: 780 us -> 699 us (0.90)
  waiting for transfers between devices: 97.7 us -> 67.2 us
  blocking collectives: 50.5 us -> 32.5 us
  other arithmetic: 65.4 us -> 49.9 us
  matrix products: 145 us -> 132 us
  local copies, waits for them, and re-layouts: 83.3 us -> 70.7 us
  starting transfers between devices: 73.7 us -> 85.9 us
    ppermute x27, starting transfers between devices: 35.3 us -> 62.9 us  [turn(): lax.ppermute(x, 'seq', [(i, (i + step) % seq_count) for i in range(seq_co...]
    ppermute x27, waiting for transfers between devices: 61.5 us -> 34.4 us  [turn(): lax.ppermute(x, 'seq', [(i, (i + step) % seq_count) for i in range(seq_co...]
    all_to_all x2 -> x0, starting transfers between devices: 18.5 us -> none  [swap_scene(): lax.all_to_all(g.reshape(scene_count, shard, -1), 'scene', 0, 0, tiled=True)]
    psum x3 -> x2, blocking collectives: 50.5 us -> 32.5 us  [the longest x1 23.3 us: per_device(): sums = lax.psum(sums, 'scene')]
    dynamic_update_slice x12 -> x8, local copies, waits for them, and re-layouts: 25.5 us -> 11 us  [in_turn(): out = lax.dynamic_update_slice_in_dim(out, block, at, 0)]
    dot_general x19 -> x20, matrix products: 133 us -> 122 us  [mxu(): lax.dot_general(left, right, dims, preferred_element_type=jnp.float32)]
    dynamic_update_slice x12 -> x16, other arithmetic: 13.2 us -> 3.71 us  [side_by_side(): lax.dynamic_update_slice_in_dim(out, got.astype(f32), behind(d) * size, 1)]
    unnamed x171 -> x176, local copies, waits for them, and re-layouts: 18.2 us -> 23.8 us
  transfers between devices with their start and end apart: 41 -> 41, of which waited for: 13 -> 11; matrix products, arithmetic and copies ran while one was open for 30% -> 29% of each run, Pallas kernels for 31% -> 34%
where the time goes in v4:
time: 699 us; the launch traced here: 690 us
  Pallas kernels  235 us (34%)
  matrix products  132 us (19%)
  starting transfers between devices  85.9 us (12%)
  local copies, waits for them, and re-layouts  70.7 us (10%)
  waiting for transfers between devices  67.2 us (10%)
  other arithmetic  49.9 us (7%)
  blocking collectives  32.5 us (5%)
  between operations  17.1 us (2%)
    pallas_call x2, Pallas kernels, attn_bwd(): pl.pallas_call(functools.partial(attn_bwd_kernel, tk=tk, tq=tk, scale=hea...  144 us
    dot_general x20, matrix products, mxu(): lax.dot_general(left, right, dims, preferred_element_type=jnp.float32)  122 us
    pallas_call x4, Pallas kernels, attn_fwd(): pl.pallas_call(functools.partial(attn_fwd_kernel, first=first, last=last,...  69.4 us
    ppermute x27, starting transfers between devices, turn(): lax.ppermute(x, 'seq', [(i, (i + step) % seq_count) for i in range(seq_co...  62.9 us
    ppermute x27, waiting for transfers between devices, turn(): lax.ppermute(x, 'seq', [(i, (i + step) % seq_count) for i in range(seq_co...  34.4 us
    ppermute x6, waiting for transfers between devices, hop(): lax.ppermute(x, 'seq', [(i, i + step) for i in range(seq_count) if 0 <= i...  31.9 us
    unnamed x176, local copies, waits for them, and re-layouts  23.8 us
    psum x1, blocking collectives, per_device(): sums = lax.psum(sums, 'scene')  23.3 us
  transfers between devices with their start and end apart: 41, of which 11 were waited for; matrix products, arithmetic and copies ran while one was open for 29% of the time, Pallas kernels for 34%

profile of v4, /device:TPU:0, one launch (start us, length us, event | category | flops | bytes accessed | tf_op | source)
XLA Modules:
  0.0 690.0 jit_solution(966153070437958622)
XLA Ops:
  11.2 2.7 convert_element_type.272
  16.9 6.8 collective-permute-start.1
  34.1 21.7 %collective-permute-done = bf16[784,1024]{1,0:T(8,128)(2,1)S(1)} collective-permute-done((bf16[784,1024]{1,0:T(8,128)(2,1)}, bf16[784,1024]{1,0:T(8,128)(2,1)S(1)}, u32[]{:S(2)}, u32[]{:S(2)}) %collective-permute-start) | collective-permute-done | bytes 1605664 | tf_op jit(solution)/shard_map/ppermute | solution.py:371
  60.1 6.2 collective-permute-start.2
  70.1 10.3 %convolution_convert_fusion.5.refs_0_.refs_1_.refs_2_ = bf16[768,3072]{1,0:T(8,128)(2,1)} fusion(bf16[768,1024]{1,0:T(8,128)(2,1)S(1)} %get-tuple-element.158, bf16[1024,3328]{0,1:T(8,128)(2,1)} %all-gather.5.cloned.1.call-done), kind=kOutput, calls=%fused_computation.8 | convolution fusion | flops 4834197504 | bytes 12582912 | tf_op jit(solution)/shard_map/dot_general | solution.py:28
  81.2 16.1 %attn_fwd.4 = (f32[8,2,80,768]{3,2,1,0:T(8,128)}, f32[8,2,768]{2,1,0:T(2,128)}) custom-call(bf16[768,3072]{1,0:T(8,128)(2,1)} %convolution_convert_fusion.5.refs_0_.refs_1_.refs_2_, bf16[768,3072]{1,0:T(8,128)(2,1)} %convolution_convert_fusion.5.refs_0_.refs_1_.refs_2_, bf16[768,3072]{1,0:T(8,128)(2,1)} %convolution_convert_fusion.5.refs_0_.refs_1_.refs_2_, ...), custom_call_target="tpu_custom_call" | custom-call | flops 9663676416 | bytes 6291456 | tf_op jit(solution)/shard_map/attn_fwd/pallas_call | solution.py:155
  98.9 5.5 collective-permute-start.4
  106.0 9.5 %convolution_convert_fusion.4.refs_1_.refs_2_ = bf16[768,3072]{1,0:T(8,128)(2,1)} fusion(bf16[768,1024]{1,0:T(8,128)(2,1)S(1)} %copy-done.11, bf16[1024,3328]{0,1:T(8,128)(2,1)} %all-gather.5.cloned.1.call-done), kind=kOutput, calls=%fused_computation.7 | convolution fusion | flops 4834197504 | bytes 12582912 | tf_op jit(solution)/shard_map/dot_general | solution.py:28
  115.5 17.6 %attn_fwd.5 = (f32[8,2,80,768]{3,2,1,0:T(8,128)}, f32[8,2,768]{2,1,0:T(2,128)}) custom-call(bf16[768,3072]{1,0:T(8,128)(2,1)} %convolution_convert_fusion.5.refs_0_.refs_1_.refs_2_, bf16[768,3072]{1,0:T(8,128)(2,1)} %convolution_convert_fusion.4.refs_1_.refs_2_, bf16[768,3072]{1,0:T(8,128)(2,1)} %convolution_convert_fusion.4.refs_1_.refs_2_, ...), custom_call_target="tpu_custom_call" | custom-call | flops 9663676416 | bytes 6291456 | tf_op jit(solution)/shard_map/attn_fwd/pallas_call | solution.py:155
  133.1 3.2 collective-permute-done.4
  136.3 5.3 collective-permute-done.5
  141.5 2.9 select_select_fusion
  151.3 2.6 fusion.29
  155.1 6.8 convolution_convert_fusion.2.refs_1_.refs_2_
  161.9 17.6 %attn_fwd.6 = (f32[8,2,80,768]{3,2,1,0:T(8,128)}, f32[8,2,768]{2,1,0:T(2,128)}) custom-call(bf16[768,3072]{1,0:T(8,128)(2,1)} %convolution_convert_fusion.5.refs_0_.refs_1_.refs_2_, bf16[768,3072]{1,0:T(8,128)(2,1)} %convolution_convert_fusion.2.refs_1_.refs_2_, bf16[768,3072]{1,0:T(8,128)(2,1)} %convolution_convert_fusion.2.refs_1_.refs_2_, ...), custom_call_target="tpu_custom_call" | custom-call | flops 9663676416 | bytes 6291456 | tf_op jit(solution)/shard_map/attn_fwd/pallas_call | solution.py:155
  179.6 9.5 %convolution_convert_fusion.3.refs_1_.refs_2_ = bf16[768,3072]{1,0:T(8,128)(2,1)} fusion(bf16[768,1024]{1,0:T(8,128)(2,1)S(1)} %copy-done.15, bf16[1024,3328]{0,1:T(8,128)(2,1)} %all-gather.5.cloned.1.call-done), kind=kOutput, calls=%fused_computation.6 | convolution fusion | flops 4834197504 | bytes 12582912 | tf_op jit(solution)/shard_map/dot_general | solution.py:28
  189.1 18.1 %attn_fwd.7 = (bf16[768,1024]{1,0:T(8,128)(2,1)}, f32[8,2,768]{2,1,0:T(2,128)}) custom-call(bf16[768,3072]{1,0:T(8,128)(2,1)} %convolution_convert_fusion.5.refs_0_.refs_1_.refs_2_, bf16[768,3072]{1,0:T(8,128)(2,1)} %convolution_convert_fusion.3.refs_1_.refs_2_, bf16[768,3072]{1,0:T(8,128)(2,1)} %convolution_convert_fusion.3.refs_1_.refs_2_, ...), custom_call_target="tpu_custom_call" | custom-call | flops 9663676416 | bytes 6291456 | tf_op jit(solution)/shard_map/attn_fwd/pallas_call | solution.py:155
  207.2 3.9 fusion.145
  214.5 21.3 %fc1_gelu.1 = (bf16[768,4096]{1,0:T(8,128)(2,1)}, bf16[768,4096]{1,0:T(8,128)(2,1)}) custom-call(bf16[768,1024]{1,0:T(8,128)(2,1)} %add_convert_fusion.x_ref, bf16[1024,4096]{1,0:T(8,128)(2,1)} %all-gather.9.cloned.1.call-done.w_ref), custom_call_target="tpu_custom_call" | custom-call | flops 6442450944 | bytes 22544384 | tf_op jit(solution)/shard_map/fc1_gelu/pallas_call | solution.py:306
  235.8 5.8 fusion.79
  249.2 6.1 fusion.53
  266.8 11.9 %convolution_convert_fusion.1 = bf16[4096,1024]{1,0:T(8,128)(2,1)} fusion(bf16[768,4096]{1,0:T(8,128)(2,1)} %get-tuple-element.104, f32[192,1024]{1,0:T(8,128)S(1)} %convolution_add_fusion, f32[576,1024]{1,0:T(8,128)S(1)} %copy-done.8), kind=kOutput, calls=%fused_computation.2 | convolution fusion | flops 6449790976 | bytes 17825792 | tf_op jit(solution)/shard_map/dot_general | solution.py:28
  290.7 11.8 %multiply_convert_fusion = bf16[768,4096]{1,0:T(8,128)(2,1)S(1)} fusion(bf16[768,4096]{1,0:T(8,128)(2,1)} %get-tuple-element.107, bf16[4096,1024]{1,0:T(8,128)(2,1)} %all-gather.11.cloned.1.call-done, f32[192,1024]{1,0:T(8,128)} %copy-done.19, f32[576,1024]{1,0:T(8,128)} %slice.178), kind=kOutput, calls=%fused_computation | convolution fusion | flops 6455033856 | bytes 24117248 | tf_op jit(solution)/shard_map/dot_general | solution.py:28
  302.5 13.1 %multiply_reduce_fusion = (bf16[1024]{0:T(1024)(128)(2,1)}, f32[768]{0:T(1024)S(1)}, f32[768]{0:T(1024)S(1)}, bf16[1024]{0:T(1024)(128)(2,1)}, f32[768,1024]{1,0:T(8,128)S(1)}) fusion(f32[768,1024]{1,0:T(8,128)S(1)} %copy-done.3, f32[768]{0:T(1024)S(1)} %add_rsqrt_fusion, f32[768]{0:T(1024)S(1)} %broadcast_multiply_fusion.4, f32[1024]{0:T(1024)S(1)} %bitcast.100, ...), kind=kOutput, calls=%fused_computation.68 | convolution fusion | flops 6449524736 | bytes 20992000 | tf_op jit(solution)/shard_map/dot_general | solution.py:28
  315.7 2.6 fusion.140
  328.1 2.7 broadcast_in_dim.103
  330.8 2.6 dynamic-slice_dynamic-update-slice_fusion.3
  343.7 9.2 %convolution_convert_fusion = bf16[1024,4096]{1,0:T(8,128)(2,1)} fusion(bf16[768,1024]{1,0:T(8,128)(2,1)S(1)} %copy-done.30, bf16[768,4096]{1,0:T(8,128)(2,1)S(1)} %bitcast.108), kind=kOutput, calls=%fused_computation.1 | convolution fusion | flops 6446645248 | bytes 16252928 | tf_op jit(solution)/shard_map/dot_general | solution.py:28
  356.9 2.8 slice-done.2
  365.8 7.0 %collective-permute-start.12 = (bf16[512,256]{1,0:T(8,128)(2,1)S(1)}, bf16[512,256]{1,0:T(8,128)(2,1)S(1)}, u32[]{:S(2)}, u32[]{:S(2)}) collective-permute-start(bf16[512,256]{1,0:T(8,128)(2,1)S(1)} %get-tuple-element.269), channel_id=1, source_target_pairs={{0,1},{1,2},{2,3},{3,0},{4,5},{5,6},{6,7},{7,4},{8,9},{9,10},{10,1... | collective-permute-start | bytes 786440 | tf_op jit(solution)/shard_map/ppermute | solution.py:376
  372.8 2.6 collective-permute-start.14
  375.4 72.0 %attn_bwd.2 = bf16[3072,384]{1,0:T(8,128)(2,1)} custom-call(bf16[3072,768]{1,0:T(8,128)(2,1)} %dynamic-slice_dynamic-update-slice_fusion.refs_0_.refs_1_.refs_2_, bf16[3072,768]{1,0:T(8,128)(2,1)} %dynamic-slice_dynamic-update-slice_fusion.refs_0_.refs_1_.refs_2_, bf16[3072,768]{1,0:T(8,128)(2,1)} %dynamic-slice_dynamic-update-slice_fusion.refs_0_.refs_1_.refs_2_, ...), custom_call_target="tpu_custom_call" | custom-call | flops 48318382080 | bytes 5505024 | tf_op jit(solution)/shard_map/attn_bwd/pallas_call | solution.py:262
  452.3 2.9 fusion.142
  460.3 72.0 %attn_bwd.3 = bf16[3072,384]{1,0:T(8,128)(2,1)} custom-call(bf16[3072,768]{1,0:T(8,128)(2,1)} %dynamic-slice_dynamic-update-slice_fusion.refs_0_.refs_1_.refs_2_, bf16[3072,768]{1,0:T(8,128)(2,1)} %dynamic-slice_dynamic-update-slice_fusion.refs_0_.refs_1_.refs_2_, bf16[3072,768]{1,0:T(8,128)(2,1)} %dynamic-slice_dynamic-update-slice_fusion.refs_0_.refs_1_.refs_2_, ...), custom_call_target="tpu_custom_call" | custom-call | flops 48318382080 | bytes 5505024 | tf_op jit(solution)/shard_map/attn_bwd/pallas_call | solution.py:262
  535.7 6.6 collective-permute-start.21
  542.3 4.4 collective-permute-start.22
  557.4 5.8 fusion.39
  563.2 12.9 %collective-permute-done.22 = bf16[768,384]{1,0:T(8,128)(2,1)S(1)} collective-permute-done((bf16[768,384]{1,0:T(8,128)(2,1)S(1)}, bf16[768,384]{1,0:T(8,128)(2,1)S(1)}, u32[]{:S(2)}, u32[]{:S(2)}) %collective-permute-start.22) | collective-permute-done | bytes 589856 | tf_op jit(solution)/shard_map/ppermute | solution.py:376
  577.2 16.5 %collective-permute-start.26 = (bf16[128,1408]{1,0:T(8,128)(2,1)}, bf16[128,1408]{1,0:T(8,128)(2,1)S(1)}, u32[]{:S(2)}, u32[]{:S(2)}) collective-permute-start(bf16[128,1408]{1,0:T(8,128)(2,1)} %pad_maximum_fusion.7), channel_id=1, source_target_pairs={{0,3},{1,0},{2,1},{3,2},{4,7},{5,4},{6,5},{7,6},{8,11},{9,8},{10,9... | collective-permute-start | bytes 1081352 | tf_op jit(solution)/shard_map/ppermute | solution.py:376
  595.8 2.7 convolution_convert_fusion.9
  598.6 2.7 convolution_convert_fusion.8
  603.0 5.1 fusion.61
  612.6 9.2 %collective-permute-done.25 = bf16[128,1408]{1,0:T(8,128)(2,1)} collective-permute-done((bf16[128,1408]{1,0:T(8,128)(2,1)}, bf16[128,1408]{1,0:T(8,128)(2,1)}, u32[]{:S(2)}, u32[]{:S(2)}) %collective-permute-start.25) | collective-permute-done | bytes 360480 | tf_op jit(solution)/shard_map/ppermute | solution.py:376
  623.8 3.7 collective-permute-start.29
  627.5 23.3 %psum.14 = f32[5,1024]{1,0:T(8,128)S(1)} all-reduce(f32[5,1024]{1,0:T(8,128)S(1)} %pad_maximum_fusion.8), channel_id=1, replica_groups=mesh['scene'=8,'seq'=4] {'scene'}, use_global_device_ids=true, to_apply=%region_25.26 | all-reduce | flops 5120 | bytes 40960 | tf_op jit(solution)/shard_map/psum | solution.py:650
  653.2 9.2 %psum.15 = f32[128,2]{0,1:T(2,128)} all-reduce(f32[128,2]{0,1:T(2,128)S(1)} %fusion.118), channel_id=1, replica_groups=mesh['scene'=8,'seq'=4] {'seq'}, use_global_device_ids=true, to_apply=%region_26.27 | all-reduce | flops 256 | bytes 2048 | tf_op jit(solution)/shard_map/psum | solution.py:651
  670.8 4.1 collective-permute-done.30
  675.0 5.8 collective-permute-done.31
  (415 shorter events, 148.3 us)
Async XLA Ops:
  7.2 59.9 %all-gather.5.cloned.1.call-start = ((), (), s32[]{:S(2)}) async-start(), calls=%async_computation.4 | async-start | bytes 7667712 | tf_op jit(solution)/shard_map/all_gather | solution.py:413
  10.3 196.9 %all-gather.7.cloned.1.call-start = ((), (), s32[]{:S(2)}) async-start(), calls=%async_computation.5 | async-start | bytes 2359296 | tf_op jit(solution)/shard_map/all_gather | solution.py:410
  11.1 203.4 %all-gather.9.cloned.1.call-start = ((), (), s32[]{:S(2)}) async-start(), calls=%async_computation.6 | async-start | bytes 9437184 | tf_op jit(solution)/shard_map/all_gather | solution.py:410
  13.9 221.9 %all-gather.11.cloned.1.call-start = ((), (), s32[]{:S(2)}) async-start(), calls=%async_computation.7 | async-start | bytes 9437184 | tf_op jit(solution)/shard_map/all_gather | solution.py:410
  15.5 40.4 %collective-permute-start = (bf16[784,1024]{1,0:T(8,128)(2,1)}, bf16[784,1024]{1,0:T(8,128)(2,1)S(1)}, u32[]{:S(2)}, u32[]{:S(2)}) collective-permute-start(bf16[784,1024]{1,0:T(8,128)(2,1)} %fusion.71), channel_id=1, source_target_pairs={{1,0},{2,1},{3,2},{5,4},{6,5},{7,6},{9,8},{10,9},{11,10},{13,12},{... | collective-permute-start | bytes 4816904 | tf_op jit(solution)/shard_map/ppermute | solution.py:371
  16.9 40.2 %collective-permute-start.1 = (bf16[784,1024]{1,0:T(8,128)(2,1)}, bf16[784,1024]{1,0:T(8,128)(2,1)}, u32[]{:S(2)}, u32[]{:S(2)}) collective-permute-start(bf16[784,1024]{1,0:T(8,128)(2,1)} %fusion.71), channel_id=1, source_target_pairs={{0,1},{1,2},{2,3},{4,5},{5,6},{6,7},{8,9},{9,10},{10,11},{12,13},{... | collective-permute-start | bytes 4816904 | tf_op jit(solution)/shard_map/ppermute | solution.py:371
  24.9 331.1 %reduce-scatter.7.cloned.1.call-start = ((), (), s32[]{:S(2)}) async-start(), calls=%async_computation.8 | async-start | bytes 9437184 | tf_op jit(solution)/shard_map/reduce_scatter | solution.py:559
  33.5 34.4 %copy-start.52 = (f32[768]{0:T(1024)}, f32[768]{0:T(1024)S(1)}, u32[]{:S(2)}) copy-start(f32[768]{0:T(1024)S(1)} %broadcast_multiply_fusion.8) | copy-start | bytes 9220
  34.1 46.2 %copy-start.56 = (f32[768]{0:T(1024)}, f32[768]{0:T(1024)S(1)}, u32[]{:S(2)}) copy-start(f32[768]{0:T(1024)S(1)} %add_rsqrt_fusion.4) | copy-start | bytes 9220
  58.8 38.9 %collective-permute-start.3 = (bf16[784,1024]{1,0:T(8,128)(2,1)}, bf16[784,1024]{1,0:T(8,128)(2,1)}, u32[]{:S(2)}, u32[]{:S(2)}) collective-permute-start(bf16[784,1024]{1,0:T(8,128)(2,1)} %copy-done.10), channel_id=1, source_target_pairs={{1,0},{2,1},{3,2},{5,4},{6,5},{7,6},{9,8},{10,9},{11,10},{13,12},{... | collective-permute-start | bytes 4816904 | tf_op jit(solution)/shard_map/ppermute | solution.py:371
  60.1 38.8 %collective-permute-start.2 = (bf16[784,1024]{1,0:T(8,128)(2,1)}, bf16[784,1024]{1,0:T(8,128)(2,1)}, u32[]{:S(2)}, u32[]{:S(2)}) collective-permute-start(bf16[784,1024]{1,0:T(8,128)(2,1)} %collective-permute-done.1), channel_id=1, source_target_pairs={{0,1},{1,2},{2,3},{4,5},{5,6},{6,7},{8,9},{9,10},{10,11},{12,13},{... | collective-permute-start | bytes 4816904 | tf_op jit(solution)/shard_map/ppermute | solution.py:371
  67.9 83.4 %copy-start.54 = (f32[1024,1]{0,1:T(1,128)}, f32[1024,1]{0,1:T(1,128)S(1)}, u32[]{:S(2)}) copy-start(f32[1024,1]{0,1:T(1,128)S(1)} %get-tuple-element.283) | copy-start | bytes 12292
  81.2 24.8 %copy-start.11 = (bf16[768,1024]{1,0:T(8,128)(2,1)S(1)}, bf16[768,1024]{1,0:T(8,128)(2,1)}, u32[]{:S(2)}) copy-start(bf16[768,1024]{1,0:T(8,128)(2,1)} %get-tuple-element.159) | copy-start | bytes 4718596
  98.9 37.3 %collective-permute-start.4 = (bf16[784,1024]{1,0:T(8,128)(2,1)}, bf16[784,1024]{1,0:T(8,128)(2,1)}, u32[]{:S(2)}, u32[]{:S(2)}) collective-permute-start(bf16[784,1024]{1,0:T(8,128)(2,1)} %collective-permute-done.2), channel_id=1, source_target_pairs={{0,1},{1,2},{2,3},{4,5},{5,6},{6,7},{8,9},{9,10},{10,11},{12,13},{... | collective-permute-start | bytes 4816904 | tf_op jit(solution)/shard_map/ppermute | solution.py:371
  104.5 37.0 %collective-permute-start.5 = (bf16[784,1024]{1,0:T(8,128)(2,1)}, bf16[784,1024]{1,0:T(8,128)(2,1)}, u32[]{:S(2)}, u32[]{:S(2)}) collective-permute-start(bf16[784,1024]{1,0:T(8,128)(2,1)} %collective-permute-done.3), channel_id=1, source_target_pairs={{1,0},{2,1},{3,2},{5,4},{6,5},{7,6},{9,8},{10,9},{11,10},{13,12},{... | collective-permute-start | bytes 4816904 | tf_op jit(solution)/shard_map/ppermute | solution.py:371
  243.7 11.7 %collective-permute-start.6 = (bf16[192,128]{1,0:T(8,128)(2,1)S(1)}, bf16[192,128]{1,0:T(8,128)(2,1)S(1)}, u32[]{:S(2)}, u32[]{:S(2)}) collective-permute-start(bf16[192,128]{1,0:T(8,128)(2,1)S(1)} %get-tuple-element.291), channel_id=1, source_target_pairs={{0,1},{1,2},{2,3},{3,0},{4,5},{5,6},{6,7},{7,4},{8,9},{9,10},{10,1... | collective-permute-start | bytes 147464 | tf_op jit(solution)/shard_map/ppermute | solution.py:376
  245.1 10.2 %collective-permute-start.7 = (bf16[192,128]{1,0:T(8,128)(2,1)S(1)}, bf16[192,128]{1,0:T(8,128)(2,1)S(1)}, u32[]{:S(2)}, u32[]{:S(2)}) collective-permute-start(bf16[192,128]{1,0:T(8,128)(2,1)S(1)} %get-tuple-element.291), channel_id=1, source_target_pairs={{0,2},{1,3},{2,0},{3,1},{4,6},{5,7},{6,4},{7,5},{8,10},{9,11},{10,... | collective-permute-start | bytes 147464 | tf_op jit(solution)/shard_map/ppermute | solution.py:376
  247.0 8.4 %collective-permute-start.8 = (bf16[192,128]{1,0:T(8,128)(2,1)S(1)}, bf16[192,128]{1,0:T(8,128)(2,1)S(1)}, u32[]{:S(2)}, u32[]{:S(2)}) collective-permute-start(bf16[192,128]{1,0:T(8,128)(2,1)S(1)} %get-tuple-element.291), channel_id=1, source_target_pairs={{0,3},{1,0},{2,1},{3,2},{4,7},{5,4},{6,5},{7,6},{8,11},{9,8},{10,9... | collective-permute-start | bytes 147464 | tf_op jit(solution)/shard_map/ppermute | solution.py:376
  278.7 255.0 %reduce-scatter.11.cloned.1.call-start = ((), (), s32[]{:S(2)}) async-start(), calls=%async_computation.10 | async-start | bytes 3538944 | tf_op jit(solution)/shard_map/reduce_scatter | solution.py:559
  324.0 31.9 %collective-permute-start.10 = (bf16[848,256]{1,0:T(8,128)(2,1)}, bf16[848,256]{1,0:T(8,128)(2,1)}, u32[]{:S(2)}, u32[]{:S(2)}) collective-permute-start(bf16[848,256]{1,0:T(8,128)(2,1)} %get-tuple-element.260), channel_id=1, source_target_pairs={{0,2},{1,3},{2,0},{3,1},{4,6},{5,7},{6,4},{7,5},{8,10},{9,11},{10,... | collective-permute-start | bytes 1302536 | tf_op jit(solution)/shard_map/ppermute | solution.py:376
  325.2 30.7 %collective-permute-start.11 = (bf16[848,256]{1,0:T(8,128)(2,1)}, bf16[848,256]{1,0:T(8,128)(2,1)}, u32[]{:S(2)}, u32[]{:S(2)}) collective-permute-start(bf16[848,256]{1,0:T(8,128)(2,1)} %get-tuple-element.259), channel_id=1, source_target_pairs={{0,3},{1,0},{2,1},{3,2},{4,7},{5,4},{6,5},{7,6},{8,11},{9,8},{10,9... | collective-permute-start | bytes 1302536 | tf_op jit(solution)/shard_map/ppermute | solution.py:376
  326.9 29.0 %collective-permute-start.9 = (bf16[848,256]{1,0:T(8,128)(2,1)S(1)}, bf16[848,256]{1,0:T(8,128)(2,1)}, u32[]{:S(2)}, u32[]{:S(2)}) collective-permute-start(bf16[848,256]{1,0:T(8,128)(2,1)S(1)} %get-tuple-element.261), channel_id=1, source_target_pairs={{0,1},{1,2},{2,3},{3,0},{4,5},{5,6},{6,7},{7,4},{8,9},{9,10},{10,1... | collective-permute-start | bytes 1302536 | tf_op jit(solution)/shard_map/ppermute | solution.py:376
  356.0 177.8 %reduce-scatter.9.cloned.1.call-start = ((), (), s32[]{:S(2)}) async-start(), calls=%async_computation.9 | async-start | bytes 9437184 | tf_op jit(solution)/shard_map/reduce_scatter | solution.py:559
  356.7 308.4 %reduce-scatter.13.cloned.1.call-start = ((), (), s32[]{:S(2)}) async-start(), calls=%async_computation.11 | async-start | bytes 1769472
  365.8 81.6 %collective-permute-start.12 = (bf16[512,256]{1,0:T(8,128)(2,1)S(1)}, bf16[512,256]{1,0:T(8,128)(2,1)S(1)}, u32[]{:S(2)}, u32[]{:S(2)}) collective-permute-start(bf16[512,256]{1,0:T(8,128)(2,1)S(1)} %get-tuple-element.269), channel_id=1, source_target_pairs={{0,1},{1,2},{2,3},{3,0},{4,5},{5,6},{6,7},{7,4},{8,9},{9,10},{10,1... | collective-permute-start | bytes 786440 | tf_op jit(solution)/shard_map/ppermute | solution.py:376
  372.8 74.6 %collective-permute-start.13 = (bf16[512,256]{1,0:T(8,128)(2,1)S(1)}, bf16[512,256]{1,0:T(8,128)(2,1)S(1)}, u32[]{:S(2)}, u32[]{:S(2)}) collective-permute-start(bf16[512,256]{1,0:T(8,128)(2,1)S(1)} %get-tuple-element.268), channel_id=1, source_target_pairs={{0,2},{1,3},{2,0},{3,1},{4,6},{5,7},{6,4},{7,5},{8,10},{9,11},{10,... | collective-permute-start | bytes 786440 | tf_op jit(solution)/shard_map/ppermute | solution.py:376
  372.8 74.6 %collective-permute-start.14 = (bf16[512,256]{1,0:T(8,128)(2,1)S(1)}, bf16[512,256]{1,0:T(8,128)(2,1)}, u32[]{:S(2)}, u32[]{:S(2)}) collective-permute-start(bf16[512,256]{1,0:T(8,128)(2,1)S(1)} %get-tuple-element.267), channel_id=1, source_target_pairs={{0,3},{1,0},{2,1},{3,2},{4,7},{5,4},{6,5},{7,6},{8,11},{9,8},{10,9... | collective-permute-start | bytes 786440 | tf_op jit(solution)/shard_map/ppermute | solution.py:376
  448.5 11.1 %collective-permute-start.18 = (bf16[512,256]{1,0:T(8,128)(2,1)S(1)}, bf16[512,256]{1,0:T(8,128)(2,1)S(1)}, u32[]{:S(2)}, u32[]{:S(2)}) collective-permute-start(bf16[512,256]{1,0:T(8,128)(2,1)S(1)} %add_convert_fusion.2), channel_id=1, source_target_pairs={{0,1},{1,2},{2,3},{3,0},{4,5},{5,6},{6,7},{7,4},{8,9},{9,10},{10,1... | collective-permute-start | bytes 786440 | tf_op jit(solution)/shard_map/ppermute | solution.py:376
  448.5 83.8 %collective-permute-start.19 = (bf16[512,256]{1,0:T(8,128)(2,1)S(1)}, bf16[512,256]{1,0:T(8,128)(2,1)S(1)}, u32[]{:S(2)}, u32[]{:S(2)}) collective-permute-start(bf16[512,256]{1,0:T(8,128)(2,1)S(1)} %add_convert_fusion.2), channel_id=1, source_target_pairs={{0,2},{1,3},{2,0},{3,1},{4,6},{5,7},{6,4},{7,5},{8,10},{9,11},{10,... | collective-permute-start | bytes 786440 | tf_op jit(solution)/shard_map/ppermute | solution.py:376
  451.0 81.3 %collective-permute-start.20 = (bf16[512,256]{1,0:T(8,128)(2,1)S(1)}, bf16[512,256]{1,0:T(8,128)(2,1)S(1)}, u32[]{:S(2)}, u32[]{:S(2)}) collective-permute-start(bf16[512,256]{1,0:T(8,128)(2,1)S(1)} %add_convert_fusion.2), channel_id=1, source_target_pairs={{0,3},{1,0},{2,1},{3,2},{4,7},{5,4},{6,5},{7,6},{8,11},{9,8},{10,9... | collective-permute-start | bytes 786440 | tf_op jit(solution)/shard_map/ppermute | solution.py:376
  455.2 77.8 %collective-permute-start.15 = (bf16[768,384]{1,0:T(8,128)(2,1)}, bf16[768,384]{1,0:T(8,128)(2,1)}, u32[]{:S(2)}, u32[]{:S(2)}) collective-permute-start(bf16[768,384]{1,0:T(8,128)(2,1)} %get-tuple-element.257), channel_id=1, source_target_pairs={{0,1},{1,2},{2,3},{3,0},{4,5},{5,6},{6,7},{7,4},{8,9},{9,10},{10,1... | collective-permute-start | bytes 1769480 | tf_op jit(solution)/shard_map/ppermute | solution.py:376
  455.9 77.8 %collective-permute-start.16 = (bf16[768,384]{1,0:T(8,128)(2,1)}, bf16[768,384]{1,0:T(8,128)(2,1)}, u32[]{:S(2)}, u32[]{:S(2)}) collective-permute-start(bf16[768,384]{1,0:T(8,128)(2,1)} %get-tuple-element.256), channel_id=1, source_target_pairs={{0,2},{1,3},{2,0},{3,1},{4,6},{5,7},{6,4},{7,5},{8,10},{9,11},{10,... | collective-permute-start | bytes 1769480 | tf_op jit(solution)/shard_map/ppermute | solution.py:376
  459.6 74.2 %collective-permute-start.17 = (bf16[768,384]{1,0:T(8,128)(2,1)S(1)}, bf16[768,384]{1,0:T(8,128)(2,1)}, u32[]{:S(2)}, u32[]{:S(2)}) collective-permute-start(bf16[768,384]{1,0:T(8,128)(2,1)S(1)} %get-tuple-element.255), channel_id=1, source_target_pairs={{0,3},{1,0},{2,1},{3,2},{4,7},{5,4},{6,5},{7,6},{8,11},{9,8},{10,9... | collective-permute-start | bytes 1769480 | tf_op jit(solution)/shard_map/ppermute | solution.py:376
  535.7 27.5 %collective-permute-start.21 = (bf16[768,384]{1,0:T(8,128)(2,1)S(1)}, bf16[768,384]{1,0:T(8,128)(2,1)S(1)}, u32[]{:S(2)}, u32[]{:S(2)}) collective-permute-start(bf16[768,384]{1,0:T(8,128)(2,1)S(1)} %get-tuple-element.253), channel_id=1, source_target_pairs={{0,1},{1,2},{2,3},{3,0},{4,5},{5,6},{6,7},{7,4},{8,9},{9,10},{10,1... | collective-permute-start | bytes 1769480 | tf_op jit(solution)/shard_map/ppermute | solution.py:376
  542.3 33.8 %collective-permute-start.22 = (bf16[768,384]{1,0:T(8,128)(2,1)S(1)}, bf16[768,384]{1,0:T(8,128)(2,1)S(1)}, u32[]{:S(2)}, u32[]{:S(2)}) collective-permute-start(bf16[768,384]{1,0:T(8,128)(2,1)S(1)} %get-tuple-element.252), channel_id=1, source_target_pairs={{0,2},{1,3},{2,0},{3,1},{4,6},{5,7},{6,4},{7,5},{8,10},{9,11},{10,... | collective-permute-start | bytes 1769480 | tf_op jit(solution)/shard_map/ppermute | solution.py:376
  546.7 29.4 %collective-permute-start.23 = (bf16[768,384]{1,0:T(8,128)(2,1)S(1)}, bf16[768,384]{1,0:T(8,128)(2,1)S(1)}, u32[]{:S(2)}, u32[]{:S(2)}) collective-permute-start(bf16[768,384]{1,0:T(8,128)(2,1)S(1)} %get-tuple-element.251), channel_id=1, source_target_pairs={{0,3},{1,0},{2,1},{3,2},{4,7},{5,4},{6,5},{7,6},{8,11},{9,8},{10,9... | collective-permute-start | bytes 1769480 | tf_op jit(solution)/shard_map/ppermute | solution.py:376
  563.2 32.6 %copy-start.22 = (bf16[3072,384]{1,0:T(8,128)(2,1)S(1)}, bf16[3072,384]{1,0:T(8,128)(2,1)}, u32[]{:S(2)}) copy-start(bf16[3072,384]{1,0:T(8,128)(2,1)} %attn_bwd.2) | copy-start | bytes 7077892
  563.2 35.3 %copy-start.74 = (bf16[768,384]{1,0:T(8,128)(2,1)}, bf16[768,384]{1,0:T(8,128)(2,1)S(1)}, u32[]{:S(2)}) copy-start(bf16[768,384]{1,0:T(8,128)(2,1)S(1)} %collective-permute-done.21) | copy-start | bytes 1769476
  576.1 22.4 %copy-start.76 = (bf16[768,384]{1,0:T(8,128)(2,1)}, bf16[768,384]{1,0:T(8,128)(2,1)S(1)}, u32[]{:S(2)}) copy-start(bf16[768,384]{1,0:T(8,128)(2,1)S(1)} %collective-permute-done.23) | copy-start | bytes 1769476
  577.2 35.4 %collective-permute-start.26 = (bf16[128,1408]{1,0:T(8,128)(2,1)}, bf16[128,1408]{1,0:T(8,128)(2,1)S(1)}, u32[]{:S(2)}, u32[]{:S(2)}) collective-permute-start(bf16[128,1408]{1,0:T(8,128)(2,1)} %pad_maximum_fusion.7), channel_id=1, source_target_pairs={{0,3},{1,0},{2,1},{3,2},{4,7},{5,4},{6,5},{7,6},{8,11},{9,8},{10,9... | collective-permute-start | bytes 1081352 | tf_op jit(solution)/shard_map/ppermute | solution.py:376
  594.5 27.3 %collective-permute-start.25 = (bf16[128,1408]{1,0:T(8,128)(2,1)}, bf16[128,1408]{1,0:T(8,128)(2,1)}, u32[]{:S(2)}, u32[]{:S(2)}) collective-permute-start(bf16[128,1408]{1,0:T(8,128)(2,1)} %pad_maximum_fusion.6), channel_id=1, source_target_pairs={{0,2},{1,3},{2,0},{3,1},{4,6},{5,7},{6,4},{7,5},{8,10},{9,11},{10,... | collective-permute-start | bytes 1081352 | tf_op jit(solution)/shard_map/ppermute | solution.py:376
  595.3 26.5 %collective-permute-start.24 = (bf16[128,1408]{1,0:T(8,128)(2,1)}, bf16[128,1408]{1,0:T(8,128)(2,1)}, u32[]{:S(2)}, u32[]{:S(2)}) collective-permute-start(bf16[128,1408]{1,0:T(8,128)(2,1)} %pad_maximum_fusion.5), channel_id=1, source_target_pairs={{0,1},{1,2},{2,3},{3,0},{4,5},{5,6},{6,7},{7,4},{8,9},{9,10},{10,1... | collective-permute-start | bytes 1081352 | tf_op jit(solution)/shard_map/ppermute | solution.py:376
  623.4 39.4 %collective-permute-start.27 = (bf16[128,1408]{1,0:T(8,128)(2,1)S(1)}, bf16[128,1408]{1,0:T(8,128)(2,1)S(1)}, u32[]{:S(2)}, u32[]{:S(2)}) collective-permute-start(bf16[128,1408]{1,0:T(8,128)(2,1)S(1)} %add_convert_fusion.1), channel_id=1, source_target_pairs={{0,1},{1,2},{2,3},{3,0},{4,5},{5,6},{6,7},{7,4},{8,9},{9,10},{10,1... | collective-permute-start | bytes 1081352 | tf_op jit(solution)/shard_map/ppermute | solution.py:376
  623.7 39.0 %collective-permute-start.28 = (bf16[128,1408]{1,0:T(8,128)(2,1)S(1)}, bf16[128,1408]{1,0:T(8,128)(2,1)S(1)}, u32[]{:S(2)}, u32[]{:S(2)}) collective-permute-start(bf16[128,1408]{1,0:T(8,128)(2,1)S(1)} %add_convert_fusion.1), channel_id=1, source_target_pairs={{0,2},{1,3},{2,0},{3,1},{4,6},{5,7},{6,4},{7,5},{8,10},{9,11},{10,... | collective-permute-start | bytes 1081352 | tf_op jit(solution)/shard_map/ppermute | solution.py:376
  623.8 39.0 %collective-permute-start.29 = (bf16[128,1408]{1,0:T(8,128)(2,1)S(1)}, bf16[128,1408]{1,0:T(8,128)(2,1)S(1)}, u32[]{:S(2)}, u32[]{:S(2)}) collective-permute-start(bf16[128,1408]{1,0:T(8,128)(2,1)S(1)} %add_convert_fusion.1), channel_id=1, source_target_pairs={{0,3},{1,0},{2,1},{3,2},{4,7},{5,4},{6,5},{7,6},{8,11},{9,8},{10,9... | collective-permute-start | bytes 1081352 | tf_op jit(solution)/shard_map/ppermute | solution.py:376
  666.5 8.4 %collective-permute-start.30 = (bf16[128,768]{0,1:T(8,128)(2,1)S(1)}, bf16[128,768]{0,1:T(8,128)(2,1)S(1)}, u32[]{:S(2)}, u32[]{:S(2)}) collective-permute-start(bf16[128,768]{0,1:T(8,128)(2,1)S(1)} %copy.122), channel_id=1, source_target_pairs={{0,1},{1,2},{2,3},{3,0},{4,5},{5,6},{6,7},{7,4},{8,9},{9,10},{10,1... | collective-permute-start | bytes 589832 | tf_op jit(solution)/shard_map/ppermute | solution.py:376
  668.2 12.5 %collective-permute-start.31 = (bf16[128,768]{0,1:T(8,128)(2,1)S(1)}, bf16[128,768]{0,1:T(8,128)(2,1)S(1)}, u32[]{:S(2)}, u32[]{:S(2)}) collective-permute-start(bf16[128,768]{0,1:T(8,128)(2,1)S(1)} %copy.122), channel_id=1, source_target_pairs={{0,2},{1,3},{2,0},{3,1},{4,6},{5,7},{6,4},{7,5},{8,10},{9,11},{10,... | collective-permute-start | bytes 589832 | tf_op jit(solution)/shard_map/ppermute | solution.py:376
  668.8 12.0 %collective-permute-start.32 = (bf16[128,768]{0,1:T(8,128)(2,1)S(1)}, bf16[128,768]{0,1:T(8,128)(2,1)S(1)}, u32[]{:S(2)}, u32[]{:S(2)}) collective-permute-start(bf16[128,768]{0,1:T(8,128)(2,1)S(1)} %copy.122), channel_id=1, source_target_pairs={{0,3},{1,0},{2,1},{3,2},{4,7},{5,4},{6,5},{7,6},{8,11},{9,8},{10,9... | collective-permute-start | bytes 589832 | tf_op jit(solution)/shard_map/ppermute | solution.py:376
  (77 other events, 491.6 us)
Sparse Core Ops, SparseCore 0:
  10.5 51.6 all-gather.4
  64.6 27.7 all-gather.6
  94.3 54.2 all-gather.8
  150.3 54.2 all-gather.10
  278.9 69.1 reduce-scatter.6
  356.1 48.5 reduce-scatter.10
  408.1 71.5 reduce-scatter.8
  603.1 37.5 reduce-scatter.12

commit v5 on v4

--- a/solution.py
+++ b/solution.py
@@ -488,9 +488,16 @@
     planes_f = all_planes.astype(f32)
     feat = planes_f[:cells] + planes_f[cells : 2 * cells] + planes_f[2 * cells :]
     dh = w_dec1.shape[1]
-    eye = jnp.eye(PP, dtype=f32)
-    dec1 = jnp.einsum("fh,pq->pfqh", w_dec1, eye).reshape(PP * TF, PP * dh)
-    dec2 = jnp.einsum("ho,pq->phoq", w_dec2, eye).reshape(PP * dh, OUT * PP)
+    def same(shape, row_of, col_of):
+        row = lax.broadcasted_iota(jnp.int32, shape, 0)
+        col = lax.broadcasted_iota(jnp.int32, shape, 1)
+        return row_of(row) == col_of(col)
+
+    diag_one = same((PP * TF, PP * dh), lambda r: r // TF, lambda c: c // dh)
+    diag_two = same((PP * dh, OUT * PP), lambda r: r // dh, lambda c: c % PP)
+    widen = same((OUT, OUT * PP), lambda r: r, lambda c: c // PP).astype(f32)
+    dec1 = jnp.where(diag_one, jnp.tile(w_dec1, (PP, PP)), 0.0)
+    dec2 = jnp.where(diag_two, jnp.tile(exact(w_dec2, widen, NN), (PP, 1)), 0.0)
     hidden_pre = exact(feat, dec1, NN) + jnp.tile(b_dec1, PP)
     zdec, zslope = gelu_parts(hidden_pre)
     decoded_all = exact(zdec, dec2, NN)
@@ -499,13 +506,12 @@
     cot_f = cot_cells.astype(f32)
     grad_hidden = exact(cot_f, dec2, NT) * zslope
     gfeat = exact(grad_hidden, dec1, NT).astype(bf16)
-    grad_w2 = jnp.einsum(
-        "phop->ho", exact(zdec, cot_f, TN).reshape(PP, dh, OUT, PP)
-    )
-    grad_b1 = jnp.sum(jnp.sum(grad_hidden, axis=0).reshape(PP, dh), axis=0)
-    grad_w1 = jnp.einsum(
-        "pfph->fh", exact(feat, grad_hidden, TN).reshape(PP, TF, PP, dh)
-    )
+    wide_w2 = jnp.where(diag_two, exact(zdec, cot_f, TN), 0.0)
+    grad_w2 = exact(sum(wide_w2[p * dh : p * dh + dh] for p in range(PP)), widen, NT)
+    wide_b1 = jnp.sum(grad_hidden, axis=0, keepdims=True)
+    grad_b1 = sum(wide_b1[0, p * dh : p * dh + dh] for p in range(PP))
+    wide_w1 = exact(feat, grad_hidden, TN)
+    grad_w1 = sum(wide_w1[p * TF : p * TF + TF, p * dh : p * dh + dh] for p in range(PP))
     plane_grad = lax.dynamic_slice_in_dim(
         jnp.concatenate([gfeat] * 4, axis=0), lax.rem(rank * tri_rows, cells), tri_rows, 0
     )
@@ -541,9 +547,9 @@
     letter, late_a2, late_pre, late_mid, qkv_rows = lax.optimization_barrier(
         (letter, a2, grad_pre, mid_grad, qkv_rows)
     )
+    late_rows = qkv_rows
     letters = [piece(letter, ahead(d), cols, 1) for d in range(seq_count)]
     letters = [turn(x, d) if d else x for d, x in enumerate(letters)]
-    own_all = in_turn([piece(x, rank, 3 * cols, 1) for x in qkv_rows])
     fc1_grad = mxu(late_a2, late_pre, TN).astype(bf16)
     norm_cols = jnp.stack([gain_grad_two, shift_grad_two], axis=1).astype(bf16)
     misc_grad = jnp.concatenate(
@@ -561,18 +567,20 @@
     fc2_part = over_scene(fc2_grad)
     dec_flat = jnp.concatenate([grad_w1.reshape(-1), grad_b1, grad_w2.reshape(-1)])
     dec_flat = jnp.pad(dec_flat, (0, -dec_flat.size % width)).reshape(-1, width)
-    own_all, letters, fc2_part, fc1_grad, misc_grad, dec_flat = lax.optimization_barrier(
-        (own_all, letters, fc2_part, fc1_grad, misc_grad, dec_flat)
+    letters, fc2_part, fc1_grad, misc_grad, dec_flat, late_rows = lax.optimization_barrier(
+        (letters, fc2_part, fc1_grad, misc_grad, dec_flat, late_rows)
     )
     fc1_part = over_scene(fc1_grad)
-    misc_part = over_scene(misc_grad)
-
-    def sum_pieces(*parts):
-        def block(at):
-            cut = [piece(part, at, part.shape[1] // seq_count, 1) for part in parts]
-            return jnp.concatenate(cut, axis=1) if len(cut) > 1 else cut[0]
-
-        return [turn(block(ahead(d)), d) if d else block(rank) for d in range(seq_count)]
+
+    def send(pieces):
+        return [turn(x, d) if d else x for d, x in enumerate(pieces)]
+
+    def cut(part):
+        size = part.shape[1] // seq_count
+        return [piece(part, ahead(d), size, 1) for d in range(seq_count)]
+
+    def sum_pieces(part):
+        return send(cut(part))
 
     def blocks_of(pieces):
         mine = sum(x.astype(f32) for x in pieces).astype(bf16)
@@ -585,25 +593,34 @@
             out = lax.dynamic_update_slice_in_dim(out, got.astype(f32), behind(d) * size, 1)
         return out
 
-    def exchange(mine):
-        pieces = [piece(mine, (seq_count - d) % seq_count, tok_rows, 0) for d in range(seq_count)]
-        return [turn(x, d) if d else x for d, x in enumerate(pieces)]
-
-    fc2_pieces = sum_pieces(fc2_part)
+    def cut_rows(mine):
+        return [piece(mine, (seq_count - d) % seq_count, tok_rows, 0) for d in range(seq_count)]
+
+    fc2_cut, late_rows = lax.optimization_barrier((cut(fc2_part), late_rows))
+    fc2_pieces = send(fc2_cut)
+    own_all = in_turn([piece(x, rank, 3 * cols, 1) for x in late_rows])
+    own_all, letters, fc2_pieces = lax.optimization_barrier((own_all, letters, fc2_pieces))
+    fc2_blocks = blocks_of(fc2_pieces)
     moved, head_grads = [], []
     for p in range(pairs_dev):
         mine = attn_bwd(own_all, letters, bias, p, head_dim)
         if p == 0:
-            own_all, mine, fc2_pieces = lax.optimization_barrier((own_all, mine, fc2_pieces))
-            fc2_blocks = blocks_of(fc2_pieces)
+            mine, fc2_blocks, fc1_part, misc_grad = lax.optimization_barrier(
+                (mine, fc2_blocks, fc1_part, misc_grad)
+            )
+            misc_part = over_scene(misc_grad)
+            own_all, rows_cut, fc1_cut = lax.optimization_barrier(
+                (own_all, cut_rows(mine), cut(fc1_part))
+            )
+            fc1_pieces = send(fc1_cut)
         else:
-            mine, moved[-1], head_grads[-1], a1, fc2_blocks, fc1_part, misc_part = (
-                lax.optimization_barrier(
-                    (mine, moved[-1], head_grads[-1], a1, fc2_blocks, fc1_part, misc_part)
-                )
+            held = (mine, moved[-1], head_grads[-1], a1, qkv_w, fc1_pieces[:-1], fc1_cut[-1], misc_part)
+            mine, moved[-1], head_grads[-1], a1, late_w, fc1_pieces[:-1], fc1_cut[-1], misc_part = (
+                lax.optimization_barrier(held)
             )
+            fc1_pieces[-1] = turn(fc1_cut[-1], seq_count - 1)
         head_grads.append(mine)
-        moved.append(exchange(mine))
+        moved.append(send(cut_rows(mine) if p else rows_cut))
     moved[-1][1], head_grads = lax.optimization_barrier((moved[-1][1], head_grads))
     a1_all = in_turn(a1)
     own_qkv = [mxu(a1_all, part, TN).astype(bf16) for part in head_grads]
@@ -614,7 +631,7 @@
         return jnp.concatenate(
             [
                 lax.dynamic_slice_in_dim(
-                    qkv_w, behind(d) * 3 * cols + p * 3 * lanes, 3 * lanes, 1
+                    late_w, behind(d) * 3 * cols + p * 3 * lanes, 3 * lanes, 1
                 )
                 for d in range(seq_count)
             ],
@@ -626,21 +643,20 @@
 
     grad_in = sum(pair_part(moved[p], pair_weights(p)) for p in range(pairs_dev - 1))
     last_weights = pair_weights(pairs_dev - 1)
-    moved[-1], grad_in, last_weights, grad_fc2, fc1_part, misc_part = lax.optimization_barrier(
-        (moved[-1], grad_in, last_weights, grad_fc2, fc1_part, misc_part)
-    )
-    wide_pieces = sum_pieces(fc1_part, misc_part)
+    moved[-1], grad_in, last_weights, fc1_pieces, misc_part = lax.optimization_barrier(
+        (moved[-1], grad_in, last_weights, fc1_pieces, misc_part)
+    )
+    fc1_blocks = blocks_of(fc1_pieces)
+    misc_pieces = sum_pieces(misc_part)
     grad_in = grad_in + pair_part(moved[-1], last_weights)
     u_one, inv_one = normalize(inputs_f)
     back_one, gain_grad_one, shift_grad_one = norm_back(grad_in, u_one, inv_one, gain_one)
     grad_tokens = (grad_mid + back_one).astype(bf16)
 
     sums = jnp.concatenate([jnp.stack([gain_grad_one, shift_grad_one]), dec_flat], axis=0)
-    sums, wide_pieces = lax.optimization_barrier((sums, wide_pieces))
-    wide_blocks = blocks_of(wide_pieces)
-    cut = w_fc1.shape[1] // seq_count
-    grad_fc1 = side_by_side([x[:, :cut] for x in wide_blocks])
-    grad_misc = side_by_side([x[:, cut:] for x in wide_blocks])
+    sums, misc_pieces = lax.optimization_barrier((sums, misc_pieces))
+    grad_fc1 = side_by_side(fc1_blocks)
+    grad_misc = side_by_side(blocks_of(misc_pieces))
     grad_proj = grad_misc[:, :width]
     grad_unp = grad_misc[:, width : width + PP * TF]
     norm_two = grad_misc[:, width + PP * TF : width + PP * TF + 2]

time: 699 us -> 743 us (1.063)
  starting transfers between devices: 85.9 us -> 107 us
  waiting for transfers between devices: 67.2 us -> 76.5 us
    ppermute x27 -> x33, starting transfers between devices: 62.9 us -> 83.4 us  [turn(): lax.ppermute(x, 'seq', [(i, (i + step) % seq_count) for i in range(seq_co...]
    ppermute x27 -> x33, waiting for transfers between devices: 34.4 us -> 47.4 us  [turn(): lax.ppermute(x, 'seq', [(i, (i + step) % seq_count) for i in range(seq_co...]
    unnamed x176 -> x221, local copies, waits for them, and re-layouts: 23.8 us -> 26.5 us
  transfers between devices with their start and end apart: 41 -> 47, of which waited for: 11 -> 13; matrix products, arithmetic and copies ran while one was open for 29% -> 29% of each run, Pallas kernels for 34% -> 32%
where the time goes in v5:
time: 743 us; the launch traced here: 732 us
  Pallas kernels  235 us (32%)
  matrix products  131 us (18%)
  starting transfers between devices  107 us (14%)
  local copies, waits for them, and re-layouts  77.5 us (10%)
  waiting for transfers between devices  76.5 us (10%)
  other arithmetic  54.8 us (7%)
  blocking collectives  33.3 us (4%)
  between operations  17.3 us (2%)
    pallas_call x2, Pallas kernels, attn_bwd(): pl.pallas_call(functools.partial(attn_bwd_kernel, tk=tk, tq=tk, scale=hea...  145 us
    dot_general x20, matrix products, mxu(): lax.dot_general(left, right, dims, preferred_element_type=jnp.float32)  120 us
    ppermute x33, starting transfers between devices, turn(): lax.ppermute(x, 'seq', [(i, (i + step) % seq_count) for i in range(seq_co...  83.4 us
    pallas_call x4, Pallas kernels, attn_fwd(): pl.pallas_call(functools.partial(attn_fwd_kernel, first=first, last=last,...  69.4 us
    ppermute x33, waiting for transfers between devices, turn(): lax.ppermute(x, 'seq', [(i, (i + step) % seq_count) for i in range(seq_co...  47.4 us
    ppermute x6, waiting for transfers between devices, hop(): lax.ppermute(x, 'seq', [(i, i + step) for i in range(seq_count) if 0 <= i...  28.9 us
    unnamed x221, local copies, waits for them, and re-layouts  26.5 us
    psum x1, blocking collectives, per_device(): sums = lax.psum(sums, 'scene')  24.1 us
  transfers between devices with their start and end apart: 47, of which 13 were waited for; matrix products, arithmetic and copies ran while one was open for 29% of the time, Pallas kernels for 32%

profile of v5, /device:TPU:0, one launch (start us, length us, event | category | flops | bytes accessed | tf_op | source)
XLA Modules:
  0.0 732.3 jit_solution(1925755068841371956)
XLA Ops:
  11.2 2.7 convert_element_type.287
  16.9 6.7 collective-permute-start.1
  37.1 18.8 %collective-permute-done = bf16[784,1024]{1,0:T(8,128)(2,1)S(1)} collective-permute-done((bf16[784,1024]{1,0:T(8,128)(2,1)}, bf16[784,1024]{1,0:T(8,128)(2,1)S(1)}, u32[]{:S(2)}, u32[]{:S(2)}) %collective-permute-start) | collective-permute-done | bytes 1605664 | tf_op jit(solution)/shard_map/ppermute | solution.py:371
  60.1 6.2 collective-permute-start.2
  70.2 10.3 %convolution_convert_fusion.5.refs_0_.refs_1_.refs_2_ = bf16[768,3072]{1,0:T(8,128)(2,1)} fusion(bf16[768,1024]{1,0:T(8,128)(2,1)S(1)} %get-tuple-element.215, bf16[1024,3328]{0,1:T(8,128)(2,1)} %all-gather.5.cloned.1.call-done), kind=kOutput, calls=%fused_computation.6 | convolution fusion | flops 4834197504 | bytes 12582912 | tf_op jit(solution)/shard_map/dot_general | solution.py:28
  81.3 16.1 %attn_fwd.4 = (f32[8,2,80,768]{3,2,1,0:T(8,128)}, f32[8,2,768]{2,1,0:T(2,128)}) custom-call(bf16[768,3072]{1,0:T(8,128)(2,1)} %convolution_convert_fusion.5.refs_0_.refs_1_.refs_2_, bf16[768,3072]{1,0:T(8,128)(2,1)} %convolution_convert_fusion.5.refs_0_.refs_1_.refs_2_, bf16[768,3072]{1,0:T(8,128)(2,1)} %convolution_convert_fusion.5.refs_0_.refs_1_.refs_2_, ...), custom_call_target="tpu_custom_call" | custom-call | flops 9663676416 | bytes 6291456 | tf_op jit(solution)/shard_map/attn_fwd/pallas_call | solution.py:155
  98.9 5.5 collective-permute-start.4
  106.0 9.5 %convolution_convert_fusion.4.refs_1_.refs_2_ = bf16[768,3072]{1,0:T(8,128)(2,1)} fusion(bf16[768,1024]{1,0:T(8,128)(2,1)S(1)} %copy-done.13, bf16[1024,3328]{0,1:T(8,128)(2,1)} %all-gather.5.cloned.1.call-done), kind=kOutput, calls=%fused_computation.5 | convolution fusion | flops 4834197504 | bytes 12582912 | tf_op jit(solution)/shard_map/dot_general | solution.py:28
  115.5 17.5 %attn_fwd.5 = (f32[8,2,80,768]{3,2,1,0:T(8,128)}, f32[8,2,768]{2,1,0:T(2,128)}) custom-call(bf16[768,3072]{1,0:T(8,128)(2,1)} %convolution_convert_fusion.5.refs_0_.refs_1_.refs_2_, bf16[768,3072]{1,0:T(8,128)(2,1)} %convolution_convert_fusion.4.refs_1_.refs_2_, bf16[768,3072]{1,0:T(8,128)(2,1)} %convolution_convert_fusion.4.refs_1_.refs_2_, ...), custom_call_target="tpu_custom_call" | custom-call | flops 9663676416 | bytes 6291456 | tf_op jit(solution)/shard_map/attn_fwd/pallas_call | solution.py:155
  133.0 3.3 collective-permute-done.4
  136.3 5.3 collective-permute-done.5
  141.5 2.9 select_select_fusion
  155.1 6.8 convolution_convert_fusion.2.refs_1_.refs_2_
  161.9 17.7 %attn_fwd.6 = (f32[8,2,80,768]{3,2,1,0:T(8,128)}, f32[8,2,768]{2,1,0:T(2,128)}) custom-call(bf16[768,3072]{1,0:T(8,128)(2,1)} %convolution_convert_fusion.5.refs_0_.refs_1_.refs_2_, bf16[768,3072]{1,0:T(8,128)(2,1)} %convolution_convert_fusion.2.refs_1_.refs_2_, bf16[768,3072]{1,0:T(8,128)(2,1)} %convolution_convert_fusion.2.refs_1_.refs_2_, ...), custom_call_target="tpu_custom_call" | custom-call | flops 9663676416 | bytes 6291456 | tf_op jit(solution)/shard_map/attn_fwd/pallas_call | solution.py:155
  179.6 9.5 %convolution_convert_fusion.3.refs_1_.refs_2_ = bf16[768,3072]{1,0:T(8,128)(2,1)} fusion(bf16[768,1024]{1,0:T(8,128)(2,1)S(1)} %copy-done.17, bf16[1024,3328]{0,1:T(8,128)(2,1)} %all-gather.5.cloned.1.call-done), kind=kOutput, calls=%fused_computation.4 | convolution fusion | flops 4834197504 | bytes 12582912 | tf_op jit(solution)/shard_map/dot_general | solution.py:28
  189.1 18.1 %attn_fwd.7 = (bf16[768,1024]{1,0:T(8,128)(2,1)}, f32[8,2,768]{2,1,0:T(2,128)}) custom-call(bf16[768,3072]{1,0:T(8,128)(2,1)} %convolution_convert_fusion.5.refs_0_.refs_1_.refs_2_, bf16[768,3072]{1,0:T(8,128)(2,1)} %convolution_convert_fusion.3.refs_1_.refs_2_, bf16[768,3072]{1,0:T(8,128)(2,1)} %convolution_convert_fusion.3.refs_1_.refs_2_, ...), custom_call_target="tpu_custom_call" | custom-call | flops 9663676416 | bytes 6291456 | tf_op jit(solution)/shard_map/attn_fwd/pallas_call | solution.py:155
  207.2 3.9 fusion.158
  214.6 21.3 %fc1_gelu.1 = (bf16[768,4096]{1,0:T(8,128)(2,1)}, bf16[768,4096]{1,0:T(8,128)(2,1)}) custom-call(bf16[768,1024]{1,0:T(8,128)(2,1)} %add_convert_fusion.x_ref, bf16[1024,4096]{1,0:T(8,128)(2,1)} %all-gather.9.cloned.1.call-done.w_ref), custom_call_target="tpu_custom_call" | custom-call | flops 6442450944 | bytes 22544384 | tf_op jit(solution)/shard_map/fc1_gelu/pallas_call | solution.py:306
  236.0 5.8 fusion.79
  249.5 6.1 fusion.51
  262.6 9.5 %convolution_convert_fusion.1 = bf16[4096,1024]{1,0:T(8,128)(2,1)} fusion(bf16[768,4096]{1,0:T(8,128)(2,1)S(1)} %copy-done.97, f32[192,1024]{1,0:T(8,128)S(1)} %convolution_add_fusion, f32[576,1024]{1,0:T(8,128)S(1)} %copy-done.10), kind=kOutput, calls=%fused_computation.2 | convolution fusion | flops 6449790976 | bytes 17825792 | tf_op jit(solution)/shard_map/dot_general | solution.py:28
  288.1 11.2 %multiply_convert_fusion = bf16[768,4096]{1,0:T(8,128)(2,1)S(1)} fusion(bf16[768,4096]{1,0:T(8,128)(2,1)} %get-tuple-element.139, bf16[4096,1024]{1,0:T(8,128)(2,1)} %all-gather.11.cloned.1.call-done, f32[192,1024]{1,0:T(8,128)} %copy-done.21, f32[576,1024]{1,0:T(8,128)} %slice.194), kind=kOutput, calls=%fused_computation | convolution fusion | flops 6455033856 | bytes 24117248 | tf_op jit(solution)/shard_map/dot_general | solution.py:28
  299.4 12.3 %multiply_reduce_fusion = (bf16[1024]{0:T(1024)(128)(2,1)S(1)}, f32[768]{0:T(1024)S(1)}, f32[768]{0:T(1024)S(1)}, bf16[1024]{0:T(1024)(128)(2,1)S(1)}, f32[768,1024]{1,0:T(8,128)S(1)}) fusion(f32[768,1024]{1,0:T(8,128)S(1)} %copy-done.5, f32[768]{0:T(1024)S(1)} %copy-done.63, f32[768]{0:T(1024)S(1)} %broadcast_multiply_fusion.4, f32[1024]{0:T(1024)S(1)} %bitcast.89, ...), kind=kOutput, calls=%fused_computation.66 | convolution fusion | flops 6449524736 | bytes 20992000 | tf_op jit(solution)/shard_map/dot_general | solution.py:28
  328.5 3.2 convolution_convert_fusion.6
  331.7 9.1 %convolution_convert_fusion = bf16[1024,4096]{1,0:T(8,128)(2,1)} fusion(bf16[768,1024]{1,0:T(8,128)(2,1)S(1)} %copy-done.30, bf16[768,4096]{1,0:T(8,128)(2,1)S(1)} %bitcast.98), kind=kOutput, calls=%fused_computation.1 | convolution fusion | flops 6446645248 | bytes 16252928 | tf_op jit(solution)/shard_map/dot_general | solution.py:28
  342.9 4.3 collective-permute-done.10.refs_6_
  347.2 5.6 collective-permute-done.9.refs_5_
  359.0 12.3 %collective-permute-start.12 = (bf16[512,256]{1,0:T(8,128)(2,1)S(1)}, bf16[512,256]{1,0:T(8,128)(2,1)S(1)}, u32[]{:S(2)}, u32[]{:S(2)}) collective-permute-start(bf16[512,256]{1,0:T(8,128)(2,1)S(1)} %get-tuple-element.163), channel_id=1, source_target_pairs={{0,1},{1,2},{2,3},{3,0},{4,5},{5,6},{6,7},{7,4},{8,9},{9,10},{10,1... | collective-permute-start | bytes 786440 | tf_op jit(solution)/shard_map/ppermute | solution.py:376
  373.7 2.9 broadcast_in_dim.108
  388.1 6.2 collective-permute-start.15
  394.3 3.4 collective-permute-start.16
  397.9 72.4 %attn_bwd.2 = bf16[3072,384]{1,0:T(8,128)(2,1)} custom-call(bf16[3072,768]{1,0:T(8,128)(2,1)} %dynamic-slice_dynamic-update-slice_fusion.refs_0_.refs_1_.refs_2_, bf16[3072,768]{1,0:T(8,128)(2,1)} %dynamic-slice_dynamic-update-slice_fusion.refs_0_.refs_1_.refs_2_, bf16[3072,768]{1,0:T(8,128)(2,1)} %dynamic-slice_dynamic-update-slice_fusion.refs_0_.refs_1_.refs_2_, ...), custom_call_target="tpu_custom_call" | custom-call | flops 48318382080 | bytes 5505024 | tf_op jit(solution)/shard_map/attn_bwd/pallas_call | solution.py:262
  471.7 3.1 fusion.155
  482.7 3.0 copy.80
  488.4 72.2 %attn_bwd.3 = bf16[3072,384]{1,0:T(8,128)(2,1)} custom-call(bf16[3072,768]{1,0:T(8,128)(2,1)} %dynamic-slice_dynamic-update-slice_fusion.refs_0_.refs_1_.refs_2_, bf16[3072,768]{1,0:T(8,128)(2,1)} %dynamic-slice_dynamic-update-slice_fusion.refs_0_.refs_1_.refs_2_, bf16[3072,768]{1,0:T(8,128)(2,1)} %dynamic-slice_dynamic-update-slice_fusion.refs_0_.refs_1_.refs_2_, ...), custom_call_target="tpu_custom_call" | custom-call | flops 48318382080 | bytes 5505024 | tf_op jit(solution)/shard_map/attn_bwd/pallas_call | solution.py:262
  577.7 5.7 fusion.37
  587.1 23.5 %collective-permute-done.26 = bf16[128,1024]{1,0:T(8,128)(2,1)S(1)} collective-permute-done((bf16[128,1024]{1,0:T(8,128)(2,1)S(1)}, bf16[128,1024]{1,0:T(8,128)(2,1)S(1)}, u32[]{:S(2)}, u32[]{:S(2)}) %collective-permute-start.26) | collective-permute-done | bytes 262176 | tf_op jit(solution)/shard_map/ppermute | solution.py:376
  614.4 13.3 %collective-permute-start.36 = (bf16[128,1024]{1,0:T(8,128)(2,1)S(1)}, bf16[128,1024]{1,0:T(8,128)(2,1)S(1)}, u32[]{:S(2)}, u32[]{:S(2)}) collective-permute-start(bf16[128,1024]{1,0:T(8,128)(2,1)S(1)} %get-tuple-element.290), channel_id=1, source_target_pairs={{0,1},{1,2},{2,3},{3,0},{4,5},{5,6},{6,7},{7,4},{8,9},{9,10},{10,1... | collective-permute-start | bytes 786440 | tf_op jit(solution)/shard_map/ppermute | solution.py:376
  628.7 2.7 convolution_convert_fusion.9
  631.5 2.7 convolution_convert_fusion.8
  638.0 3.2 collective-permute-start.29
  641.2 5.0 fusion.59
  651.1 8.1 %collective-permute-start.30 = (bf16[128,384]{0,1:T(8,128)(2,1)S(1)}, bf16[128,384]{0,1:T(8,128)(2,1)S(1)}, u32[]{:S(2)}, u32[]{:S(2)}) collective-permute-start(bf16[128,384]{0,1:T(8,128)(2,1)S(1)} %add_convert_fusion.3), channel_id=1, source_target_pairs={{0,1},{1,2},{2,3},{3,0},{4,5},{5,6},{6,7},{7,4},{8,9},{9,10},{10,1... | collective-permute-start | bytes 294920 | tf_op jit(solution)/shard_map/ppermute | solution.py:376
  659.2 3.4 collective-permute-start.31
  662.6 24.1 %psum.14 = f32[5,1024]{1,0:T(8,128)S(1)} all-reduce(f32[5,1024]{1,0:T(8,128)S(1)} %pad_maximum_fusion.5), channel_id=1, replica_groups=mesh['scene'=8,'seq'=4] {'scene'}, use_global_device_ids=true, to_apply=%region_22.23 | all-reduce | flops 5120 | bytes 40960 | tf_op jit(solution)/shard_map/psum | solution.py:666
  689.0 9.2 %psum.15 = f32[128,2]{0,1:T(2,128)} all-reduce(f32[128,2]{0,1:T(2,128)S(1)} %fusion.131), channel_id=1, replica_groups=mesh['scene'=8,'seq'=4] {'seq'}, use_global_device_ids=true, to_apply=%region_23.24 | all-reduce | flops 256 | bytes 2048 | tf_op jit(solution)/shard_map/psum | solution.py:667
  713.2 4.1 collective-permute-done.33
  717.3 5.8 collective-permute-done.34
  (477 shorter events, 179.3 us)
Async XLA Ops:
  7.2 60.0 %all-gather.5.cloned.1.call-start = ((), (), s32[]{:S(2)}) async-start(), calls=%async_computation.4 | async-start | bytes 7667712 | tf_op jit(solution)/shard_map/all_gather | solution.py:413
  10.3 196.9 %all-gather.7.cloned.1.call-start = ((), (), s32[]{:S(2)}) async-start(), calls=%async_computation.5 | async-start | bytes 2359296 | tf_op jit(solution)/shard_map/all_gather | solution.py:410
  11.2 203.4 %all-gather.9.cloned.1.call-start = ((), (), s32[]{:S(2)}) async-start(), calls=%async_computation.6 | async-start | bytes 9437184 | tf_op jit(solution)/shard_map/all_gather | solution.py:410
  13.9 222.0 %all-gather.11.cloned.1.call-start = ((), (), s32[]{:S(2)}) async-start(), calls=%async_computation.7 | async-start | bytes 9437184 | tf_op jit(solution)/shard_map/all_gather | solution.py:410
  15.5 40.4 %collective-permute-start = (bf16[784,1024]{1,0:T(8,128)(2,1)}, bf16[784,1024]{1,0:T(8,128)(2,1)S(1)}, u32[]{:S(2)}, u32[]{:S(2)}) collective-permute-start(bf16[784,1024]{1,0:T(8,128)(2,1)} %fusion.69), channel_id=1, source_target_pairs={{1,0},{2,1},{3,2},{5,4},{6,5},{7,6},{9,8},{10,9},{11,10},{13,12},{... | collective-permute-start | bytes 4816904 | tf_op jit(solution)/shard_map/ppermute | solution.py:371
  16.9 40.2 %collective-permute-start.1 = (bf16[784,1024]{1,0:T(8,128)(2,1)}, bf16[784,1024]{1,0:T(8,128)(2,1)}, u32[]{:S(2)}, u32[]{:S(2)}) collective-permute-start(bf16[784,1024]{1,0:T(8,128)(2,1)} %fusion.69), channel_id=1, source_target_pairs={{0,1},{1,2},{2,3},{4,5},{5,6},{6,7},{8,9},{9,10},{10,11},{12,13},{... | collective-permute-start | bytes 4816904 | tf_op jit(solution)/shard_map/ppermute | solution.py:371
  24.9 327.9 %reduce-scatter.9.cloned.1.call-start = ((), (), s32[]{:S(2)}) async-start(), calls=%async_computation.8 | async-start | bytes 9437184 | tf_op jit(solution)/shard_map/reduce_scatter | solution.py:565
  25.7 251.4 %copy-start.73 = (pred[16]{0:T(512)(128)(4,1)}, pred[16]{0:T(512)(128)(4,1)S(1)}, u32[]{:S(2)}) copy-start(pred[16]{0:T(512)(128)(4,1)S(1)} %get-tuple-element.351) | copy-start | bytes 52
  58.8 38.9 %collective-permute-start.3 = (bf16[784,1024]{1,0:T(8,128)(2,1)}, bf16[784,1024]{1,0:T(8,128)(2,1)}, u32[]{:S(2)}, u32[]{:S(2)}) collective-permute-start(bf16[784,1024]{1,0:T(8,128)(2,1)} %copy-done.12), channel_id=1, source_target_pairs={{1,0},{2,1},{3,2},{5,4},{6,5},{7,6},{9,8},{10,9},{11,10},{13,12},{... | collective-permute-start | bytes 4816904 | tf_op jit(solution)/shard_map/ppermute | solution.py:371
  60.1 38.8 %collective-permute-start.2 = (bf16[784,1024]{1,0:T(8,128)(2,1)}, bf16[784,1024]{1,0:T(8,128)(2,1)}, u32[]{:S(2)}, u32[]{:S(2)}) collective-permute-start(bf16[784,1024]{1,0:T(8,128)(2,1)} %collective-permute-done.1), channel_id=1, source_target_pairs={{0,1},{1,2},{2,3},{4,5},{5,6},{6,7},{8,9},{9,10},{10,11},{12,13},{... | collective-permute-start | bytes 4816904 | tf_op jit(solution)/shard_map/ppermute | solution.py:371
  98.9 37.3 %collective-permute-start.4 = (bf16[784,1024]{1,0:T(8,128)(2,1)}, bf16[784,1024]{1,0:T(8,128)(2,1)}, u32[]{:S(2)}, u32[]{:S(2)}) collective-permute-start(bf16[784,1024]{1,0:T(8,128)(2,1)} %collective-permute-done.2), channel_id=1, source_target_pairs={{0,1},{1,2},{2,3},{4,5},{5,6},{6,7},{8,9},{9,10},{10,11},{12,13},{... | collective-permute-start | bytes 4816904 | tf_op jit(solution)/shard_map/ppermute | solution.py:371
  104.5 37.0 %collective-permute-start.5 = (bf16[784,1024]{1,0:T(8,128)(2,1)}, bf16[784,1024]{1,0:T(8,128)(2,1)}, u32[]{:S(2)}, u32[]{:S(2)}) collective-permute-start(bf16[784,1024]{1,0:T(8,128)(2,1)} %collective-permute-done.3), channel_id=1, source_target_pairs={{1,0},{2,1},{3,2},{5,4},{6,5},{7,6},{9,8},{10,9},{11,10},{13,12},{... | collective-permute-start | bytes 4816904 | tf_op jit(solution)/shard_map/ppermute | solution.py:371
  244.0 11.7 %collective-permute-start.6 = (bf16[192,128]{1,0:T(8,128)(2,1)S(1)}, bf16[192,128]{1,0:T(8,128)(2,1)S(1)}, u32[]{:S(2)}, u32[]{:S(2)}) collective-permute-start(bf16[192,128]{1,0:T(8,128)(2,1)S(1)} %get-tuple-element.344), channel_id=1, source_target_pairs={{0,1},{1,2},{2,3},{3,0},{4,5},{5,6},{6,7},{7,4},{8,9},{9,10},{10,1... | collective-permute-start | bytes 147464 | tf_op jit(solution)/shard_map/ppermute | solution.py:376
  245.4 10.2 %collective-permute-start.7 = (bf16[192,128]{1,0:T(8,128)(2,1)S(1)}, bf16[192,128]{1,0:T(8,128)(2,1)S(1)}, u32[]{:S(2)}, u32[]{:S(2)}) collective-permute-start(bf16[192,128]{1,0:T(8,128)(2,1)S(1)} %get-tuple-element.344), channel_id=1, source_target_pairs={{0,2},{1,3},{2,0},{3,1},{4,6},{5,7},{6,4},{7,5},{8,10},{9,11},{10,... | collective-permute-start | bytes 147464 | tf_op jit(solution)/shard_map/ppermute | solution.py:376
  247.4 8.3 %collective-permute-start.8 = (bf16[192,128]{1,0:T(8,128)(2,1)S(1)}, bf16[192,128]{1,0:T(8,128)(2,1)S(1)}, u32[]{:S(2)}, u32[]{:S(2)}) collective-permute-start(bf16[192,128]{1,0:T(8,128)(2,1)S(1)} %get-tuple-element.344), channel_id=1, source_target_pairs={{0,3},{1,0},{2,1},{3,2},{4,7},{5,4},{6,5},{7,6},{8,11},{9,8},{10,9... | collective-permute-start | bytes 147464 | tf_op jit(solution)/shard_map/ppermute | solution.py:376
  272.1 198.9 %reduce-scatter.11.cloned.1.call-start = ((), (), s32[]{:S(2)}) async-start(), calls=%async_computation.9 | async-start | bytes 9437184 | tf_op jit(solution)/shard_map/reduce_scatter | solution.py:565
  324.3 22.9 %collective-permute-start.10 = (bf16[848,256]{1,0:T(8,128)(2,1)}, bf16[848,256]{1,0:T(8,128)(2,1)}, u32[]{:S(2)}, u32[]{:S(2)}) collective-permute-start(bf16[848,256]{1,0:T(8,128)(2,1)} %get-tuple-element.313), channel_id=1, source_target_pairs={{0,2},{1,3},{2,0},{3,1},{4,6},{5,7},{6,4},{7,5},{8,10},{9,11},{10,... | collective-permute-start | bytes 1302536 | tf_op jit(solution)/shard_map/ppermute | solution.py:376
  324.8 22.4 %collective-permute-start.11 = (bf16[848,256]{1,0:T(8,128)(2,1)}, bf16[848,256]{1,0:T(8,128)(2,1)}, u32[]{:S(2)}, u32[]{:S(2)}) collective-permute-start(bf16[848,256]{1,0:T(8,128)(2,1)} %get-tuple-element.312), channel_id=1, source_target_pairs={{0,3},{1,0},{2,1},{3,2},{4,7},{5,4},{6,5},{7,6},{8,11},{9,8},{10,9... | collective-permute-start | bytes 1302536 | tf_op jit(solution)/shard_map/ppermute | solution.py:376
  326.6 26.2 %collective-permute-start.9 = (bf16[848,256]{1,0:T(8,128)(2,1)}, bf16[848,256]{1,0:T(8,128)(2,1)}, u32[]{:S(2)}, u32[]{:S(2)}) collective-permute-start(bf16[848,256]{1,0:T(8,128)(2,1)} %get-tuple-element.314), channel_id=1, source_target_pairs={{0,1},{1,2},{2,3},{3,0},{4,5},{5,6},{6,7},{7,4},{8,9},{9,10},{10,1... | collective-permute-start | bytes 1302536 | tf_op jit(solution)/shard_map/ppermute | solution.py:376
  352.8 211.3 %reduce-scatter.13.cloned.1.call-start = ((), (), s32[]{:S(2)}) async-start(), calls=%async_computation.10 | async-start | bytes 3538944
  359.0 27.5 %collective-permute-start.12 = (bf16[512,256]{1,0:T(8,128)(2,1)S(1)}, bf16[512,256]{1,0:T(8,128)(2,1)S(1)}, u32[]{:S(2)}, u32[]{:S(2)}) collective-permute-start(bf16[512,256]{1,0:T(8,128)(2,1)S(1)} %get-tuple-element.163), channel_id=1, source_target_pairs={{0,1},{1,2},{2,3},{3,0},{4,5},{5,6},{6,7},{7,4},{8,9},{9,10},{10,1... | collective-permute-start | bytes 786440 | tf_op jit(solution)/shard_map/ppermute | solution.py:376
  371.3 15.2 %collective-permute-start.13 = (bf16[512,256]{1,0:T(8,128)(2,1)S(1)}, bf16[512,256]{1,0:T(8,128)(2,1)S(1)}, u32[]{:S(2)}, u32[]{:S(2)}) collective-permute-start(bf16[512,256]{1,0:T(8,128)(2,1)S(1)} %get-tuple-element.164), channel_id=1, source_target_pairs={{0,2},{1,3},{2,0},{3,1},{4,6},{5,7},{6,4},{7,5},{8,10},{9,11},{10,... | collective-permute-start | bytes 786440 | tf_op jit(solution)/shard_map/ppermute | solution.py:376
  371.3 16.7 %collective-permute-start.14 = (bf16[512,256]{1,0:T(8,128)(2,1)S(1)}, bf16[512,256]{1,0:T(8,128)(2,1)S(1)}, u32[]{:S(2)}, u32[]{:S(2)}) collective-permute-start(bf16[512,256]{1,0:T(8,128)(2,1)S(1)} %get-tuple-element.165), channel_id=1, source_target_pairs={{0,3},{1,0},{2,1},{3,2},{4,7},{5,4},{6,5},{7,6},{8,11},{9,8},{10,9... | collective-permute-start | bytes 786440 | tf_op jit(solution)/shard_map/ppermute | solution.py:376
  388.1 82.2 %collective-permute-start.15 = (bf16[512,256]{1,0:T(8,128)(2,1)S(1)}, bf16[512,256]{1,0:T(8,128)(2,1)S(1)}, u32[]{:S(2)}, u32[]{:S(2)}) collective-permute-start(bf16[512,256]{1,0:T(8,128)(2,1)S(1)} %add_convert_fusion.2), channel_id=1, source_target_pairs={{0,1},{1,2},{2,3},{3,0},{4,5},{5,6},{6,7},{7,4},{8,9},{9,10},{10,1... | collective-permute-start | bytes 786440 | tf_op jit(solution)/shard_map/ppermute | solution.py:376
  394.3 76.0 %collective-permute-start.16 = (bf16[512,256]{1,0:T(8,128)(2,1)S(1)}, bf16[512,256]{1,0:T(8,128)(2,1)S(1)}, u32[]{:S(2)}, u32[]{:S(2)}) collective-permute-start(bf16[512,256]{1,0:T(8,128)(2,1)S(1)} %add_convert_fusion.2), channel_id=1, source_target_pairs={{0,2},{1,3},{2,0},{3,1},{4,6},{5,7},{6,4},{7,5},{8,10},{9,11},{10,... | collective-permute-start | bytes 786440 | tf_op jit(solution)/shard_map/ppermute | solution.py:376
  397.7 73.3 %collective-permute-start.17 = (bf16[512,256]{1,0:T(8,128)(2,1)S(1)}, bf16[512,256]{1,0:T(8,128)(2,1)}, u32[]{:S(2)}, u32[]{:S(2)}) collective-permute-start(bf16[512,256]{1,0:T(8,128)(2,1)S(1)} %add_convert_fusion.2), channel_id=1, source_target_pairs={{0,3},{1,0},{2,1},{3,2},{4,7},{5,4},{6,5},{7,6},{8,11},{9,8},{10,9... | collective-permute-start | bytes 786440 | tf_op jit(solution)/shard_map/ppermute | solution.py:376
  475.8 89.6 %collective-permute-start.18 = (bf16[768,384]{1,0:T(8,128)(2,1)}, bf16[768,384]{1,0:T(8,128)(2,1)}, u32[]{:S(2)}, u32[]{:S(2)}) collective-permute-start(bf16[768,384]{1,0:T(8,128)(2,1)} %get-tuple-element.181), channel_id=1, source_target_pairs={{0,1},{1,2},{2,3},{3,0},{4,5},{5,6},{6,7},{7,4},{8,9},{9,10},{10,1... | collective-permute-start | bytes 1769480 | tf_op jit(solution)/shard_map/ppermute | solution.py:376
  477.8 87.6 %collective-permute-start.19 = (bf16[768,384]{1,0:T(8,128)(2,1)}, bf16[768,384]{1,0:T(8,128)(2,1)}, u32[]{:S(2)}, u32[]{:S(2)}) collective-permute-start(bf16[768,384]{1,0:T(8,128)(2,1)} %get-tuple-element.182), channel_id=1, source_target_pairs={{0,2},{1,3},{2,0},{3,1},{4,6},{5,7},{6,4},{7,5},{8,10},{9,11},{10,... | collective-permute-start | bytes 1769480 | tf_op jit(solution)/shard_map/ppermute | solution.py:376
  477.8 87.6 %collective-permute-start.20 = (bf16[768,384]{1,0:T(8,128)(2,1)}, bf16[768,384]{1,0:T(8,128)(2,1)}, u32[]{:S(2)}, u32[]{:S(2)}) collective-permute-start(bf16[768,384]{1,0:T(8,128)(2,1)} %get-tuple-element.183), channel_id=1, source_target_pairs={{0,3},{1,0},{2,1},{3,2},{4,7},{5,4},{6,5},{7,6},{8,11},{9,8},{10,9... | collective-permute-start | bytes 1769480 | tf_op jit(solution)/shard_map/ppermute | solution.py:376
  480.1 85.2 %collective-permute-start.21 = (bf16[128,1024]{1,0:T(8,128)(2,1)}, bf16[128,1024]{1,0:T(8,128)(2,1)}, u32[]{:S(2)}, u32[]{:S(2)}) collective-permute-start(bf16[128,1024]{1,0:T(8,128)(2,1)} %get-tuple-element.185), channel_id=1, source_target_pairs={{0,1},{1,2},{2,3},{3,0},{4,5},{5,6},{6,7},{7,4},{8,9},{9,10},{10,1... | collective-permute-start | bytes 786440 | tf_op jit(solution)/shard_map/ppermute | solution.py:376
  480.2 85.2 %collective-permute-start.22 = (bf16[128,1024]{1,0:T(8,128)(2,1)}, bf16[128,1024]{1,0:T(8,128)(2,1)}, u32[]{:S(2)}, u32[]{:S(2)}) collective-permute-start(bf16[128,1024]{1,0:T(8,128)(2,1)} %get-tuple-element.186), channel_id=1, source_target_pairs={{0,2},{1,3},{2,0},{3,1},{4,6},{5,7},{6,4},{7,5},{8,10},{9,11},{10,... | collective-permute-start | bytes 786440 | tf_op jit(solution)/shard_map/ppermute | solution.py:376
  485.7 222.0 %reduce-scatter.15.cloned.1.call-start = ((), (), s32[]{:S(2)}) async-start(), calls=%async_computation.11 | async-start | bytes 1769472
  566.5 20.6 %collective-permute-start.23 = (bf16[768,384]{1,0:T(8,128)(2,1)S(1)}, bf16[768,384]{1,0:T(8,128)(2,1)S(1)}, u32[]{:S(2)}, u32[]{:S(2)}) collective-permute-start(bf16[768,384]{1,0:T(8,128)(2,1)S(1)} %get-tuple-element.306), channel_id=1, source_target_pairs={{0,1},{1,2},{2,3},{3,0},{4,5},{5,6},{6,7},{7,4},{8,9},{9,10},{10,1... | collective-permute-start | bytes 1769480 | tf_op jit(solution)/shard_map/ppermute | solution.py:376
  568.3 42.4 %collective-permute-start.24 = (bf16[768,384]{1,0:T(8,128)(2,1)S(1)}, bf16[768,384]{1,0:T(8,128)(2,1)S(1)}, u32[]{:S(2)}, u32[]{:S(2)}) collective-permute-start(bf16[768,384]{1,0:T(8,128)(2,1)S(1)} %get-tuple-element.305), channel_id=1, source_target_pairs={{0,2},{1,3},{2,0},{3,1},{4,6},{5,7},{6,4},{7,5},{8,10},{9,11},{10,... | collective-permute-start | bytes 1769480 | tf_op jit(solution)/shard_map/ppermute | solution.py:376
  568.9 41.8 %collective-permute-start.25 = (bf16[768,384]{1,0:T(8,128)(2,1)S(1)}, bf16[768,384]{1,0:T(8,128)(2,1)S(1)}, u32[]{:S(2)}, u32[]{:S(2)}) collective-permute-start(bf16[768,384]{1,0:T(8,128)(2,1)S(1)} %get-tuple-element.304), channel_id=1, source_target_pairs={{0,3},{1,0},{2,1},{3,2},{4,7},{5,4},{6,5},{7,6},{8,11},{9,8},{10,9... | collective-permute-start | bytes 1769480 | tf_op jit(solution)/shard_map/ppermute | solution.py:376
  570.7 40.0 %collective-permute-start.26 = (bf16[128,1024]{1,0:T(8,128)(2,1)S(1)}, bf16[128,1024]{1,0:T(8,128)(2,1)S(1)}, u32[]{:S(2)}, u32[]{:S(2)}) collective-permute-start(bf16[128,1024]{1,0:T(8,128)(2,1)S(1)} %copy-done.43), channel_id=1, source_target_pairs={{0,3},{1,0},{2,1},{3,2},{4,7},{5,4},{6,5},{7,6},{8,11},{9,8},{10,9... | collective-permute-start | bytes 786440 | tf_op jit(solution)/shard_map/ppermute | solution.py:376
  614.4 90.9 %collective-permute-start.36 = (bf16[128,1024]{1,0:T(8,128)(2,1)S(1)}, bf16[128,1024]{1,0:T(8,128)(2,1)S(1)}, u32[]{:S(2)}, u32[]{:S(2)}) collective-permute-start(bf16[128,1024]{1,0:T(8,128)(2,1)S(1)} %get-tuple-element.290), channel_id=1, source_target_pairs={{0,1},{1,2},{2,3},{3,0},{4,5},{5,6},{6,7},{7,4},{8,9},{9,10},{10,1... | collective-permute-start | bytes 786440 | tf_op jit(solution)/shard_map/ppermute | solution.py:376
  627.6 78.4 %collective-permute-start.37 = (bf16[128,1024]{1,0:T(8,128)(2,1)S(1)}, bf16[128,1024]{1,0:T(8,128)(2,1)S(1)}, u32[]{:S(2)}, u32[]{:S(2)}) collective-permute-start(bf16[128,1024]{1,0:T(8,128)(2,1)S(1)} %get-tuple-element.290), channel_id=1, source_target_pairs={{0,2},{1,3},{2,0},{3,1},{4,6},{5,7},{6,4},{7,5},{8,10},{9,11},{10,... | collective-permute-start | bytes 786440 | tf_op jit(solution)/shard_map/ppermute | solution.py:376
  636.0 14.7 %collective-permute-start.27 = (bf16[128,384]{0,1:T(8,128)(2,1)S(1)}, bf16[128,384]{0,1:T(8,128)(2,1)S(1)}, u32[]{:S(2)}, u32[]{:S(2)}) collective-permute-start(bf16[128,384]{0,1:T(8,128)(2,1)S(1)} %get-tuple-element.326), channel_id=1, source_target_pairs={{0,1},{1,2},{2,3},{3,0},{4,5},{5,6},{6,7},{7,4},{8,9},{9,10},{10,1... | collective-permute-start | bytes 294920 | tf_op jit(solution)/shard_map/ppermute | solution.py:376
  636.1 14.9 %collective-permute-start.28 = (bf16[128,384]{0,1:T(8,128)(2,1)S(1)}, bf16[128,384]{0,1:T(8,128)(2,1)S(1)}, u32[]{:S(2)}, u32[]{:S(2)}) collective-permute-start(bf16[128,384]{0,1:T(8,128)(2,1)S(1)} %get-tuple-element.325), channel_id=1, source_target_pairs={{0,2},{1,3},{2,0},{3,1},{4,6},{5,7},{6,4},{7,5},{8,10},{9,11},{10,... | collective-permute-start | bytes 294920 | tf_op jit(solution)/shard_map/ppermute | solution.py:376
  638.0 12.9 %collective-permute-start.29 = (bf16[128,384]{0,1:T(8,128)(2,1)S(1)}, bf16[128,384]{0,1:T(8,128)(2,1)S(1)}, u32[]{:S(2)}, u32[]{:S(2)}) collective-permute-start(bf16[128,384]{0,1:T(8,128)(2,1)S(1)} %get-tuple-element.324), channel_id=1, source_target_pairs={{0,3},{1,0},{2,1},{3,2},{4,7},{5,4},{6,5},{7,6},{8,11},{9,8},{10,9... | collective-permute-start | bytes 294920 | tf_op jit(solution)/shard_map/ppermute | solution.py:376
  650.7 56.2 %collective-permute-start.38 = (bf16[128,1024]{1,0:T(8,128)(2,1)S(1)}, bf16[128,1024]{1,0:T(8,128)(2,1)S(1)}, u32[]{:S(2)}, u32[]{:S(2)}) collective-permute-start(bf16[128,1024]{1,0:T(8,128)(2,1)S(1)} %get-tuple-element.290), channel_id=1, source_target_pairs={{0,3},{1,0},{2,1},{3,2},{4,7},{5,4},{6,5},{7,6},{8,11},{9,8},{10,9... | collective-permute-start | bytes 786440 | tf_op jit(solution)/shard_map/ppermute | solution.py:376
  651.1 47.1 %collective-permute-start.30 = (bf16[128,384]{0,1:T(8,128)(2,1)S(1)}, bf16[128,384]{0,1:T(8,128)(2,1)S(1)}, u32[]{:S(2)}, u32[]{:S(2)}) collective-permute-start(bf16[128,384]{0,1:T(8,128)(2,1)S(1)} %add_convert_fusion.3), channel_id=1, source_target_pairs={{0,1},{1,2},{2,3},{3,0},{4,5},{5,6},{6,7},{7,4},{8,9},{9,10},{10,1... | collective-permute-start | bytes 294920 | tf_op jit(solution)/shard_map/ppermute | solution.py:376
  659.2 41.0 %collective-permute-start.31 = (bf16[128,384]{0,1:T(8,128)(2,1)S(1)}, bf16[128,384]{0,1:T(8,128)(2,1)S(1)}, u32[]{:S(2)}, u32[]{:S(2)}) collective-permute-start(bf16[128,384]{0,1:T(8,128)(2,1)S(1)} %add_convert_fusion.3), channel_id=1, source_target_pairs={{0,2},{1,3},{2,0},{3,1},{4,6},{5,7},{6,4},{7,5},{8,10},{9,11},{10,... | collective-permute-start | bytes 294920 | tf_op jit(solution)/shard_map/ppermute | solution.py:376
  698.3 4.7 collective-permute-start.32
  708.9 8.4 %collective-permute-start.33 = (bf16[128,768]{0,1:T(8,128)(2,1)S(1)}, bf16[128,768]{0,1:T(8,128)(2,1)S(1)}, u32[]{:S(2)}, u32[]{:S(2)}) collective-permute-start(bf16[128,768]{0,1:T(8,128)(2,1)S(1)} %copy.83), channel_id=1, source_target_pairs={{0,1},{1,2},{2,3},{3,0},{4,5},{5,6},{6,7},{7,4},{8,9},{9,10},{10,1... | collective-permute-start | bytes 589832 | tf_op jit(solution)/shard_map/ppermute | solution.py:376
  710.6 12.5 %collective-permute-start.34 = (bf16[128,768]{0,1:T(8,128)(2,1)S(1)}, bf16[128,768]{0,1:T(8,128)(2,1)S(1)}, u32[]{:S(2)}, u32[]{:S(2)}) collective-permute-start(bf16[128,768]{0,1:T(8,128)(2,1)S(1)} %copy.83), channel_id=1, source_target_pairs={{0,2},{1,3},{2,0},{3,1},{4,6},{5,7},{6,4},{7,5},{8,10},{9,11},{10,... | collective-permute-start | bytes 589832 | tf_op jit(solution)/shard_map/ppermute | solution.py:376
  713.0 10.2 %collective-permute-start.35 = (bf16[128,768]{0,1:T(8,128)(2,1)S(1)}, bf16[128,768]{0,1:T(8,128)(2,1)S(1)}, u32[]{:S(2)}, u32[]{:S(2)}) collective-permute-start(bf16[128,768]{0,1:T(8,128)(2,1)S(1)} %copy.83), channel_id=1, source_target_pairs={{0,3},{1,0},{2,1},{3,2},{4,7},{5,4},{6,5},{7,6},{8,11},{9,8},{10,9... | collective-permute-start | bytes 589832 | tf_op jit(solution)/shard_map/ppermute | solution.py:376
  (105 other events, 1703.6 us)
Sparse Core Ops, SparseCore 0:
  10.5 51.6 all-gather.4
  64.6 27.7 all-gather.6
  94.3 54.2 all-gather.8
  150.3 54.2 all-gather.10
  272.2 69.1 reduce-scatter.8
  353.0 82.8 reduce-scatter.10
  485.8 47.0 reduce-scatter.12
  636.1 40.2 reduce-scatter.14

commit v6 on v4

--- a/solution.py
+++ b/solution.py
@@ -499,13 +499,6 @@
     cot_f = cot_cells.astype(f32)
     grad_hidden = exact(cot_f, dec2, NT) * zslope
     gfeat = exact(grad_hidden, dec1, NT).astype(bf16)
-    grad_w2 = jnp.einsum(
-        "phop->ho", exact(zdec, cot_f, TN).reshape(PP, dh, OUT, PP)
-    )
-    grad_b1 = jnp.sum(jnp.sum(grad_hidden, axis=0).reshape(PP, dh), axis=0)
-    grad_w1 = jnp.einsum(
-        "pfph->fh", exact(feat, grad_hidden, TN).reshape(PP, TF, PP, dh)
-    )
     plane_grad = lax.dynamic_slice_in_dim(
         jnp.concatenate([gfeat] * 4, axis=0), lax.rem(rank * tri_rows, cells), tri_rows, 0
     )
@@ -559,20 +552,21 @@
         return lax.psum_scatter(g, "scene", scatter_dimension=0, tiled=True)
 
     fc2_part = over_scene(fc2_grad)
-    dec_flat = jnp.concatenate([grad_w1.reshape(-1), grad_b1, grad_w2.reshape(-1)])
-    dec_flat = jnp.pad(dec_flat, (0, -dec_flat.size % width)).reshape(-1, width)
-    own_all, letters, fc2_part, fc1_grad, misc_grad, dec_flat = lax.optimization_barrier(
-        (own_all, letters, fc2_part, fc1_grad, misc_grad, dec_flat)
+    own_all, letters, fc2_part, fc1_grad, misc_grad = lax.optimization_barrier(
+        (own_all, letters, fc2_part, fc1_grad, misc_grad)
     )
     fc1_part = over_scene(fc1_grad)
     misc_part = over_scene(misc_grad)
 
-    def sum_pieces(*parts):
-        def block(at):
-            cut = [piece(part, at, part.shape[1] // seq_count, 1) for part in parts]
-            return jnp.concatenate(cut, axis=1) if len(cut) > 1 else cut[0]
-
-        return [turn(block(ahead(d)), d) if d else block(rank) for d in range(seq_count)]
+    def send(pieces):
+        return [turn(x, d) if d else x for d, x in enumerate(pieces)]
+
+    def cut(part):
+        size = part.shape[1] // seq_count
+        return [piece(part, ahead(d), size, 1) for d in range(seq_count)]
+
+    def sum_pieces(part):
+        return send(cut(part))
 
     def blocks_of(pieces):
         mine = sum(x.astype(f32) for x in pieces).astype(bf16)
@@ -597,9 +591,10 @@
             own_all, mine, fc2_pieces = lax.optimization_barrier((own_all, mine, fc2_pieces))
             fc2_blocks = blocks_of(fc2_pieces)
         else:
-            mine, moved[-1], head_grads[-1], a1, fc2_blocks, fc1_part, misc_part = (
+            decoder = (feat, zdec, cot_f, grad_hidden)
+            mine, moved[-1], head_grads[-1], a1, fc2_blocks, fc1_part, misc_part, decoder = (
                 lax.optimization_barrier(
-                    (mine, moved[-1], head_grads[-1], a1, fc2_blocks, fc1_part, misc_part)
+                    (mine, moved[-1], head_grads[-1], a1, fc2_blocks, fc1_part, misc_part, decoder)
                 )
             )
         head_grads.append(mine)
@@ -607,7 +602,7 @@
     moved[-1][1], head_grads = lax.optimization_barrier((moved[-1][1], head_grads))
     a1_all = in_turn(a1)
     own_qkv = [mxu(a1_all, part, TN).astype(bf16) for part in head_grads]
-    qkv_part = over_scene(jnp.concatenate(own_qkv, axis=1))
+    qkv_sum = jnp.concatenate(own_qkv, axis=1)
     grad_fc2 = side_by_side(fc2_blocks)
 
     def pair_weights(p):
@@ -626,30 +621,45 @@
 
     grad_in = sum(pair_part(moved[p], pair_weights(p)) for p in range(pairs_dev - 1))
     last_weights = pair_weights(pairs_dev - 1)
-    moved[-1], grad_in, last_weights, grad_fc2, fc1_part, misc_part = lax.optimization_barrier(
-        (moved[-1], grad_in, last_weights, grad_fc2, fc1_part, misc_part)
-    )
-    wide_pieces = sum_pieces(fc1_part, misc_part)
+    feat, zdec, cot_f, grad_hidden = decoder
+    grad_w2 = jnp.einsum(
+        "phop->ho", exact(zdec, cot_f, TN).reshape(PP, dh, OUT, PP)
+    )
+    grad_b1 = jnp.sum(jnp.sum(grad_hidden, axis=0).reshape(PP, dh), axis=0)
+    grad_w1 = jnp.einsum(
+        "pfph->fh", exact(feat, grad_hidden, TN).reshape(PP, TF, PP, dh)
+    )
+    dec_flat = jnp.concatenate([grad_w1.reshape(-1), grad_b1, grad_w2.reshape(-1)])
+    dec_rows = jnp.pad(dec_flat, (0, -dec_flat.size % width)).reshape(-1, width)
+    used = dec_rows.shape[0]
+    dec_all = lax.all_gather(jnp.pad(dec_rows, ((0, 64 - used), (0, 0))), "scene")
+    wide_cut = [
+        jnp.concatenate([x, y], axis=1) for x, y in zip(cut(fc1_part), cut(misc_part))
+    ]
+    moved[-1], grad_in, last_weights, grad_fc2, wide_cut, dec_rows = lax.optimization_barrier(
+        (moved[-1], grad_in, last_weights, grad_fc2, wide_cut, dec_rows)
+    )
     grad_in = grad_in + pair_part(moved[-1], last_weights)
     u_one, inv_one = normalize(inputs_f)
     back_one, gain_grad_one, shift_grad_one = norm_back(grad_in, u_one, inv_one, gain_one)
     grad_tokens = (grad_mid + back_one).astype(bf16)
 
-    sums = jnp.concatenate([jnp.stack([gain_grad_one, shift_grad_one]), dec_flat], axis=0)
-    sums, wide_pieces = lax.optimization_barrier((sums, wide_pieces))
-    wide_blocks = blocks_of(wide_pieces)
-    cut = w_fc1.shape[1] // seq_count
-    grad_fc1 = side_by_side([x[:, :cut] for x in wide_blocks])
-    grad_misc = side_by_side([x[:, cut:] for x in wide_blocks])
+    sums = jnp.stack([gain_grad_one, shift_grad_one])
+    sums, wide_cut, qkv_sum, dec_all = lax.optimization_barrier((sums, wide_cut, qkv_sum, dec_all))
+    wide_blocks = blocks_of(send(wide_cut))
+    edge = w_fc1.shape[1] // seq_count
+    grad_fc1 = side_by_side([x[:, :edge] for x in wide_blocks])
+    grad_misc = side_by_side([x[:, edge:] for x in wide_blocks])
     grad_proj = grad_misc[:, :width]
     grad_unp = grad_misc[:, width : width + PP * TF]
     norm_two = grad_misc[:, width + PP * TF : width + PP * TF + 2]
+    qkv_part = over_scene(qkv_sum)
     qkv_all = side_by_side([turn(qkv_part, d) if d else qkv_part for d in range(seq_count)])
     grad_qkv = qkv_all.reshape(shard, pairs, 3, lanes).transpose(0, 2, 1, 3).reshape(shard, 3 * width)
 
     sums = lax.psum(sums, "scene")
-    norm_one = lax.psum(lax.dynamic_slice_in_dim(sums[:2], scene_rank * shard, shard, 1), "seq").T
-    dec_flat = sums[2:].reshape(-1)
+    norm_one = lax.psum(lax.dynamic_slice_in_dim(sums, scene_rank * shard, shard, 1), "seq").T
+    dec_flat = jnp.sum(dec_all[:, :used], axis=0).reshape(-1)
     ends = (w_dec1.size, w_dec1.size + dh, w_dec1.size + dh + w_dec2.size)
     dec_grads = (
         dec_flat[: ends[0]].reshape(w_dec1.shape),

time: 699 us -> 691 us (0.989)
  waiting for transfers between devices: 67.2 us -> 77 us
  matrix products: 132 us -> 123 us
  blocking collectives: 32.5 us -> 25.2 us
    psum x1, blocking collectives: 23.3 us -> 14.3 us  [per_device(): sums = lax.psum(sums, 'scene')]
    ppermute x27, waiting for transfers between devices: 34.4 us -> 43.3 us  [turn(): lax.ppermute(x, 'seq', [(i, (i + step) % seq_count) for i in range(seq_co...]
    unnamed x176 -> x180, local copies, waits for them, and re-layouts: 23.8 us -> 23.3 us
  transfers between devices with their start and end apart: 41 -> 42, of which waited for: 11 -> 13; matrix products, arithmetic and copies ran while one was open for 29% -> 28% of each run, Pallas kernels for 34% -> 35%
where the time goes in v6:
time: 691 us; the launch traced here: 679 us
  Pallas kernels  235 us (34%)
  matrix products  123 us (18%)
  starting transfers between devices  88 us (13%)
  waiting for transfers between devices  77 us (11%)
  local copies, waits for them, and re-layouts  64.3 us (9%)
  other arithmetic  49.5 us (7%)
  blocking collectives  25.2 us (4%)
  between operations  16.9 us (2%)
    pallas_call x2, Pallas kernels, attn_bwd(): pl.pallas_call(functools.partial(attn_bwd_kernel, tk=tk, tq=tk, scale=hea...  144 us
    dot_general x20, matrix products, mxu(): lax.dot_general(left, right, dims, preferred_element_type=jnp.float32)  119 us
    pallas_call x4, Pallas kernels, attn_fwd(): pl.pallas_call(functools.partial(attn_fwd_kernel, first=first, last=last,...  69.5 us
    ppermute x27, starting transfers between devices, turn(): lax.ppermute(x, 'seq', [(i, (i + step) % seq_count) for i in range(seq_co...  64.6 us
    ppermute x27, waiting for transfers between devices, turn(): lax.ppermute(x, 'seq', [(i, (i + step) % seq_count) for i in range(seq_co...  43.3 us
    ppermute x6, waiting for transfers between devices, hop(): lax.ppermute(x, 'seq', [(i, i + step) for i in range(seq_count) if 0 <= i...  31.9 us
    unnamed x180, local copies, waits for them, and re-layouts  23.3 us
    ppermute x6, starting transfers between devices, hop(): lax.ppermute(x, 'seq', [(i, i + step) for i in range(seq_count) if 0 <= i...  22.7 us
  transfers between devices with their start and end apart: 42, of which 13 were waited for; matrix products, arithmetic and copies ran while one was open for 28% of the time, Pallas kernels for 35%

profile of v6, /device:TPU:0, one launch (start us, length us, event | category | flops | bytes accessed | tf_op | source)
XLA Modules:
  0.0 679.0 jit_solution(15648536357683339348)
XLA Ops:
  11.2 2.8 convert_element_type.276
  17.0 6.8 collective-permute-start.1
  34.2 21.7 %collective-permute-done = bf16[784,1024]{1,0:T(8,128)(2,1)S(1)} collective-permute-done((bf16[784,1024]{1,0:T(8,128)(2,1)}, bf16[784,1024]{1,0:T(8,128)(2,1)S(1)}, u32[]{:S(2)}, u32[]{:S(2)}) %collective-permute-start) | collective-permute-done | bytes 1605664 | tf_op jit(solution)/shard_map/ppermute | solution.py:371
  60.2 6.2 collective-permute-start.2
  70.3 10.3 %convolution_convert_fusion.5.refs_0_.refs_1_.refs_2_ = bf16[768,3072]{1,0:T(8,128)(2,1)} fusion(bf16[768,1024]{1,0:T(8,128)(2,1)S(1)} %get-tuple-element.165, bf16[1024,3328]{0,1:T(8,128)(2,1)} %all-gather.7.cloned.1.call-done), kind=kOutput, calls=%fused_computation.8 | convolution fusion | flops 4834197504 | bytes 12582912 | tf_op jit(solution)/shard_map/dot_general | solution.py:28
  81.4 16.1 %attn_fwd.4 = (f32[8,2,80,768]{3,2,1,0:T(8,128)}, f32[8,2,768]{2,1,0:T(2,128)}) custom-call(bf16[768,3072]{1,0:T(8,128)(2,1)} %convolution_convert_fusion.5.refs_0_.refs_1_.refs_2_, bf16[768,3072]{1,0:T(8,128)(2,1)} %convolution_convert_fusion.5.refs_0_.refs_1_.refs_2_, bf16[768,3072]{1,0:T(8,128)(2,1)} %convolution_convert_fusion.5.refs_0_.refs_1_.refs_2_, ...), custom_call_target="tpu_custom_call" | custom-call | flops 9663676416 | bytes 6291456 | tf_op jit(solution)/shard_map/attn_fwd/pallas_call | solution.py:155
  99.0 5.5 collective-permute-start.4
  106.1 9.5 %convolution_convert_fusion.4.refs_1_.refs_2_ = bf16[768,3072]{1,0:T(8,128)(2,1)} fusion(bf16[768,1024]{1,0:T(8,128)(2,1)S(1)} %copy-done.10, bf16[1024,3328]{0,1:T(8,128)(2,1)} %all-gather.7.cloned.1.call-done), kind=kOutput, calls=%fused_computation.7 | convolution fusion | flops 4834197504 | bytes 12582912 | tf_op jit(solution)/shard_map/dot_general | solution.py:28
  115.6 17.5 %attn_fwd.5 = (f32[8,2,80,768]{3,2,1,0:T(8,128)}, f32[8,2,768]{2,1,0:T(2,128)}) custom-call(bf16[768,3072]{1,0:T(8,128)(2,1)} %convolution_convert_fusion.5.refs_0_.refs_1_.refs_2_, bf16[768,3072]{1,0:T(8,128)(2,1)} %convolution_convert_fusion.4.refs_1_.refs_2_, bf16[768,3072]{1,0:T(8,128)(2,1)} %convolution_convert_fusion.4.refs_1_.refs_2_, ...), custom_call_target="tpu_custom_call" | custom-call | flops 9663676416 | bytes 6291456 | tf_op jit(solution)/shard_map/attn_fwd/pallas_call | solution.py:155
  133.1 3.2 collective-permute-done.4
  136.3 5.3 collective-permute-done.5
  141.6 2.9 select_select_fusion
  155.2 6.7 convolution_convert_fusion.2.refs_1_.refs_2_
  161.9 17.7 %attn_fwd.6 = (f32[8,2,80,768]{3,2,1,0:T(8,128)}, f32[8,2,768]{2,1,0:T(2,128)}) custom-call(bf16[768,3072]{1,0:T(8,128)(2,1)} %convolution_convert_fusion.5.refs_0_.refs_1_.refs_2_, bf16[768,3072]{1,0:T(8,128)(2,1)} %convolution_convert_fusion.2.refs_1_.refs_2_, bf16[768,3072]{1,0:T(8,128)(2,1)} %convolution_convert_fusion.2.refs_1_.refs_2_, ...), custom_call_target="tpu_custom_call" | custom-call | flops 9663676416 | bytes 6291456 | tf_op jit(solution)/shard_map/attn_fwd/pallas_call | solution.py:155
  179.6 9.5 %convolution_convert_fusion.3.refs_1_.refs_2_ = bf16[768,3072]{1,0:T(8,128)(2,1)} fusion(bf16[768,1024]{1,0:T(8,128)(2,1)S(1)} %copy-done.14, bf16[1024,3328]{0,1:T(8,128)(2,1)} %all-gather.7.cloned.1.call-done), kind=kOutput, calls=%fused_computation.6 | convolution fusion | flops 4834197504 | bytes 12582912 | tf_op jit(solution)/shard_map/dot_general | solution.py:28
  189.1 18.1 %attn_fwd.7 = (bf16[768,1024]{1,0:T(8,128)(2,1)}, f32[8,2,768]{2,1,0:T(2,128)}) custom-call(bf16[768,3072]{1,0:T(8,128)(2,1)} %convolution_convert_fusion.5.refs_0_.refs_1_.refs_2_, bf16[768,3072]{1,0:T(8,128)(2,1)} %convolution_convert_fusion.3.refs_1_.refs_2_, bf16[768,3072]{1,0:T(8,128)(2,1)} %convolution_convert_fusion.3.refs_1_.refs_2_, ...), custom_call_target="tpu_custom_call" | custom-call | flops 9663676416 | bytes 6291456 | tf_op jit(solution)/shard_map/attn_fwd/pallas_call | solution.py:155
  207.2 3.9 fusion.115
  214.6 21.3 %fc1_gelu.1 = (bf16[768,4096]{1,0:T(8,128)(2,1)}, bf16[768,4096]{1,0:T(8,128)(2,1)}) custom-call(bf16[768,1024]{1,0:T(8,128)(2,1)} %add_convert_fusion.x_ref, bf16[1024,4096]{1,0:T(8,128)(2,1)} %all-gather.11.cloned.1.call-done.w_ref), custom_call_target="tpu_custom_call" | custom-call | flops 6442450944 | bytes 22544384 | tf_op jit(solution)/shard_map/fc1_gelu/pallas_call | solution.py:306
  235.9 5.8 fusion.79
  249.4 6.1 fusion.53
  261.6 9.4 %convolution_convert_fusion.1 = bf16[4096,1024]{1,0:T(8,128)(2,1)} fusion(bf16[768,4096]{1,0:T(8,128)(2,1)S(1)} %copy-done.77, f32[192,1024]{1,0:T(8,128)S(1)} %convolution_add_fusion, f32[576,1024]{1,0:T(8,128)S(1)} %copy-done.7), kind=kOutput, calls=%fused_computation.2 | convolution fusion | flops 6449790976 | bytes 17825792 | tf_op jit(solution)/shard_map/dot_general | solution.py:28
  275.5 13.3 %multiply_convert_fusion = bf16[768,4096]{1,0:T(8,128)(2,1)S(1)} fusion(bf16[768,4096]{1,0:T(8,128)(2,1)} %get-tuple-element.114, bf16[4096,1024]{1,0:T(8,128)(2,1)} %all-gather.13.cloned.1.call-done, f32[192,1024]{1,0:T(8,128)} %copy-done.18, f32[576,1024]{1,0:T(8,128)} %slice.173), kind=kOutput, calls=%fused_computation | convolution fusion | flops 6455033856 | bytes 24117248 | tf_op jit(solution)/shard_map/dot_general | solution.py:28
  288.8 13.1 %multiply_reduce_fusion = (bf16[1024]{0:T(1024)(128)(2,1)}, f32[768]{0:T(1024)S(1)}, f32[768]{0:T(1024)S(1)}, bf16[1024]{0:T(1024)(128)(2,1)}, f32[768,1024]{1,0:T(8,128)S(1)}) fusion(f32[768,1024]{1,0:T(8,128)S(1)} %copy-done.3, f32[768]{0:T(1024)S(1)} %add_rsqrt_fusion, f32[768]{0:T(1024)S(1)} %broadcast_multiply_fusion.4, f32[1024]{0:T(1024)S(1)} %bitcast.92, ...), kind=kOutput, calls=%fused_computation.68 | convolution fusion | flops 6449524736 | bytes 20992000 | tf_op jit(solution)/shard_map/dot_general | solution.py:28
  312.7 2.7 broadcast_in_dim.103
  328.2 9.2 %convolution_convert_fusion = bf16[1024,4096]{1,0:T(8,128)(2,1)} fusion(bf16[768,1024]{1,0:T(8,128)(2,1)S(1)} %copy-done.32, bf16[768,4096]{1,0:T(8,128)(2,1)S(1)} %bitcast.101), kind=kOutput, calls=%fused_computation.1 | convolution fusion | flops 6446645248 | bytes 16252928 | tf_op jit(solution)/shard_map/dot_general | solution.py:28
  341.4 2.8 slice-done.4
  350.3 5.6 collective-permute-start.12
  358.6 72.0 %attn_bwd.2 = bf16[3072,384]{1,0:T(8,128)(2,1)} custom-call(bf16[3072,768]{1,0:T(8,128)(2,1)} %dynamic-slice_dynamic-update-slice_fusion.refs_0_.refs_1_.refs_2_, bf16[3072,768]{1,0:T(8,128)(2,1)} %dynamic-slice_dynamic-update-slice_fusion.refs_0_.refs_1_.refs_2_, bf16[3072,768]{1,0:T(8,128)(2,1)} %dynamic-slice_dynamic-update-slice_fusion.refs_0_.refs_1_.refs_2_, ...), custom_call_target="tpu_custom_call" | custom-call | flops 48318382080 | bytes 5505024 | tf_op jit(solution)/shard_map/attn_bwd/pallas_call | solution.py:262
  434.6 2.8 fusion.113
  443.3 72.1 %attn_bwd.3 = bf16[3072,384]{1,0:T(8,128)(2,1)} custom-call(bf16[3072,768]{1,0:T(8,128)(2,1)} %dynamic-slice_dynamic-update-slice_fusion.refs_0_.refs_1_.refs_2_, bf16[3072,768]{1,0:T(8,128)(2,1)} %dynamic-slice_dynamic-update-slice_fusion.refs_0_.refs_1_.refs_2_, bf16[3072,768]{1,0:T(8,128)(2,1)} %dynamic-slice_dynamic-update-slice_fusion.refs_0_.refs_1_.refs_2_, ...), custom_call_target="tpu_custom_call" | custom-call | flops 48318382080 | bytes 5505024 | tf_op jit(solution)/shard_map/attn_bwd/pallas_call | solution.py:262
  516.1 3.1 fusion.112
  519.1 6.8 %collective-permute-start.21 = (bf16[768,384]{1,0:T(8,128)(2,1)}, bf16[768,384]{1,0:T(8,128)(2,1)}, u32[]{:S(2)}, u32[]{:S(2)}) collective-permute-start(bf16[768,384]{1,0:T(8,128)(2,1)} %get-tuple-element.280), channel_id=1, source_target_pairs={{0,1},{1,2},{2,3},{3,0},{4,5},{5,6},{6,7},{7,4},{8,9},{9,10},{10,1... | collective-permute-start | bytes 1769480 | tf_op jit(solution)/shard_map/ppermute | solution.py:376
  527.8 4.1 collective-permute-start.22
  539.6 4.2 fusion.39
  546.4 11.7 %collective-permute-done.22 = bf16[768,384]{1,0:T(8,128)(2,1)} collective-permute-done((bf16[768,384]{1,0:T(8,128)(2,1)}, bf16[768,384]{1,0:T(8,128)(2,1)}, u32[]{:S(2)}, u32[]{:S(2)}) %collective-permute-start.22) | collective-permute-done | bytes 589856 | tf_op jit(solution)/shard_map/ppermute | solution.py:376
  558.1 4.2 fusion.61
  562.3 3.2 fusion.24
  565.5 2.7 convolution_convert_fusion.9
  571.1 13.1 %collective-permute-start.24 = (bf16[128,1408]{1,0:T(8,128)(2,1)}, bf16[128,1408]{1,0:T(8,128)(2,1)}, u32[]{:S(2)}, u32[]{:S(2)}) collective-permute-start(bf16[128,1408]{1,0:T(8,128)(2,1)} %pad_maximum_fusion.5), channel_id=1, source_target_pairs={{0,1},{1,2},{2,3},{3,0},{4,5},{5,6},{6,7},{7,4},{8,9},{9,10},{10,1... | collective-permute-start | bytes 1081352 | tf_op jit(solution)/shard_map/ppermute | solution.py:376
  587.0 4.3 fusion.23
  596.2 14.3 %psum.14 = f32[2,1024]{1,0:T(2,128)S(1)} all-reduce(f32[2,1024]{1,0:T(2,128)S(1)} %pad_maximum_fusion.8), channel_id=1, replica_groups=mesh['scene'=8,'seq'=4] {'scene'}, use_global_device_ids=true, to_apply=%region_25.26 | all-reduce | flops 2048 | bytes 16384 | tf_op jit(solution)/shard_map/psum | solution.py:660
  610.4 10.9 %psum.15 = f32[128,2]{0,1:T(2,128)} all-reduce(f32[128,2]{0,1:T(2,128)S(1)} %fusion.100), channel_id=1, replica_groups=mesh['scene'=8,'seq'=4] {'seq'}, use_global_device_ids=true, to_apply=%region_26.27 | all-reduce | flops 256 | bytes 2048 | tf_op jit(solution)/shard_map/psum | solution.py:661
  623.5 3.2 collective-permute-start.29
  627.0 8.9 %collective-permute-done.27 = bf16[128,1408]{1,0:T(8,128)(2,1)S(1)} collective-permute-done((bf16[128,1408]{1,0:T(8,128)(2,1)S(1)}, bf16[128,1408]{1,0:T(8,128)(2,1)S(1)}, u32[]{:S(2)}, u32[]{:S(2)}) %collective-permute-start.27) | collective-permute-done | bytes 360480 | tf_op jit(solution)/shard_map/ppermute | solution.py:376
  636.0 11.0 %collective-permute-done.28 = bf16[128,1408]{1,0:T(8,128)(2,1)S(1)} collective-permute-done((bf16[128,1408]{1,0:T(8,128)(2,1)S(1)}, bf16[128,1408]{1,0:T(8,128)(2,1)S(1)}, u32[]{:S(2)}, u32[]{:S(2)}) %collective-permute-start.28) | collective-permute-done | bytes 360480 | tf_op jit(solution)/shard_map/ppermute | solution.py:376
  650.8 7.4 %collective-permute-start.30 = (bf16[128,768]{0,1:T(8,128)(2,1)S(1)}, bf16[128,768]{0,1:T(8,128)(2,1)S(1)}, u32[]{:S(2)}, u32[]{:S(2)}) collective-permute-start(bf16[128,768]{0,1:T(8,128)(2,1)S(1)} %copy.120), channel_id=1, source_target_pairs={{0,1},{1,2},{2,3},{3,0},{4,5},{5,6},{6,7},{7,4},{8,9},{9,10},{10,1... | collective-permute-start | bytes 589832 | tf_op jit(solution)/shard_map/ppermute | solution.py:376
  660.7 2.7 collective-permute-done.30
  663.5 6.6 collective-permute-done.31
  (427 shorter events, 139.7 us)
Async XLA Ops:
  7.2 60.1 %all-gather.7.cloned.1.call-start = ((), (), s32[]{:S(2)}) async-start(), calls=%async_computation.4 | async-start | bytes 7667712 | tf_op jit(solution)/shard_map/all_gather | solution.py:413
  10.3 196.9 %all-gather.9.cloned.1.call-start = ((), (), s32[]{:S(2)}) async-start(), calls=%async_computation.5 | async-start | bytes 2359296 | tf_op jit(solution)/shard_map/all_gather | solution.py:410
  11.1 203.5 %all-gather.11.cloned.1.call-start = ((), (), s32[]{:S(2)}) async-start(), calls=%async_computation.6 | async-start | bytes 9437184 | tf_op jit(solution)/shard_map/all_gather | solution.py:410
  14.0 221.9 %all-gather.13.cloned.1.call-start = ((), (), s32[]{:S(2)}) async-start(), calls=%async_computation.7 | async-start | bytes 9437184 | tf_op jit(solution)/shard_map/all_gather | solution.py:410
  15.6 40.4 %collective-permute-start = (bf16[784,1024]{1,0:T(8,128)(2,1)}, bf16[784,1024]{1,0:T(8,128)(2,1)S(1)}, u32[]{:S(2)}, u32[]{:S(2)}) collective-permute-start(bf16[784,1024]{1,0:T(8,128)(2,1)} %fusion.71), channel_id=1, source_target_pairs={{1,0},{2,1},{3,2},{5,4},{6,5},{7,6},{9,8},{10,9},{11,10},{13,12},{... | collective-permute-start | bytes 4816904 | tf_op jit(solution)/shard_map/ppermute | solution.py:371
  17.0 40.2 %collective-permute-start.1 = (bf16[784,1024]{1,0:T(8,128)(2,1)}, bf16[784,1024]{1,0:T(8,128)(2,1)}, u32[]{:S(2)}, u32[]{:S(2)}) collective-permute-start(bf16[784,1024]{1,0:T(8,128)(2,1)} %fusion.71), channel_id=1, source_target_pairs={{0,1},{1,2},{2,3},{4,5},{5,6},{6,7},{8,9},{9,10},{10,11},{12,13},{... | collective-permute-start | bytes 4816904 | tf_op jit(solution)/shard_map/ppermute | solution.py:371
  25.0 315.3 %reduce-scatter.7.cloned.1.call-start = ((), (), s32[]{:S(2)}) async-start(), calls=%async_computation.8 | async-start | bytes 9437184 | tf_op jit(solution)/shard_map/reduce_scatter | solution.py:552
  33.6 34.4 %copy-start.58 = (f32[768]{0:T(1024)}, f32[768]{0:T(1024)S(1)}, u32[]{:S(2)}) copy-start(f32[768]{0:T(1024)S(1)} %broadcast_multiply_fusion.8) | copy-start | bytes 9220
  34.2 46.3 %copy-start.62 = (f32[768]{0:T(1024)}, f32[768]{0:T(1024)S(1)}, u32[]{:S(2)}) copy-start(f32[768]{0:T(1024)S(1)} %add_rsqrt_fusion.4) | copy-start | bytes 9220
  58.9 38.9 %collective-permute-start.3 = (bf16[784,1024]{1,0:T(8,128)(2,1)}, bf16[784,1024]{1,0:T(8,128)(2,1)}, u32[]{:S(2)}, u32[]{:S(2)}) collective-permute-start(bf16[784,1024]{1,0:T(8,128)(2,1)} %copy-done.9), channel_id=1, source_target_pairs={{1,0},{2,1},{3,2},{5,4},{6,5},{7,6},{9,8},{10,9},{11,10},{13,12},{... | collective-permute-start | bytes 4816904 | tf_op jit(solution)/shard_map/ppermute | solution.py:371
  60.2 38.8 %collective-permute-start.2 = (bf16[784,1024]{1,0:T(8,128)(2,1)}, bf16[784,1024]{1,0:T(8,128)(2,1)}, u32[]{:S(2)}, u32[]{:S(2)}) collective-permute-start(bf16[784,1024]{1,0:T(8,128)(2,1)} %collective-permute-done.1), channel_id=1, source_target_pairs={{0,1},{1,2},{2,3},{4,5},{5,6},{6,7},{8,9},{9,10},{10,11},{12,13},{... | collective-permute-start | bytes 4816904 | tf_op jit(solution)/shard_map/ppermute | solution.py:371
  68.1 83.3 %copy-start.60 = (f32[1024,1]{0,1:T(1,128)}, f32[1024,1]{0,1:T(1,128)S(1)}, u32[]{:S(2)}) copy-start(f32[1024,1]{0,1:T(1,128)S(1)} %get-tuple-element.308) | copy-start | bytes 12292
  81.4 24.7 %copy-start.10 = (bf16[768,1024]{1,0:T(8,128)(2,1)S(1)}, bf16[768,1024]{1,0:T(8,128)(2,1)}, u32[]{:S(2)}) copy-start(bf16[768,1024]{1,0:T(8,128)(2,1)} %get-tuple-element.166) | copy-start | bytes 4718596
  99.0 37.3 %collective-permute-start.4 = (bf16[784,1024]{1,0:T(8,128)(2,1)}, bf16[784,1024]{1,0:T(8,128)(2,1)}, u32[]{:S(2)}, u32[]{:S(2)}) collective-permute-start(bf16[784,1024]{1,0:T(8,128)(2,1)} %collective-permute-done.2), channel_id=1, source_target_pairs={{0,1},{1,2},{2,3},{4,5},{5,6},{6,7},{8,9},{9,10},{10,11},{12,13},{... | collective-permute-start | bytes 4816904 | tf_op jit(solution)/shard_map/ppermute | solution.py:371
  104.6 37.0 %collective-permute-start.5 = (bf16[784,1024]{1,0:T(8,128)(2,1)}, bf16[784,1024]{1,0:T(8,128)(2,1)}, u32[]{:S(2)}, u32[]{:S(2)}) collective-permute-start(bf16[784,1024]{1,0:T(8,128)(2,1)} %collective-permute-done.3), channel_id=1, source_target_pairs={{1,0},{2,1},{3,2},{5,4},{6,5},{7,6},{9,8},{10,9},{11,10},{13,12},{... | collective-permute-start | bytes 4816904 | tf_op jit(solution)/shard_map/ppermute | solution.py:371
  214.6 21.3 %copy-start.3 = (f32[768,1024]{1,0:T(8,128)S(1)}, f32[768,1024]{1,0:T(8,128)}, u32[]{:S(2)}) copy-start(f32[768,1024]{1,0:T(8,128)} %copy-done.2) | copy-start | bytes 9437188
  235.9 23.1 %slice-start.2 = ((s8[6815744]{0:T(1024)(128)(4,1)}), s8[4194304]{0:T(1024)(128)(4,1)S(1)}, s32[]{:S(2)}) async-start(s8[6815744]{0:T(1024)(128)(4,1)} %bitcast.79), calls=%async_computation.15 | async-start | bytes 8388608
  243.8 11.6 %collective-permute-start.6 = (bf16[192,128]{1,0:T(8,128)(2,1)S(1)}, bf16[192,128]{1,0:T(8,128)(2,1)S(1)}, u32[]{:S(2)}, u32[]{:S(2)}) collective-permute-start(bf16[192,128]{1,0:T(8,128)(2,1)S(1)} %get-tuple-element.316), channel_id=1, source_target_pairs={{0,1},{1,2},{2,3},{3,0},{4,5},{5,6},{6,7},{7,4},{8,9},{9,10},{10,1... | collective-permute-start | bytes 147464 | tf_op jit(solution)/shard_map/ppermute | solution.py:376
  245.3 10.2 %collective-permute-start.7 = (bf16[192,128]{1,0:T(8,128)(2,1)S(1)}, bf16[192,128]{1,0:T(8,128)(2,1)S(1)}, u32[]{:S(2)}, u32[]{:S(2)}) collective-permute-start(bf16[192,128]{1,0:T(8,128)(2,1)S(1)} %get-tuple-element.316), channel_id=1, source_target_pairs={{0,2},{1,3},{2,0},{3,1},{4,6},{5,7},{6,4},{7,5},{8,10},{9,11},{10,... | collective-permute-start | bytes 147464 | tf_op jit(solution)/shard_map/ppermute | solution.py:376
  247.2 8.3 %collective-permute-start.8 = (bf16[192,128]{1,0:T(8,128)(2,1)S(1)}, bf16[192,128]{1,0:T(8,128)(2,1)S(1)}, u32[]{:S(2)}, u32[]{:S(2)}) collective-permute-start(bf16[192,128]{1,0:T(8,128)(2,1)S(1)} %get-tuple-element.316), channel_id=1, source_target_pairs={{0,3},{1,0},{2,1},{3,2},{4,7},{5,4},{6,5},{7,6},{8,11},{9,8},{10,9... | collective-permute-start | bytes 147464 | tf_op jit(solution)/shard_map/ppermute | solution.py:376
  271.0 245.0 %reduce-scatter.11.cloned.1.call-start = ((), (), s32[]{:S(2)}) async-start(), calls=%async_computation.10 | async-start | bytes 3538944 | tf_op jit(solution)/shard_map/reduce_scatter | solution.py:552
  310.3 29.1 %collective-permute-start.10 = (bf16[848,256]{1,0:T(8,128)(2,1)}, bf16[848,256]{1,0:T(8,128)(2,1)}, u32[]{:S(2)}, u32[]{:S(2)}) collective-permute-start(bf16[848,256]{1,0:T(8,128)(2,1)} %get-tuple-element.287), channel_id=1, source_target_pairs={{0,2},{1,3},{2,0},{3,1},{4,6},{5,7},{6,4},{7,5},{8,10},{9,11},{10,... | collective-permute-start | bytes 1302536 | tf_op jit(solution)/shard_map/ppermute | solution.py:376
  310.3 29.1 %collective-permute-start.11 = (bf16[848,256]{1,0:T(8,128)(2,1)}, bf16[848,256]{1,0:T(8,128)(2,1)}, u32[]{:S(2)}, u32[]{:S(2)}) collective-permute-start(bf16[848,256]{1,0:T(8,128)(2,1)} %get-tuple-element.286), channel_id=1, source_target_pairs={{0,3},{1,0},{2,1},{3,2},{4,7},{5,4},{6,5},{7,6},{8,11},{9,8},{10,9... | collective-permute-start | bytes 1302536 | tf_op jit(solution)/shard_map/ppermute | solution.py:376
  311.9 27.6 %collective-permute-start.9 = (bf16[848,256]{1,0:T(8,128)(2,1)S(1)}, bf16[848,256]{1,0:T(8,128)(2,1)}, u32[]{:S(2)}, u32[]{:S(2)}) collective-permute-start(bf16[848,256]{1,0:T(8,128)(2,1)S(1)} %get-tuple-element.288), channel_id=1, source_target_pairs={{0,1},{1,2},{2,3},{3,0},{4,5},{5,6},{6,7},{7,4},{8,9},{9,10},{10,1... | collective-permute-start | bytes 1302536 | tf_op jit(solution)/shard_map/ppermute | solution.py:376
  340.3 175.8 %reduce-scatter.9.cloned.1.call-start = ((), (), s32[]{:S(2)}) async-start(), calls=%async_computation.9 | async-start | bytes 9437184 | tf_op jit(solution)/shard_map/reduce_scatter | solution.py:552
  341.1 230.0 %all-gather.15.cloned.1.call-start = ((), (), s32[]{:S(2)}) async-start(), calls=%async_computation.11 | async-start | bytes 2359296 | tf_op jit(solution)/shard_map/all_gather | solution.py:635
  350.3 80.2 %collective-permute-start.12 = (bf16[512,256]{1,0:T(8,128)(2,1)S(1)}, bf16[512,256]{1,0:T(8,128)(2,1)S(1)}, u32[]{:S(2)}, u32[]{:S(2)}) collective-permute-start(bf16[512,256]{1,0:T(8,128)(2,1)S(1)} %get-tuple-element.296), channel_id=1, source_target_pairs={{0,1},{1,2},{2,3},{3,0},{4,5},{5,6},{6,7},{7,4},{8,9},{9,10},{10,1... | collective-permute-start | bytes 786440 | tf_op jit(solution)/shard_map/ppermute | solution.py:376
  355.9 74.6 %collective-permute-start.13 = (bf16[512,256]{1,0:T(8,128)(2,1)S(1)}, bf16[512,256]{1,0:T(8,128)(2,1)S(1)}, u32[]{:S(2)}, u32[]{:S(2)}) collective-permute-start(bf16[512,256]{1,0:T(8,128)(2,1)S(1)} %get-tuple-element.295), channel_id=1, source_target_pairs={{0,2},{1,3},{2,0},{3,1},{4,6},{5,7},{6,4},{7,5},{8,10},{9,11},{10,... | collective-permute-start | bytes 786440 | tf_op jit(solution)/shard_map/ppermute | solution.py:376
  355.9 74.6 %collective-permute-start.14 = (bf16[512,256]{1,0:T(8,128)(2,1)S(1)}, bf16[512,256]{1,0:T(8,128)(2,1)S(1)}, u32[]{:S(2)}, u32[]{:S(2)}) collective-permute-start(bf16[512,256]{1,0:T(8,128)(2,1)S(1)} %get-tuple-element.294), channel_id=1, source_target_pairs={{0,3},{1,0},{2,1},{3,2},{4,7},{5,4},{6,5},{7,6},{8,11},{9,8},{10,9... | collective-permute-start | bytes 786440 | tf_op jit(solution)/shard_map/ppermute | solution.py:376
  430.7 11.0 %collective-permute-start.18 = (bf16[512,256]{1,0:T(8,128)(2,1)S(1)}, bf16[512,256]{1,0:T(8,128)(2,1)S(1)}, u32[]{:S(2)}, u32[]{:S(2)}) collective-permute-start(bf16[512,256]{1,0:T(8,128)(2,1)S(1)} %add_convert_fusion.2), channel_id=1, source_target_pairs={{0,1},{1,2},{2,3},{3,0},{4,5},{5,6},{6,7},{7,4},{8,9},{9,10},{10,1... | collective-permute-start | bytes 786440 | tf_op jit(solution)/shard_map/ppermute | solution.py:376
  430.8 84.6 %collective-permute-start.19 = (bf16[512,256]{1,0:T(8,128)(2,1)S(1)}, bf16[512,256]{1,0:T(8,128)(2,1)S(1)}, u32[]{:S(2)}, u32[]{:S(2)}) collective-permute-start(bf16[512,256]{1,0:T(8,128)(2,1)S(1)} %add_convert_fusion.2), channel_id=1, source_target_pairs={{0,2},{1,3},{2,0},{3,1},{4,6},{5,7},{6,4},{7,5},{8,10},{9,11},{10,... | collective-permute-start | bytes 786440 | tf_op jit(solution)/shard_map/ppermute | solution.py:376
  433.3 82.1 %collective-permute-start.20 = (bf16[512,256]{1,0:T(8,128)(2,1)S(1)}, bf16[512,256]{1,0:T(8,128)(2,1)S(1)}, u32[]{:S(2)}, u32[]{:S(2)}) collective-permute-start(bf16[512,256]{1,0:T(8,128)(2,1)S(1)} %add_convert_fusion.2), channel_id=1, source_target_pairs={{0,3},{1,0},{2,1},{3,2},{4,7},{5,4},{6,5},{7,6},{8,11},{9,8},{10,9... | collective-permute-start | bytes 786440 | tf_op jit(solution)/shard_map/ppermute | solution.py:376
  437.5 78.0 %collective-permute-start.15 = (bf16[768,384]{1,0:T(8,128)(2,1)}, bf16[768,384]{1,0:T(8,128)(2,1)}, u32[]{:S(2)}, u32[]{:S(2)}) collective-permute-start(bf16[768,384]{1,0:T(8,128)(2,1)} %get-tuple-element.284), channel_id=1, source_target_pairs={{0,1},{1,2},{2,3},{3,0},{4,5},{5,6},{6,7},{7,4},{8,9},{9,10},{10,1... | collective-permute-start | bytes 1769480 | tf_op jit(solution)/shard_map/ppermute | solution.py:376
  438.1 77.3 %collective-permute-start.16 = (bf16[768,384]{1,0:T(8,128)(2,1)S(1)}, bf16[768,384]{1,0:T(8,128)(2,1)}, u32[]{:S(2)}, u32[]{:S(2)}) collective-permute-start(bf16[768,384]{1,0:T(8,128)(2,1)S(1)} %get-tuple-element.283), channel_id=1, source_target_pairs={{0,2},{1,3},{2,0},{3,1},{4,6},{5,7},{6,4},{7,5},{8,10},{9,11},{10,... | collective-permute-start | bytes 1769480 | tf_op jit(solution)/shard_map/ppermute | solution.py:376
  442.5 73.6 %collective-permute-start.17 = (bf16[768,384]{1,0:T(8,128)(2,1)S(1)}, bf16[768,384]{1,0:T(8,128)(2,1)}, u32[]{:S(2)}, u32[]{:S(2)}) collective-permute-start(bf16[768,384]{1,0:T(8,128)(2,1)S(1)} %get-tuple-element.282), channel_id=1, source_target_pairs={{0,3},{1,0},{2,1},{3,2},{4,7},{5,4},{6,5},{7,6},{8,11},{9,8},{10,9... | collective-permute-start | bytes 1769480 | tf_op jit(solution)/shard_map/ppermute | solution.py:376
  519.1 27.2 %collective-permute-start.21 = (bf16[768,384]{1,0:T(8,128)(2,1)}, bf16[768,384]{1,0:T(8,128)(2,1)}, u32[]{:S(2)}, u32[]{:S(2)}) collective-permute-start(bf16[768,384]{1,0:T(8,128)(2,1)} %get-tuple-element.280), channel_id=1, source_target_pairs={{0,1},{1,2},{2,3},{3,0},{4,5},{5,6},{6,7},{7,4},{8,9},{9,10},{10,1... | collective-permute-start | bytes 1769480 | tf_op jit(solution)/shard_map/ppermute | solution.py:376
  527.8 30.2 %collective-permute-start.22 = (bf16[768,384]{1,0:T(8,128)(2,1)}, bf16[768,384]{1,0:T(8,128)(2,1)}, u32[]{:S(2)}, u32[]{:S(2)}) collective-permute-start(bf16[768,384]{1,0:T(8,128)(2,1)} %get-tuple-element.279), channel_id=1, source_target_pairs={{0,2},{1,3},{2,0},{3,1},{4,6},{5,7},{6,4},{7,5},{8,10},{9,11},{10,... | collective-permute-start | bytes 1769480 | tf_op jit(solution)/shard_map/ppermute | solution.py:376
  532.0 26.1 %collective-permute-start.23 = (bf16[768,384]{1,0:T(8,128)(2,1)}, bf16[768,384]{1,0:T(8,128)(2,1)}, u32[]{:S(2)}, u32[]{:S(2)}) collective-permute-start(bf16[768,384]{1,0:T(8,128)(2,1)} %get-tuple-element.278), channel_id=1, source_target_pairs={{0,3},{1,0},{2,1},{3,2},{4,7},{5,4},{6,5},{7,6},{8,11},{9,8},{10,9... | collective-permute-start | bytes 1769480 | tf_op jit(solution)/shard_map/ppermute | solution.py:376
  533.9 115.5 %reduce-scatter.13.cloned.1.call-start = ((), (), s32[]{:S(2)}) async-start(), calls=%async_computation.12 | async-start | bytes 1769472
  571.1 50.3 %collective-permute-start.24 = (bf16[128,1408]{1,0:T(8,128)(2,1)}, bf16[128,1408]{1,0:T(8,128)(2,1)}, u32[]{:S(2)}, u32[]{:S(2)}) collective-permute-start(bf16[128,1408]{1,0:T(8,128)(2,1)} %pad_maximum_fusion.5), channel_id=1, source_target_pairs={{0,1},{1,2},{2,3},{3,0},{4,5},{5,6},{6,7},{7,4},{8,9},{9,10},{10,1... | collective-permute-start | bytes 1081352 | tf_op jit(solution)/shard_map/ppermute | solution.py:376
  584.3 37.1 %collective-permute-start.25 = (bf16[128,1408]{1,0:T(8,128)(2,1)}, bf16[128,1408]{1,0:T(8,128)(2,1)}, u32[]{:S(2)}, u32[]{:S(2)}) collective-permute-start(bf16[128,1408]{1,0:T(8,128)(2,1)} %pad_maximum_fusion.6), channel_id=1, source_target_pairs={{0,2},{1,3},{2,0},{3,1},{4,6},{5,7},{6,4},{7,5},{8,10},{9,11},{10,... | collective-permute-start | bytes 1081352 | tf_op jit(solution)/shard_map/ppermute | solution.py:376
  584.7 36.7 %collective-permute-start.26 = (bf16[128,1408]{1,0:T(8,128)(2,1)}, bf16[128,1408]{1,0:T(8,128)(2,1)}, u32[]{:S(2)}, u32[]{:S(2)}) collective-permute-start(bf16[128,1408]{1,0:T(8,128)(2,1)} %pad_maximum_fusion.7), channel_id=1, source_target_pairs={{0,3},{1,0},{2,1},{3,2},{4,7},{5,4},{6,5},{7,6},{8,11},{9,8},{10,9... | collective-permute-start | bytes 1081352 | tf_op jit(solution)/shard_map/ppermute | solution.py:376
  622.8 13.2 %collective-permute-start.27 = (bf16[128,1408]{1,0:T(8,128)(2,1)S(1)}, bf16[128,1408]{1,0:T(8,128)(2,1)S(1)}, u32[]{:S(2)}, u32[]{:S(2)}) collective-permute-start(bf16[128,1408]{1,0:T(8,128)(2,1)S(1)} %add_convert_fusion.1), channel_id=1, source_target_pairs={{0,1},{1,2},{2,3},{3,0},{4,5},{5,6},{6,7},{7,4},{8,9},{9,10},{10,1... | collective-permute-start | bytes 1081352 | tf_op jit(solution)/shard_map/ppermute | solution.py:376
  622.9 24.2 %collective-permute-start.28 = (bf16[128,1408]{1,0:T(8,128)(2,1)S(1)}, bf16[128,1408]{1,0:T(8,128)(2,1)S(1)}, u32[]{:S(2)}, u32[]{:S(2)}) collective-permute-start(bf16[128,1408]{1,0:T(8,128)(2,1)S(1)} %add_convert_fusion.1), channel_id=1, source_target_pairs={{0,2},{1,3},{2,0},{3,1},{4,6},{5,7},{6,4},{7,5},{8,10},{9,11},{10,... | collective-permute-start | bytes 1081352 | tf_op jit(solution)/shard_map/ppermute | solution.py:376
  623.5 23.6 %collective-permute-start.29 = (bf16[128,1408]{1,0:T(8,128)(2,1)S(1)}, bf16[128,1408]{1,0:T(8,128)(2,1)S(1)}, u32[]{:S(2)}, u32[]{:S(2)}) collective-permute-start(bf16[128,1408]{1,0:T(8,128)(2,1)S(1)} %add_convert_fusion.1), channel_id=1, source_target_pairs={{0,3},{1,0},{2,1},{3,2},{4,7},{5,4},{6,5},{7,6},{8,11},{9,8},{10,9... | collective-permute-start | bytes 1081352 | tf_op jit(solution)/shard_map/ppermute | solution.py:376
  650.8 12.7 %collective-permute-start.30 = (bf16[128,768]{0,1:T(8,128)(2,1)S(1)}, bf16[128,768]{0,1:T(8,128)(2,1)S(1)}, u32[]{:S(2)}, u32[]{:S(2)}) collective-permute-start(bf16[128,768]{0,1:T(8,128)(2,1)S(1)} %copy.120), channel_id=1, source_target_pairs={{0,1},{1,2},{2,3},{3,0},{4,5},{5,6},{6,7},{7,4},{8,9},{9,10},{10,1... | collective-permute-start | bytes 589832 | tf_op jit(solution)/shard_map/ppermute | solution.py:376
  658.1 11.9 %collective-permute-start.31 = (bf16[128,768]{0,1:T(8,128)(2,1)S(1)}, bf16[128,768]{0,1:T(8,128)(2,1)S(1)}, u32[]{:S(2)}, u32[]{:S(2)}) collective-permute-start(bf16[128,768]{0,1:T(8,128)(2,1)S(1)} %copy.120), channel_id=1, source_target_pairs={{0,2},{1,3},{2,0},{3,1},{4,6},{5,7},{6,4},{7,5},{8,10},{9,11},{10,... | collective-permute-start | bytes 589832 | tf_op jit(solution)/shard_map/ppermute | solution.py:376
  658.5 11.7 %collective-permute-start.32 = (bf16[128,768]{0,1:T(8,128)(2,1)S(1)}, bf16[128,768]{0,1:T(8,128)(2,1)S(1)}, u32[]{:S(2)}, u32[]{:S(2)}) collective-permute-start(bf16[128,768]{0,1:T(8,128)(2,1)S(1)} %copy.120), channel_id=1, source_target_pairs={{0,3},{1,0},{2,1},{3,2},{4,7},{5,4},{6,5},{7,6},{8,11},{9,8},{10,9... | collective-permute-start | bytes 589832 | tf_op jit(solution)/shard_map/ppermute | solution.py:376
  (80 other events, 443.6 us)
Sparse Core Ops, SparseCore 0:
  10.5 51.6 all-gather.6
  64.6 27.7 all-gather.8
  94.3 54.2 all-gather.10
  150.3 54.2 all-gather.12
  271.2 69.1 reduce-scatter.6
  343.5 46.0 reduce-scatter.10
  393.1 71.5 reduce-scatter.8
  534.0 24.3 all-gather.14
  594.4 38.2 reduce-scatter.12

commit v7 on v6

--- a/solution.py
+++ b/solution.py
@@ -476,7 +476,6 @@
         image_live[:, None], middle[:IMG_DEV] + mxu(act[:IMG_DEV], fc2_w, NN), 0.0
     ).astype(bf16)
     image_out, all_planes = lax.optimization_barrier((image_out, all_planes))
-    block_out = jnp.concatenate([image_out, triplane], axis=0)
 
     cot_rows = jnp.zeros((seq_count, width), bf16)
     for d in range(seq_count):
@@ -495,7 +494,6 @@
     zdec, zslope = gelu_parts(hidden_pre)
     decoded_all = exact(zdec, dec2, NN)
     cells_dev = cells // seq_count
-    decoded = lax.dynamic_slice_in_dim(decoded_all, rank * cells_dev, cells_dev, 0)
     cot_f = cot_cells.astype(f32)
     grad_hidden = exact(cot_f, dec2, NT) * zslope
     gfeat = exact(grad_hidden, dec1, NT).astype(bf16)
@@ -579,9 +577,8 @@
             out = lax.dynamic_update_slice_in_dim(out, got.astype(f32), behind(d) * size, 1)
         return out
 
-    def exchange(mine):
-        pieces = [piece(mine, (seq_count - d) % seq_count, tok_rows, 0) for d in range(seq_count)]
-        return [turn(x, d) if d else x for d, x in enumerate(pieces)]
+    def cut_rows(mine):
+        return [piece(mine, (seq_count - d) % seq_count, tok_rows, 0) for d in range(seq_count)]
 
     fc2_pieces = sum_pieces(fc2_part)
     moved, head_grads = [], []
@@ -591,25 +588,28 @@
             own_all, mine, fc2_pieces = lax.optimization_barrier((own_all, mine, fc2_pieces))
             fc2_blocks = blocks_of(fc2_pieces)
         else:
-            decoder = (feat, zdec, cot_f, grad_hidden)
+            decoder = (feat, zdec, cot_f, grad_hidden, qkv_w)
             mine, moved[-1], head_grads[-1], a1, fc2_blocks, fc1_part, misc_part, decoder = (
                 lax.optimization_barrier(
                     (mine, moved[-1], head_grads[-1], a1, fc2_blocks, fc1_part, misc_part, decoder)
                 )
             )
         head_grads.append(mine)
-        moved.append(exchange(mine))
-    moved[-1][1], head_grads = lax.optimization_barrier((moved[-1][1], head_grads))
+        moved.append(send(cut_rows(mine)))
+    moved[-1][1], head_grads, decoder = lax.optimization_barrier(
+        (moved[-1][1], head_grads, decoder)
+    )
     a1_all = in_turn(a1)
     own_qkv = [mxu(a1_all, part, TN).astype(bf16) for part in head_grads]
     qkv_sum = jnp.concatenate(own_qkv, axis=1)
     grad_fc2 = side_by_side(fc2_blocks)
 
+    feat, zdec, cot_f, grad_hidden, late_w = decoder
     def pair_weights(p):
         return jnp.concatenate(
             [
                 lax.dynamic_slice_in_dim(
-                    qkv_w, behind(d) * 3 * cols + p * 3 * lanes, 3 * lanes, 1
+                    late_w, behind(d) * 3 * cols + p * 3 * lanes, 3 * lanes, 1
                 )
                 for d in range(seq_count)
             ],
@@ -621,7 +621,6 @@
 
     grad_in = sum(pair_part(moved[p], pair_weights(p)) for p in range(pairs_dev - 1))
     last_weights = pair_weights(pairs_dev - 1)
-    feat, zdec, cot_f, grad_hidden = decoder
     grad_w2 = jnp.einsum(
         "phop->ho", exact(zdec, cot_f, TN).reshape(PP, dh, OUT, PP)
     )
@@ -632,32 +631,41 @@
     dec_flat = jnp.concatenate([grad_w1.reshape(-1), grad_b1, grad_w2.reshape(-1)])
     dec_rows = jnp.pad(dec_flat, (0, -dec_flat.size % width)).reshape(-1, width)
     used = dec_rows.shape[0]
-    dec_all = lax.all_gather(jnp.pad(dec_rows, ((0, 64 - used), (0, 0))), "scene")
     wide_cut = [
         jnp.concatenate([x, y], axis=1) for x, y in zip(cut(fc1_part), cut(misc_part))
     ]
-    moved[-1], grad_in, last_weights, grad_fc2, wide_cut, dec_rows = lax.optimization_barrier(
-        (moved[-1], grad_in, last_weights, grad_fc2, wide_cut, dec_rows)
-    )
+    qkv_part = over_scene(qkv_sum)
+    moved[-1], grad_in, last_weights, grad_fc2, wide_cut, qkv_sum, dec_rows = (
+        lax.optimization_barrier(
+            (moved[-1], grad_in, last_weights, grad_fc2, wide_cut, qkv_sum, dec_rows)
+        )
+    )
+    dec_all = lax.all_gather(jnp.pad(dec_rows, ((0, 64 - used), (0, 0))), "scene")
     grad_in = grad_in + pair_part(moved[-1], last_weights)
     u_one, inv_one = normalize(inputs_f)
     back_one, gain_grad_one, shift_grad_one = norm_back(grad_in, u_one, inv_one, gain_one)
     grad_tokens = (grad_mid + back_one).astype(bf16)
 
     sums = jnp.stack([gain_grad_one, shift_grad_one])
-    sums, wide_cut, qkv_sum, dec_all = lax.optimization_barrier((sums, wide_cut, qkv_sum, dec_all))
-    wide_blocks = blocks_of(send(wide_cut))
+    sums, wide_cut = lax.optimization_barrier((sums, wide_cut))
+    wide_pieces = send(wide_cut)
+    sums = lax.psum(sums, "scene")
+    sums, wide_pieces, qkv_part, image_out, triplane, decoded_all = lax.optimization_barrier(
+        (sums, wide_pieces, qkv_part, image_out, triplane, decoded_all)
+    )
+    block_out = jnp.concatenate([image_out, triplane], axis=0)
+    decoded = lax.dynamic_slice_in_dim(decoded_all, rank * cells_dev, cells_dev, 0)
+    qkv_blocks = send([qkv_part] * seq_count)
+    wide_blocks = blocks_of(wide_pieces)
     edge = w_fc1.shape[1] // seq_count
     grad_fc1 = side_by_side([x[:, :edge] for x in wide_blocks])
     grad_misc = side_by_side([x[:, edge:] for x in wide_blocks])
     grad_proj = grad_misc[:, :width]
     grad_unp = grad_misc[:, width : width + PP * TF]
     norm_two = grad_misc[:, width + PP * TF : width + PP * TF + 2]
-    qkv_part = over_scene(qkv_sum)
-    qkv_all = side_by_side([turn(qkv_part, d) if d else qkv_part for d in range(seq_count)])
+    qkv_all = side_by_side(qkv_blocks)
     grad_qkv = qkv_all.reshape(shard, pairs, 3, lanes).transpose(0, 2, 1, 3).reshape(shard, 3 * width)
 
-    sums = lax.psum(sums, "scene")
     norm_one = lax.psum(lax.dynamic_slice_in_dim(sums, scene_rank * shard, shard, 1), "seq").T
     dec_flat = jnp.sum(dec_all[:, :used], axis=0).reshape(-1)
     ends = (w_dec1.size, w_dec1.size + dh, w_dec1.size + dh + w_dec2.size)

time: 691 us -> 705 us (1.020)
  waiting for transfers between devices: 77 us -> 39.7 us
  blocking collectives: 25.2 us -> 44.8 us
  local copies, waits for them, and re-layouts: 64.3 us -> 76.3 us
  starting transfers between devices: 88 us -> 96.1 us
  matrix products: 123 us -> 131 us
  other arithmetic: 49.5 us -> 56.6 us
    ppermute x27, waiting for transfers between devices: 43.3 us -> 5.51 us  [turn(): lax.ppermute(x, 'seq', [(i, (i + step) % seq_count) for i in range(seq_co...]
    psum x1, blocking collectives: 10.9 us -> 32.4 us  [per_device(): lax.psum(lax.dynamic_slice_in_dim(sums, scene_rank * shard, shard, 1), 's...]
    dynamic_update_slice x16, other arithmetic: 0.6 us -> 9.78 us  [side_by_side(): lax.dynamic_update_slice_in_dim(out, got.astype(f32), behind(d) * size, 1)]
    ppermute x27, starting transfers between devices: 64.6 us -> 72.8 us  [turn(): lax.ppermute(x, 'seq', [(i, (i + step) % seq_count) for i in range(seq_co...]
    dot_general x20, matrix products: 119 us -> 126 us  [mxu(): lax.dot_general(left, right, dims, preferred_element_type=jnp.float32)]
    unnamed x180 -> x169, local copies, waits for them, and re-layouts: 23.3 us -> 21.2 us
  transfers between devices with their start and end apart: 42 -> 42, of which waited for: 13 -> 9; matrix products, arithmetic and copies ran while one was open for 28% -> 32% of each run, Pallas kernels for 35% -> 34%
where the time goes in v7:
time: 705 us; the launch traced here: 696 us
  Pallas kernels  235 us (33%)
  matrix products  131 us (19%)
  starting transfers between devices  96.1 us (14%)
  local copies, waits for them, and re-layouts  76.3 us (11%)
  other arithmetic  56.6 us (8%)
  blocking collectives  44.8 us (6%)
  waiting for transfers between devices  39.7 us (6%)
  between operations  16.8 us (2%)
    pallas_call x2, Pallas kernels, attn_bwd(): pl.pallas_call(functools.partial(attn_bwd_kernel, tk=tk, tq=tk, scale=hea...  144 us
    dot_general x20, matrix products, mxu(): lax.dot_general(left, right, dims, preferred_element_type=jnp.float32)  126 us
    ppermute x27, starting transfers between devices, turn(): lax.ppermute(x, 'seq', [(i, (i + step) % seq_count) for i in range(seq_co...  72.8 us
    pallas_call x4, Pallas kernels, attn_fwd(): pl.pallas_call(functools.partial(attn_fwd_kernel, first=first, last=last,...  69.4 us
    psum x1, blocking collectives, per_device(): lax.psum(lax.dynamic_slice_in_dim(sums, scene_rank * shard, shard, 1), 's...  32.4 us
    ppermute x6, waiting for transfers between devices, hop(): lax.ppermute(x, 'seq', [(i, i + step) for i in range(seq_count) if 0 <= i...  32.1 us
    ppermute x6, starting transfers between devices, hop(): lax.ppermute(x, 'seq', [(i, i + step) for i in range(seq_count) if 0 <= i...  22.7 us
    pallas_call x1, Pallas kernels, fc1_gelu(): pl.pallas_call(fc1_kernel, grid=(cols // tile,), in_specs=[pl.BlockSpec((...  21.3 us
  transfers between devices with their start and end apart: 42, of which 9 were waited for; matrix products, arithmetic and copies ran while one was open for 32% of the time, Pallas kernels for 34%

profile of v7, /device:TPU:0, one launch (start us, length us, event | category | flops | bytes accessed | tf_op | source)
XLA Modules:
  0.0 696.1 jit_solution(5491981716768221388)
XLA Ops:
  11.2 2.7 convert_element_type.277
  16.9 6.8 collective-permute-start.1
  34.0 21.9 %collective-permute-done = bf16[784,1024]{1,0:T(8,128)(2,1)S(1)} collective-permute-done((bf16[784,1024]{1,0:T(8,128)(2,1)}, bf16[784,1024]{1,0:T(8,128)(2,1)S(1)}, u32[]{:S(2)}, u32[]{:S(2)}) %collective-permute-start) | collective-permute-done | bytes 1605664 | tf_op jit(solution)/shard_map/ppermute | solution.py:371
  60.1 6.2 collective-permute-start.2
  70.2 10.3 %convolution_convert_fusion.5.refs_0_.refs_1_.refs_2_ = bf16[768,3072]{1,0:T(8,128)(2,1)} fusion(bf16[768,1024]{1,0:T(8,128)(2,1)S(1)} %get-tuple-element.170, bf16[1024,3328]{0,1:T(8,128)(2,1)} %all-gather.7.cloned.1.call-done), kind=kOutput, calls=%fused_computation.8 | convolution fusion | flops 4834197504 | bytes 12582912 | tf_op jit(solution)/shard_map/dot_general | solution.py:28
  81.3 16.1 %attn_fwd.4 = (f32[8,2,80,768]{3,2,1,0:T(8,128)}, f32[8,2,768]{2,1,0:T(2,128)}) custom-call(bf16[768,3072]{1,0:T(8,128)(2,1)} %convolution_convert_fusion.5.refs_0_.refs_1_.refs_2_, bf16[768,3072]{1,0:T(8,128)(2,1)} %convolution_convert_fusion.5.refs_0_.refs_1_.refs_2_, bf16[768,3072]{1,0:T(8,128)(2,1)} %convolution_convert_fusion.5.refs_0_.refs_1_.refs_2_, ...), custom_call_target="tpu_custom_call" | custom-call | flops 9663676416 | bytes 6291456 | tf_op jit(solution)/shard_map/attn_fwd/pallas_call | solution.py:155
  99.0 5.5 collective-permute-start.4
  106.0 9.5 %convolution_convert_fusion.4.refs_1_.refs_2_ = bf16[768,3072]{1,0:T(8,128)(2,1)} fusion(bf16[768,1024]{1,0:T(8,128)(2,1)S(1)} %copy-done.10, bf16[1024,3328]{0,1:T(8,128)(2,1)} %all-gather.7.cloned.1.call-done), kind=kOutput, calls=%fused_computation.7 | convolution fusion | flops 4834197504 | bytes 12582912 | tf_op jit(solution)/shard_map/dot_general | solution.py:28
  115.5 17.5 %attn_fwd.5 = (f32[8,2,80,768]{3,2,1,0:T(8,128)}, f32[8,2,768]{2,1,0:T(2,128)}) custom-call(bf16[768,3072]{1,0:T(8,128)(2,1)} %convolution_convert_fusion.5.refs_0_.refs_1_.refs_2_, bf16[768,3072]{1,0:T(8,128)(2,1)} %convolution_convert_fusion.4.refs_1_.refs_2_, bf16[768,3072]{1,0:T(8,128)(2,1)} %convolution_convert_fusion.4.refs_1_.refs_2_, ...), custom_call_target="tpu_custom_call" | custom-call | flops 9663676416 | bytes 6291456 | tf_op jit(solution)/shard_map/attn_fwd/pallas_call | solution.py:155
  133.0 3.2 collective-permute-done.4
  136.3 5.3 collective-permute-done.5
  141.5 2.9 select_select_fusion.1
  153.5 9.5 %convolution_convert_fusion.2.refs_1_.refs_2_ = bf16[768,3072]{1,0:T(8,128)(2,1)} fusion(bf16[768,1024]{1,0:T(8,128)(2,1)S(1)} %get-tuple-element.172, bf16[1024,3328]{0,1:T(8,128)(2,1)} %all-gather.7.cloned.1.call-done), kind=kOutput, calls=%fused_computation.5 | convolution fusion | flops 4834197504 | bytes 12582912 | tf_op jit(solution)/shard_map/dot_general | solution.py:28
  163.0 17.7 %attn_fwd.6 = (f32[8,2,80,768]{3,2,1,0:T(8,128)}, f32[8,2,768]{2,1,0:T(2,128)}) custom-call(bf16[768,3072]{1,0:T(8,128)(2,1)} %convolution_convert_fusion.5.refs_0_.refs_1_.refs_2_, bf16[768,3072]{1,0:T(8,128)(2,1)} %convolution_convert_fusion.2.refs_1_.refs_2_, bf16[768,3072]{1,0:T(8,128)(2,1)} %convolution_convert_fusion.2.refs_1_.refs_2_, ...), custom_call_target="tpu_custom_call" | custom-call | flops 9663676416 | bytes 6291456 | tf_op jit(solution)/shard_map/attn_fwd/pallas_call | solution.py:155
  180.7 9.5 %convolution_convert_fusion.3.refs_1_.refs_2_ = bf16[768,3072]{1,0:T(8,128)(2,1)} fusion(bf16[768,1024]{1,0:T(8,128)(2,1)S(1)} %copy-done.14, bf16[1024,3328]{0,1:T(8,128)(2,1)} %all-gather.7.cloned.1.call-done), kind=kOutput, calls=%fused_computation.6 | convolution fusion | flops 4834197504 | bytes 12582912 | tf_op jit(solution)/shard_map/dot_general | solution.py:28
  190.2 18.1 %attn_fwd.7 = (bf16[768,1024]{1,0:T(8,128)(2,1)}, f32[8,2,768]{2,1,0:T(2,128)}) custom-call(bf16[768,3072]{1,0:T(8,128)(2,1)} %convolution_convert_fusion.5.refs_0_.refs_1_.refs_2_, bf16[768,3072]{1,0:T(8,128)(2,1)} %convolution_convert_fusion.3.refs_1_.refs_2_, bf16[768,3072]{1,0:T(8,128)(2,1)} %convolution_convert_fusion.3.refs_1_.refs_2_, ...), custom_call_target="tpu_custom_call" | custom-call | flops 9663676416 | bytes 6291456 | tf_op jit(solution)/shard_map/attn_fwd/pallas_call | solution.py:155
  208.3 3.9 fusion.115
  215.6 21.3 %fc1_gelu.1 = (bf16[768,4096]{1,0:T(8,128)(2,1)}, bf16[768,4096]{1,0:T(8,128)(2,1)}) custom-call(bf16[768,1024]{1,0:T(8,128)(2,1)} %add_convert_fusion.x_ref, bf16[1024,4096]{1,0:T(8,128)(2,1)} %all-gather.11.cloned.1.call-done.w_ref), custom_call_target="tpu_custom_call" | custom-call | flops 6442450944 | bytes 22544384 | tf_op jit(solution)/shard_map/fc1_gelu/pallas_call | solution.py:306
  237.0 5.8 fusion.79
  247.7 2.8 collective-permute-start.8
  250.6 6.2 fusion.53
  262.9 9.0 %convolution_convert_fusion.1 = bf16[4096,1024]{1,0:T(8,128)(2,1)} fusion(bf16[768,4096]{1,0:T(8,128)(2,1)S(1)} %copy-done.76, f32[192,1024]{1,0:T(8,128)S(1)} %convolution_add_fusion, f32[576,1024]{1,0:T(8,128)S(1)} %copy-done.7), kind=kOutput, calls=%fused_computation.2 | convolution fusion | flops 6449790976 | bytes 17825792 | tf_op jit(solution)/shard_map/dot_general | solution.py:28
  276.4 13.2 %multiply_convert_fusion = bf16[768,4096]{1,0:T(8,128)(2,1)S(1)} fusion(bf16[768,4096]{1,0:T(8,128)(2,1)} %get-tuple-element.127, bf16[4096,1024]{1,0:T(8,128)(2,1)} %all-gather.13.cloned.1.call-done, f32[192,1024]{1,0:T(8,128)} %copy-done.18, f32[576,1024]{1,0:T(8,128)} %slice.158), kind=kOutput, calls=%fused_computation | convolution fusion | flops 6455033856 | bytes 24117248 | tf_op jit(solution)/shard_map/dot_general | solution.py:28
  289.7 13.1 %multiply_reduce_fusion = (bf16[1024]{0:T(1024)(128)(2,1)}, f32[768]{0:T(1024)S(1)}, f32[768]{0:T(1024)S(1)}, bf16[1024]{0:T(1024)(128)(2,1)}, f32[768,1024]{1,0:T(8,128)S(1)}) fusion(f32[768,1024]{1,0:T(8,128)S(1)} %copy-done.3, f32[768]{0:T(1024)S(1)} %add_rsqrt_fusion, f32[768]{0:T(1024)S(1)} %broadcast_multiply_fusion.4, f32[1024]{0:T(1024)S(1)} %bitcast.88, ...), kind=kOutput, calls=%fused_computation.68 | convolution fusion | flops 6449524736 | bytes 20992000 | tf_op jit(solution)/shard_map/dot_general | solution.py:28
  328.9 9.0 %convolution_convert_fusion = bf16[1024,4096]{1,0:T(8,128)(2,1)} fusion(bf16[768,1024]{1,0:T(8,128)(2,1)S(1)} %copy-done.32, bf16[768,4096]{1,0:T(8,128)(2,1)S(1)} %bitcast.97), kind=kOutput, calls=%fused_computation.1 | convolution fusion | flops 6446645248 | bytes 16252928 | tf_op jit(solution)/shard_map/dot_general | solution.py:28
  342.4 6.2 slice.164
  349.1 6.0 collective-permute-start.12
  355.4 3.0 collective-permute-start.14
  358.4 72.0 %attn_bwd.2 = bf16[3072,384]{1,0:T(8,128)(2,1)} custom-call(bf16[3072,768]{1,0:T(8,128)(2,1)} %dynamic-slice_dynamic-update-slice_fusion.refs_0_.refs_1_.refs_2_, bf16[3072,768]{1,0:T(8,128)(2,1)} %dynamic-slice_dynamic-update-slice_fusion.refs_0_.refs_1_.refs_2_, bf16[3072,768]{1,0:T(8,128)(2,1)} %dynamic-slice_dynamic-update-slice_fusion.refs_0_.refs_1_.refs_2_, ...), custom_call_target="tpu_custom_call" | custom-call | flops 48318382080 | bytes 5505024 | tf_op jit(solution)/shard_map/attn_bwd/pallas_call | solution.py:262
  434.4 2.7 fusion.113
  442.4 72.1 %attn_bwd.3 = bf16[3072,384]{1,0:T(8,128)(2,1)} custom-call(bf16[3072,768]{1,0:T(8,128)(2,1)} %dynamic-slice_dynamic-update-slice_fusion.refs_0_.refs_1_.refs_2_, bf16[3072,768]{1,0:T(8,128)(2,1)} %dynamic-slice_dynamic-update-slice_fusion.refs_0_.refs_1_.refs_2_, bf16[3072,768]{1,0:T(8,128)(2,1)} %dynamic-slice_dynamic-update-slice_fusion.refs_0_.refs_1_.refs_2_, ...), custom_call_target="tpu_custom_call" | custom-call | flops 48318382080 | bytes 5505024 | tf_op jit(solution)/shard_map/attn_bwd/pallas_call | solution.py:262
  515.3 2.9 fusion.112
  518.2 5.6 collective-permute-start.21
  523.8 4.4 collective-permute-start.22
  529.4 3.5 broadcast_in_dim.105
  548.8 5.6 convolution_convert_fusion.9
  554.4 5.4 convolution_convert_fusion.8
  561.9 3.5 constant_dynamic-slice_fusion.13
  566.7 3.9 fusion.39
  570.7 4.0 fusion.61
  574.7 3.1 fusion.20
  577.9 14.6 %collective-permute-start.24 = (bf16[128,1408]{1,0:T(8,128)(2,1)}, bf16[128,1408]{1,0:T(8,128)(2,1)S(1)}, u32[]{:S(2)}, u32[]{:S(2)}) collective-permute-start(bf16[128,1408]{1,0:T(8,128)(2,1)} %pad_maximum_fusion.5), channel_id=1, source_target_pairs={{0,1},{1,2},{2,3},{3,0},{4,5},{5,6},{6,7},{7,4},{8,9},{9,10},{10,1... | collective-permute-start | bytes 1081352 | tf_op jit(solution)/shard_map/ppermute | solution.py:376
  594.4 2.8 collective-permute-start.26
  597.9 12.4 %psum.14 = f32[2,1024]{1,0:T(2,128)S(1)} all-reduce(f32[2,1024]{1,0:T(2,128)S(1)} %pad_maximum_fusion.8), channel_id=1, replica_groups=mesh['scene'=8,'seq'=4] {'scene'}, use_global_device_ids=true, to_apply=%region_23.24 | all-reduce | flops 2048 | bytes 16384 | tf_op jit(solution)/shard_map/psum | solution.py:652
  610.4 4.4 fusion.24
  623.8 32.4 %psum.15 = f32[128,2]{0,1:T(2,128)} all-reduce(f32[128,2]{0,1:T(2,128)S(1)} %fusion.100), channel_id=1, replica_groups=mesh['scene'=8,'seq'=4] {'seq'}, use_global_device_ids=true, to_apply=%region_27.28 | all-reduce | flops 256 | bytes 2048 | tf_op jit(solution)/shard_map/psum | solution.py:669
  660.0 12.4 %collective-permute-start.32 = (bf16[128,768]{0,1:T(8,128)(2,1)S(1)}, bf16[128,768]{0,1:T(8,128)(2,1)S(1)}, u32[]{:S(2)}, u32[]{:S(2)}) collective-permute-start(bf16[128,768]{0,1:T(8,128)(2,1)S(1)} %copy.120), channel_id=1, source_target_pairs={{0,3},{1,0},{2,1},{3,2},{4,7},{5,4},{6,5},{7,6},{8,11},{9,8},{10,9... | collective-permute-start | bytes 589832 | tf_op jit(solution)/shard_map/ppermute | solution.py:376
  672.4 3.1 collective-permute-done.32
  (414 shorter events, 146.1 us)
Async XLA Ops:
  7.2 60.0 %all-gather.7.cloned.1.call-start = ((), (), s32[]{:S(2)}) async-start(), calls=%async_computation.4 | async-start | bytes 7667712 | tf_op jit(solution)/shard_map/all_gather | solution.py:413
  10.3 197.9 %all-gather.9.cloned.1.call-start = ((), (), s32[]{:S(2)}) async-start(), calls=%async_computation.5 | async-start | bytes 2359296 | tf_op jit(solution)/shard_map/all_gather | solution.py:410
  11.1 204.5 %all-gather.11.cloned.1.call-start = ((), (), s32[]{:S(2)}) async-start(), calls=%async_computation.6 | async-start | bytes 9437184 | tf_op jit(solution)/shard_map/all_gather | solution.py:410
  13.9 223.1 %all-gather.13.cloned.1.call-start = ((), (), s32[]{:S(2)}) async-start(), calls=%async_computation.7 | async-start | bytes 9437184 | tf_op jit(solution)/shard_map/all_gather | solution.py:410
  15.5 40.4 %collective-permute-start = (bf16[784,1024]{1,0:T(8,128)(2,1)}, bf16[784,1024]{1,0:T(8,128)(2,1)S(1)}, u32[]{:S(2)}, u32[]{:S(2)}) collective-permute-start(bf16[784,1024]{1,0:T(8,128)(2,1)} %fusion.71), channel_id=1, source_target_pairs={{1,0},{2,1},{3,2},{5,4},{6,5},{7,6},{9,8},{10,9},{11,10},{13,12},{... | collective-permute-start | bytes 4816904 | tf_op jit(solution)/shard_map/ppermute | solution.py:371
  16.9 40.2 %collective-permute-start.1 = (bf16[784,1024]{1,0:T(8,128)(2,1)}, bf16[784,1024]{1,0:T(8,128)(2,1)}, u32[]{:S(2)}, u32[]{:S(2)}) collective-permute-start(bf16[784,1024]{1,0:T(8,128)(2,1)} %fusion.71), channel_id=1, source_target_pairs={{0,1},{1,2},{2,3},{4,5},{5,6},{6,7},{8,9},{9,10},{10,11},{12,13},{... | collective-permute-start | bytes 4816904 | tf_op jit(solution)/shard_map/ppermute | solution.py:371
  24.9 316.4 %reduce-scatter.7.cloned.1.call-start = ((), (), s32[]{:S(2)}) async-start(), calls=%async_computation.8 | async-start | bytes 9437184 | tf_op jit(solution)/shard_map/reduce_scatter | solution.py:550
  33.4 34.6 %copy-start.53 = (f32[768]{0:T(1024)}, f32[768]{0:T(1024)S(1)}, u32[]{:S(2)}) copy-start(f32[768]{0:T(1024)S(1)} %broadcast_multiply_fusion.8) | copy-start | bytes 9220
  34.0 46.5 %copy-start.57 = (f32[768]{0:T(1024)}, f32[768]{0:T(1024)S(1)}, u32[]{:S(2)}) copy-start(f32[768]{0:T(1024)S(1)} %add_rsqrt_fusion.4) | copy-start | bytes 9220
  58.8 38.9 %collective-permute-start.3 = (bf16[784,1024]{1,0:T(8,128)(2,1)}, bf16[784,1024]{1,0:T(8,128)(2,1)}, u32[]{:S(2)}, u32[]{:S(2)}) collective-permute-start(bf16[784,1024]{1,0:T(8,128)(2,1)} %copy-done.9), channel_id=1, source_target_pairs={{1,0},{2,1},{3,2},{5,4},{6,5},{7,6},{9,8},{10,9},{11,10},{13,12},{... | collective-permute-start | bytes 4816904 | tf_op jit(solution)/shard_map/ppermute | solution.py:371
  60.1 38.8 %collective-permute-start.2 = (bf16[784,1024]{1,0:T(8,128)(2,1)}, bf16[784,1024]{1,0:T(8,128)(2,1)}, u32[]{:S(2)}, u32[]{:S(2)}) collective-permute-start(bf16[784,1024]{1,0:T(8,128)(2,1)} %collective-permute-done.1), channel_id=1, source_target_pairs={{0,1},{1,2},{2,3},{4,5},{5,6},{6,7},{8,9},{9,10},{10,11},{12,13},{... | collective-permute-start | bytes 4816904 | tf_op jit(solution)/shard_map/ppermute | solution.py:371
  68.0 81.8 %copy-start.55 = (f32[1024,1]{0,1:T(1,128)}, f32[1024,1]{0,1:T(1,128)S(1)}, u32[]{:S(2)}) copy-start(f32[1024,1]{0,1:T(1,128)S(1)} %get-tuple-element.336) | copy-start | bytes 12292
  81.3 24.7 %copy-start.10 = (bf16[768,1024]{1,0:T(8,128)(2,1)S(1)}, bf16[768,1024]{1,0:T(8,128)(2,1)}, u32[]{:S(2)}) copy-start(bf16[768,1024]{1,0:T(8,128)(2,1)} %get-tuple-element.171) | copy-start | bytes 4718596
  99.0 37.3 %collective-permute-start.4 = (bf16[784,1024]{1,0:T(8,128)(2,1)}, bf16[784,1024]{1,0:T(8,128)(2,1)}, u32[]{:S(2)}, u32[]{:S(2)}) collective-permute-start(bf16[784,1024]{1,0:T(8,128)(2,1)} %collective-permute-done.2), channel_id=1, source_target_pairs={{0,1},{1,2},{2,3},{4,5},{5,6},{6,7},{8,9},{9,10},{10,11},{12,13},{... | collective-permute-start | bytes 4816904 | tf_op jit(solution)/shard_map/ppermute | solution.py:371
  104.5 37.0 %collective-permute-start.5 = (bf16[784,1024]{1,0:T(8,128)(2,1)}, bf16[784,1024]{1,0:T(8,128)(2,1)}, u32[]{:S(2)}, u32[]{:S(2)}) collective-permute-start(bf16[784,1024]{1,0:T(8,128)(2,1)} %collective-permute-done.3), channel_id=1, source_target_pairs={{1,0},{2,1},{3,2},{5,4},{6,5},{7,6},{9,8},{10,9},{11,10},{13,12},{... | collective-permute-start | bytes 4816904 | tf_op jit(solution)/shard_map/ppermute | solution.py:371
  242.8 83.5 %copy-start.30 = (bf16[192,1024]{1,0:T(8,128)(2,1)}, bf16[192,1024]{1,0:T(8,128)(2,1)S(1)}, u32[]{:S(2)}) copy-start(bf16[192,1024]{1,0:T(8,128)(2,1)S(1)} %fusion.79) | copy-start | bytes 1179652
  245.0 11.7 %collective-permute-start.6 = (bf16[192,128]{1,0:T(8,128)(2,1)S(1)}, bf16[192,128]{1,0:T(8,128)(2,1)S(1)}, u32[]{:S(2)}, u32[]{:S(2)}) collective-permute-start(bf16[192,128]{1,0:T(8,128)(2,1)S(1)} %get-tuple-element.344), channel_id=1, source_target_pairs={{0,1},{1,2},{2,3},{3,0},{4,5},{5,6},{6,7},{7,4},{8,9},{9,10},{10,1... | collective-permute-start | bytes 147464 | tf_op jit(solution)/shard_map/ppermute | solution.py:376
  246.3 10.4 %collective-permute-start.7 = (bf16[192,128]{1,0:T(8,128)(2,1)S(1)}, bf16[192,128]{1,0:T(8,128)(2,1)S(1)}, u32[]{:S(2)}, u32[]{:S(2)}) collective-permute-start(bf16[192,128]{1,0:T(8,128)(2,1)S(1)} %get-tuple-element.344), channel_id=1, source_target_pairs={{0,2},{1,3},{2,0},{3,1},{4,6},{5,7},{6,4},{7,5},{8,10},{9,11},{10,... | collective-permute-start | bytes 147464 | tf_op jit(solution)/shard_map/ppermute | solution.py:376
  247.7 9.1 %collective-permute-start.8 = (bf16[192,128]{1,0:T(8,128)(2,1)S(1)}, bf16[192,128]{1,0:T(8,128)(2,1)S(1)}, u32[]{:S(2)}, u32[]{:S(2)}) collective-permute-start(bf16[192,128]{1,0:T(8,128)(2,1)S(1)} %get-tuple-element.344), channel_id=1, source_target_pairs={{0,3},{1,0},{2,1},{3,2},{4,7},{5,4},{6,5},{7,6},{8,11},{9,8},{10,9... | collective-permute-start | bytes 147464 | tf_op jit(solution)/shard_map/ppermute | solution.py:376
  271.9 243.4 %reduce-scatter.11.cloned.1.call-start = ((), (), s32[]{:S(2)}) async-start(), calls=%async_computation.10 | async-start | bytes 3538944 | tf_op jit(solution)/shard_map/reduce_scatter | solution.py:550
  311.1 28.8 %collective-permute-start.10 = (bf16[848,256]{1,0:T(8,128)(2,1)}, bf16[848,256]{1,0:T(8,128)(2,1)}, u32[]{:S(2)}, u32[]{:S(2)}) collective-permute-start(bf16[848,256]{1,0:T(8,128)(2,1)} %get-tuple-element.315), channel_id=1, source_target_pairs={{0,2},{1,3},{2,0},{3,1},{4,6},{5,7},{6,4},{7,5},{8,10},{9,11},{10,... | collective-permute-start | bytes 1302536 | tf_op jit(solution)/shard_map/ppermute | solution.py:376
  311.1 28.8 %collective-permute-start.11 = (bf16[848,256]{1,0:T(8,128)(2,1)}, bf16[848,256]{1,0:T(8,128)(2,1)}, u32[]{:S(2)}, u32[]{:S(2)}) collective-permute-start(bf16[848,256]{1,0:T(8,128)(2,1)} %get-tuple-element.314), channel_id=1, source_target_pairs={{0,3},{1,0},{2,1},{3,2},{4,7},{5,4},{6,5},{7,6},{8,11},{9,8},{10,9... | collective-permute-start | bytes 1302536 | tf_op jit(solution)/shard_map/ppermute | solution.py:376
  312.1 27.8 %collective-permute-start.9 = (bf16[848,256]{1,0:T(8,128)(2,1)S(1)}, bf16[848,256]{1,0:T(8,128)(2,1)}, u32[]{:S(2)}, u32[]{:S(2)}) collective-permute-start(bf16[848,256]{1,0:T(8,128)(2,1)S(1)} %get-tuple-element.316), channel_id=1, source_target_pairs={{0,1},{1,2},{2,3},{3,0},{4,5},{5,6},{6,7},{7,4},{8,9},{9,10},{10,1... | collective-permute-start | bytes 1302536 | tf_op jit(solution)/shard_map/ppermute | solution.py:376
  341.3 174.0 %reduce-scatter.9.cloned.1.call-start = ((), (), s32[]{:S(2)}) async-start(), calls=%async_computation.9 | async-start | bytes 9437184 | tf_op jit(solution)/shard_map/reduce_scatter | solution.py:550
  342.0 272.7 %reduce-scatter.13.cloned.1.call-start = ((), (), s32[]{:S(2)}) async-start(), calls=%async_computation.12 | async-start | bytes 1769472
  349.1 81.2 %collective-permute-start.12 = (bf16[512,256]{1,0:T(8,128)(2,1)S(1)}, bf16[512,256]{1,0:T(8,128)(2,1)S(1)}, u32[]{:S(2)}, u32[]{:S(2)}) collective-permute-start(bf16[512,256]{1,0:T(8,128)(2,1)S(1)} %get-tuple-element.324), channel_id=1, source_target_pairs={{0,1},{1,2},{2,3},{3,0},{4,5},{5,6},{6,7},{7,4},{8,9},{9,10},{10,1... | collective-permute-start | bytes 786440 | tf_op jit(solution)/shard_map/ppermute | solution.py:376
  355.1 75.2 %collective-permute-start.13 = (bf16[512,256]{1,0:T(8,128)(2,1)S(1)}, bf16[512,256]{1,0:T(8,128)(2,1)S(1)}, u32[]{:S(2)}, u32[]{:S(2)}) collective-permute-start(bf16[512,256]{1,0:T(8,128)(2,1)S(1)} %get-tuple-element.323), channel_id=1, source_target_pairs={{0,2},{1,3},{2,0},{3,1},{4,6},{5,7},{6,4},{7,5},{8,10},{9,11},{10,... | collective-permute-start | bytes 786440 | tf_op jit(solution)/shard_map/ppermute | solution.py:376
  355.4 75.0 %collective-permute-start.14 = (bf16[512,256]{1,0:T(8,128)(2,1)S(1)}, bf16[512,256]{1,0:T(8,128)(2,1)S(1)}, u32[]{:S(2)}, u32[]{:S(2)}) collective-permute-start(bf16[512,256]{1,0:T(8,128)(2,1)S(1)} %get-tuple-element.322), channel_id=1, source_target_pairs={{0,3},{1,0},{2,1},{3,2},{4,7},{5,4},{6,5},{7,6},{8,11},{9,8},{10,9... | collective-permute-start | bytes 786440 | tf_op jit(solution)/shard_map/ppermute | solution.py:376
  430.5 11.1 %collective-permute-start.18 = (bf16[512,256]{1,0:T(8,128)(2,1)S(1)}, bf16[512,256]{1,0:T(8,128)(2,1)S(1)}, u32[]{:S(2)}, u32[]{:S(2)}) collective-permute-start(bf16[512,256]{1,0:T(8,128)(2,1)S(1)} %add_convert_fusion.2), channel_id=1, source_target_pairs={{0,1},{1,2},{2,3},{3,0},{4,5},{5,6},{6,7},{7,4},{8,9},{9,10},{10,1... | collective-permute-start | bytes 786440 | tf_op jit(solution)/shard_map/ppermute | solution.py:376
  430.6 83.9 %collective-permute-start.19 = (bf16[512,256]{1,0:T(8,128)(2,1)S(1)}, bf16[512,256]{1,0:T(8,128)(2,1)S(1)}, u32[]{:S(2)}, u32[]{:S(2)}) collective-permute-start(bf16[512,256]{1,0:T(8,128)(2,1)S(1)} %add_convert_fusion.2), channel_id=1, source_target_pairs={{0,2},{1,3},{2,0},{3,1},{4,6},{5,7},{6,4},{7,5},{8,10},{9,11},{10,... | collective-permute-start | bytes 786440 | tf_op jit(solution)/shard_map/ppermute | solution.py:376
  432.6 81.9 %collective-permute-start.20 = (bf16[512,256]{1,0:T(8,128)(2,1)S(1)}, bf16[512,256]{1,0:T(8,128)(2,1)S(1)}, u32[]{:S(2)}, u32[]{:S(2)}) collective-permute-start(bf16[512,256]{1,0:T(8,128)(2,1)S(1)} %add_convert_fusion.2), channel_id=1, source_target_pairs={{0,3},{1,0},{2,1},{3,2},{4,7},{5,4},{6,5},{7,6},{8,11},{9,8},{10,9... | collective-permute-start | bytes 786440 | tf_op jit(solution)/shard_map/ppermute | solution.py:376
  437.1 77.4 %collective-permute-start.15 = (bf16[768,384]{1,0:T(8,128)(2,1)S(1)}, bf16[768,384]{1,0:T(8,128)(2,1)S(1)}, u32[]{:S(2)}, u32[]{:S(2)}) collective-permute-start(bf16[768,384]{1,0:T(8,128)(2,1)S(1)} %get-tuple-element.312), channel_id=1, source_target_pairs={{0,1},{1,2},{2,3},{3,0},{4,5},{5,6},{6,7},{7,4},{8,9},{9,10},{10,1... | collective-permute-start | bytes 1769480 | tf_op jit(solution)/shard_map/ppermute | solution.py:376
  437.8 76.8 %collective-permute-start.16 = (bf16[768,384]{1,0:T(8,128)(2,1)S(1)}, bf16[768,384]{1,0:T(8,128)(2,1)}, u32[]{:S(2)}, u32[]{:S(2)}) collective-permute-start(bf16[768,384]{1,0:T(8,128)(2,1)S(1)} %get-tuple-element.311), channel_id=1, source_target_pairs={{0,2},{1,3},{2,0},{3,1},{4,6},{5,7},{6,4},{7,5},{8,10},{9,11},{10,... | collective-permute-start | bytes 1769480 | tf_op jit(solution)/shard_map/ppermute | solution.py:376
  441.6 73.7 %collective-permute-start.17 = (bf16[768,384]{1,0:T(8,128)(2,1)S(1)}, bf16[768,384]{1,0:T(8,128)(2,1)}, u32[]{:S(2)}, u32[]{:S(2)}) collective-permute-start(bf16[768,384]{1,0:T(8,128)(2,1)S(1)} %get-tuple-element.310), channel_id=1, source_target_pairs={{0,3},{1,0},{2,1},{3,2},{4,7},{5,4},{6,5},{7,6},{8,11},{9,8},{10,9... | collective-permute-start | bytes 1769480 | tf_op jit(solution)/shard_map/ppermute | solution.py:376
  518.2 27.9 %collective-permute-start.21 = (bf16[768,384]{1,0:T(8,128)(2,1)S(1)}, bf16[768,384]{1,0:T(8,128)(2,1)S(1)}, u32[]{:S(2)}, u32[]{:S(2)}) collective-permute-start(bf16[768,384]{1,0:T(8,128)(2,1)S(1)} %get-tuple-element.308), channel_id=1, source_target_pairs={{0,1},{1,2},{2,3},{3,0},{4,5},{5,6},{6,7},{7,4},{8,9},{9,10},{10,1... | collective-permute-start | bytes 1769480 | tf_op jit(solution)/shard_map/ppermute | solution.py:376
  523.8 46.8 %collective-permute-start.22 = (bf16[768,384]{1,0:T(8,128)(2,1)}, bf16[768,384]{1,0:T(8,128)(2,1)}, u32[]{:S(2)}, u32[]{:S(2)}) collective-permute-start(bf16[768,384]{1,0:T(8,128)(2,1)} %get-tuple-element.307), channel_id=1, source_target_pairs={{0,2},{1,3},{2,0},{3,1},{4,6},{5,7},{6,4},{7,5},{8,10},{9,11},{10,... | collective-permute-start | bytes 1769480 | tf_op jit(solution)/shard_map/ppermute | solution.py:376
  528.2 42.4 %collective-permute-start.23 = (bf16[768,384]{1,0:T(8,128)(2,1)}, bf16[768,384]{1,0:T(8,128)(2,1)}, u32[]{:S(2)}, u32[]{:S(2)}) collective-permute-start(bf16[768,384]{1,0:T(8,128)(2,1)} %get-tuple-element.306), channel_id=1, source_target_pairs={{0,3},{1,0},{2,1},{3,2},{4,7},{5,4},{6,5},{7,6},{8,11},{9,8},{10,9... | collective-permute-start | bytes 1769480 | tf_op jit(solution)/shard_map/ppermute | solution.py:376
  561.6 124.2 %all-gather.15.cloned.1.call-start = ((), (), s32[]{:S(2)}) async-start(), calls=%async_computation.11 | async-start | bytes 2359296 | tf_op jit(solution)/shard_map/all_gather | solution.py:643
  577.9 38.0 %collective-permute-start.24 = (bf16[128,1408]{1,0:T(8,128)(2,1)}, bf16[128,1408]{1,0:T(8,128)(2,1)S(1)}, u32[]{:S(2)}, u32[]{:S(2)}) collective-permute-start(bf16[128,1408]{1,0:T(8,128)(2,1)} %pad_maximum_fusion.5), channel_id=1, source_target_pairs={{0,1},{1,2},{2,3},{3,0},{4,5},{5,6},{6,7},{7,4},{8,9},{9,10},{10,1... | collective-permute-start | bytes 1081352 | tf_op jit(solution)/shard_map/ppermute | solution.py:376
  592.5 23.4 %collective-permute-start.25 = (bf16[128,1408]{1,0:T(8,128)(2,1)}, bf16[128,1408]{1,0:T(8,128)(2,1)S(1)}, u32[]{:S(2)}, u32[]{:S(2)}) collective-permute-start(bf16[128,1408]{1,0:T(8,128)(2,1)} %pad_maximum_fusion.6), channel_id=1, source_target_pairs={{0,2},{1,3},{2,0},{3,1},{4,6},{5,7},{6,4},{7,5},{8,10},{9,11},{10,... | collective-permute-start | bytes 1081352 | tf_op jit(solution)/shard_map/ppermute | solution.py:376
  594.4 22.3 %collective-permute-start.26 = (bf16[128,1408]{1,0:T(8,128)(2,1)}, bf16[128,1408]{1,0:T(8,128)(2,1)}, u32[]{:S(2)}, u32[]{:S(2)}) collective-permute-start(bf16[128,1408]{1,0:T(8,128)(2,1)} %pad_maximum_fusion.7), channel_id=1, source_target_pairs={{0,3},{1,0},{2,1},{3,2},{4,7},{5,4},{6,5},{7,6},{8,11},{9,8},{10,9... | collective-permute-start | bytes 1081352 | tf_op jit(solution)/shard_map/ppermute | solution.py:376
  610.4 46.5 %copy-start.31 = (bf16[192,1024]{1,0:T(8,128)(2,1)S(1)}, bf16[192,1024]{1,0:T(8,128)(2,1)}, u32[]{:S(2)}) copy-start(bf16[192,1024]{1,0:T(8,128)(2,1)} %copy-done.30) | copy-start | bytes 1179652
  617.9 59.5 %collective-permute-start.27 = (bf16[128,1408]{1,0:T(8,128)(2,1)S(1)}, bf16[128,1408]{1,0:T(8,128)(2,1)S(1)}, u32[]{:S(2)}, u32[]{:S(2)}) collective-permute-start(bf16[128,1408]{1,0:T(8,128)(2,1)S(1)} %add_convert_fusion.1), channel_id=1, source_target_pairs={{0,1},{1,2},{2,3},{3,0},{4,5},{5,6},{6,7},{7,4},{8,9},{9,10},{10,1... | collective-permute-start | bytes 1081352 | tf_op jit(solution)/shard_map/ppermute | solution.py:376
  618.1 59.3 %collective-permute-start.28 = (bf16[128,1408]{1,0:T(8,128)(2,1)S(1)}, bf16[128,1408]{1,0:T(8,128)(2,1)}, u32[]{:S(2)}, u32[]{:S(2)}) collective-permute-start(bf16[128,1408]{1,0:T(8,128)(2,1)S(1)} %add_convert_fusion.1), channel_id=1, source_target_pairs={{0,2},{1,3},{2,0},{3,1},{4,6},{5,7},{6,4},{7,5},{8,10},{9,11},{10,... | collective-permute-start | bytes 1081352 | tf_op jit(solution)/shard_map/ppermute | solution.py:376
  620.5 57.8 %collective-permute-start.29 = (bf16[128,1408]{1,0:T(8,128)(2,1)S(1)}, bf16[128,1408]{1,0:T(8,128)(2,1)}, u32[]{:S(2)}, u32[]{:S(2)}) collective-permute-start(bf16[128,1408]{1,0:T(8,128)(2,1)S(1)} %add_convert_fusion.1), channel_id=1, source_target_pairs={{0,3},{1,0},{2,1},{3,2},{4,7},{5,4},{6,5},{7,6},{8,11},{9,8},{10,9... | collective-permute-start | bytes 1081352 | tf_op jit(solution)/shard_map/ppermute | solution.py:376
  622.0 38.0 %collective-permute-start.30 = (bf16[128,768]{0,1:T(8,128)(2,1)S(1)}, bf16[128,768]{0,1:T(8,128)(2,1)S(1)}, u32[]{:S(2)}, u32[]{:S(2)}) collective-permute-start(bf16[128,768]{0,1:T(8,128)(2,1)S(1)} %copy.120), channel_id=1, source_target_pairs={{0,1},{1,2},{2,3},{3,0},{4,5},{5,6},{6,7},{7,4},{8,9},{9,10},{10,1... | collective-permute-start | bytes 589832 | tf_op jit(solution)/shard_map/ppermute | solution.py:376
  622.5 49.9 %collective-permute-start.31 = (bf16[128,768]{0,1:T(8,128)(2,1)S(1)}, bf16[128,768]{0,1:T(8,128)(2,1)S(1)}, u32[]{:S(2)}, u32[]{:S(2)}) collective-permute-start(bf16[128,768]{0,1:T(8,128)(2,1)S(1)} %copy.120), channel_id=1, source_target_pairs={{0,2},{1,3},{2,0},{3,1},{4,6},{5,7},{6,4},{7,5},{8,10},{9,11},{10,... | collective-permute-start | bytes 589832 | tf_op jit(solution)/shard_map/ppermute | solution.py:376
  660.0 15.6 %collective-permute-start.32 = (bf16[128,768]{0,1:T(8,128)(2,1)S(1)}, bf16[128,768]{0,1:T(8,128)(2,1)S(1)}, u32[]{:S(2)}, u32[]{:S(2)}) collective-permute-start(bf16[128,768]{0,1:T(8,128)(2,1)S(1)} %copy.120), channel_id=1, source_target_pairs={{0,3},{1,0},{2,1},{3,2},{4,7},{5,4},{6,5},{7,6},{8,11},{9,8},{10,9... | collective-permute-start | bytes 589832 | tf_op jit(solution)/shard_map/ppermute | solution.py:376
  (74 other events, 412.5 us)
Sparse Core Ops, SparseCore 0:
  10.5 51.6 all-gather.6
  64.6 27.7 all-gather.8
  94.3 54.2 all-gather.10
  150.3 54.2 all-gather.12
  272.1 69.1 reduce-scatter.6
  344.5 46.0 reduce-scatter.10
  394.1 71.5 reduce-scatter.8
  561.7 51.7 reduce-scatter.12
  615.3 27.7 all-gather.14

commit v8 on v7

--- a/solution.py
+++ b/solution.py
@@ -656,17 +656,36 @@
     block_out = jnp.concatenate([image_out, triplane], axis=0)
     decoded = lax.dynamic_slice_in_dim(decoded_all, rank * cells_dev, cells_dev, 0)
     qkv_blocks = send([qkv_part] * seq_count)
-    wide_blocks = blocks_of(wide_pieces)
+    norm_parts, rest = [], lax.dynamic_slice_in_dim(sums, scene_rank * shard, shard, 1).T
+    for _ in range(3):
+        top = lax.reduce_precision(rest, 8, 7)
+        norm_parts.append(top.astype(bf16))
+        rest = rest - top
+    mine = jnp.concatenate(
+        [
+            sum(x.astype(f32) for x in wide_pieces).astype(bf16),
+            jnp.pad(jnp.concatenate(norm_parts, axis=1), ((0, 0), (0, 122))),
+        ],
+        axis=1,
+    )
+    wide_blocks = send([mine] * seq_count)
+    last = mine.shape[1] - 128
+    norm_all = jnp.zeros((seq_count, shard, 6), f32)
+    for d, got in enumerate(wide_blocks):
+        norm_all = lax.dynamic_update_slice_in_dim(
+            norm_all, got[None, :, last : last + 6].astype(f32), behind(d), 0
+        )
+    norm_all = jnp.sum(norm_all, axis=0)
+    norm_one = norm_all[:, :2] + norm_all[:, 2:4] + norm_all[:, 4:]
     edge = w_fc1.shape[1] // seq_count
     grad_fc1 = side_by_side([x[:, :edge] for x in wide_blocks])
-    grad_misc = side_by_side([x[:, edge:] for x in wide_blocks])
+    grad_misc = side_by_side([x[:, edge:last] for x in wide_blocks])
     grad_proj = grad_misc[:, :width]
     grad_unp = grad_misc[:, width : width + PP * TF]
     norm_two = grad_misc[:, width + PP * TF : width + PP * TF + 2]
     qkv_all = side_by_side(qkv_blocks)
     grad_qkv = qkv_all.reshape(shard, pairs, 3, lanes).transpose(0, 2, 1, 3).reshape(shard, 3 * width)
 
-    norm_one = lax.psum(lax.dynamic_slice_in_dim(sums, scene_rank * shard, shard, 1), "seq").T
     dec_flat = jnp.sum(dec_all[:, :used], axis=0).reshape(-1)
     ends = (w_dec1.size, w_dec1.size + dh, w_dec1.size + dh + w_dec2.size)
     dec_grads = (

time: 705 us -> 705 us (level)
  waiting for transfers between devices: 39.7 us -> 80.6 us
  blocking collectives: 44.8 us -> 12.3 us
  starting transfers between devices: 96.1 us -> 83.7 us
    ppermute x27, waiting for transfers between devices: 5.51 us -> 46.4 us  [turn(): lax.ppermute(x, 'seq', [(i, (i + step) % seq_count) for i in range(seq_co...]
    psum x1 -> x0, blocking collectives: 32.4 us -> none  [per_device(): lax.psum(lax.dynamic_slice_in_dim(sums, scene_rank * shard, shard, 1), 's...]
    ppermute x27, starting transfers between devices: 72.8 us -> 60.2 us  [turn(): lax.ppermute(x, 'seq', [(i, (i + step) % seq_count) for i in range(seq_co...]
    unnamed x169 -> x178, local copies, waits for them, and re-layouts: 21.2 us -> 21.8 us
  transfers between devices with their start and end apart: 42 -> 42, of which waited for: 9 -> 11; matrix products, arithmetic and copies ran while one was open for 32% -> 32% of each run, Pallas kernels for 34% -> 34%
where the time goes in v8:
time: 705 us; the launch traced here: 696 us
  Pallas kernels  235 us (33%)
  matrix products  131 us (19%)
  starting transfers between devices  83.7 us (12%)
  waiting for transfers between devices  80.6 us (11%)
  local copies, waits for them, and re-layouts  77.3 us (11%)
  other arithmetic  59.5 us (8%)
  between operations  16.9 us (2%)
  blocking collectives  12.3 us (2%)
    pallas_call x2, Pallas kernels, attn_bwd(): pl.pallas_call(functools.partial(attn_bwd_kernel, tk=tk, tq=tk, scale=hea...  144 us
    dot_general x20, matrix products, mxu(): lax.dot_general(left, right, dims, preferred_element_type=jnp.float32)  126 us
    pallas_call x4, Pallas kernels, attn_fwd(): pl.pallas_call(functools.partial(attn_fwd_kernel, first=first, last=last,...  69.4 us
    ppermute x27, starting transfers between devices, turn(): lax.ppermute(x, 'seq', [(i, (i + step) % seq_count) for i in range(seq_co...  60.2 us
    ppermute x27, waiting for transfers between devices, turn(): lax.ppermute(x, 'seq', [(i, (i + step) % seq_count) for i in range(seq_co...  46.4 us
    ppermute x6, waiting for transfers between devices, hop(): lax.ppermute(x, 'seq', [(i, i + step) for i in range(seq_count) if 0 <= i...  32.1 us
    ppermute x6, starting transfers between devices, hop(): lax.ppermute(x, 'seq', [(i, i + step) for i in range(seq_count) if 0 <= i...  22.8 us
    unnamed x178, local copies, waits for them, and re-layouts  21.8 us
  transfers between devices with their start and end apart: 42, of which 11 were waited for; matrix products, arithmetic and copies ran while one was open for 32% of the time, Pallas kernels for 34%

profile of v8, /device:TPU:0, one launch (start us, length us, event | category | flops | bytes accessed | tf_op | source)
XLA Modules:
  0.0 696.1 jit_solution(14488808466326241121)
XLA Ops:
  16.9 6.8 collective-permute-start.1
  34.0 21.9 %collective-permute-done = bf16[784,1024]{1,0:T(8,128)(2,1)S(1)} collective-permute-done((bf16[784,1024]{1,0:T(8,128)(2,1)}, bf16[784,1024]{1,0:T(8,128)(2,1)S(1)}, u32[]{:S(2)}, u32[]{:S(2)}) %collective-permute-start) | collective-permute-done | bytes 1605664 | tf_op jit(solution)/shard_map/ppermute | solution.py:371
  60.1 6.2 collective-permute-start.2
  70.2 10.2 %convolution_convert_fusion.5.refs_0_.refs_1_.refs_2_ = bf16[768,3072]{1,0:T(8,128)(2,1)} fusion(bf16[768,1024]{1,0:T(8,128)(2,1)S(1)} %get-tuple-element.170, bf16[1024,3328]{0,1:T(8,128)(2,1)} %all-gather.7.cloned.1.call-done), kind=kOutput, calls=%fused_computation.8 | convolution fusion | flops 4834197504 | bytes 12582912 | tf_op jit(solution)/shard_map/dot_general | solution.py:28
  81.3 16.1 %attn_fwd.4 = (f32[8,2,80,768]{3,2,1,0:T(8,128)}, f32[8,2,768]{2,1,0:T(2,128)}) custom-call(bf16[768,3072]{1,0:T(8,128)(2,1)} %convolution_convert_fusion.5.refs_0_.refs_1_.refs_2_, bf16[768,3072]{1,0:T(8,128)(2,1)} %convolution_convert_fusion.5.refs_0_.refs_1_.refs_2_, bf16[768,3072]{1,0:T(8,128)(2,1)} %convolution_convert_fusion.5.refs_0_.refs_1_.refs_2_, ...), custom_call_target="tpu_custom_call" | custom-call | flops 9663676416 | bytes 6291456 | tf_op jit(solution)/shard_map/attn_fwd/pallas_call | solution.py:155
  98.9 5.6 collective-permute-start.4
  106.0 9.5 %convolution_convert_fusion.4.refs_1_.refs_2_ = bf16[768,3072]{1,0:T(8,128)(2,1)} fusion(bf16[768,1024]{1,0:T(8,128)(2,1)S(1)} %copy-done.10, bf16[1024,3328]{0,1:T(8,128)(2,1)} %all-gather.7.cloned.1.call-done), kind=kOutput, calls=%fused_computation.7 | convolution fusion | flops 4834197504 | bytes 12582912 | tf_op jit(solution)/shard_map/dot_general | solution.py:28
  115.5 17.5 %attn_fwd.5 = (f32[8,2,80,768]{3,2,1,0:T(8,128)}, f32[8,2,768]{2,1,0:T(2,128)}) custom-call(bf16[768,3072]{1,0:T(8,128)(2,1)} %convolution_convert_fusion.5.refs_0_.refs_1_.refs_2_, bf16[768,3072]{1,0:T(8,128)(2,1)} %convolution_convert_fusion.4.refs_1_.refs_2_, bf16[768,3072]{1,0:T(8,128)(2,1)} %convolution_convert_fusion.4.refs_1_.refs_2_, ...), custom_call_target="tpu_custom_call" | custom-call | flops 9663676416 | bytes 6291456 | tf_op jit(solution)/shard_map/attn_fwd/pallas_call | solution.py:155
  133.0 3.2 collective-permute-done.4
  136.2 5.3 collective-permute-done.5
  141.5 2.9 select_select_fusion.1
  153.5 9.5 %convolution_convert_fusion.2.refs_1_.refs_2_ = bf16[768,3072]{1,0:T(8,128)(2,1)} fusion(bf16[768,1024]{1,0:T(8,128)(2,1)S(1)} %get-tuple-element.172, bf16[1024,3328]{0,1:T(8,128)(2,1)} %all-gather.7.cloned.1.call-done), kind=kOutput, calls=%fused_computation.5 | convolution fusion | flops 4834197504 | bytes 12582912 | tf_op jit(solution)/shard_map/dot_general | solution.py:28
  163.0 17.7 %attn_fwd.6 = (f32[8,2,80,768]{3,2,1,0:T(8,128)}, f32[8,2,768]{2,1,0:T(2,128)}) custom-call(bf16[768,3072]{1,0:T(8,128)(2,1)} %convolution_convert_fusion.5.refs_0_.refs_1_.refs_2_, bf16[768,3072]{1,0:T(8,128)(2,1)} %convolution_convert_fusion.2.refs_1_.refs_2_, bf16[768,3072]{1,0:T(8,128)(2,1)} %convolution_convert_fusion.2.refs_1_.refs_2_, ...), custom_call_target="tpu_custom_call" | custom-call | flops 9663676416 | bytes 6291456 | tf_op jit(solution)/shard_map/attn_fwd/pallas_call | solution.py:155
  180.7 9.5 %convolution_convert_fusion.3.refs_1_.refs_2_ = bf16[768,3072]{1,0:T(8,128)(2,1)} fusion(bf16[768,1024]{1,0:T(8,128)(2,1)S(1)} %copy-done.14, bf16[1024,3328]{0,1:T(8,128)(2,1)} %all-gather.7.cloned.1.call-done), kind=kOutput, calls=%fused_computation.6 | convolution fusion | flops 4834197504 | bytes 12582912 | tf_op jit(solution)/shard_map/dot_general | solution.py:28
  190.1 18.1 %attn_fwd.7 = (bf16[768,1024]{1,0:T(8,128)(2,1)}, f32[8,2,768]{2,1,0:T(2,128)}) custom-call(bf16[768,3072]{1,0:T(8,128)(2,1)} %convolution_convert_fusion.5.refs_0_.refs_1_.refs_2_, bf16[768,3072]{1,0:T(8,128)(2,1)} %convolution_convert_fusion.3.refs_1_.refs_2_, bf16[768,3072]{1,0:T(8,128)(2,1)} %convolution_convert_fusion.3.refs_1_.refs_2_, ...), custom_call_target="tpu_custom_call" | custom-call | flops 9663676416 | bytes 6291456 | tf_op jit(solution)/shard_map/attn_fwd/pallas_call | solution.py:155
  208.2 3.9 fusion.119
  215.6 21.3 %fc1_gelu.1 = (bf16[768,4096]{1,0:T(8,128)(2,1)}, bf16[768,4096]{1,0:T(8,128)(2,1)}) custom-call(bf16[768,1024]{1,0:T(8,128)(2,1)} %add_convert_fusion.x_ref, bf16[1024,4096]{1,0:T(8,128)(2,1)} %all-gather.11.cloned.1.call-done.w_ref), custom_call_target="tpu_custom_call" | custom-call | flops 6442450944 | bytes 22544384 | tf_op jit(solution)/shard_map/fc1_gelu/pallas_call | solution.py:306
  236.9 5.8 fusion.79
  247.7 2.8 collective-permute-start.8
  250.5 6.1 fusion.53
  262.9 9.0 %convolution_convert_fusion.1 = bf16[4096,1024]{1,0:T(8,128)(2,1)} fusion(bf16[768,4096]{1,0:T(8,128)(2,1)S(1)} %copy-done.80, f32[192,1024]{1,0:T(8,128)S(1)} %convolution_add_fusion, f32[576,1024]{1,0:T(8,128)S(1)} %copy-done.7), kind=kOutput, calls=%fused_computation.2 | convolution fusion | flops 6449790976 | bytes 17825792 | tf_op jit(solution)/shard_map/dot_general | solution.py:28
  276.3 13.2 %multiply_convert_fusion = bf16[768,4096]{1,0:T(8,128)(2,1)S(1)} fusion(bf16[768,4096]{1,0:T(8,128)(2,1)} %get-tuple-element.127, bf16[4096,1024]{1,0:T(8,128)(2,1)} %all-gather.13.cloned.1.call-done, f32[192,1024]{1,0:T(8,128)} %copy-done.18, f32[576,1024]{1,0:T(8,128)} %slice.183), kind=kOutput, calls=%fused_computation | convolution fusion | flops 6455033856 | bytes 24117248 | tf_op jit(solution)/shard_map/dot_general | solution.py:28
  289.6 13.1 %multiply_reduce_fusion = (bf16[1024]{0:T(1024)(128)(2,1)}, f32[768]{0:T(1024)S(1)}, f32[768]{0:T(1024)S(1)}, bf16[1024]{0:T(1024)(128)(2,1)}, f32[768,1024]{1,0:T(8,128)S(1)}) fusion(f32[768,1024]{1,0:T(8,128)S(1)} %copy-done.3, f32[768]{0:T(1024)S(1)} %add_rsqrt_fusion, f32[768]{0:T(1024)S(1)} %broadcast_multiply_fusion.4, f32[1024]{0:T(1024)S(1)} %bitcast.112, ...), kind=kOutput, calls=%fused_computation.68 | convolution fusion | flops 6449524736 | bytes 20992000 | tf_op jit(solution)/shard_map/dot_general | solution.py:28
  313.5 2.7 broadcast_in_dim.60
  328.9 9.1 %convolution_convert_fusion = bf16[1024,4096]{1,0:T(8,128)(2,1)} fusion(bf16[768,1024]{1,0:T(8,128)(2,1)S(1)} %copy-done.36, bf16[768,4096]{1,0:T(8,128)(2,1)S(1)} %bitcast.124), kind=kOutput, calls=%fused_computation.1 | convolution fusion | flops 6446645248 | bytes 16252928 | tf_op jit(solution)/shard_map/dot_general | solution.py:28
  342.4 6.2 slice.189
  349.1 6.0 collective-permute-start.12
  355.3 3.0 collective-permute-start.14
  358.3 72.0 %attn_bwd.2 = bf16[3072,384]{1,0:T(8,128)(2,1)} custom-call(bf16[3072,768]{1,0:T(8,128)(2,1)} %dynamic-slice_dynamic-update-slice_fusion.refs_0_.refs_1_.refs_2_, bf16[3072,768]{1,0:T(8,128)(2,1)} %dynamic-slice_dynamic-update-slice_fusion.refs_0_.refs_1_.refs_2_, bf16[3072,768]{1,0:T(8,128)(2,1)} %dynamic-slice_dynamic-update-slice_fusion.refs_0_.refs_1_.refs_2_, ...), custom_call_target="tpu_custom_call" | custom-call | flops 48318382080 | bytes 5505024 | tf_op jit(solution)/shard_map/attn_bwd/pallas_call | solution.py:262
  434.3 2.7 fusion.117
  442.3 72.1 %attn_bwd.3 = bf16[3072,384]{1,0:T(8,128)(2,1)} custom-call(bf16[3072,768]{1,0:T(8,128)(2,1)} %dynamic-slice_dynamic-update-slice_fusion.refs_0_.refs_1_.refs_2_, bf16[3072,768]{1,0:T(8,128)(2,1)} %dynamic-slice_dynamic-update-slice_fusion.refs_0_.refs_1_.refs_2_, bf16[3072,768]{1,0:T(8,128)(2,1)} %dynamic-slice_dynamic-update-slice_fusion.refs_0_.refs_1_.refs_2_, ...), custom_call_target="tpu_custom_call" | custom-call | flops 48318382080 | bytes 5505024 | tf_op jit(solution)/shard_map/attn_bwd/pallas_call | solution.py:262
  515.3 2.9 fusion.116
  518.2 5.6 collective-permute-start.21
  523.8 4.4 collective-permute-start.22
  529.3 3.5 broadcast_in_dim.112
  548.8 5.6 convolution_convert_fusion.9
  554.4 5.4 convolution_convert_fusion.8
  561.9 3.5 constant_dynamic-slice_fusion.13
  566.7 3.9 fusion.39
  570.7 4.0 fusion.61
  574.7 3.2 fusion.20
  577.9 14.5 %collective-permute-start.24 = (bf16[128,1408]{1,0:T(8,128)(2,1)}, bf16[128,1408]{1,0:T(8,128)(2,1)S(1)}, u32[]{:S(2)}, u32[]{:S(2)}) collective-permute-start(bf16[128,1408]{1,0:T(8,128)(2,1)} %pad_maximum_fusion.5), channel_id=1, source_target_pairs={{0,1},{1,2},{2,3},{3,0},{4,5},{5,6},{6,7},{7,4},{8,9},{9,10},{10,1... | collective-permute-start | bytes 1081352 | tf_op jit(solution)/shard_map/ppermute | solution.py:376
  594.4 2.8 collective-permute-start.26
  597.9 12.3 %psum.7 = f32[2,1024]{1,0:T(2,128)S(1)} all-reduce(f32[2,1024]{1,0:T(2,128)S(1)} %pad_maximum_fusion.8), channel_id=1, replica_groups=mesh['scene'=8,'seq'=4] {'scene'}, use_global_device_ids=true, to_apply=%region_23.24 | all-reduce | flops 2048 | bytes 16384 | tf_op jit(solution)/shard_map/psum | solution.py:652
  610.3 4.3 fusion.24
  628.5 25.4 %collective-permute-done.30 = bf16[128,768]{0,1:T(8,128)(2,1)S(1)} collective-permute-done((bf16[128,768]{0,1:T(8,128)(2,1)S(1)}, bf16[128,768]{0,1:T(8,128)(2,1)S(1)}, u32[]{:S(2)}, u32[]{:S(2)}) %collective-permute-start.30) | collective-permute-done | bytes 196640 | tf_op jit(solution)/shard_map/ppermute | solution.py:376
  654.0 14.6 %collective-permute-done.31 = bf16[128,768]{0,1:T(8,128)(2,1)S(1)} collective-permute-done((bf16[128,768]{0,1:T(8,128)(2,1)S(1)}, bf16[128,768]{0,1:T(8,128)(2,1)S(1)}, u32[]{:S(2)}, u32[]{:S(2)}) %collective-permute-start.31) | collective-permute-done | bytes 196640 | tf_op jit(solution)/shard_map/ppermute | solution.py:376
  668.7 4.0 collective-permute-done.32
  (434 shorter events, 149.9 us)
Async XLA Ops:
  7.2 60.0 %all-gather.7.cloned.1.call-start = ((), (), s32[]{:S(2)}) async-start(), calls=%async_computation.4 | async-start | bytes 7667712 | tf_op jit(solution)/shard_map/all_gather | solution.py:413
  10.3 197.9 %all-gather.9.cloned.1.call-start = ((), (), s32[]{:S(2)}) async-start(), calls=%async_computation.5 | async-start | bytes 2359296 | tf_op jit(solution)/shard_map/all_gather | solution.py:410
  11.1 204.5 %all-gather.11.cloned.1.call-start = ((), (), s32[]{:S(2)}) async-start(), calls=%async_computation.6 | async-start | bytes 9437184 | tf_op jit(solution)/shard_map/all_gather | solution.py:410
  13.9 223.0 %all-gather.13.cloned.1.call-start = ((), (), s32[]{:S(2)}) async-start(), calls=%async_computation.7 | async-start | bytes 9437184 | tf_op jit(solution)/shard_map/all_gather | solution.py:410
  15.5 40.4 %collective-permute-start = (bf16[784,1024]{1,0:T(8,128)(2,1)}, bf16[784,1024]{1,0:T(8,128)(2,1)S(1)}, u32[]{:S(2)}, u32[]{:S(2)}) collective-permute-start(bf16[784,1024]{1,0:T(8,128)(2,1)} %fusion.71), channel_id=1, source_target_pairs={{1,0},{2,1},{3,2},{5,4},{6,5},{7,6},{9,8},{10,9},{11,10},{13,12},{... | collective-permute-start | bytes 4816904 | tf_op jit(solution)/shard_map/ppermute | solution.py:371
  16.9 40.2 %collective-permute-start.1 = (bf16[784,1024]{1,0:T(8,128)(2,1)}, bf16[784,1024]{1,0:T(8,128)(2,1)}, u32[]{:S(2)}, u32[]{:S(2)}) collective-permute-start(bf16[784,1024]{1,0:T(8,128)(2,1)} %fusion.71), channel_id=1, source_target_pairs={{0,1},{1,2},{2,3},{4,5},{5,6},{6,7},{8,9},{9,10},{10,11},{12,13},{... | collective-permute-start | bytes 4816904 | tf_op jit(solution)/shard_map/ppermute | solution.py:371
  24.8 316.4 %reduce-scatter.7.cloned.1.call-start = ((), (), s32[]{:S(2)}) async-start(), calls=%async_computation.8 | async-start | bytes 9437184 | tf_op jit(solution)/shard_map/reduce_scatter | solution.py:550
  33.4 34.6 %copy-start.57 = (f32[768]{0:T(1024)}, f32[768]{0:T(1024)S(1)}, u32[]{:S(2)}) copy-start(f32[768]{0:T(1024)S(1)} %broadcast_multiply_fusion.8) | copy-start | bytes 9220
  34.0 46.4 %copy-start.61 = (f32[768]{0:T(1024)}, f32[768]{0:T(1024)S(1)}, u32[]{:S(2)}) copy-start(f32[768]{0:T(1024)S(1)} %add_rsqrt_fusion.4) | copy-start | bytes 9220
  58.8 38.9 %collective-permute-start.3 = (bf16[784,1024]{1,0:T(8,128)(2,1)}, bf16[784,1024]{1,0:T(8,128)(2,1)}, u32[]{:S(2)}, u32[]{:S(2)}) collective-permute-start(bf16[784,1024]{1,0:T(8,128)(2,1)} %copy-done.9), channel_id=1, source_target_pairs={{1,0},{2,1},{3,2},{5,4},{6,5},{7,6},{9,8},{10,9},{11,10},{13,12},{... | collective-permute-start | bytes 4816904 | tf_op jit(solution)/shard_map/ppermute | solution.py:371
  60.1 38.8 %collective-permute-start.2 = (bf16[784,1024]{1,0:T(8,128)(2,1)}, bf16[784,1024]{1,0:T(8,128)(2,1)}, u32[]{:S(2)}, u32[]{:S(2)}) collective-permute-start(bf16[784,1024]{1,0:T(8,128)(2,1)} %collective-permute-done.1), channel_id=1, source_target_pairs={{0,1},{1,2},{2,3},{4,5},{5,6},{6,7},{8,9},{9,10},{10,11},{12,13},{... | collective-permute-start | bytes 4816904 | tf_op jit(solution)/shard_map/ppermute | solution.py:371
  68.0 81.7 %copy-start.59 = (f32[1024,1]{0,1:T(1,128)}, f32[1024,1]{0,1:T(1,128)S(1)}, u32[]{:S(2)}) copy-start(f32[1024,1]{0,1:T(1,128)S(1)} %get-tuple-element.336) | copy-start | bytes 12292
  98.9 37.3 %collective-permute-start.4 = (bf16[784,1024]{1,0:T(8,128)(2,1)}, bf16[784,1024]{1,0:T(8,128)(2,1)}, u32[]{:S(2)}, u32[]{:S(2)}) collective-permute-start(bf16[784,1024]{1,0:T(8,128)(2,1)} %collective-permute-done.2), channel_id=1, source_target_pairs={{0,1},{1,2},{2,3},{4,5},{5,6},{6,7},{8,9},{9,10},{10,11},{12,13},{... | collective-permute-start | bytes 4816904 | tf_op jit(solution)/shard_map/ppermute | solution.py:371
  104.5 37.0 %collective-permute-start.5 = (bf16[784,1024]{1,0:T(8,128)(2,1)}, bf16[784,1024]{1,0:T(8,128)(2,1)}, u32[]{:S(2)}, u32[]{:S(2)}) collective-permute-start(bf16[784,1024]{1,0:T(8,128)(2,1)} %collective-permute-done.3), channel_id=1, source_target_pairs={{1,0},{2,1},{3,2},{5,4},{6,5},{7,6},{9,8},{10,9},{11,10},{13,12},{... | collective-permute-start | bytes 4816904 | tf_op jit(solution)/shard_map/ppermute | solution.py:371
  242.7 83.6 %copy-start.34 = (bf16[192,1024]{1,0:T(8,128)(2,1)}, bf16[192,1024]{1,0:T(8,128)(2,1)S(1)}, u32[]{:S(2)}) copy-start(bf16[192,1024]{1,0:T(8,128)(2,1)S(1)} %fusion.79) | copy-start | bytes 1179652
  244.9 11.7 %collective-permute-start.6 = (bf16[192,128]{1,0:T(8,128)(2,1)S(1)}, bf16[192,128]{1,0:T(8,128)(2,1)S(1)}, u32[]{:S(2)}, u32[]{:S(2)}) collective-permute-start(bf16[192,128]{1,0:T(8,128)(2,1)S(1)} %get-tuple-element.347), channel_id=1, source_target_pairs={{0,1},{1,2},{2,3},{3,0},{4,5},{5,6},{6,7},{7,4},{8,9},{9,10},{10,1... | collective-permute-start | bytes 147464 | tf_op jit(solution)/shard_map/ppermute | solution.py:376
  246.3 10.4 %collective-permute-start.7 = (bf16[192,128]{1,0:T(8,128)(2,1)S(1)}, bf16[192,128]{1,0:T(8,128)(2,1)S(1)}, u32[]{:S(2)}, u32[]{:S(2)}) collective-permute-start(bf16[192,128]{1,0:T(8,128)(2,1)S(1)} %get-tuple-element.347), channel_id=1, source_target_pairs={{0,2},{1,3},{2,0},{3,1},{4,6},{5,7},{6,4},{7,5},{8,10},{9,11},{10,... | collective-permute-start | bytes 147464 | tf_op jit(solution)/shard_map/ppermute | solution.py:376
  247.7 9.0 %collective-permute-start.8 = (bf16[192,128]{1,0:T(8,128)(2,1)S(1)}, bf16[192,128]{1,0:T(8,128)(2,1)S(1)}, u32[]{:S(2)}, u32[]{:S(2)}) collective-permute-start(bf16[192,128]{1,0:T(8,128)(2,1)S(1)} %get-tuple-element.347), channel_id=1, source_target_pairs={{0,3},{1,0},{2,1},{3,2},{4,7},{5,4},{6,5},{7,6},{8,11},{9,8},{10,9... | collective-permute-start | bytes 147464 | tf_op jit(solution)/shard_map/ppermute | solution.py:376
  271.9 243.4 %reduce-scatter.11.cloned.1.call-start = ((), (), s32[]{:S(2)}) async-start(), calls=%async_computation.10 | async-start | bytes 3538944 | tf_op jit(solution)/shard_map/reduce_scatter | solution.py:550
  311.1 28.9 %collective-permute-start.10 = (bf16[848,256]{1,0:T(8,128)(2,1)}, bf16[848,256]{1,0:T(8,128)(2,1)}, u32[]{:S(2)}, u32[]{:S(2)}) collective-permute-start(bf16[848,256]{1,0:T(8,128)(2,1)} %get-tuple-element.315), channel_id=1, source_target_pairs={{0,2},{1,3},{2,0},{3,1},{4,6},{5,7},{6,4},{7,5},{8,10},{9,11},{10,... | collective-permute-start | bytes 1302536 | tf_op jit(solution)/shard_map/ppermute | solution.py:376
  311.1 28.9 %collective-permute-start.11 = (bf16[848,256]{1,0:T(8,128)(2,1)}, bf16[848,256]{1,0:T(8,128)(2,1)}, u32[]{:S(2)}, u32[]{:S(2)}) collective-permute-start(bf16[848,256]{1,0:T(8,128)(2,1)} %get-tuple-element.314), channel_id=1, source_target_pairs={{0,3},{1,0},{2,1},{3,2},{4,7},{5,4},{6,5},{7,6},{8,11},{9,8},{10,9... | collective-permute-start | bytes 1302536 | tf_op jit(solution)/shard_map/ppermute | solution.py:376
  312.1 28.0 %collective-permute-start.9 = (bf16[848,256]{1,0:T(8,128)(2,1)S(1)}, bf16[848,256]{1,0:T(8,128)(2,1)}, u32[]{:S(2)}, u32[]{:S(2)}) collective-permute-start(bf16[848,256]{1,0:T(8,128)(2,1)S(1)} %get-tuple-element.316), channel_id=1, source_target_pairs={{0,1},{1,2},{2,3},{3,0},{4,5},{5,6},{6,7},{7,4},{8,9},{9,10},{10,1... | collective-permute-start | bytes 1302536 | tf_op jit(solution)/shard_map/ppermute | solution.py:376
  341.2 174.1 %reduce-scatter.9.cloned.1.call-start = ((), (), s32[]{:S(2)}) async-start(), calls=%async_computation.9 | async-start | bytes 9437184 | tf_op jit(solution)/shard_map/reduce_scatter | solution.py:550
  342.0 272.7 %reduce-scatter.13.cloned.1.call-start = ((), (), s32[]{:S(2)}) async-start(), calls=%async_computation.12 | async-start | bytes 1769472
  349.1 81.2 %collective-permute-start.12 = (bf16[512,256]{1,0:T(8,128)(2,1)S(1)}, bf16[512,256]{1,0:T(8,128)(2,1)S(1)}, u32[]{:S(2)}, u32[]{:S(2)}) collective-permute-start(bf16[512,256]{1,0:T(8,128)(2,1)S(1)} %get-tuple-element.324), channel_id=1, source_target_pairs={{0,1},{1,2},{2,3},{3,0},{4,5},{5,6},{6,7},{7,4},{8,9},{9,10},{10,1... | collective-permute-start | bytes 786440 | tf_op jit(solution)/shard_map/ppermute | solution.py:376
  355.1 75.2 %collective-permute-start.13 = (bf16[512,256]{1,0:T(8,128)(2,1)S(1)}, bf16[512,256]{1,0:T(8,128)(2,1)S(1)}, u32[]{:S(2)}, u32[]{:S(2)}) collective-permute-start(bf16[512,256]{1,0:T(8,128)(2,1)S(1)} %get-tuple-element.323), channel_id=1, source_target_pairs={{0,2},{1,3},{2,0},{3,1},{4,6},{5,7},{6,4},{7,5},{8,10},{9,11},{10,... | collective-permute-start | bytes 786440 | tf_op jit(solution)/shard_map/ppermute | solution.py:376
  355.3 75.0 %collective-permute-start.14 = (bf16[512,256]{1,0:T(8,128)(2,1)S(1)}, bf16[512,256]{1,0:T(8,128)(2,1)S(1)}, u32[]{:S(2)}, u32[]{:S(2)}) collective-permute-start(bf16[512,256]{1,0:T(8,128)(2,1)S(1)} %get-tuple-element.322), channel_id=1, source_target_pairs={{0,3},{1,0},{2,1},{3,2},{4,7},{5,4},{6,5},{7,6},{8,11},{9,8},{10,9... | collective-permute-start | bytes 786440 | tf_op jit(solution)/shard_map/ppermute | solution.py:376
  430.5 11.1 %collective-permute-start.18 = (bf16[512,256]{1,0:T(8,128)(2,1)S(1)}, bf16[512,256]{1,0:T(8,128)(2,1)S(1)}, u32[]{:S(2)}, u32[]{:S(2)}) collective-permute-start(bf16[512,256]{1,0:T(8,128)(2,1)S(1)} %add_convert_fusion.2), channel_id=1, source_target_pairs={{0,1},{1,2},{2,3},{3,0},{4,5},{5,6},{6,7},{7,4},{8,9},{9,10},{10,1... | collective-permute-start | bytes 786440 | tf_op jit(solution)/shard_map/ppermute | solution.py:376
  430.5 83.9 %collective-permute-start.19 = (bf16[512,256]{1,0:T(8,128)(2,1)S(1)}, bf16[512,256]{1,0:T(8,128)(2,1)S(1)}, u32[]{:S(2)}, u32[]{:S(2)}) collective-permute-start(bf16[512,256]{1,0:T(8,128)(2,1)S(1)} %add_convert_fusion.2), channel_id=1, source_target_pairs={{0,2},{1,3},{2,0},{3,1},{4,6},{5,7},{6,4},{7,5},{8,10},{9,11},{10,... | collective-permute-start | bytes 786440 | tf_op jit(solution)/shard_map/ppermute | solution.py:376
  432.5 81.9 %collective-permute-start.20 = (bf16[512,256]{1,0:T(8,128)(2,1)S(1)}, bf16[512,256]{1,0:T(8,128)(2,1)S(1)}, u32[]{:S(2)}, u32[]{:S(2)}) collective-permute-start(bf16[512,256]{1,0:T(8,128)(2,1)S(1)} %add_convert_fusion.2), channel_id=1, source_target_pairs={{0,3},{1,0},{2,1},{3,2},{4,7},{5,4},{6,5},{7,6},{8,11},{9,8},{10,9... | collective-permute-start | bytes 786440 | tf_op jit(solution)/shard_map/ppermute | solution.py:376
  437.1 77.4 %collective-permute-start.15 = (bf16[768,384]{1,0:T(8,128)(2,1)S(1)}, bf16[768,384]{1,0:T(8,128)(2,1)S(1)}, u32[]{:S(2)}, u32[]{:S(2)}) collective-permute-start(bf16[768,384]{1,0:T(8,128)(2,1)S(1)} %get-tuple-element.312), channel_id=1, source_target_pairs={{0,1},{1,2},{2,3},{3,0},{4,5},{5,6},{6,7},{7,4},{8,9},{9,10},{10,1... | collective-permute-start | bytes 1769480 | tf_op jit(solution)/shard_map/ppermute | solution.py:376
  437.8 76.8 %collective-permute-start.16 = (bf16[768,384]{1,0:T(8,128)(2,1)S(1)}, bf16[768,384]{1,0:T(8,128)(2,1)}, u32[]{:S(2)}, u32[]{:S(2)}) collective-permute-start(bf16[768,384]{1,0:T(8,128)(2,1)S(1)} %get-tuple-element.311), channel_id=1, source_target_pairs={{0,2},{1,3},{2,0},{3,1},{4,6},{5,7},{6,4},{7,5},{8,10},{9,11},{10,... | collective-permute-start | bytes 1769480 | tf_op jit(solution)/shard_map/ppermute | solution.py:376
  441.6 73.7 %collective-permute-start.17 = (bf16[768,384]{1,0:T(8,128)(2,1)S(1)}, bf16[768,384]{1,0:T(8,128)(2,1)}, u32[]{:S(2)}, u32[]{:S(2)}) collective-permute-start(bf16[768,384]{1,0:T(8,128)(2,1)S(1)} %get-tuple-element.310), channel_id=1, source_target_pairs={{0,3},{1,0},{2,1},{3,2},{4,7},{5,4},{6,5},{7,6},{8,11},{9,8},{10,9... | collective-permute-start | bytes 1769480 | tf_op jit(solution)/shard_map/ppermute | solution.py:376
  518.2 27.9 %collective-permute-start.21 = (bf16[768,384]{1,0:T(8,128)(2,1)S(1)}, bf16[768,384]{1,0:T(8,128)(2,1)S(1)}, u32[]{:S(2)}, u32[]{:S(2)}) collective-permute-start(bf16[768,384]{1,0:T(8,128)(2,1)S(1)} %get-tuple-element.308), channel_id=1, source_target_pairs={{0,1},{1,2},{2,3},{3,0},{4,5},{5,6},{6,7},{7,4},{8,9},{9,10},{10,1... | collective-permute-start | bytes 1769480 | tf_op jit(solution)/shard_map/ppermute | solution.py:376
  523.8 46.9 %collective-permute-start.22 = (bf16[768,384]{1,0:T(8,128)(2,1)}, bf16[768,384]{1,0:T(8,128)(2,1)}, u32[]{:S(2)}, u32[]{:S(2)}) collective-permute-start(bf16[768,384]{1,0:T(8,128)(2,1)} %get-tuple-element.307), channel_id=1, source_target_pairs={{0,2},{1,3},{2,0},{3,1},{4,6},{5,7},{6,4},{7,5},{8,10},{9,11},{10,... | collective-permute-start | bytes 1769480 | tf_op jit(solution)/shard_map/ppermute | solution.py:376
  528.2 42.5 %collective-permute-start.23 = (bf16[768,384]{1,0:T(8,128)(2,1)}, bf16[768,384]{1,0:T(8,128)(2,1)}, u32[]{:S(2)}, u32[]{:S(2)}) collective-permute-start(bf16[768,384]{1,0:T(8,128)(2,1)} %get-tuple-element.306), channel_id=1, source_target_pairs={{0,3},{1,0},{2,1},{3,2},{4,7},{5,4},{6,5},{7,6},{8,11},{9,8},{10,9... | collective-permute-start | bytes 1769480 | tf_op jit(solution)/shard_map/ppermute | solution.py:376
  561.5 124.1 %all-gather.15.cloned.1.call-start = ((), (), s32[]{:S(2)}) async-start(), calls=%async_computation.11 | async-start | bytes 2359296 | tf_op jit(solution)/shard_map/all_gather | solution.py:643
  577.9 37.9 %collective-permute-start.24 = (bf16[128,1408]{1,0:T(8,128)(2,1)}, bf16[128,1408]{1,0:T(8,128)(2,1)S(1)}, u32[]{:S(2)}, u32[]{:S(2)}) collective-permute-start(bf16[128,1408]{1,0:T(8,128)(2,1)} %pad_maximum_fusion.5), channel_id=1, source_target_pairs={{0,1},{1,2},{2,3},{3,0},{4,5},{5,6},{6,7},{7,4},{8,9},{9,10},{10,1... | collective-permute-start | bytes 1081352 | tf_op jit(solution)/shard_map/ppermute | solution.py:376
  592.5 23.4 %collective-permute-start.25 = (bf16[128,1408]{1,0:T(8,128)(2,1)}, bf16[128,1408]{1,0:T(8,128)(2,1)S(1)}, u32[]{:S(2)}, u32[]{:S(2)}) collective-permute-start(bf16[128,1408]{1,0:T(8,128)(2,1)} %pad_maximum_fusion.6), channel_id=1, source_target_pairs={{0,2},{1,3},{2,0},{3,1},{4,6},{5,7},{6,4},{7,5},{8,10},{9,11},{10,... | collective-permute-start | bytes 1081352 | tf_op jit(solution)/shard_map/ppermute | solution.py:376
  594.4 21.5 %collective-permute-start.26 = (bf16[128,1408]{1,0:T(8,128)(2,1)}, bf16[128,1408]{1,0:T(8,128)(2,1)}, u32[]{:S(2)}, u32[]{:S(2)}) collective-permute-start(bf16[128,1408]{1,0:T(8,128)(2,1)} %pad_maximum_fusion.7), channel_id=1, source_target_pairs={{0,3},{1,0},{2,1},{3,2},{4,7},{5,4},{6,5},{7,6},{8,11},{9,8},{10,9... | collective-permute-start | bytes 1081352 | tf_op jit(solution)/shard_map/ppermute | solution.py:376
  618.8 55.7 %collective-permute-start.27 = (bf16[128,1536]{1,0:T(8,128)(2,1)}, bf16[128,1536]{1,0:T(8,128)(2,1)}, u32[]{:S(2)}, u32[]{:S(2)}) collective-permute-start(bf16[128,1536]{1,0:T(8,128)(2,1)} %fusion.84), channel_id=1, source_target_pairs={{0,1},{1,2},{2,3},{3,0},{4,5},{5,6},{6,7},{7,4},{8,9},{9,10},{10,1... | collective-permute-start | bytes 1179656 | tf_op jit(solution)/shard_map/ppermute | solution.py:376
  619.0 56.6 %collective-permute-start.28 = (bf16[128,1536]{1,0:T(8,128)(2,1)}, bf16[128,1536]{1,0:T(8,128)(2,1)}, u32[]{:S(2)}, u32[]{:S(2)}) collective-permute-start(bf16[128,1536]{1,0:T(8,128)(2,1)} %fusion.84), channel_id=1, source_target_pairs={{0,2},{1,3},{2,0},{3,1},{4,6},{5,7},{6,4},{7,5},{8,10},{9,11},{10,... | collective-permute-start | bytes 1179656 | tf_op jit(solution)/shard_map/ppermute | solution.py:376
  621.4 55.1 %collective-permute-start.29 = (bf16[128,1536]{1,0:T(8,128)(2,1)}, bf16[128,1536]{1,0:T(8,128)(2,1)}, u32[]{:S(2)}, u32[]{:S(2)}) collective-permute-start(bf16[128,1536]{1,0:T(8,128)(2,1)} %fusion.84), channel_id=1, source_target_pairs={{0,3},{1,0},{2,1},{3,2},{4,7},{5,4},{6,5},{7,6},{8,11},{9,8},{10,9... | collective-permute-start | bytes 1179656 | tf_op jit(solution)/shard_map/ppermute | solution.py:376
  622.8 31.1 %collective-permute-start.30 = (bf16[128,768]{0,1:T(8,128)(2,1)S(1)}, bf16[128,768]{0,1:T(8,128)(2,1)S(1)}, u32[]{:S(2)}, u32[]{:S(2)}) collective-permute-start(bf16[128,768]{0,1:T(8,128)(2,1)S(1)} %copy.133), channel_id=1, source_target_pairs={{0,1},{1,2},{2,3},{3,0},{4,5},{5,6},{6,7},{7,4},{8,9},{9,10},{10,1... | collective-permute-start | bytes 589832 | tf_op jit(solution)/shard_map/ppermute | solution.py:376
  623.4 45.2 %collective-permute-start.31 = (bf16[128,768]{0,1:T(8,128)(2,1)S(1)}, bf16[128,768]{0,1:T(8,128)(2,1)S(1)}, u32[]{:S(2)}, u32[]{:S(2)}) collective-permute-start(bf16[128,768]{0,1:T(8,128)(2,1)S(1)} %copy.133), channel_id=1, source_target_pairs={{0,2},{1,3},{2,0},{3,1},{4,6},{5,7},{6,4},{7,5},{8,10},{9,11},{10,... | collective-permute-start | bytes 589832 | tf_op jit(solution)/shard_map/ppermute | solution.py:376
  628.4 44.3 %copy-start.27 = (f32[128,4096]{1,0:T(8,128)}, f32[128,4096]{1,0:T(8,128)S(1)}, u32[]{:S(2)}) copy-start(f32[128,4096]{1,0:T(8,128)S(1)} %convert_dynamic-update-slice_fusion.3) | copy-start | bytes 6291460
  628.5 44.2 %copy-start.20 = (f32[128,1536]{1,0:T(8,128)}, f32[128,1536]{1,0:T(8,128)S(1)}, u32[]{:S(2)}) copy-start(f32[128,1536]{1,0:T(8,128)S(1)} %convert_dynamic-update-slice_fusion.15) | copy-start | bytes 2359300
  654.0 18.7 %collective-permute-start.32 = (bf16[128,768]{0,1:T(8,128)(2,1)S(1)}, bf16[128,768]{0,1:T(8,128)(2,1)S(1)}, u32[]{:S(2)}, u32[]{:S(2)}) collective-permute-start(bf16[128,768]{0,1:T(8,128)(2,1)S(1)} %copy.133), channel_id=1, source_target_pairs={{0,3},{1,0},{2,1},{3,2},{4,7},{5,4},{6,5},{7,6},{8,11},{9,8},{10,9... | collective-permute-start | bytes 589832 | tf_op jit(solution)/shard_map/ppermute | solution.py:376
  (78 other events, 445.6 us)
Sparse Core Ops, SparseCore 0:
  10.5 51.6 all-gather.6
  64.6 27.7 all-gather.8
  94.3 54.2 all-gather.10
  150.3 54.2 all-gather.12
  272.0 69.1 reduce-scatter.6
  344.5 46.0 reduce-scatter.10
  394.0 71.5 reduce-scatter.8
  561.7 51.7 reduce-scatter.12
  615.4 27.7 all-gather.14
